TPU v7x, 32 devices: a whole 2x2x4 slice. The times are simulated.
32 devices in a mesh: section: 2 (over y), tensor: 2 (over core), dp: 8 (over z, x).
Axes of the slice: x: 2, y: 2, z: 4, core: 2. Of those that a mesh axis runs over, the one named last changes fastest.
Arguments:
- patches: bfloat16 [18688, 768], P('dp'), may hold values from -6 to 6
- out_grad: bfloat16 [18688, 768], P('dp'), may hold values from -6 to 6
- large_place: int32 [16], P('dp'), may hold values from 0 to 3, as said below
- norm1_gain: float32 [2, 768], P('section'), may hold values from 0.5 to 1.5
- norm1_bias: float32 [2, 768], P('section'), may hold values from -1.75 to 1.75
- qkv_weight: bfloat16 [2, 3, 768, 768], P('section', None, None, 'tensor'), may hold values from -0.21875 to 0.21875
- qv_bias: float32 [2, 2, 768], P('section', None, 'tensor'), may hold values from -1.75 to 1.75
- proj_weight: bfloat16 [2, 768, 768], P('section', 'tensor'), may hold values from -1.75 to 1.75
- proj_bias: float32 [2, 768], P('section'), may hold values from -1.75 to 1.75
- norm2_gain: float32 [2, 768], P('section'), may hold values from 0.5 to 1.5
- norm2_bias: float32 [2, 768], P('section'), may hold values from -1.75 to 1.75
- up_weight: bfloat16 [2, 768, 3072], P('section', None, 'tensor'), may hold values from -0.21875 to 0.21875
- up_bias: float32 [2, 3072], P('section', 'tensor'), may hold values from -1.75 to 1.75
- down_weight: bfloat16 [2, 3072, 768], P('section', 'tensor'), may hold values from -0.109375 to 0.109375
- down_bias: float32 [2, 768], P('section'), may hold values from -1.75 to 1.75
Outputs:
- layer_outputs: bfloat16 [2, 18688, 768], P('section', 'dp')
- layer_input_grads: bfloat16 [2, 18688, 768], P('section', 'dp')
- grad_norm1_gain: float32 [2, 768], P('section')
- grad_norm1_bias: float32 [2, 768], P('section')
- grad_qkv_weight: float32 [2, 3, 768, 768], P('section', None, None, 'tensor')
- grad_qv_bias: float32 [2, 2, 768], P('section', None, 'tensor')
- grad_proj_weight: float32 [2, 768, 768], P('section', 'tensor')
- grad_proj_bias: float32 [2, 768], P('section')
- grad_norm2_gain: float32 [2, 768], P('section')
- grad_norm2_bias: float32 [2, 768], P('section')
- grad_up_weight: float32 [2, 768, 3072], P('section', None, 'tensor')
- grad_up_bias: float32 [2, 3072], P('section', 'tensor')
- grad_down_weight: float32 [2, 3072, 768], P('section', 'tensor')
- grad_down_bias: float32 [2, 768], P('section')
Inputs may be any that keep to these rules, and one draw needn't show every extreme that they name: `large_place`: the large image's slot within its micro-batch of 4 images; every slot occurs.
All inputs are finite; a program needn't handle non-finite values.
Results may differ from a plain program's by a relative error of at most 0.018.
Values may be sent and summed in bfloat16 or wider, within the bound.
A program may use at most 320 MiB of HBM per device.

v0:
```python
import jax
import jax.numpy as jnp
from jax import lax
from jax.sharding import PartitionSpec as P

HD = 64
LEN_SMALL = 197
LEN_LARGE = 577
SMALL_MB = 3


EPSILON = 1e-06
MASKED = -1e30


def shifted(array, axis, by):
    count = lax.axis_size(axis)
    pairs = [(i, i + by) for i in range(count) if 0 <= i + by < count]
    return lax.ppermute(array, axis, pairs)


def layer_norm(values, scale_gain, offset):
    average = jnp.mean(values, axis=-1, keepdims=True)
    centred = values - average
    variance = jnp.mean(centred * centred, axis=-1, keepdims=True)
    return centred * lax.rsqrt(variance + EPSILON) * scale_gain + offset


def gelu_exact(values):
    return jax.nn.gelu(values, approximate=False)


def inner_rows(left_side, right_side):
    return lax.dot_general(
        left_side, right_side, (((0,), (0,)), ((), ())), preferred_element_type=jnp.float32
    )


def times_transpose(left_side, right_side):
    return lax.dot_general(
        left_side, right_side, (((1,), (1,)), ((), ())), preferred_element_type=jnp.float32
    )


def segment_ids(large_slot, length):
    position = jnp.arange(length, dtype=jnp.int32)
    slot_marks = jnp.arange(1, SMALL_MB + 1, dtype=jnp.int32)
    starts = slot_marks * LEN_SMALL + (LEN_LARGE - LEN_SMALL) * (slot_marks > large_slot).astype(
        jnp.int32
    )
    return jnp.sum((position[:, None] >= starts[None, :]).astype(jnp.int32), axis=1)


def block_scores(query_block, keys_all, segment_block, segment):
    scores = jnp.einsum(
        "qhd,khd->hqk", query_block, keys_all, preferred_element_type=jnp.float32
    ) * HD ** (-0.5)
    same_image = segment_block[:, None] == segment[None, :]
    return jnp.where(same_image[None], scores, MASKED)


def split_heads(qkv_all):
    num_rows, local_width = (qkv_all.shape[1], qkv_all.shape[2])
    local_heads = local_width // HD
    return (
        qkv_all[0].reshape(num_rows, local_heads, HD),
        qkv_all[1].reshape(num_rows, local_heads, HD),
        qkv_all[2].reshape(num_rows, local_heads, HD),
    )


def attend_forward(qkv_all, segment):
    num_rows, local_width = (qkv_all.shape[1], qkv_all.shape[2])
    queries, keys_all, values_all = split_heads(qkv_all)
    half_rows = num_rows // 2
    pieces_out = []
    log_totals = []
    for block_num in range(2):
        row_start = block_num * half_rows
        row_stop = row_start + half_rows
        scores = block_scores(
            queries[row_start:row_stop], keys_all, segment[row_start:row_stop], segment
        )
        top_score = jnp.max(scores, axis=-1, keepdims=True)
        exp_scores = jnp.exp(scores - top_score)
        row_total = jnp.sum(exp_scores, axis=-1, keepdims=True)
        probabilities = (exp_scores / row_total).astype(jnp.bfloat16)
        pieces_out.append(
            jnp.einsum(
                "hqk,khd->qhd", probabilities, values_all, preferred_element_type=jnp.float32
            )
        )
        log_totals.append((top_score + jnp.log(row_total))[..., 0])
    attended = (
        jnp.concatenate(pieces_out, axis=0).reshape(num_rows, local_width).astype(jnp.bfloat16)
    )
    return (attended, jnp.concatenate(log_totals, axis=1))


def attend_backward(qkv_all, segment, log_totals, grad_attended):
    num_rows, local_width = (qkv_all.shape[1], qkv_all.shape[2])
    queries, keys_all, values_all = split_heads(qkv_all)
    grad_heads = grad_attended.reshape(queries.shape)
    half_rows = num_rows // 2
    grad_keys = jnp.zeros(keys_all.shape, jnp.float32)
    grad_values = jnp.zeros(values_all.shape, jnp.float32)
    grad_query_list = []
    for block_num in range(2):
        row_start = block_num * half_rows
        row_stop = row_start + half_rows
        scores = block_scores(
            queries[row_start:row_stop], keys_all, segment[row_start:row_stop], segment
        )
        probabilities = jnp.exp(scores - log_totals[:, row_start:row_stop, None])
        grad_block = grad_heads[row_start:row_stop]
        grad_values = grad_values + jnp.einsum(
            "hqk,qhd->khd",
            probabilities.astype(jnp.bfloat16),
            grad_block,
            preferred_element_type=jnp.float32,
        )
        grad_probs = jnp.einsum(
            "qhd,khd->hqk", grad_block, values_all, preferred_element_type=jnp.float32
        )
        grad_scores = (
            probabilities
            * (grad_probs - jnp.sum(probabilities * grad_probs, axis=-1, keepdims=True))
        ).astype(jnp.bfloat16)
        grad_query_list.append(
            jnp.einsum("hqk,khd->qhd", grad_scores, keys_all, preferred_element_type=jnp.float32)
            * HD ** (-0.5)
        )
        grad_keys = grad_keys + jnp.einsum(
            "hqk,qhd->khd",
            grad_scores,
            queries[row_start:row_stop],
            preferred_element_type=jnp.float32,
        ) * HD ** (-0.5)
    grad_queries = jnp.concatenate(grad_query_list, axis=0)
    return jnp.stack([grad_queries, grad_keys, grad_values]).reshape(3, num_rows, local_width)


def layer_forward(inputs, segment, weights):
    (
        gain_one,
        offset_one,
        weight_qkv,
        bias_qv,
        weight_proj,
        bias_proj,
        gain_two,
        offset_two,
        weight_up,
        bias_up,
        weight_down,
        bias_down,
    ) = weights
    normed = layer_norm(inputs, gain_one, offset_one).astype(jnp.bfloat16)
    qkv_all = jnp.einsum("td,sde->ste", normed, weight_qkv, preferred_element_type=jnp.float32)
    bias_all = jnp.stack([bias_qv[0], jnp.zeros_like(bias_qv[0]), bias_qv[1]])
    qkv_all = (qkv_all + bias_all[:, None, :]).astype(jnp.bfloat16)
    attended, log_totals = attend_forward(qkv_all, segment)
    branch = lax.psum(jnp.dot(attended, weight_proj, preferred_element_type=jnp.float32), "tensor")
    middle = inputs + (branch + bias_proj)
    normed_two = layer_norm(middle, gain_two, offset_two).astype(jnp.bfloat16)
    before_act = jnp.dot(normed_two, weight_up, preferred_element_type=jnp.float32) + bias_up
    activated = gelu_exact(before_act).astype(jnp.bfloat16)
    mlp_out = lax.psum(
        jnp.dot(activated, weight_down, preferred_element_type=jnp.float32), "tensor"
    )
    result = middle + (mlp_out + bias_down)
    return (
        result,
        (normed, qkv_all, attended, log_totals, middle, normed_two, before_act, activated),
    )


def layer_backward(inputs, segment, weights, kept_values, grad_out):
    (
        gain_one,
        offset_one,
        weight_qkv,
        bias_qv,
        weight_proj,
        bias_proj,
        gain_two,
        offset_two,
        weight_up,
        bias_up,
        weight_down,
        bias_down,
    ) = weights
    normed, qkv_all, attended, log_totals, middle, normed_two, before_act, activated = kept_values
    grad_down = grad_out.astype(jnp.bfloat16)
    grad_bias_down = jnp.sum(grad_down, axis=0, dtype=jnp.float32)
    grad_weight_down = inner_rows(activated, grad_down)
    grad_act = times_transpose(grad_down, weight_down)
    grad_pre = jax.vjp(gelu_exact, before_act)[1](grad_act)[0].astype(jnp.bfloat16)
    grad_bias_up = jnp.sum(grad_pre, axis=0, dtype=jnp.float32)
    grad_weight_up = inner_rows(normed_two, grad_pre)
    grad_normed_two = lax.psum(times_transpose(grad_pre, weight_up), "tensor")
    grad_middle, grad_gain_two, grad_offset_two = jax.vjp(layer_norm, middle, gain_two, offset_two)[
        1
    ](grad_normed_two)
    grad_middle = grad_middle + grad_out
    grad_branch = grad_middle.astype(jnp.bfloat16)
    grad_bias_proj = jnp.sum(grad_branch, axis=0, dtype=jnp.float32)
    grad_weight_proj = inner_rows(attended, grad_branch)
    grad_attended = times_transpose(grad_branch, weight_proj).astype(jnp.bfloat16)
    grad_qkv = attend_backward(qkv_all, segment, log_totals, grad_attended).astype(jnp.bfloat16)
    grad_bias_qv = jnp.stack(
        [
            jnp.sum(grad_qkv[0], axis=0, dtype=jnp.float32),
            jnp.sum(grad_qkv[2], axis=0, dtype=jnp.float32),
        ]
    )
    grad_weight_qkv = jnp.einsum(
        "td,ste->sde", normed, grad_qkv, preferred_element_type=jnp.float32
    )
    grad_normed = lax.psum(
        jnp.einsum("ste,sde->td", grad_qkv, weight_qkv, preferred_element_type=jnp.float32),
        "tensor",
    )
    grad_inputs, grad_gain_one, grad_offset_one = jax.vjp(layer_norm, inputs, gain_one, offset_one)[
        1
    ](grad_normed)
    return (
        grad_inputs + grad_middle,
        (
            grad_gain_one,
            grad_offset_one,
            grad_weight_qkv,
            grad_bias_qv,
            grad_weight_proj,
            grad_bias_proj,
            grad_gain_two,
            grad_offset_two,
            grad_weight_up,
            grad_bias_up,
            grad_weight_down,
            grad_bias_down,
        ),
    )


def store(buffer, mb_slot, is_valid, member):
    current = lax.dynamic_index_in_dim(buffer, mb_slot, 0, keepdims=False)
    return lax.dynamic_update_index_in_dim(buffer, jnp.where(is_valid, member, current), mb_slot, 0)


def body(
    patches,
    out_grad,
    large_place,
    norm1_gain,
    norm1_bias,
    qkv_weight,
    qv_bias,
    proj_weight,
    proj_bias,
    norm2_gain,
    norm2_bias,
    up_weight,
    up_bias,
    down_weight,
    down_bias,
):
    weights = (
        norm1_gain[0],
        norm1_bias[0],
        qkv_weight[0],
        qv_bias[0],
        proj_weight[0],
        proj_bias[0],
        norm2_gain[0],
        norm2_bias[0],
        up_weight[0],
        up_bias[0],
        down_weight[0],
        down_bias[0],
    )
    micro_count = large_place.shape[0]
    num_rows = patches.shape[0] // micro_count
    model_width = patches.shape[1]
    local_width = qkv_weight.shape[-1]
    local_heads = local_width // HD
    local_hidden = up_weight.shape[-1]
    section_id = lax.axis_index("section")
    first_section = section_id == 0
    inputs_all = patches.reshape(micro_count, num_rows, model_width)
    cotangents = out_grad.reshape(micro_count, num_rows, model_width)
    stash_shapes = (
        ((num_rows, model_width), jnp.bfloat16),
        ((3, num_rows, local_width), jnp.bfloat16),
        ((num_rows, local_width), jnp.bfloat16),
        ((local_heads, num_rows), jnp.float32),
        ((num_rows, model_width), jnp.float32),
        ((num_rows, model_width), jnp.bfloat16),
        ((num_rows, local_hidden), jnp.float32),
        ((num_rows, local_hidden), jnp.bfloat16),
    )
    stash_all = tuple(
        (jnp.zeros((micro_count,) + shape_one, kind_one) for shape_one, kind_one in stash_shapes)
    )
    empty_rows = jnp.zeros((num_rows, model_width), jnp.bfloat16)
    empty_batch = jnp.zeros((micro_count, num_rows, model_width), jnp.bfloat16)

    def forward_step(step_num, state_now):
        received, outputs, layer_inputs, stash_now = state_now
        micro_index = step_num - section_id
        is_valid = (micro_index >= 0) & (micro_index < micro_count)
        mb_slot = jnp.clip(micro_index, 0, micro_count - 1)
        own_block = lax.dynamic_index_in_dim(inputs_all, mb_slot, 0, keepdims=False)
        entering = jnp.where(first_section, own_block, received)
        segment = segment_ids(large_place[mb_slot], num_rows)
        result, kept_values = layer_forward(entering.astype(jnp.float32), segment, weights)
        leaving = result.astype(jnp.bfloat16)
        outputs = store(outputs, mb_slot, is_valid, leaving)
        layer_inputs = store(layer_inputs, mb_slot, is_valid, entering)
        stash_now = tuple(
            (
                store(buffer, mb_slot, is_valid, member)
                for buffer, member in zip(stash_now, kept_values)
            )
        )
        received = shifted(leaving, "section", 1)
        return (received, outputs, layer_inputs, stash_now)

    received, outputs, layer_inputs, stash_all = lax.fori_loop(
        0, micro_count + 1, forward_step, (empty_rows, empty_batch, empty_batch, stash_all)
    )
    zero_grads = tuple((jnp.zeros(member.shape, jnp.float32) for member in weights))

    def backward_step(step_num, state_now):
        received, input_grads, totals = state_now
        micro_index = jnp.where(first_section, micro_count - step_num, micro_count - 1 - step_num)
        is_valid = (micro_index >= 0) & (micro_index < micro_count)
        mb_slot = jnp.clip(micro_index, 0, micro_count - 1)
        entering = lax.dynamic_index_in_dim(layer_inputs, mb_slot, 0, keepdims=False).astype(
            jnp.float32
        )
        segment = segment_ids(large_place[mb_slot], num_rows)
        kept_values = tuple(
            (lax.dynamic_index_in_dim(buffer, mb_slot, 0, keepdims=False) for buffer in stash_all)
        )
        own_cot = lax.dynamic_index_in_dim(cotangents, mb_slot, 0, keepdims=False)
        grad_out = jnp.where(first_section, received, own_cot).astype(jnp.float32)
        grad_in, weight_grads = layer_backward(entering, segment, weights, kept_values, grad_out)
        valid_factor = is_valid.astype(jnp.float32)
        weight_grads = tuple((member * valid_factor for member in weight_grads))
        totals = tuple((previous + current for previous, current in zip(totals, weight_grads)))
        leaving = grad_in.astype(jnp.bfloat16)
        input_grads = store(input_grads, mb_slot, is_valid, leaving)
        received = shifted(leaving, "section", -1)
        return (received, input_grads, totals)

    received, input_grads, totals = lax.fori_loop(
        0, micro_count + 1, backward_step, (empty_rows, empty_batch, zero_grads)
    )
    totals = lax.psum(
        (
            totals[0],
            totals[1],
            totals[2],
            totals[3],
            totals[4],
            totals[5],
            totals[6],
            totals[7],
            totals[8],
            totals[9],
            totals[10],
            totals[11],
        ),
        "dp",
    )
    return (
        outputs.reshape(1, micro_count * num_rows, model_width),
        input_grads.reshape(1, micro_count * num_rows, model_width),
        totals[0][None],
        totals[1][None],
        totals[2][None],
        totals[3][None],
        totals[4][None],
        totals[5][None],
        totals[6][None],
        totals[7][None],
        totals[8][None],
        totals[9][None],
        totals[10][None],
        totals[11][None],
    )


def solution(mesh):
    placed = (
        P("dp", None),
        P("dp", None),
        P("dp"),
        P("section", None),
        P("section", None),
        P("section", None, None, "tensor"),
        P("section", None, "tensor"),
        P("section", "tensor", None),
        P("section", None),
        P("section", None),
        P("section", None),
        P("section", None, "tensor"),
        P("section", "tensor"),
        P("section", "tensor", None),
        P("section", None),
    )
    return jax.shard_map(
        body,
        mesh=mesh,
        in_specs=placed,
        out_specs=(
            P("section", "dp", None),
            P("section", "dp", None),
            P("section", None),
            P("section", None),
            P("section", None, None, "tensor"),
            P("section", None, "tensor"),
            P("section", "tensor", None),
            P("section", None),
            P("section", None),
            P("section", None),
            P("section", None, "tensor"),
            P("section", "tensor"),
            P("section", "tensor", None),
            P("section", None),
        ),
        check_vma=False,
    )
```

profile of v0, /device:TPU:0, one launch (start us, length us, event | category | flops | bytes accessed | tf_op | source)
XLA Modules:
  0.0 2001.9 jit_solution(14324049124545629773)
XLA Ops:
  36.3 684.1 %while.73 = (s32[]{:T(128)}, bf16[1168,768]{1,0:T(8,128)(2,1)}, bf16[2,1168,768]{2,1,0:T(8,128)(2,1)}, bf16[2,1168,768]{2,1,0:T(8,128)(2,1)}, bf16[2,1168,768]{2...) while((s32[]{:T(128)}, bf16[1168,768]{1,0:T(8,128)(2,1)}, ...), condition=%wide.region_12.13_spmd, body=%wide.region_0.12_spmd.sunk | while | flops 10598827008 | bytes 487971072 | solution.py:329
  129.6 18.8 all-reduce.10.cloned.1.call-done
  160.6 22.9 %bitcast_dynamic-update-slice_fusion.20 = (bf16[2,1168,1536]{2,1,0:T(8,128)(2,1)}, bf16[1168,1536]{1,0:T(8,128)(2,1)S(1)}, f32[1168,1536]{1,0:T(8,128)}) fusion(bf16[2,1168,1536]{2,1,0:T(8,128)(2,1)} %get-tuple-element.1969, s32[]{:T(128)S(6)} %min.19, bf16[1,1168,1536]{2,1,0:T(8,128)(2,1)} %constant_dynamic-slice_fusion.29, pred[]{:T(512)S(6)} %and.18, ...), kind=kOutput, calls=%fused_computation.44.clone.1 | convolution fusion | flops 2880344064 | bytes 23909508 | tf_op jit(solution)/shard_map/while/body/eval_jaxpr/dot_general | solution.py:166
  232.5 31.5 %collective-permute-done = bf16[1168,768]{1,0:T(8,128)(2,1)S(1)} collective-permute-done((bf16[1168,768]{1,0:T(8,128)(2,1)}, bf16[1168,768]{1,0:T(8,128)(2,1)S(1)}, u32[]{:S(2)}, u32[]{:S(2)}) %collective-permute-start) | collective-permute-done | bytes 1794080 | tf_op jit(solution)/shard_map/while/body/eval_jaxpr/ppermute | solution.py:19
  358.4 17.9 all-reduce.10.cloned.1.call-done
  388.4 23.0 %bitcast_dynamic-update-slice_fusion.20 = (bf16[2,1168,1536]{2,1,0:T(8,128)(2,1)}, bf16[1168,1536]{1,0:T(8,128)(2,1)S(1)}, f32[1168,1536]{1,0:T(8,128)}) fusion(bf16[2,1168,1536]{2,1,0:T(8,128)(2,1)} %get-tuple-element.1969, s32[]{:T(128)S(6)} %min.19, bf16[1,1168,1536]{2,1,0:T(8,128)(2,1)} %constant_dynamic-slice_fusion.29, pred[]{:T(512)S(6)} %and.18, ...), kind=kOutput, calls=%fused_computation.44.clone.1 | convolution fusion | flops 2880344064 | bytes 23909508 | tf_op jit(solution)/shard_map/while/body/eval_jaxpr/dot_general | solution.py:166
  459.8 31.4 %collective-permute-done = bf16[1168,768]{1,0:T(8,128)(2,1)S(1)} collective-permute-done((bf16[1168,768]{1,0:T(8,128)(2,1)}, bf16[1168,768]{1,0:T(8,128)(2,1)S(1)}, u32[]{:S(2)}, u32[]{:S(2)}) %collective-permute-start) | collective-permute-done | bytes 1794080 | tf_op jit(solution)/shard_map/while/body/eval_jaxpr/ppermute | solution.py:19
  585.4 17.5 all-reduce.10.cloned.1.call-done
  615.1 23.3 %bitcast_dynamic-update-slice_fusion.20 = (bf16[2,1168,1536]{2,1,0:T(8,128)(2,1)}, bf16[1168,1536]{1,0:T(8,128)(2,1)S(1)}, f32[1168,1536]{1,0:T(8,128)}) fusion(bf16[2,1168,1536]{2,1,0:T(8,128)(2,1)} %get-tuple-element.1969, s32[]{:T(128)S(6)} %min.19, bf16[1,1168,1536]{2,1,0:T(8,128)(2,1)} %constant_dynamic-slice_fusion.29, pred[]{:T(512)S(6)} %and.18, ...), kind=kOutput, calls=%fused_computation.44.clone.1 | convolution fusion | flops 2880344064 | bytes 23909508 | tf_op jit(solution)/shard_map/while/body/eval_jaxpr/dot_general | solution.py:166
  683.4 34.4 %collective-permute-done = bf16[1168,768]{1,0:T(8,128)(2,1)S(1)} collective-permute-done((bf16[1168,768]{1,0:T(8,128)(2,1)}, bf16[1168,768]{1,0:T(8,128)(2,1)S(1)}, u32[]{:S(2)}, u32[]{:S(2)}) %collective-permute-start) | collective-permute-done | bytes 1794080 | tf_op jit(solution)/shard_map/while/body/eval_jaxpr/ppermute | solution.py:19
  722.6 817.4 %while.74 = (s32[]{:T(128)}, bf16[1168,768]{1,0:T(8,128)(2,1)S(1)}, bf16[2,1168,768]{2,1,0:T(8,128)(2,1)}, f32[768]{0:T(1024)}, f32[768]{0:T(1024)}, /*index=5*/...) while((s32[]{:T(128)}, bf16[1168,768]{1,0:T(8,128)(2,1)S(1)}, ...), condition=%wide.region_36.37_spmd.clone, body=%wide.region_13.36_spmd.clone.sunk | while | flops 22061871104 | bytes 875443136 | solution.py:357
  726.9 22.3 %convert_reduce_fusion.21 = (f32[1536]{0:T(1024)}, bf16[1168,1536]{1,0:T(8,128)(2,1)S(1)}) fusion(f32[2,1168,1536]{2,1,0:T(8,128)} %get-tuple-element.2125, s32[]{:T(128)S(6)} %min.20, bf16[1168,768]{1,0:T(8,128)(2,1)S(1)} %get-tuple-element.1884, bf16[1536,768]{1,0:T(8,128)(2,1)S(1)} %copy-done.108), kind=kOutput, calls=%fused_computation.125.clone.1 | convolution fusion | flops 2888415744 | bytes 14923780 | tf_op jit(solution)/shard_map/while/body/eval_jaxpr/dot_general | solution.py:40
  804.4 16.4 multiply_reduce_fusion.15
  820.9 12.1 multiply_convert_fusion.4
  849.4 16.5 multiply_reduce_fusion.14
  866.0 9.5 fusion.313
  959.5 36.7 %collective-permute-done.1 = bf16[1168,768]{1,0:T(8,128)(2,1)S(1)} collective-permute-done((bf16[1168,768]{1,0:T(8,128)(2,1)S(1)}, bf16[1168,768]{1,0:T(8,128)(2,1)S(1)}, u32[]{:S(2)}, u32[]{:S(2)}) %collective-permute-start.1) | collective-permute-done | bytes 1794080 | tf_op jit(solution)/shard_map/while/body/eval_jaxpr/ppermute | solution.py:19
  999.3 22.3 %convert_reduce_fusion.21 = (f32[1536]{0:T(1024)}, bf16[1168,1536]{1,0:T(8,128)(2,1)S(1)}) fusion(f32[2,1168,1536]{2,1,0:T(8,128)} %get-tuple-element.2125, s32[]{:T(128)S(6)} %min.20, bf16[1168,768]{1,0:T(8,128)(2,1)S(1)} %get-tuple-element.1884, bf16[1536,768]{1,0:T(8,128)(2,1)S(1)} %copy-done.108), kind=kOutput, calls=%fused_computation.125.clone.1 | convolution fusion | flops 2888415744 | bytes 14923780 | tf_op jit(solution)/shard_map/while/body/eval_jaxpr/dot_general | solution.py:40
  1075.4 16.4 multiply_reduce_fusion.15
  1091.8 12.4 multiply_convert_fusion.4
  1120.7 16.5 multiply_reduce_fusion.14
  1137.2 9.5 fusion.313
  1191.5 10.2 select_add_fusion.21
  1230.4 36.7 %collective-permute-done.1 = bf16[1168,768]{1,0:T(8,128)(2,1)S(1)} collective-permute-done((bf16[1168,768]{1,0:T(8,128)(2,1)S(1)}, bf16[1168,768]{1,0:T(8,128)(2,1)S(1)}, u32[]{:S(2)}, u32[]{:S(2)}) %collective-permute-start.1) | collective-permute-done | bytes 1794080 | tf_op jit(solution)/shard_map/while/body/eval_jaxpr/ppermute | solution.py:19
  1270.4 22.3 %convert_reduce_fusion.21 = (f32[1536]{0:T(1024)}, bf16[1168,1536]{1,0:T(8,128)(2,1)S(1)}) fusion(f32[2,1168,1536]{2,1,0:T(8,128)} %get-tuple-element.2125, s32[]{:T(128)S(6)} %min.20, bf16[1168,768]{1,0:T(8,128)(2,1)S(1)} %get-tuple-element.1884, bf16[1536,768]{1,0:T(8,128)(2,1)S(1)} %copy-done.108), kind=kOutput, calls=%fused_computation.125.clone.1 | convolution fusion | flops 2888415744 | bytes 14923780 | tf_op jit(solution)/shard_map/while/body/eval_jaxpr/dot_general | solution.py:40
  1346.4 16.4 multiply_reduce_fusion.15
  1362.8 12.1 multiply_convert_fusion.4
  1391.4 16.5 multiply_reduce_fusion.14
  1462.3 10.2 select_add_fusion.21
  1501.4 36.8 %collective-permute-done.1 = bf16[1168,768]{1,0:T(8,128)(2,1)S(1)} collective-permute-done((bf16[1168,768]{1,0:T(8,128)(2,1)S(1)}, bf16[1168,768]{1,0:T(8,128)(2,1)S(1)}, u32[]{:S(2)}, u32[]{:S(2)}) %collective-permute-start.1) | collective-permute-done | bytes 1794080 | tf_op jit(solution)/shard_map/while/body/eval_jaxpr/ppermute | solution.py:19
  1546.1 40.2 %all-reduce = (f32[1,768]{1,0:T(1,128)}, f32[1,768]{1,0:T(1,128)}, f32[1,2,384]{2,1,0:T(2,128)}, f32[1,768]{1,0:T(1,128)}, f32[1,768]{1,0:T(1,128)}, /*index=5*/...) all-reduce(f32[1,768]{1,0:T(1,128)S(1)} %broadcast_in_dim.368, ...), channel_id=1, replica_groups=mesh['section'=2,'tensor'=2,'dp'=8] {'dp'}, use_global_device_ids=true, to_apply=%region_37.38 | all-reduce | flops 6912 | bytes 55296 | tf_op jit(solution)/shard_map/psum | solution.py:360
  1586.2 397.1 %all-reduce.8.cloned.1.call-done = (f32[1,3,768,384]{3,2,1,0:T(8,128)}, f32[1,384,768]{2,1,0:T(8,128)}, f32[1,768,1536]{2,1,0:T(8,128)}, f32[1,1536,768]{2,1,0:T(8,128)}) async-done(((f32[1,3,768,384]{3,2,1,0:T(8,128)}, f32[1,384,768]{2,1,0:T(8,128)}, f32[1,768,1536]{2,1,0:T(8,128)}, f32[1,1536,768]{2,1,0:T(8,128)}), (f32[1,3,768,384]{3,2,1,0:T(8,128)}, f32[1,384,768]{2,1,0:T(8,128)}, ...) | async-done | bytes 14155792 | tf_op jit(solution)/shard_map/psum | solution.py:360
  (1106 shorter events, 965.5 us)
Async XLA Ops:
  36.7 111.8 %all-reduce.10.cloned.1.call-start = ((), (), s32[]{:S(2)}) async-start(), calls=%async_computation.1 | async-start | bytes 7176192 | tf_op jit(solution)/shard_map/while/body/eval_jaxpr/psum | solution.py:163
  120.8 93.1 %all-reduce.12.cloned.1.call-start = ((), (), s32[]{:S(2)}) async-start(), calls=%async_computation.2 | async-start | bytes 7176192 | tf_op jit(solution)/shard_map/while/body/eval_jaxpr/psum | solution.py:168
  220.2 43.9 %collective-permute-start = (bf16[1168,768]{1,0:T(8,128)(2,1)}, bf16[1168,768]{1,0:T(8,128)(2,1)S(1)}, u32[]{:S(2)}, u32[]{:S(2)}) collective-permute-start(bf16[1168,768]{1,0:T(8,128)(2,1)} %get-tuple-element.1841), channel_id=1, source_target_pairs={{0,16},{1,17},{2,18},{3,19},{4,20},{5,21},{6,22},{7,23},{8,24},{9,... | collective-permute-start | bytes 5382152 | tf_op jit(solution)/shard_map/while/body/eval_jaxpr/ppermute | solution.py:19
  225.0 40.4 %copy-start.68 = (f32[1,768]{1,0:T(1,128)S(1)}, f32[1,768]{1,0:T(1,128)}, u32[]{:S(2)}) copy-start(f32[1,768]{1,0:T(1,128)} %get-tuple-element.2232) | copy-start | bytes 9220 | tf_op jit(solution)/shard_map/while
  225.0 40.4 %copy-start.100 = (f32[1,2,384]{2,1,0:T(2,128)S(1)}, f32[1,2,384]{2,1,0:T(2,128)}, u32[]{:S(2)}) copy-start(f32[1,2,384]{2,1,0:T(2,128)} %get-tuple-element.2268) | copy-start | bytes 9220 | tf_op jit(solution)/shard_map/while
  225.0 40.4 %copy-start.102 = (f32[1,768]{1,0:T(1,128)S(1)}, f32[1,768]{1,0:T(1,128)}, u32[]{:S(2)}) copy-start(f32[1,768]{1,0:T(1,128)} %get-tuple-element.2305) | copy-start | bytes 9220 | tf_op jit(solution)/shard_map/while
  225.0 40.3 %copy-start.111 = (s32[2]{0:T(128)S(1)}, s32[2]{0:T(128)}, u32[]{:S(2)}) copy-start(s32[2]{0:T(128)} %get-tuple-element.2343) | copy-start | bytes 28 | tf_op jit(solution)/shard_map/while
  265.8 110.5 %all-reduce.10.cloned.1.call-start = ((), (), s32[]{:S(2)}) async-start(), calls=%async_computation.1 | async-start | bytes 7176192 | tf_op jit(solution)/shard_map/while/body/eval_jaxpr/psum | solution.py:163
  349.4 92.3 %all-reduce.12.cloned.1.call-start = ((), (), s32[]{:S(2)}) async-start(), calls=%async_computation.2 | async-start | bytes 7176192 | tf_op jit(solution)/shard_map/while/body/eval_jaxpr/psum | solution.py:168
  448.2 42.9 %collective-permute-start = (bf16[1168,768]{1,0:T(8,128)(2,1)}, bf16[1168,768]{1,0:T(8,128)(2,1)S(1)}, u32[]{:S(2)}, u32[]{:S(2)}) collective-permute-start(bf16[1168,768]{1,0:T(8,128)(2,1)} %get-tuple-element.1841), channel_id=1, source_target_pairs={{0,16},{1,17},{2,18},{3,19},{4,20},{5,21},{6,22},{7,23},{8,24},{9,... | collective-permute-start | bytes 5382152 | tf_op jit(solution)/shard_map/while/body/eval_jaxpr/ppermute | solution.py:19
  492.6 110.3 %all-reduce.10.cloned.1.call-start = ((), (), s32[]{:S(2)}) async-start(), calls=%async_computation.1 | async-start | bytes 7176192 | tf_op jit(solution)/shard_map/while/body/eval_jaxpr/psum | solution.py:163
  576.2 93.4 %all-reduce.12.cloned.1.call-start = ((), (), s32[]{:S(2)}) async-start(), calls=%async_computation.2 | async-start | bytes 7176192 | tf_op jit(solution)/shard_map/while/body/eval_jaxpr/psum | solution.py:168
  675.9 42.0 %collective-permute-start = (bf16[1168,768]{1,0:T(8,128)(2,1)}, bf16[1168,768]{1,0:T(8,128)(2,1)S(1)}, u32[]{:S(2)}, u32[]{:S(2)}) collective-permute-start(bf16[1168,768]{1,0:T(8,128)(2,1)} %get-tuple-element.1841), channel_id=1, source_target_pairs={{0,16},{1,17},{2,18},{3,19},{4,20},{5,21},{6,22},{7,23},{8,24},{9,... | collective-permute-start | bytes 5382152 | tf_op jit(solution)/shard_map/while/body/eval_jaxpr/ppermute | solution.py:19
  724.0 58.0 %all-reduce.14.cloned.1.call-start = ((), (), s32[]{:S(2)}) async-start(), calls=%async_computation.3 | async-start | bytes 7176192 | tf_op jit(solution)/shard_map/while/body/eval_jaxpr/psum | solution.py:201
  755.8 184.5 %all-reduce.16.cloned.1.call-start = ((), (), s32[]{:S(2)}) async-start(), calls=%async_computation.4 | async-start | bytes 7176192 | tf_op jit(solution)/shard_map/while/body/eval_jaxpr/psum | solution.py:220
  758.5 90.9 %copy-start.20 = (bf16[1,1,584,384]{2,3,1,0:T(8,128)(2,1)}, bf16[1,1,584,384]{2,3,1,0:T(8,128)(2,1)S(1)}, u32[]{:S(2)}) copy-start(bf16[1,1,584,384]{2,3,1,0:T(8,128)(2,1)S(1)} %copy.100) | copy-start | bytes 1345540 | tf_op jit(solution)/shard_map/while
  763.8 85.7 %copy-start.6 = (bf16[1,1,1168,384]{2,3,1,0:T(8,128)(2,1)}, bf16[1,1,1168,384]{2,3,1,0:T(8,128)(2,1)S(1)}, u32[]{:S(2)}) copy-start(bf16[1,1,1168,384]{2,3,1,0:T(8,128)(2,1)S(1)} %copy.101) | copy-start | bytes 2691076 | tf_op jit(solution)/shard_map/while
  952.8 43.4 %collective-permute-start.1 = (bf16[1168,768]{1,0:T(8,128)(2,1)S(1)}, bf16[1168,768]{1,0:T(8,128)(2,1)S(1)}, u32[]{:S(2)}, u32[]{:S(2)}) collective-permute-start(bf16[1168,768]{1,0:T(8,128)(2,1)S(1)} %get-tuple-element.1911), channel_id=1, source_target_pairs={{16,0},{17,1},{18,2},{19,3},{20,4},{21,5},{22,6},{23,7},{24,8},{25... | collective-permute-start | bytes 5382152 | tf_op jit(solution)/shard_map/while/body/eval_jaxpr/ppermute | solution.py:19
  955.9 40.3 %copy-start.72 = (f32[1,768]{1,0:T(1,128)S(1)}, f32[1,768]{1,0:T(1,128)}, u32[]{:S(2)}) copy-start(f32[1,768]{1,0:T(1,128)} %copy-done.71) | copy-start | bytes 9220 | tf_op jit(solution)/shard_map/while
  996.4 56.5 %all-reduce.14.cloned.1.call-start = ((), (), s32[]{:S(2)}) async-start(), calls=%async_computation.3 | async-start | bytes 7176192 | tf_op jit(solution)/shard_map/while/body/eval_jaxpr/psum | solution.py:201
  1028.2 183.3 %all-reduce.16.cloned.1.call-start = ((), (), s32[]{:S(2)}) async-start(), calls=%async_computation.4 | async-start | bytes 7176192 | tf_op jit(solution)/shard_map/while/body/eval_jaxpr/psum | solution.py:220
  1030.6 90.1 %copy-start.20 = (bf16[1,1,584,384]{2,3,1,0:T(8,128)(2,1)}, bf16[1,1,584,384]{2,3,1,0:T(8,128)(2,1)S(1)}, u32[]{:S(2)}) copy-start(bf16[1,1,584,384]{2,3,1,0:T(8,128)(2,1)S(1)} %copy.100) | copy-start | bytes 1345540 | tf_op jit(solution)/shard_map/while
  1036.0 84.6 %copy-start.6 = (bf16[1,1,1168,384]{2,3,1,0:T(8,128)(2,1)}, bf16[1,1,1168,384]{2,3,1,0:T(8,128)(2,1)S(1)}, u32[]{:S(2)}) copy-start(bf16[1,1,1168,384]{2,3,1,0:T(8,128)(2,1)S(1)} %copy.101) | copy-start | bytes 2691076 | tf_op jit(solution)/shard_map/while
  1223.7 43.4 %collective-permute-start.1 = (bf16[1168,768]{1,0:T(8,128)(2,1)S(1)}, bf16[1168,768]{1,0:T(8,128)(2,1)S(1)}, u32[]{:S(2)}, u32[]{:S(2)}) collective-permute-start(bf16[1168,768]{1,0:T(8,128)(2,1)S(1)} %get-tuple-element.1911), channel_id=1, source_target_pairs={{16,0},{17,1},{18,2},{19,3},{20,4},{21,5},{22,6},{23,7},{24,8},{25... | collective-permute-start | bytes 5382152 | tf_op jit(solution)/shard_map/while/body/eval_jaxpr/ppermute | solution.py:19
  1267.5 56.5 %all-reduce.14.cloned.1.call-start = ((), (), s32[]{:S(2)}) async-start(), calls=%async_computation.3 | async-start | bytes 7176192 | tf_op jit(solution)/shard_map/while/body/eval_jaxpr/psum | solution.py:201
  1299.2 183.0 %all-reduce.16.cloned.1.call-start = ((), (), s32[]{:S(2)}) async-start(), calls=%async_computation.4 | async-start | bytes 7176192 | tf_op jit(solution)/shard_map/while/body/eval_jaxpr/psum | solution.py:220
  1301.9 89.5 %copy-start.20 = (bf16[1,1,584,384]{2,3,1,0:T(8,128)(2,1)}, bf16[1,1,584,384]{2,3,1,0:T(8,128)(2,1)S(1)}, u32[]{:S(2)}) copy-start(bf16[1,1,584,384]{2,3,1,0:T(8,128)(2,1)S(1)} %copy.100) | copy-start | bytes 1345540 | tf_op jit(solution)/shard_map/while
  1307.3 84.1 %copy-start.6 = (bf16[1,1,1168,384]{2,3,1,0:T(8,128)(2,1)}, bf16[1,1,1168,384]{2,3,1,0:T(8,128)(2,1)S(1)}, u32[]{:S(2)}) copy-start(bf16[1,1,1168,384]{2,3,1,0:T(8,128)(2,1)S(1)} %copy.101) | copy-start | bytes 2691076 | tf_op jit(solution)/shard_map/while
  1494.7 43.4 %collective-permute-start.1 = (bf16[1168,768]{1,0:T(8,128)(2,1)S(1)}, bf16[1168,768]{1,0:T(8,128)(2,1)S(1)}, u32[]{:S(2)}, u32[]{:S(2)}) collective-permute-start(bf16[1168,768]{1,0:T(8,128)(2,1)S(1)} %get-tuple-element.1911), channel_id=1, source_target_pairs={{16,0},{17,1},{18,2},{19,3},{20,4},{21,5},{22,6},{23,7},{24,8},{25... | collective-permute-start | bytes 5382152 | tf_op jit(solution)/shard_map/while/body/eval_jaxpr/ppermute | solution.py:19
  1497.8 40.3 %copy-start.72 = (f32[1,768]{1,0:T(1,128)S(1)}, f32[1,768]{1,0:T(1,128)}, u32[]{:S(2)}) copy-start(f32[1,768]{1,0:T(1,128)} %copy-done.71) | copy-start | bytes 9220 | tf_op jit(solution)/shard_map/while
  1497.8 40.3 %copy-start.113 = (s32[2]{0:T(128)S(1)}, s32[2]{0:T(128)}, u32[]{:S(2)}) copy-start(s32[2]{0:T(128)} %copy-done.112) | copy-start | bytes 28 | tf_op jit(solution)/shard_map/while
  1540.0 443.3 %all-reduce.8.cloned.1.call-start = ((), (), s32[]{:S(2)}) async-start(), calls=%async_computation | async-start | bytes 28311552 | tf_op jit(solution)/shard_map/psum | solution.py:360
  (313 other events, 2750.5 us)
Sparse Core Ops, SparseCore 0:
  120.9 27.4 all-reduce.9
  188.5 25.3 all-reduce.11
  349.5 26.6 all-reduce.9
  416.3 25.3 all-reduce.11
  576.4 26.5 all-reduce.9
  643.2 25.3 all-reduce.11
  755.9 26.0 all-reduce.13
  914.9 25.3 all-reduce.15
  1028.3 24.5 all-reduce.13
  1186.1 25.3 all-reduce.15
  1299.4 24.5 all-reduce.13
  1456.8 25.3 all-reduce.15
Sparse Core Ops, SparseCore 1:
  1546.4 436.9 all-reduce.7
where the time goes:
time: 2010 us; the launch traced here: 2000 us
  waiting for transfers between devices  697 us (35%)
  matrix products  620 us (31%)
  other arithmetic  323 us (16%)
  local copies, waits for them, and re-layouts  277 us (14%)
  blocking collectives  40.2 us (2%)
    psum x1, waiting for transfers between devices, body(): lax.psum((totals[0], totals[1], totals[2], totals[3], totals[4], totals[5...  397 us
    ppermute x6, waiting for transfers between devices, shifted(): return lax.ppermute(array, axis, pairs)  208 us
    dot_general x12, matrix products, block_scores(): jnp.einsum('qhd,khd->hqk', query_block, keys_all, preferred_element_type=...  154 us
    dynamic_slice x30, local copies, waits for them, and re-layouts, store(): current = lax.dynamic_index_in_dim(buffer, mb_slot, 0, keepdims=False)  106 us
    dynamic_update_slice x21, other arithmetic, store(): lax.dynamic_update_index_in_dim(buffer, jnp.where(is_valid, member, curre...  87.6 us
    dot_general x9, matrix products, times_transpose(): lax.dot_general(left_side, right_side, (((1,), (1,)), ((), ())), preferre...  84.6 us
    dot_general x3, matrix products, layer_forward(): jnp.dot(normed_two, weight_up, preferred_element_type=jnp.float32) + bias_up  69.1 us
    convert_element_type x6, other arithmetic, attend_backward(): grad_scores = (probabilities * (grad_probs - jnp.sum(probabilities * grad...  58.2 us
  transfers between devices with their start and end apart: 19, of which 18 were waited for; matrix products, arithmetic and copies ran while one was open for 12% of the time, Pallas kernels for 0%

commit v1 on v0

v1 whole, which is shorter than its diff:
```python
import functools

import jax
import jax.numpy as jnp
from jax import lax
from jax.experimental import pallas as pl
from jax.experimental.pallas import tpu as pltpu
from jax.sharding import PartitionSpec as P

HD = 64
LEN_SMALL = 197
LEN_LARGE = 577
SMALL_MB = 3
EPSILON = 1e-06
MASKED = -1e30
SCALE = HD ** (-0.5)
BF = jnp.bfloat16
F32 = jnp.float32
VMEM_LIMIT = 56 * 1024 * 1024
CHUNKS = ((1, 592, LEN_LARGE), (SMALL_MB, 208, LEN_SMALL))


def params(**more):
    return pltpu.CompilerParams(vmem_limit_bytes=VMEM_LIMIT, **more)


def nn(a, b):
    return jnp.dot(a, b, preferred_element_type=F32)


def nt(a, b):
    return lax.dot_general(a, b, (((1,), (1,)), ((), ())), preferred_element_type=F32)


def tn(a, b):
    return lax.dot_general(a, b, (((0,), (0,)), ((), ())), preferred_element_type=F32)


def whole(shape):
    zeros = (0,) * len(shape)
    return pl.BlockSpec(shape, lambda *_: zeros)


def sds(shape, dtype):
    return jax.ShapeDtypeStruct(shape, dtype)


def norm_parts(values):
    mean = jnp.mean(values, axis=-1, keepdims=True)
    centred = values - mean
    rstd = lax.rsqrt(jnp.mean(centred * centred, axis=-1, keepdims=True) + EPSILON)
    return centred * rstd, rstd


def norm_back(xhat, rstd, grad, gain):
    scaled = grad * gain
    m1 = jnp.mean(scaled, axis=-1, keepdims=True)
    m2 = jnp.mean(scaled * xhat, axis=-1, keepdims=True)
    return rstd * (scaled - m1 - xhat * m2)


def rowsum(values):
    return jnp.sum(values.astype(F32), axis=0, keepdims=True)


def pre_fwd_kernel(x_ref, g_ref, b_ref, wo_ref, wp_ref, bias_ref, normed_ref, qkv_ref):
    @pl.when(pl.program_id(0) == 0)
    def _():
        xhat, _ = norm_parts(x_ref[...].astype(F32))
        normed_ref[...] = (xhat * g_ref[...] + b_ref[...]).astype(BF)

    weight = jnp.concatenate([wo_ref[0], wp_ref[0]], axis=1)
    qkv_ref[0] = (nn(normed_ref[...], weight) + bias_ref[0]).astype(BF)


def pre_fwd(x, w):
    n, d = x.shape
    half = w["wqkv_o"].shape[-1]
    return pl.pallas_call(
        pre_fwd_kernel,
        grid=(3,),
        in_specs=[
            whole((n, d)),
            whole((1, d)),
            whole((1, d)),
            pl.BlockSpec((1, d, half), lambda s: (s, 0, 0)),
            pl.BlockSpec((1, d, half), lambda s: (s, 0, 0)),
            pl.BlockSpec((1, 1, 2 * half), lambda s: (s, 0, 0)),
        ],
        out_specs=[whole((n, d)), pl.BlockSpec((1, n, 2 * half), lambda s: (s, 0, 0))],
        out_shape=[sds((n, d), BF), sds((3, n, 2 * half), BF)],
        compiler_params=params(),
        name="pre_fwd",
    )(x, w["g1"], w["b1"], w["wqkv_o"], w["wqkv_p"], w["bqkv"])


def mask_keys(scores, vlen):
    rows = scores.shape[0]
    keep = vlen // 8 * 8
    tail = scores[keep:]
    idx = lax.broadcasted_iota(jnp.int32, tail.shape, 0) + keep
    return jnp.concatenate([scores[:keep], jnp.where(idx < vlen, tail, MASKED)], axis=0)


def qblocks(plen):
    return [(q, min(256, plen - q)) for q in range(0, plen, 256)]


def attn_fwd_kernel(q_ref, k_ref, v_ref, o_ref, l_ref, *, nimg, plen, vlen):
    for im in range(nimg):
        r0 = im * plen
        k = k_ref[0, r0 : r0 + plen]
        vt = v_ref[0, r0 : r0 + plen].T
        for q0, qw in qblocks(plen):
            q = q_ref[0, r0 + q0 : r0 + q0 + qw]
            head = lax.broadcasted_iota(jnp.int32, q.shape, 1) // HD
            outs = []
            for h in range(2):
                qm = jnp.where(head == h, q, jnp.zeros_like(q))
                st = mask_keys(nt(k, qm), vlen)
                top = jnp.max(st, axis=0, keepdims=True)
                e = jnp.exp((st - top) * SCALE)
                total = jnp.sum(e, axis=0, keepdims=True)
                p = (e * (1.0 / total)).astype(BF)
                outs.append(nn(vt[h * HD : (h + 1) * HD], p))
                l_ref[0, h : h + 1, r0 + q0 : r0 + q0 + qw] = top * SCALE + jnp.log(total)
            o_ref[r0 + q0 : r0 + q0 + qw] = jnp.concatenate(outs, axis=0).T.astype(BF)


def attn_fwd(qkv, chunk):
    nimg, plen, vlen = chunk
    _, n, d = qkv.shape
    pairs = d // 128
    return pl.pallas_call(
        functools.partial(attn_fwd_kernel, nimg=nimg, plen=plen, vlen=vlen),
        grid=(pairs,),
        in_specs=[
            pl.BlockSpec((1, n, 128), lambda p, s=s: (s, 0, p)) for s in range(3)
        ],
        out_specs=[
            pl.BlockSpec((n, 128), lambda p: (0, p)),
            pl.BlockSpec((1, 2, n), lambda p: (p, 0, 0)),
        ],
        out_shape=[sds((n, d), BF), sds((pairs, 2, n), F32)],
        compiler_params=params(),
        name="attn_fwd",
    )(qkv, qkv, qkv)


def gelu_parts(x):
    cdf = 0.5 + 0.5 * lax.erf(x * (2.0**-0.5))
    pdf = jnp.exp(-0.5 * x * x) * 0.3989422804014327
    return x * cdf, cdf + x * pdf


def post_fwd_kernel(
    x_ref, att_ref, pwo_ref, pwp_ref, pb_ref, g_ref, b_ref, uo_ref, up_ref, ubo_ref, ubp_ref,
    do_ref, dp_ref, db_ref,
    mid_ref, n2_ref, ao_ref, ap_ref, go_ref, gp_ref, out_ref, acc_ref,
):
    j = pl.program_id(0)

    @pl.when(j == 0)
    def _():
        weight = jnp.concatenate([pwo_ref[...], pwp_ref[...]], axis=0)
        mid = x_ref[...].astype(F32) + (nn(att_ref[...], weight) + pb_ref[...])
        mid_ref[...] = mid
        xhat, _ = norm_parts(mid)
        n2_ref[...] = (xhat * g_ref[...] + b_ref[...]).astype(BF)
        acc_ref[...] = mid + db_ref[...]

    n2 = n2_ref[...]
    for u_ref, ub_ref, d_ref, a_ref, dg_ref in (
        (uo_ref, ubo_ref, do_ref, ao_ref, go_ref),
        (up_ref, ubp_ref, dp_ref, ap_ref, gp_ref),
    ):
        act, slope = gelu_parts(nn(n2, u_ref[...]) + ub_ref[...])
        act = act.astype(BF)
        a_ref[...] = act
        dg_ref[...] = slope.astype(BF)
        acc_ref[...] += nn(act, d_ref[...])

    @pl.when(j == pl.num_programs(0) - 1)
    def _():
        out_ref[...] = acc_ref[...].astype(BF)


def post_fwd(x, att, w):
    n, d = x.shape
    half = w["pw_o"].shape[0]
    fh = w["up_o"].shape[1]
    fb = fh // 2
    cols = lambda rows: pl.BlockSpec((rows, fb), lambda j: (0, j))
    rows_ = pl.BlockSpec((fb, d), lambda j: (j, 0))
    return pl.pallas_call(
        post_fwd_kernel,
        grid=(2,),
        in_specs=[
            whole((n, d)), whole((n, d)), whole((half, d)), whole((half, d)), whole((1, d)),
            whole((1, d)), whole((1, d)), cols(d), cols(d), cols(1), cols(1), rows_, rows_,
            whole((1, d)),
        ],
        out_specs=[
            whole((n, d)), whole((n, d)), cols(n), cols(n), cols(n), cols(n), whole((n, d)),
        ],
        out_shape=[
            sds((n, d), F32), sds((n, d), BF), sds((n, fh), BF), sds((n, fh), BF),
            sds((n, fh), BF), sds((n, fh), BF), sds((n, d), BF),
        ],
        scratch_shapes=[pltpu.VMEM((n, d), F32)],
        compiler_params=params(),
        name="post_fwd",
    )(
        x, att, w["pw_o"], w["pw_p"], w["pb"], w["g2"], w["b2"], w["up_o"], w["up_p"],
        w["ub_o"], w["ub_p"], w["dn_o"], w["dn_p"], w["db"],
    )


def forward(x, w, chunk):
    normed, qkv = pre_fwd(x, w)
    att, lse = attn_fwd(qkv, chunk)
    mid, n2, act_o, act_p, dg_o, dg_p, out = post_fwd(x, att, w)
    return (x, normed, qkv, att, lse, mid, n2, act_o, act_p, dg_o, dg_p, out)


def post_bwd_kernel(
    g_ref, mid_ref, gain_ref, go_ref, gp_ref, uo_ref, up_ref, do_ref, dp_ref, pwo_ref, pwp_ref,
    qo_ref, qp_ref, gm_ref, gb_ref, ga_ref, sums_ref, so_ref, sp_ref, acc_ref,
):
    j = pl.program_id(0)
    g = g_ref[...]

    @pl.when(j == 0)
    def _():
        acc_ref[...] = jnp.zeros_like(acc_ref)

    for dg_ref, u_ref, d_ref, q_ref, s_ref in (
        (go_ref, uo_ref, do_ref, qo_ref, so_ref),
        (gp_ref, up_ref, dp_ref, qp_ref, sp_ref),
    ):
        pre = (nt(g, d_ref[...]) * dg_ref[...].astype(F32)).astype(BF)
        q_ref[...] = pre
        s_ref[...] = rowsum(pre)
        acc_ref[...] += nt(pre, u_ref[...])

    @pl.when(j == pl.num_programs(0) - 1)
    def _():
        gn = acc_ref[...]
        xhat, rstd = norm_parts(mid_ref[...])
        gm = norm_back(xhat, rstd, gn, gain_ref[...]) + g.astype(F32)
        gm_ref[...] = gm
        gb = gm.astype(BF)
        gb_ref[...] = gb
        weight = jnp.concatenate([pwo_ref[...], pwp_ref[...]], axis=0)
        ga_ref[...] = nt(gb, weight).astype(BF)
        sums_ref[...] = jnp.concatenate(
            [rowsum(gn * xhat), rowsum(gn), rowsum(gb), rowsum(g)]
            + [jnp.zeros((4, gn.shape[1]), F32)], axis=0
        )


def post_bwd(g, kept, w):
    n, d = g.shape
    half = w["pw_o"].shape[0]
    fh = w["up_o"].shape[1]
    fb = fh // 2
    cols = lambda rows: pl.BlockSpec((rows, fb), lambda j: (0, j))
    rows_ = pl.BlockSpec((fb, d), lambda j: (j, 0))
    return pl.pallas_call(
        post_bwd_kernel,
        grid=(2,),
        in_specs=[
            whole((n, d)), whole((n, d)), whole((1, d)), cols(n), cols(n), cols(d), cols(d),
            rows_, rows_, whole((half, d)), whole((half, d)),
        ],
        out_specs=[
            cols(n), cols(n), whole((n, d)), whole((n, d)), whole((n, d)), whole((8, d)),
            cols(1), cols(1),
        ],
        out_shape=[
            sds((n, fh), BF), sds((n, fh), BF), sds((n, d), F32), sds((n, d), BF),
            sds((n, d), BF), sds((8, d), F32), sds((1, fh), F32), sds((1, fh), F32),
        ],
        scratch_shapes=[pltpu.VMEM((n, d), F32)],
        compiler_params=params(),
        name="post_bwd",
    )(
        g, kept["mid"], w["g2"], kept["dg_o"], kept["dg_p"], w["up_o"], w["up_p"], w["dn_o"],
        w["dn_p"], w["pw_o"], w["pw_p"],
    )


def attn_bwd_kernel(q_ref, k_ref, v_ref, ga_ref, l_ref, d_ref, s_ref, *, nimg, plen, vlen):
    sums = [jnp.zeros((1, 128), F32) for _ in range(3)]
    for im in range(nimg):
        r0 = im * plen
        k = k_ref[0, r0 : r0 + plen]
        v = v_ref[0, r0 : r0 + plen]
        kt = k.T
        dk = jnp.zeros((plen, 128), F32)
        dv = jnp.zeros((plen, 128), F32)
        for q0, qw in qblocks(plen):
            q = q_ref[0, r0 + q0 : r0 + q0 + qw]
            ga = ga_ref[r0 + q0 : r0 + q0 + qw]
            head = lax.broadcasted_iota(jnp.int32, q.shape, 1) // HD
            outs = []
            for h in range(2):
                qm = jnp.where(head == h, q, jnp.zeros_like(q))
                gam = jnp.where(head == h, ga, jnp.zeros_like(ga))
                lse = l_ref[0, h : h + 1, r0 + q0 : r0 + q0 + qw]
                st = mask_keys(nt(k, qm), vlen)
                p = jnp.exp(st * SCALE - lse)
                gp = nt(v, gam)
                dv += nn(p.astype(BF), gam)
                pg = p * gp
                ds = (pg - p * jnp.sum(pg, axis=0, keepdims=True)).astype(BF)
                dk += nn(ds, qm)
                outs.append(nn(kt[h * HD : (h + 1) * HD], ds))
            dq = (jnp.concatenate(outs, axis=0).T * SCALE).astype(BF)
            d_ref[0, r0 + q0 : r0 + q0 + qw] = dq
            sums[0] += rowsum(dq)
        dkb = (dk * SCALE).astype(BF)
        dvb = dv.astype(BF)
        d_ref[1, r0 : r0 + plen] = dkb
        d_ref[2, r0 : r0 + plen] = dvb
        sums[2] += rowsum(dvb)
    s_ref[...] = jnp.concatenate(sums + [jnp.zeros((5, 128), F32)], axis=0)


def attn_bwd(qkv, ga, lse, chunk):
    nimg, plen, vlen = chunk
    _, n, d = qkv.shape
    pairs = d // 128
    return pl.pallas_call(
        functools.partial(attn_bwd_kernel, nimg=nimg, plen=plen, vlen=vlen),
        grid=(pairs,),
        in_specs=[pl.BlockSpec((1, n, 128), lambda p, s=s: (s, 0, p)) for s in range(3)]
        + [pl.BlockSpec((n, 128), lambda p: (0, p)), pl.BlockSpec((1, 2, n), lambda p: (p, 0, 0))],
        out_specs=[
            pl.BlockSpec((3, n, 128), lambda p: (0, 0, p)),
            pl.BlockSpec((8, 128), lambda p: (0, p)),
        ],
        out_shape=[sds((3, n, d), BF), sds((8, d), F32)],
        compiler_params=params(),
        name="attn_bwd",
    )(qkv, qkv, qkv, ga, lse)


def pre_bwd_kernel(d_ref, wo_ref, wp_ref, x_ref, gain_ref, gm_ref, out_ref, sums_ref, acc_ref):
    j = pl.program_id(0)
    weight = jnp.concatenate([wo_ref[0], wp_ref[0]], axis=1)
    part = nt(d_ref[0], weight)

    @pl.when(j == 0)
    def _():
        acc_ref[...] = part

    @pl.when(j > 0)
    def _():
        acc_ref[...] += part

    @pl.when(j == pl.num_programs(0) - 1)
    def _():
        gn = acc_ref[...]
        xhat, rstd = norm_parts(x_ref[...].astype(F32))
        out_ref[...] = (norm_back(xhat, rstd, gn, gain_ref[...]) + gm_ref[...]).astype(BF)
        sums_ref[...] = jnp.concatenate(
            [rowsum(gn * xhat), rowsum(gn), jnp.zeros((6, gn.shape[1]), F32)], axis=0
        )


def pre_bwd(dqkv, x, gm, w):
    _, n, d = dqkv.shape
    half = w["wqkv_o"].shape[-1]
    return pl.pallas_call(
        pre_bwd_kernel,
        grid=(3,),
        in_specs=[
            pl.BlockSpec((1, n, d), lambda s: (s, 0, 0)),
            pl.BlockSpec((1, d, half), lambda s: (s, 0, 0)),
            pl.BlockSpec((1, d, half), lambda s: (s, 0, 0)),
            whole((n, d)), whole((1, d)), whole((n, d)),
        ],
        out_specs=[whole((n, d)), whole((8, d))],
        out_shape=[sds((n, d), BF), sds((8, d), F32)],
        scratch_shapes=[pltpu.VMEM((n, d), F32)],
        compiler_params=params(),
        name="pre_bwd",
    )(dqkv, w["wqkv_o"], w["wqkv_p"], x, w["g1"], gm)


def backward(g, kept, w, chunk):
    pre_o, pre_p, gm, gb, ga, sums2, so, sp = post_bwd(g, kept, w)
    dqkv, sums_qkv = attn_bwd(kept["qkv"], ga, kept["lse"], chunk)
    gx, sums1 = pre_bwd(dqkv, kept["x"], gm, w)
    return (g, pre_o, pre_p, gb, dqkv, sums2, so, sp, sums_qkv, sums1, gx)


def wgrad_qkv_kernel(*refs, count):
    a_refs, g_refs, (o_ref, p_ref) = refs[:count], refs[count : 2 * count], refs[2 * count :]
    total = sum(tn(a[...], g[0]) for a, g in zip(a_refs, g_refs))
    half = o_ref.shape[-1]
    o_ref[0] = total[:, :half].astype(BF)
    p_ref[0] = total[:, half:].astype(BF)


def wgrad_qkv(a_list, g_list):
    d = a_list[0].shape[1]
    half = d // 2
    return pl.pallas_call(
        functools.partial(wgrad_qkv_kernel, count=len(a_list)),
        grid=(3,),
        in_specs=[whole(a.shape) for a in a_list]
        + [pl.BlockSpec((1,) + g.shape[1:], lambda s: (s, 0, 0)) for g in g_list],
        out_specs=[pl.BlockSpec((1, d, half), lambda s: (s, 0, 0))] * 2,
        out_shape=[sds((3, d, half), BF)] * 2,
        compiler_params=params(),
        name="wgrad_qkv",
    )(*a_list, *g_list)


def wgrad_kernel(*refs, count):
    a_refs, g_refs, o_ref = refs[:count], refs[count : 2 * count], refs[2 * count]
    o_ref[...] = sum(tn(a[...], g[...]) for a, g in zip(a_refs, g_refs)).astype(BF)


def wgrad(a_list, g_list, split_a, block):
    m, k = a_list[0].shape[1], g_list[0].shape[1]
    whole_m = whole if split_a else None
    if split_a:
        grid = m // block
        a_specs = [pl.BlockSpec((a.shape[0], block), lambda j: (0, j)) for a in a_list]
        g_specs = [whole(g.shape) for g in g_list]
        out = pl.BlockSpec((block, k), lambda j: (j, 0))
    else:
        grid = k // block
        a_specs = [whole(a.shape) for a in a_list]
        g_specs = [pl.BlockSpec((g.shape[0], block), lambda j: (0, j)) for g in g_list]
        out = pl.BlockSpec((m, block), lambda j: (0, j))
    return pl.pallas_call(
        functools.partial(wgrad_kernel, count=len(a_list)),
        grid=(grid,),
        in_specs=a_specs + g_specs,
        out_specs=out,
        out_shape=sds((m, k), BF),
        compiler_params=params(),
        name="wgrad",
    )(*a_list, *g_list)


def blank_kernel(*refs):
    pass


def blank(like):
    shapes = [sds(a.shape, a.dtype) for a in like]
    return tuple(
        pl.pallas_call(
            blank_kernel,
            out_shape=shapes,
            out_specs=[pl.BlockSpec(memory_space=pl.ANY) for _ in shapes],
            name="blank",
        )()
    )


KEPT = ("x", "normed", "qkv", "att", "lse", "mid", "n2", "act_o", "act_p", "dg_o", "dg_p", "out")


def swap(array, axis, pairs):
    return lax.ppermute(array, axis, pairs)


def body(
    patches, out_grad, large_place, norm1_gain, norm1_bias, qkv_weight, qv_bias, proj_weight,
    proj_bias, norm2_gain, norm2_bias, up_weight, up_bias, down_weight, down_bias,
):
    d = patches.shape[1]
    rows = LEN_LARGE + SMALL_MB * LEN_SMALL
    half = qkv_weight.shape[-1]
    section = lax.axis_index("section")
    lane = lax.axis_index("tensor")
    both = [(0, 1), (1, 0)]
    other = lambda array: lax.ppermute(array, "tensor", both)

    wqkv, pw, up, dn = qkv_weight[0], proj_weight[0], up_weight[0], down_weight[0]
    small = jnp.concatenate([qv_bias[0].reshape(-1), up_bias[0]])
    small_p = other(small)
    zero_bias = jnp.zeros((half,), F32)

    def qkv_bias(own, partner):
        own, partner = own[: 2 * half].reshape(2, half), partner[: 2 * half].reshape(2, half)
        return jnp.stack(
            [
                jnp.concatenate([own[0], partner[0]]),
                jnp.concatenate([zero_bias, zero_bias]),
                jnp.concatenate([own[1], partner[1]]),
            ]
        )[:, None, :]

    w = {
        "g1": norm1_gain, "b1": norm1_bias, "g2": norm2_gain, "b2": norm2_bias,
        "pb": proj_bias, "db": down_bias,
        "wqkv_o": wqkv, "wqkv_p": other(wqkv), "pw_o": pw, "pw_p": other(pw),
        "up_o": up, "up_p": other(up), "dn_o": dn, "dn_p": other(dn),
        "bqkv": qkv_bias(small, small_p),
        "ub_o": small[None, 2 * half :], "ub_p": small_p[None, 2 * half :],
    }

    place = lax.dynamic_index_in_dim(large_place, lane, 0, keepdims=False)
    base = lane * rows
    starts = [place * LEN_SMALL]
    for j in range(SMALL_MB):
        slot = j + (j >= place).astype(jnp.int32)
        starts.append(slot * LEN_SMALL + (LEN_LARGE - LEN_SMALL) * (slot > place).astype(jnp.int32))
    lens = [LEN_LARGE] + [LEN_SMALL] * SMALL_MB

    def pieces(array):
        out, at = [], 0
        for nimg, plen, vlen in CHUNKS:
            parts = []
            for _ in range(nimg):
                part = lax.dynamic_slice(array, (base + starts[at], 0), (vlen, d))
                parts.append(jnp.pad(part, ((0, plen - vlen), (0, 0))))
                at += 1
            out.append(parts[0] if nimg == 1 else jnp.concatenate(parts, axis=0))
        return out

    def restore(parts):
        mine = jnp.zeros((rows, d), BF)
        at = 0
        for (nimg, plen, vlen), part in zip(CHUNKS, parts):
            for i in range(nimg):
                mine = lax.dynamic_update_slice(
                    mine, part[i * plen : i * plen + vlen], (starts[at], 0)
                )
                at += 1
        theirs = other(mine)
        first = lane == 0
        return jnp.concatenate([jnp.where(first, mine, theirs), jnp.where(first, theirs, mine)])

    xs = pieces(patches)
    gs = pieces(out_grad)

    fwd_like = [
        jax.eval_shape(functools.partial(forward, chunk=chunk), x, w)
        for x, chunk in zip(xs, CHUNKS)
    ]
    kept = []
    for x, chunk, like in zip(xs, CHUNKS, fwd_like):
        kept.append(
            lax.cond(
                section == 0,
                lambda x=x, chunk=chunk: tuple(forward(x, w, chunk)),
                lambda like=like: blank(like),
            )
        )
    received = [lax.ppermute(k[-1], "section", [(0, 1)]) for k in kept]
    kept = [
        lax.cond(
            section == 1,
            lambda r=r, chunk=chunk: tuple(forward(r, w, chunk)),
            lambda k=k: tuple(k),
        )
        for r, k, chunk in zip(received, kept, CHUNKS)
    ]
    outputs = restore([k[-1] for k in kept])
    kept = [dict(zip(KEPT, k)) for k in kept]

    order = list(reversed(range(len(CHUNKS))))
    back = [None] * len(CHUNKS)
    for c in order:
        like = jax.eval_shape(
            functools.partial(backward, chunk=CHUNKS[c]), gs[c], kept[c], w
        )
        back[c] = lax.cond(
            section == 1,
            lambda c=c: tuple(backward(gs[c], kept[c], w, CHUNKS[c])),
            lambda like=like: blank(like),
        )
    received = [lax.ppermute(b[-1], "section", [(1, 0)]) for b in back]
    for c in order:
        back[c] = lax.cond(
            section == 0,
            lambda c=c: tuple(backward(received[c], kept[c], w, CHUNKS[c])),
            lambda c=c: tuple(back[c]),
        )
    input_grads = restore([b[-1] for b in back])

    g_all = [b[0] for b in back]
    pre_o = [b[1] for b in back]
    pre_p = [b[2] for b in back]
    gb = [b[3] for b in back]
    dqkv = [b[4] for b in back]
    field = lambda name: [k[name] for k in kept]

    def reduce(own, partner):
        return lax.psum(own + other(partner), "dp").astype(F32)

    g_dn = reduce(
        wgrad(field("act_o"), g_all, True, 768), wgrad(field("act_p"), g_all, True, 768)
    )
    g_up = reduce(
        wgrad(field("n2"), pre_o, False, 768), wgrad(field("n2"), pre_p, False, 768)
    )
    pw_all = wgrad(field("att"), gb, True, d)
    g_pw = reduce(pw_all[:half], pw_all[half:])
    g_qkv = reduce(*wgrad_qkv(field("normed"), dqkv))

    total = lambda i: sum(b[i] for b in back)
    sums2, so, sp, sums_qkv, sums1 = (total(i) for i in range(5, 10))
    full = jnp.concatenate([sums1[:2].reshape(-1), sums2[:4].reshape(-1)])
    qv = jnp.stack([sums_qkv[0], sums_qkv[2]])
    mine = jnp.concatenate([full, qv[:, :half].reshape(-1), so[0]])
    theirs = jnp.concatenate([full, qv[:, half:].reshape(-1), sp[0]])
    vec = lax.psum((mine + other(theirs)).reshape(-1, 128), "dp").reshape(-1)
    one = lambda i: vec[None, i * d : (i + 1) * d]
    return (
        outputs[None],
        input_grads[None],
        one(0),
        one(1),
        g_qkv[None],
        vec[6 * d : 6 * d + 2 * half].reshape(1, 2, half),
        g_pw[None],
        one(4),
        one(2),
        one(3),
        g_up[None],
        vec[None, 6 * d + 2 * half :],
        g_dn[None],
        one(5),
    )


def solution(mesh):
    placed = (
        P("dp", None), P("dp", None), P("dp"), P("section", None), P("section", None),
        P("section", None, None, "tensor"), P("section", None, "tensor"),
        P("section", "tensor", None), P("section", None), P("section", None),
        P("section", None), P("section", None, "tensor"), P("section", "tensor"),
        P("section", "tensor", None), P("section", None),
    )
    return jax.shard_map(
        body,
        mesh=mesh,
        in_specs=placed,
        out_specs=(
            P("section", "dp", None), P("section", "dp", None), P("section", None),
            P("section", None), P("section", None, None, "tensor"), P("section", None, "tensor"),
            P("section", "tensor", None), P("section", None), P("section", None),
            P("section", None), P("section", None, "tensor"), P("section", "tensor"),
            P("section", "tensor", None), P("section", None),
        ),
        check_vma=False,
    )
```

time: 2010 us -> 672 us (0.33)
  matrix products: 620 us -> 0 us
  waiting for transfers between devices: 697 us -> 291 us
  other arithmetic: 323 us -> 32 us
  local copies, waits for them, and re-layouts: 277 us -> 50.9 us
  Pallas kernels: 0 us -> 202 us
    dot_general x78 -> x0, matrix products: 620 us -> none  [the longest x12 154 us: block_scores(): jnp.einsum('qhd,khd->hqk', query_block, keys_all, preferred_element_type=...]
    psum x13 -> x1, waiting for transfers between devices: 489 us -> 149 us  [reduce(): return lax.psum(own + other(partner), 'dp').astype(F32)]
    pallas_call x0 -> x20, Pallas kernels: none -> 202 us  [the longest x2 36.9 us: attn_bwd(): pl.pallas_call(functools.partial(attn_bwd_kernel, nimg=nimg, plen=plen, v...]
    reduce_sum x57 -> x0, other arithmetic: 157 us -> none  [the longest x6 54.4 us: attend_forward(): row_total = jnp.sum(exp_scores, axis=-1, keepdims=True)]
    dynamic_slice x36 -> x4, local copies, waits for them, and re-layouts: 109 us -> 6.88 us  [the longest x3 5.64 us: pieces(): part = lax.dynamic_slice(array, (base + starts[at], 0), (vlen, d))]
    dynamic_update_slice x21 -> x0, other arithmetic: 87.6 us -> none  [store(): lax.dynamic_update_index_in_dim(buffer, jnp.where(is_valid, member, curre...]
    ppermute x6 -> x16, waiting for transfers between devices: 208 us -> 142 us  [the longest x2 136 us: body(): received = [lax.ppermute(b[-1], 'section', [(1, 0)]) for b in back]]
    convert_element_type x9 -> x0, other arithmetic: 59.1 us -> none  [the longest x6 58.2 us: attend_backward(): grad_scores = (probabilities * (grad_probs - jnp.sum(probabilities * grad...]
  transfers between devices with their start and end apart: 19 -> 17, of which waited for: 18 -> 3; matrix products, arithmetic and copies ran while one was open for 12% -> 10% of each run, Pallas kernels for 0% -> 18%
where the time goes in v1:
time: 672 us; the launch traced here: 664 us
  waiting for transfers between devices  291 us (43%)
  Pallas kernels  202 us (30%)
  local copies, waits for them, and re-layouts  50.9 us (8%)
  blocking collectives  42 us (6%)
  other arithmetic  32 us (5%)
  between operations  19.7 us (3%)
  loops' own time  16.2 us (2%)
  starting transfers between devices  10.6 us (2%)
    psum x1, waiting for transfers between devices, reduce(): return lax.psum(own + other(partner), 'dp').astype(F32)  149 us
    ppermute x2, waiting for transfers between devices, body(): received = [lax.ppermute(b[-1], 'section', [(1, 0)]) for b in back]  136 us
    psum x1, blocking collectives, body(): vec = lax.psum((mine + other(theirs)).reshape(-1, 128), 'dp').reshape(-1)  42 us
    pallas_call x2, Pallas kernels, attn_bwd(): pl.pallas_call(functools.partial(attn_bwd_kernel, nimg=nimg, plen=plen, v...  36.9 us
    pallas_call x2, Pallas kernels, post_bwd(): pl.pallas_call(post_bwd_kernel, grid=(2,), in_specs=[whole((n, d)), whole...  32.5 us
    pallas_call x2, Pallas kernels, attn_fwd(): pl.pallas_call(functools.partial(attn_fwd_kernel, nimg=nimg, plen=plen, v...  32.3 us
    pallas_call x5, Pallas kernels, wgrad(): pl.pallas_call(functools.partial(wgrad_kernel, count=len(a_list)), grid=(...  32 us
    pallas_call x2, Pallas kernels, post_fwd(): pl.pallas_call(post_fwd_kernel, grid=(2,), in_specs=[whole((n, d)), whole...  29.4 us
  transfers between devices with their start and end apart: 17, of which 3 were waited for; matrix products, arithmetic and copies ran while one was open for 10% of the time, Pallas kernels for 18%

profile of v1, /device:TPU:0, one launch (start us, length us, event | category | flops | bytes accessed | tf_op | source)
XLA Modules:
  0.0 663.7 jit_solution(2107640730488546928)
XLA Ops:
  19.8 32.5 %conditional.10 = ((bf16[624,768]{1,0:T(8,128)(2,1)}, bf16[624,768]{1,0:T(8,128)(2,1)}, bf16[3,624,768]{2,1,0:T(8,128)(2,1)}, bf16[624,768]{1,0:T(8,128)(2,1)}, ...) conditional(s32[]{:T(128)} %convert_element_type.21, () %tuple.83, ...), branch_computations={%region_4.5_spmd, %region_5.6_spmd} | conditional | bytes 15335584 | solution.py:552
  19.8 6.2 pre_fwd.6
  26.0 11.1 %attn_fwd.6 = (bf16[624,768]{1,0:T(8,128)(2,1)}, f32[6,2,624]{2,1,0:T(2,128)S(1)}) custom-call(bf16[3,624,768]{2,1,0:T(8,128)(2,1)S(1)} %get-tuple-element.968.q_ref.k_ref.v_ref, bf16[3,624,768]{2,1,0:T(8,128)(2,1)S(1)} %get-tuple-element.968.q_ref.k_ref.v_ref, bf16[3,624,768]{2,1,0:T(8,128)(2,1)S(1)} %get-tuple-element.968.q_ref.k_ref.v_ref), custom_call_target="tpu_custom_call" | custom-call | tf_op jit(solution)/shard_map/cond/branch_1_fun/attn_fwd/pallas_call | solution.py:134
  37.2 15.1 %post_fwd.6 = (f32[624,768]{1,0:T(8,128)}, bf16[624,768]{1,0:T(8,128)(2,1)}, bf16[624,1536]{1,0:T(8,128)(2,1)}, bf16[624,1536]{1,0:T(8,128)(2,1)}, bf16[624,1536...) custom-call(bf16[624,768]{1,0:T(8,128)(2,1)S(1)} %copy-done.14, ...), custom_call_target="tpu_custom_call" | custom-call | tf_op jit(solution)/shard_map/cond/branch_1_fun/post_fwd/pallas_call | solution.py:195
  57.7 42.6 %conditional.8 = ((bf16[592,768]{1,0:T(8,128)(2,1)}, bf16[592,768]{1,0:T(8,128)(2,1)}, bf16[3,592,768]{2,1,0:T(8,128)(2,1)}, bf16[592,768]{1,0:T(8,128)(2,1)}, f...) conditional(s32[]{:T(128)} %convert_element_type.21, () %tuple.80, ...), branch_computations={%region_0.1_spmd, %region_1.2_spmd} | conditional | bytes 16711868 | solution.py:552
  58.2 6.7 %pre_fwd.4 = (bf16[592,768]{1,0:T(8,128)(2,1)}, bf16[3,592,768]{2,1,0:T(8,128)(2,1)}) custom-call(bf16[592,768]{1,0:T(8,128)(2,1)} %get-tuple-element.918.x_ref, f32[1,768]{1,0:T(1,128)S(1)} %get-tuple-element.469.g_ref, f32[1,768]{1,0:T(1,128)S(1)} %get-tuple-element.470.b_ref, bf16[3,768,384]{2,1,0:T(8,128)(2,1)} %get-tuple-element.471.wo_ref, ...), custom_call_target="tpu_custom_call" | custom-call | tf_op jit(solution)/shard_map/cond/branch_1_fun/pre_fwd/pallas_call | solution.py:79
  64.9 21.1 %attn_fwd.4 = (bf16[592,768]{1,0:T(8,128)(2,1)S(1)}, f32[6,2,592]{2,1,0:T(2,128)S(1)}) custom-call(bf16[3,592,768]{2,1,0:T(8,128)(2,1)} %get-tuple-element.920.q_ref.k_ref.v_ref, bf16[3,592,768]{2,1,0:T(8,128)(2,1)} %get-tuple-element.920.q_ref.k_ref.v_ref, bf16[3,592,768]{2,1,0:T(8,128)(2,1)} %get-tuple-element.920.q_ref.k_ref.v_ref), custom_call_target="tpu_custom_call" | custom-call | tf_op jit(solution)/shard_map/cond/branch_1_fun/attn_fwd/pallas_call | solution.py:134
  86.1 14.2 %post_fwd.4 = (f32[592,768]{1,0:T(8,128)}, bf16[592,768]{1,0:T(8,128)(2,1)}, bf16[592,1536]{1,0:T(8,128)(2,1)}, bf16[592,1536]{1,0:T(8,128)(2,1)}, bf16[592,1536...) custom-call(bf16[592,768]{1,0:T(8,128)(2,1)S(1)} %copy-done.15, ...), custom_call_target="tpu_custom_call" | custom-call | tf_op jit(solution)/shard_map/cond/branch_1_fun/post_fwd/pallas_call | solution.py:195
  104.8 7.0 %conditional.14 = ((bf16[624,768]{1,0:T(8,128)(2,1)}, bf16[624,1536]{1,0:T(8,128)(2,1)}, bf16[624,1536]{1,0:T(8,128)(2,1)}, bf16[624,768]{1,0:T(8,128)(2,1)}, bf...) conditional(s32[]{:T(128)} %convert_element_type.20, () %tuple.89, ...), branch_computations={%region_12.13_spmd, %region_13.14_spmd} | conditional | bytes 18579608 | solution.py:576
  115.5 6.4 collective-permute-done.5
  122.1 7.5 %conditional.12 = ((bf16[592,768]{1,0:T(8,128)(2,1)}, bf16[592,1536]{1,0:T(8,128)(2,1)}, bf16[592,1536]{1,0:T(8,128)(2,1)}, bf16[592,768]{1,0:T(8,128)(2,1)}, bf...) conditional(s32[]{:T(128)} %convert_element_type.20, () %tuple.86, ...), branch_computations={%region_8.9_spmd, %region_9.10_spmd} | conditional | bytes 10715288 | solution.py:576
  130.9 135.6 %collective-permute-done.8 = bf16[592,768]{1,0:T(8,128)(2,1)} collective-permute-done((bf16[592,768]{1,0:T(8,128)(2,1)}, bf16[592,768]{1,0:T(8,128)(2,1)}, u32[]{:S(2)}, u32[]{:S(2)}) %collective-permute-start.8) | collective-permute-done | bytes 909344 | tf_op jit(solution)/shard_map/ppermute | solution.py:581
  266.6 48.2 %conditional.13 = ((bf16[592,768]{1,0:T(8,128)(2,1)}, bf16[592,1536]{1,0:T(8,128)(2,1)}, bf16[592,1536]{1,0:T(8,128)(2,1)}, bf16[592,768]{1,0:T(8,128)(2,1)}, bf...) conditional(s32[]{:T(128)} %convert_element_type.21, ...), branch_computations={%region_10.11_spmd, %region_11.12_spmd} | conditional | bytes 12533912 | solution.py:583
  266.7 15.9 %post_bwd.5 = (bf16[592,1536]{1,0:T(8,128)(2,1)}, bf16[592,1536]{1,0:T(8,128)(2,1)}, f32[592,768]{1,0:T(8,128)}, bf16[592,768]{1,0:T(8,128)(2,1)}, bf16[592,768]...) custom-call(bf16[592,768]{1,0:T(8,128)(2,1)} %get-tuple-element.1035.g_ref, ...), custom_call_target="tpu_custom_call" | custom-call | tf_op jit(solution)/shard_map/cond/branch_1_fun/post_bwd/pallas_call | solution.py:269
  282.7 22.0 %attn_bwd.5 = (bf16[3,592,768]{2,1,0:T(8,128)(2,1)}, f32[8,768]{1,0:T(8,128)}) custom-call(bf16[3,592,768]{2,1,0:T(8,128)(2,1)} %get-tuple-element.627.q_ref.k_ref.v_ref, bf16[3,592,768]{2,1,0:T(8,128)(2,1)} %get-tuple-element.627.q_ref.k_ref.v_ref, bf16[3,592,768]{2,1,0:T(8,128)(2,1)} %get-tuple-element.627.q_ref.k_ref.v_ref, ...), custom_call_target="tpu_custom_call" | custom-call | tf_op jit(solution)/shard_map/cond/branch_1_fun/attn_bwd/pallas_call | solution.py:334
  304.8 7.9 %pre_bwd.5 = (bf16[592,768]{1,0:T(8,128)(2,1)}, f32[8,768]{1,0:T(8,128)}) custom-call(bf16[3,592,768]{2,1,0:T(8,128)(2,1)} %get-tuple-element.1039.d_ref, bf16[3,768,384]{2,1,0:T(8,128)(2,1)S(1)} %copy-done.9, bf16[3,768,384]{2,1,0:T(8,128)(2,1)} %get-tuple-element.636.wp_ref, bf16[592,768]{1,0:T(8,128)(2,1)S(1)} %copy-done.17, ...), custom_call_target="tpu_custom_call" | custom-call | tf_op jit(solution)/shard_map/cond/branch_1_fun/pre_bwd/pallas_call | solution.py:375
  314.8 42.8 %conditional.15 = ((bf16[624,768]{1,0:T(8,128)(2,1)}, bf16[624,1536]{1,0:T(8,128)(2,1)}, bf16[624,1536]{1,0:T(8,128)(2,1)}, bf16[624,768]{1,0:T(8,128)(2,1)}, bf...) conditional(s32[]{:T(128)} %convert_element_type.21, ...), branch_computations={%region_14.15_spmd, %region_15.16_spmd} | conditional | bytes 20496536 | solution.py:583
  315.0 16.6 %post_bwd.7 = (bf16[624,1536]{1,0:T(8,128)(2,1)}, bf16[624,1536]{1,0:T(8,128)(2,1)}, f32[624,768]{1,0:T(8,128)}, bf16[624,768]{1,0:T(8,128)(2,1)}, bf16[624,768]...) custom-call(bf16[624,768]{1,0:T(8,128)(2,1)} %get-tuple-element.1079.g_ref, ...), custom_call_target="tpu_custom_call" | custom-call | tf_op jit(solution)/shard_map/cond/branch_1_fun/post_bwd/pallas_call | solution.py:269
  331.6 14.9 %attn_bwd.7 = (bf16[3,624,768]{2,1,0:T(8,128)(2,1)S(1)}, f32[8,768]{1,0:T(8,128)}) custom-call(bf16[3,624,768]{2,1,0:T(8,128)(2,1)S(1)} %get-tuple-element.685.q_ref.k_ref.v_ref, bf16[3,624,768]{2,1,0:T(8,128)(2,1)S(1)} %get-tuple-element.685.q_ref.k_ref.v_ref, bf16[3,624,768]{2,1,0:T(8,128)(2,1)S(1)} %get-tuple-element.685.q_ref.k_ref.v_ref, ...), custom_call_target="tpu_custom_call" | custom-call | tf_op jit(solution)/shard_map/cond/branch_1_fun/attn_bwd/pallas_call | solution.py:334
  346.5 8.7 %pre_bwd.7 = (bf16[624,768]{1,0:T(8,128)(2,1)}, f32[8,768]{1,0:T(8,128)}) custom-call(bf16[3,624,768]{2,1,0:T(8,128)(2,1)S(1)} %get-tuple-element.1083.d_ref, bf16[3,768,384]{2,1,0:T(8,128)(2,1)S(1)} %copy-done.10, bf16[3,768,384]{2,1,0:T(8,128)(2,1)} %get-tuple-element.694.wp_ref, bf16[624,768]{1,0:T(8,128)(2,1)} %get-tuple-element.695.x_ref, ...), custom_call_target="tpu_custom_call" | custom-call | tf_op jit(solution)/shard_map/cond/branch_1_fun/pre_bwd/pallas_call | solution.py:375
  357.6 7.3 %wgrad.9 = bf16[1536,768]{1,0:T(8,128)(2,1)} custom-call(bf16[592,1536]{1,0:T(8,128)(2,1)} %get-tuple-element.851.refs_0_, bf16[624,1536]{1,0:T(8,128)(2,1)} %get-tuple-element.817.refs_1_, bf16[592,768]{1,0:T(8,128)(2,1)} %get-tuple-element.855.refs_2_, bf16[624,768]{1,0:T(8,128)(2,1)} %get-tuple-element.815.refs_3_), custom_call_target="tpu_custom_call" | custom-call | tf_op jit(solution)/shard_map/wgrad/pallas_call | solution.py:440
  364.9 9.1 %wgrad_qkv.1 = (bf16[3,768,384]{2,1,0:T(8,128)(2,1)}, bf16[3,768,384]{2,1,0:T(8,128)(2,1)}) custom-call(bf16[592,768]{1,0:T(8,128)(2,1)} %get-tuple-element.844.refs_0_, bf16[624,768]{1,0:T(8,128)(2,1)} %get-tuple-element.797.refs_1_, bf16[3,592,768]{2,1,0:T(8,128)(2,1)} %get-tuple-element.859.refs_2_, bf16[3,624,768]{2,1,0:T(8,128)(2,1)S(1)} %copy-done.13), custom_call_target="tpu_custom_call" | custom-call | tf_op jit(solution)/shard_map/wgrad_qkv/pallas_call | solution.py:410
  374.5 6.7 %wgrad.7 = bf16[768,1536]{1,0:T(8,128)(2,1)} custom-call(bf16[592,768]{1,0:T(8,128)(2,1)S(1)} %copy-done.29, bf16[624,768]{1,0:T(8,128)(2,1)S(1)} %copy-done.28, bf16[592,1536]{1,0:T(8,128)(2,1)} %get-tuple-element.857.refs_2_, bf16[624,1536]{1,0:T(8,128)(2,1)} %get-tuple-element.811.refs_3_), custom_call_target="tpu_custom_call" | custom-call | tf_op jit(solution)/shard_map/wgrad/pallas_call | solution.py:440
  381.3 4.7 wgrad.5
  388.4 6.6 wgrad.8
  395.0 6.7 %wgrad.6 = bf16[768,1536]{1,0:T(8,128)(2,1)} custom-call(bf16[592,768]{1,0:T(8,128)(2,1)S(1)} %copy-done.29, bf16[624,768]{1,0:T(8,128)(2,1)S(1)} %copy-done.28, bf16[592,1536]{1,0:T(8,128)(2,1)} %get-tuple-element.856.refs_2_, bf16[624,1536]{1,0:T(8,128)(2,1)} %get-tuple-element.809.refs_3_), custom_call_target="tpu_custom_call" | custom-call | tf_op jit(solution)/shard_map/wgrad/pallas_call | solution.py:440
  408.9 3.3 add_bitcast_fusion.1
  414.8 5.1 dynamic_update_slice.24
  430.1 4.3 dynamic_update_slice.28
  442.6 42.0 %psum.35 = f32[54,128]{1,0:T(8,128)S(1)} all-reduce(f32[54,128]{1,0:T(8,128)S(1)} %fusion.12), channel_id=1, replica_groups=mesh['section'=2,'tensor'=2,'dp'=8] {'dp'}, use_global_device_ids=true, to_apply=%region_16.17 | all-reduce | flops 6912 | bytes 55296 | tf_op jit(solution)/shard_map/psum | solution.py:616
  497.4 148.7 %all-reduce.11.cloned.1.call-done = (bf16[1,3,768,384]{3,2,1,0:T(8,128)(2,1)}, bf16[1,384,768]{2,1,0:T(8,128)(2,1)}, bf16[1,768,1536]{2,1,0:T(8,128)(2,1)}, bf16[1,1536,768]{2,1,0:T(8,128)(2,1)}) async-done(((bf16[1,3,768,384]{3,2,1,0:T(8,128)(2,1)}, bf16[1,384,768]{2,1,0:T(8,128)(2,1)}, bf16[1,768,1536]{2,1,0:T(8,128)(2,1)}, bf16[1,1536,768]{2,1,0:T(8,128)(2,1)}), (bf16[1,3,768,384]{3,2,1,0:T(8,128)(2,1)}, ...) | async-done | bytes 7077904 | tf_op jit(solution)/shard_map/psum | solution.py:598
  646.1 4.6 broadcast_in_dim.71
  (189 shorter events, 76.6 us)
Async XLA Ops:
  7.2 638.9 %all-reduce.11.cloned.1.call-start = ((), (), s32[]{:S(2)}) async-start(), calls=%async_computation | async-start | bytes 14155776 | tf_op jit(solution)/shard_map/psum | solution.py:598
  7.2 12.4 %collective-permute-start.3 = (bf16[768,1536]{1,0:T(8,128)(2,1)}, bf16[768,1536]{1,0:T(8,128)(2,1)}, u32[]{:S(2)}, u32[]{:S(2)}) collective-permute-start(bf16[768,1536]{1,0:T(8,128)(2,1)} %bitcast.62), channel_id=1, source_target_pairs={{0,8},{8,0},{1,9},{9,1},{2,10},{10,2},{3,11},{11,3},{4,12},{12,4},... | collective-permute-start | bytes 7077896 | tf_op jit(solution)/shard_map/ppermute | solution.py:484
  7.8 11.9 %collective-permute-start.4 = (bf16[1536,768]{1,0:T(8,128)(2,1)}, bf16[1536,768]{1,0:T(8,128)(2,1)}, u32[]{:S(2)}, u32[]{:S(2)}) collective-permute-start(bf16[1536,768]{1,0:T(8,128)(2,1)} %bitcast.71), channel_id=1, source_target_pairs={{0,8},{8,0},{1,9},{9,1},{2,10},{10,2},{3,11},{11,3},{4,12},{12,4},... | collective-permute-start | bytes 7077896 | tf_op jit(solution)/shard_map/ppermute | solution.py:484
  7.9 11.8 %collective-permute-start = (bf16[3,768,384]{2,1,0:T(8,128)(2,1)}, bf16[3,768,384]{2,1,0:T(8,128)(2,1)}, u32[]{:S(2)}, u32[]{:S(2)}) collective-permute-start(bf16[3,768,384]{2,1,0:T(8,128)(2,1)} %bitcast.80), channel_id=1, source_target_pairs={{0,8},{8,0},{1,9},{9,1},{2,10},{10,2},{3,11},{11,3},{4,12},{12,4},... | collective-permute-start | bytes 5308424 | tf_op jit(solution)/shard_map/ppermute | solution.py:484
  9.7 9.8 %collective-permute-start.1 = (f32[2304]{0:T(1024)S(1)}, f32[2304]{0:T(1024)S(1)}, u32[]{:S(2)}, u32[]{:S(2)}) collective-permute-start(f32[2304]{0:T(1024)S(1)} %pad_maximum_fusion.2), channel_id=1, source_target_pairs={{0,8},{8,0},{1,9},{9,1},{2,10},{10,2},{3,11},{11,3},{4,12},{12,4},... | collective-permute-start | bytes 27656 | tf_op jit(solution)/shard_map/ppermute | solution.py:484
  9.9 9.8 %collective-permute-start.2 = (bf16[384,768]{1,0:T(8,128)(2,1)}, bf16[384,768]{1,0:T(8,128)(2,1)}, u32[]{:S(2)}, u32[]{:S(2)}) collective-permute-start(bf16[384,768]{1,0:T(8,128)(2,1)} %bitcast.89), channel_id=1, source_target_pairs={{0,8},{8,0},{1,9},{9,1},{2,10},{10,2},{3,11},{11,3},{4,12},{12,4},... | collective-permute-start | bytes 1769480 | tf_op jit(solution)/shard_map/ppermute | solution.py:484
  26.0 11.1 %copy-start = (bf16[3,624,768]{2,1,0:T(8,128)(2,1)}, bf16[3,624,768]{2,1,0:T(8,128)(2,1)S(1)}, u32[]{:S(2)}) copy-start(bf16[3,624,768]{2,1,0:T(8,128)(2,1)S(1)} %get-tuple-element.968.q_ref.k_ref.v_ref) | copy-start | bytes 8626180 | tf_op jit(solution)/shard_map/cond
  26.0 11.1 %copy-start.14 = (bf16[624,768]{1,0:T(8,128)(2,1)S(1)}, bf16[624,768]{1,0:T(8,128)(2,1)}, u32[]{:S(2)}) copy-start(bf16[624,768]{1,0:T(8,128)(2,1)} %get-tuple-element.966.x_ref) | copy-start | bytes 2875396 | tf_op jit(solution)/shard_map/cond
  52.3 52.3 %collective-permute-start.6 = (bf16[624,768]{1,0:T(8,128)(2,1)}, bf16[624,768]{1,0:T(8,128)(2,1)}, u32[]{:S(2)}, u32[]{:S(2)}) collective-permute-start(bf16[624,768]{1,0:T(8,128)(2,1)} %get-tuple-element.768), channel_id=1, source_target_pairs={{0,16},{1,17},{2,18},{3,19},{4,20},{5,21},{6,22},{7,23},{8,24},{9,... | collective-permute-start | bytes 2875400 | tf_op jit(solution)/shard_map/ppermute | solution.py:558
  64.9 21.2 %copy-start.5 = (bf16[1536,768]{1,0:T(8,128)(2,1)S(1)}, bf16[1536,768]{1,0:T(8,128)(2,1)}, u32[]{:S(2)}) copy-start(bf16[1536,768]{1,0:T(8,128)(2,1)} %get-tuple-element.487.do_ref) | copy-start | bytes 7077892 | tf_op jit(solution)/shard_map/cond
  64.9 21.2 %copy-start.15 = (bf16[592,768]{1,0:T(8,128)(2,1)S(1)}, bf16[592,768]{1,0:T(8,128)(2,1)}, u32[]{:S(2)}) copy-start(bf16[592,768]{1,0:T(8,128)(2,1)} %get-tuple-element.918.x_ref) | copy-start | bytes 2727940 | tf_op jit(solution)/shard_map/cond
  86.0 14.3 %copy-start.24 = (bf16[592,768]{1,0:T(8,128)(2,1)}, bf16[592,768]{1,0:T(8,128)(2,1)S(1)}, u32[]{:S(2)}) copy-start(bf16[592,768]{1,0:T(8,128)(2,1)S(1)} %get-tuple-element.921.att_ref) | copy-start | bytes 2727940 | tf_op jit(solution)/shard_map/cond
  100.3 21.5 %collective-permute-start.5 = (bf16[592,768]{1,0:T(8,128)(2,1)}, bf16[592,768]{1,0:T(8,128)(2,1)}, u32[]{:S(2)}, u32[]{:S(2)}) collective-permute-start(bf16[592,768]{1,0:T(8,128)(2,1)} %get-tuple-element.766), channel_id=1, source_target_pairs={{0,16},{1,17},{2,18},{3,19},{4,20},{5,21},{6,22},{7,23},{8,24},{9,... | collective-permute-start | bytes 2727944 | tf_op jit(solution)/shard_map/ppermute | solution.py:558
  111.8 203.0 %collective-permute-start.9 = (bf16[624,768]{1,0:T(8,128)(2,1)}, bf16[624,768]{1,0:T(8,128)(2,1)}, u32[]{:S(2)}, u32[]{:S(2)}) collective-permute-start(bf16[624,768]{1,0:T(8,128)(2,1)} %get-tuple-element.784), channel_id=1, source_target_pairs={{16,0},{17,1},{18,2},{19,3},{20,4},{21,5},{22,6},{23,7},{24,8},{25... | collective-permute-start | bytes 2875400 | tf_op jit(solution)/shard_map/ppermute | solution.py:581
  129.6 136.9 %collective-permute-start.8 = (bf16[592,768]{1,0:T(8,128)(2,1)}, bf16[592,768]{1,0:T(8,128)(2,1)}, u32[]{:S(2)}, u32[]{:S(2)}) collective-permute-start(bf16[592,768]{1,0:T(8,128)(2,1)} %get-tuple-element.776), channel_id=1, source_target_pairs={{16,0},{17,1},{18,2},{19,3},{20,4},{21,5},{22,6},{23,7},{24,8},{25... | collective-permute-start | bytes 2727944 | tf_op jit(solution)/shard_map/ppermute | solution.py:581
  266.6 48.2 %copy-start.2 = (bf16[3,624,768]{2,1,0:T(8,128)(2,1)S(1)}, bf16[3,624,768]{2,1,0:T(8,128)(2,1)}, u32[]{:S(2)}) copy-start(bf16[3,624,768]{2,1,0:T(8,128)(2,1)} %get-tuple-element.781) | copy-start | bytes 8626180
  282.7 22.1 %copy-start.9 = (bf16[3,768,384]{2,1,0:T(8,128)(2,1)S(1)}, bf16[3,768,384]{2,1,0:T(8,128)(2,1)}, u32[]{:S(2)}) copy-start(bf16[3,768,384]{2,1,0:T(8,128)(2,1)} %get-tuple-element.635.wo_ref) | copy-start | bytes 5308420 | tf_op jit(solution)/shard_map/cond
  282.7 22.1 %copy-start.17 = (bf16[592,768]{1,0:T(8,128)(2,1)S(1)}, bf16[592,768]{1,0:T(8,128)(2,1)}, u32[]{:S(2)}) copy-start(bf16[592,768]{1,0:T(8,128)(2,1)} %get-tuple-element.637.x_ref) | copy-start | bytes 2727940 | tf_op jit(solution)/shard_map/cond
  331.6 14.9 %copy-start.10 = (bf16[3,768,384]{2,1,0:T(8,128)(2,1)S(1)}, bf16[3,768,384]{2,1,0:T(8,128)(2,1)}, u32[]{:S(2)}) copy-start(bf16[3,768,384]{2,1,0:T(8,128)(2,1)} %get-tuple-element.693.wo_ref) | copy-start | bytes 5308420 | tf_op jit(solution)/shard_map/cond
  346.5 8.7 %copy-start.12 = (bf16[3,624,768]{2,1,0:T(8,128)(2,1)}, bf16[3,624,768]{2,1,0:T(8,128)(2,1)S(1)}, u32[]{:S(2)}) copy-start(bf16[3,624,768]{2,1,0:T(8,128)(2,1)S(1)} %get-tuple-element.1083.d_ref) | copy-start | bytes 8626180 | tf_op jit(solution)/shard_map/cond
  357.6 7.3 %copy-start.13 = (bf16[3,624,768]{2,1,0:T(8,128)(2,1)S(1)}, bf16[3,624,768]{2,1,0:T(8,128)(2,1)}, u32[]{:S(2)}) copy-start(bf16[3,624,768]{2,1,0:T(8,128)(2,1)} %get-tuple-element.799.refs_3_) | copy-start | bytes 8626180
  364.9 41.5 %collective-permute-start.15 = (bf16[1536,768]{1,0:T(8,128)(2,1)}, bf16[1536,768]{1,0:T(8,128)(2,1)S(1)}, u32[]{:S(2)}, u32[]{:S(2)}) collective-permute-start(bf16[1536,768]{1,0:T(8,128)(2,1)} %wgrad.9), channel_id=1, source_target_pairs={{0,8},{8,0},{1,9},{9,1},{2,10},{10,2},{3,11},{11,3},{4,12},{12,4},... | collective-permute-start | bytes 7077896 | tf_op jit(solution)/shard_map/ppermute | solution.py:484
  364.9 9.6 %copy-start.28 = (bf16[624,768]{1,0:T(8,128)(2,1)S(1)}, bf16[624,768]{1,0:T(8,128)(2,1)}, u32[]{:S(2)}) copy-start(bf16[624,768]{1,0:T(8,128)(2,1)} %get-tuple-element.807.refs_1_) | copy-start | bytes 2875396
  364.9 9.6 %copy-start.29 = (bf16[592,768]{1,0:T(8,128)(2,1)S(1)}, bf16[592,768]{1,0:T(8,128)(2,1)}, u32[]{:S(2)}) copy-start(bf16[592,768]{1,0:T(8,128)(2,1)} %get-tuple-element.849.refs_0_) | copy-start | bytes 2727940
  374.1 28.5 %collective-permute-start.12 = (bf16[3,768,384]{2,1,0:T(8,128)(2,1)}, bf16[3,768,384]{2,1,0:T(8,128)(2,1)}, u32[]{:S(2)}, u32[]{:S(2)}) collective-permute-start(bf16[3,768,384]{2,1,0:T(8,128)(2,1)} %get-tuple-element.801), channel_id=1, source_target_pairs={{0,8},{8,0},{1,9},{9,1},{2,10},{10,2},{3,11},{11,3},{4,12},{12,4},... | collective-permute-start | bytes 5308424 | tf_op jit(solution)/shard_map/ppermute | solution.py:484
  381.3 26.8 %collective-permute-start.14 = (bf16[768,1536]{1,0:T(8,128)(2,1)}, bf16[768,1536]{1,0:T(8,128)(2,1)}, u32[]{:S(2)}, u32[]{:S(2)}) collective-permute-start(bf16[768,1536]{1,0:T(8,128)(2,1)} %wgrad.7), channel_id=1, source_target_pairs={{0,8},{8,0},{1,9},{9,1},{2,10},{10,2},{3,11},{11,3},{4,12},{12,4},... | collective-permute-start | bytes 7077896 | tf_op jit(solution)/shard_map/ppermute | solution.py:484
  381.3 7.1 %copy-start.19 = (bf16[592,768]{1,0:T(8,128)(2,1)S(1)}, bf16[592,768]{1,0:T(8,128)(2,1)}, u32[]{:S(2)}) copy-start(bf16[592,768]{1,0:T(8,128)(2,1)} %get-tuple-element.855.refs_2_) | copy-start | bytes 2727940
  387.9 13.8 %collective-permute-start.13 = (bf16[384,768]{1,0:T(8,128)(2,1)}, bf16[384,768]{1,0:T(8,128)(2,1)S(1)}, u32[]{:S(2)}, u32[]{:S(2)}) collective-permute-start(bf16[384,768]{1,0:T(8,128)(2,1)} %slice.164), channel_id=1, source_target_pairs={{0,8},{8,0},{1,9},{9,1},{2,10},{10,2},{3,11},{11,3},{4,12},{12,4},... | collective-permute-start | bytes 1769480 | tf_op jit(solution)/shard_map/ppermute | solution.py:484
  428.5 60.7 %collective-permute-start.7 = (bf16[1168,768]{1,0:T(8,128)(2,1)}, bf16[1168,768]{1,0:T(8,128)(2,1)}, u32[]{:S(2)}, u32[]{:S(2)}) collective-permute-start(bf16[1168,768]{1,0:T(8,128)(2,1)} %dynamic_update_slice.27), channel_id=1, source_target_pairs={{0,8},{8,0},{1,9},{9,1},{2,10},{10,2},{3,11},{11,3},{4,12},{12,4},... | collective-permute-start | bytes 5382152 | tf_op jit(solution)/shard_map/ppermute | solution.py:484
  435.2 7.3 %copy-start.48 = (f32[1,1536]{1,0:T(1,128)S(1)}, f32[1,1536]{1,0:T(1,128)}, u32[]{:S(2)}) copy-start(f32[1,1536]{1,0:T(1,128)} %get-tuple-element.861) | copy-start | bytes 18436
  435.3 7.2 %collective-permute-start.11 = (f32[6912]{0:T(1024)S(1)}, f32[6912]{0:T(1024)S(1)}, u32[]{:S(2)}, u32[]{:S(2)}) collective-permute-start(f32[6912]{0:T(1024)S(1)} %pad_maximum_fusion.1), channel_id=1, source_target_pairs={{0,8},{8,0},{1,9},{9,1},{2,10},{10,2},{3,11},{11,3},{4,12},{12,4},... | collective-permute-start | bytes 82952 | tf_op jit(solution)/shard_map/ppermute | solution.py:484
  442.4 51.2 %collective-permute-start.10 = (bf16[1168,768]{1,0:T(8,128)(2,1)S(1)}, bf16[1168,768]{1,0:T(8,128)(2,1)}, u32[]{:S(2)}, u32[]{:S(2)}) collective-permute-start(bf16[1168,768]{1,0:T(8,128)(2,1)S(1)} %dynamic_update_slice.31), channel_id=1, source_target_pairs={{0,8},{8,0},{1,9},{9,1},{2,10},{10,2},{3,11},{11,3},{4,12},{12,4},... | collective-permute-start | bytes 5382152 | tf_op jit(solution)/shard_map/ppermute | solution.py:484
  (27 other events, 97.0 us)
Sparse Core Ops, SparseCore 0:
  412.4 233.6 all-reduce.10

commit v2 on v1

--- a/solution.py
+++ b/solution.py
@@ -396,56 +396,284 @@
     return (g, pre_o, pre_p, gb, dqkv, sums2, so, sp, sums_qkv, sums1, gx)
 
 
-def wgrad_qkv_kernel(*refs, count):
-    a_refs, g_refs, (o_ref, p_ref) = refs[:count], refs[count : 2 * count], refs[2 * count :]
-    total = sum(tn(a[...], g[0]) for a, g in zip(a_refs, g_refs))
+def wgrad_mlp_kernel(*refs, more):
+    ao, ap, n2, po, pp, g = refs[:6]
+    init = refs[6 : 6 + more]
+    outs = refs[6 + more :]
+    g, n2 = g[...], n2[...]
+    results = (
+        tn(ao[...], g), tn(ap[...], g), tn(n2, po[...]), tn(n2, pp[...]),
+    )
+    for i, (out, value) in enumerate(zip(outs, results)):
+        if more:
+            value += init[i][...].astype(F32)
+        out[...] = value.astype(BF)
+
+
+def wgrad_mlp(kept, back, init=()):
+    n, d = back["g"].shape
+    fh = kept["act_o"].shape[1]
+    fb = fh // 4
+    cols = lambda rows: pl.BlockSpec((rows, fb), lambda j: (0, j))
+    rows_ = pl.BlockSpec((fb, d), lambda j: (j, 0))
+    outs = [rows_, rows_, cols(d), cols(d)]
+    return pl.pallas_call(
+        functools.partial(wgrad_mlp_kernel, more=len(init)),
+        grid=(4,),
+        in_specs=[cols(n), cols(n), whole((n, d)), cols(n), cols(n), whole((n, d))]
+        + outs[: len(init)],
+        out_specs=outs,
+        out_shape=[sds((fh, d), BF)] * 2 + [sds((d, fh), BF)] * 2,
+        compiler_params=params(),
+        name="wgrad_mlp",
+    )(kept["act_o"], kept["act_p"], kept["n2"], back["pre_o"], back["pre_p"], back["g"], *init)
+
+
+def wgrad_attn_kernel(*refs, more):
+    normed, dqkv, att, gb = refs[:4]
+    init = refs[4 : 4 + more]
+    o_ref, p_ref, w_ref = refs[4 + more :]
+    total = tn(normed[...], dqkv[0])
+    branch = tn(att[...], gb[...])
     half = o_ref.shape[-1]
-    o_ref[0] = total[:, :half].astype(BF)
-    p_ref[0] = total[:, half:].astype(BF)
-
-
-def wgrad_qkv(a_list, g_list):
-    d = a_list[0].shape[1]
-    half = d // 2
-    return pl.pallas_call(
-        functools.partial(wgrad_qkv_kernel, count=len(a_list)),
+    own, partner = total[:, :half], total[:, half:]
+    if more:
+        own += init[0][0].astype(F32)
+        partner += init[1][0].astype(F32)
+        branch += init[2][...].astype(F32)
+    o_ref[0] = own.astype(BF)
+    p_ref[0] = partner.astype(BF)
+    w_ref[...] = branch.astype(BF)
+
+
+def wgrad_attn(kept, back, init=()):
+    n, d = kept["normed"].shape
+    half, block = d // 2, d // 3
+    part = pl.BlockSpec((1, d, half), lambda s: (s, 0, 0))
+    outs = [part, part, pl.BlockSpec((block, d), lambda s: (s, 0))]
+    return pl.pallas_call(
+        functools.partial(wgrad_attn_kernel, more=len(init)),
         grid=(3,),
-        in_specs=[whole(a.shape) for a in a_list]
-        + [pl.BlockSpec((1,) + g.shape[1:], lambda s: (s, 0, 0)) for g in g_list],
-        out_specs=[pl.BlockSpec((1, d, half), lambda s: (s, 0, 0))] * 2,
-        out_shape=[sds((3, d, half), BF)] * 2,
-        compiler_params=params(),
-        name="wgrad_qkv",
-    )(*a_list, *g_list)
-
-
-def wgrad_kernel(*refs, count):
-    a_refs, g_refs, o_ref = refs[:count], refs[count : 2 * count], refs[2 * count]
-    o_ref[...] = sum(tn(a[...], g[...]) for a, g in zip(a_refs, g_refs)).astype(BF)
-
-
-def wgrad(a_list, g_list, split_a, block):
-    m, k = a_list[0].shape[1], g_list[0].shape[1]
-    whole_m = whole if split_a else None
-    if split_a:
-        grid = m // block
-        a_specs = [pl.BlockSpec((a.shape[0], block), lambda j: (0, j)) for a in a_list]
-        g_specs = [whole(g.shape) for g in g_list]
-        out = pl.BlockSpec((block, k), lambda j: (j, 0))
-    else:
-        grid = k // block
-        a_specs = [whole(a.shape) for a in a_list]
-        g_specs = [pl.BlockSpec((g.shape[0], block), lambda j: (0, j)) for g in g_list]
-        out = pl.BlockSpec((m, block), lambda j: (0, j))
-    return pl.pallas_call(
-        functools.partial(wgrad_kernel, count=len(a_list)),
-        grid=(grid,),
-        in_specs=a_specs + g_specs,
-        out_specs=out,
-        out_shape=sds((m, k), BF),
-        compiler_params=params(),
-        name="wgrad",
-    )(*a_list, *g_list)
+        in_specs=[
+            whole((n, d)), pl.BlockSpec((1, n, d), lambda s: (s, 0, 0)),
+            pl.BlockSpec((n, block), lambda s: (0, s)), whole((n, d)),
+        ]
+        + outs[: len(init)],
+        out_specs=outs,
+        out_shape=[sds((3, d, half), BF)] * 2 + [sds((d, d), BF)],
+        compiler_params=params(),
+        name="wgrad_attn",
+    )(kept["normed"], back["dqkv"], kept["att"], back["gb"], *init)
+
+
+RING = 8
+WAYS = (1, 1, -1, -1, -1)
+
+
+def ring_kernel(*refs, n):
+    owns, others, vec_ref = refs[:n], refs[n : 2 * n], refs[2 * n]
+    outs, vsum_ref = refs[2 * n + 1 : 3 * n + 1], refs[3 * n + 1]
+    slots, vslot = refs[3 * n + 2 : 4 * n + 2], refs[4 * n + 2]
+    send, recv, vsend, vrecv = refs[4 * n + 3 :]
+    me = lax.axis_index("dp")
+    z, x = me // 2, me % 2
+    pos = z + x * (RING - 1 - 2 * z)
+
+    def member(p):
+        p = p % RING
+        return {"dp": 2 * p + (p // (RING // 2)) * (2 * RING - 1 - 4 * p)}
+
+    barrier = pltpu.get_barrier_semaphore()
+    for k in range(1, RING):
+        pl.semaphore_signal(
+            barrier, inc=1, device_id=member(pos + k), device_id_type=pl.DeviceIdType.MESH
+        )
+    pl.semaphore_wait(barrier, RING - 1)
+
+    def part(ref, chunk):
+        rows = ref.shape[0] // RING
+        return ref.at[pl.ds(pl.multiple_of((chunk % RING) * rows, rows), rows)]
+
+    def mine(a, chunk):
+        return part(owns[a], chunk)[...].astype(F32) + part(others[a], chunk)[...].astype(F32)
+
+    def remote(src, dst, a, step):
+        return pltpu.make_async_remote_copy(
+            src_ref=src,
+            dst_ref=dst,
+            send_sem=send.at[a, step],
+            recv_sem=recv.at[a, step],
+            device_id=member(pos + WAYS[a] + RING),
+            device_id_type=pl.DeviceIdType.MESH,
+        )
+
+    def vcopy(k):
+        return pltpu.make_async_remote_copy(
+            src_ref=vec_ref,
+            dst_ref=vslot.at[k - 1],
+            send_sem=vsend.at[k - 1],
+            recv_sem=vrecv.at[k - 1],
+            device_id=member(pos + k),
+            device_id_type=pl.DeviceIdType.MESH,
+        )
+
+    for a in range(n):
+        slots[a][0] = mine(a, pos).astype(BF)
+        remote(slots[a].at[0], slots[a].at[1], a, 0).start()
+    for k in range(1, RING):
+        vcopy(k).start()
+
+    def scatter(s, carry):
+        for a in range(n):
+            here = slots[a].at[s]
+            remote(here, here, a, s - 1).wait_recv()
+            here[...] = (here[...].astype(F32) + mine(a, pos + 2 * RING - WAYS[a] * s)).astype(BF)
+            remote(here, slots[a].at[s + 1], a, s).start()
+        return carry
+
+    lax.fori_loop(1, RING - 1, scatter, 0)
+    for a in range(n):
+        last = slots[a].at[RING - 1]
+        remote(last, last, a, RING - 2).wait_recv()
+        own = part(outs[a], pos + RING + WAYS[a])
+        own[...] = (last[...].astype(F32) + mine(a, pos + RING + WAYS[a])).astype(BF)
+        remote(own, own, a, RING - 1).start()
+
+    def gather(t, carry):
+        for a in range(n):
+            here = part(outs[a], pos + 2 * RING + WAYS[a] * (1 - t))
+            remote(here, here, a, RING - 2 + t).wait_recv()
+            remote(here, here, a, RING - 1 + t).start()
+        return carry
+
+    lax.fori_loop(1, RING - 1, gather, 0)
+    total = vec_ref[...]
+    for k in range(1, RING):
+        vcopy(k).wait()
+        total += vslot[k - 1]
+    vsum_ref[...] = total
+    for a in range(n):
+        here = part(outs[a], pos + 2 * RING + WAYS[a] * (2 - RING))
+        remote(here, here, a, 2 * RING - 3).wait_recv()
+    for a in range(n):
+        for s in range(RING - 1):
+            remote(slots[a].at[0], slots[a].at[0], a, s).wait_send()
+            remote(part(outs[a], pos), part(outs[a], pos), a, RING - 1 + s).wait_send()
+
+
+def ring(owns, others, vec):
+    n = len(owns)
+    vmem = pl.BlockSpec(memory_space=pltpu.VMEM)
+    out = pl.pallas_call(
+        functools.partial(ring_kernel, n=n),
+        in_specs=[vmem] * (2 * n + 1),
+        out_specs=[vmem] * (n + 1),
+        out_shape=[sds(a.shape, BF) for a in owns] + [sds(vec.shape, F32)],
+        scratch_shapes=[pltpu.VMEM((RING, a.shape[0] // RING, a.shape[1]), BF) for a in owns]
+        + [
+            pltpu.VMEM((RING - 1,) + vec.shape, F32),
+            pltpu.SemaphoreType.DMA((n, 2 * RING - 2)),
+            pltpu.SemaphoreType.DMA((n, 2 * RING - 2)),
+            pltpu.SemaphoreType.DMA((RING - 1,)),
+            pltpu.SemaphoreType.DMA((RING - 1,)),
+        ],
+        compiler_params=params(collective_id=1, has_side_effects=True),
+        name="ring",
+    )(*owns, *others, vec)
+    return out[:n], out[n]
+
+
+def dp_sum(owns, others, vec):
+    if lax.axis_size("dp") == RING:
+        return ring(owns, others, vec)
+    return [lax.psum(a + b, "dp") for a, b in zip(owns, others)], lax.psum(vec, "dp")
+
+
+def starts_of(place):
+    slots = [j + (j >= place) for j in range(SMALL_MB)]
+    return [place * LEN_SMALL] + [
+        slot * LEN_SMALL + (LEN_LARGE - LEN_SMALL) * (slot > place) for slot in slots
+    ]
+
+
+def layout(place):
+    at = 0
+    starts = starts_of(place)
+    for c, (nimg, plen, vlen) in enumerate(CHUNKS):
+        for i in range(nimg):
+            yield starts[at], c, i * plen, plen, vlen
+            at += 1
+
+
+def cut_kernel(meta_ref, x_ref, *refs):
+    outs, flat = refs[:-1], refs[-1]
+    rows = x_ref.shape[0]
+    flat[:rows] = x_ref[...].astype(F32)
+    flat[rows:] = jnp.zeros((flat.shape[0] - rows, flat.shape[1]), F32)
+    for place in range(SMALL_MB + 1):
+
+        @pl.when(meta_ref[1] == place)
+        def _():
+            for start, c, r0, plen, vlen in layout(place):
+                value = flat[start : start + plen]
+                row = lax.broadcasted_iota(jnp.int32, value.shape, 0)
+                outs[c][r0 : r0 + plen] = jnp.where(row < vlen, value, 0.0).astype(BF)
+
+
+def cut(array, meta):
+    rows = LEN_LARGE + SMALL_MB * LEN_SMALL
+    d = array.shape[1]
+    block = d // 3
+    return pl.pallas_call(
+        cut_kernel,
+        grid_spec=pltpu.PrefetchScalarGridSpec(
+            num_scalar_prefetch=1,
+            grid=(3,),
+            in_specs=[pl.BlockSpec((rows, block), lambda j, m: (m[0], j))],
+            out_specs=[pl.BlockSpec((k * p, block), lambda j, m: (0, j)) for k, p, _ in CHUNKS],
+            scratch_shapes=[pltpu.VMEM((rows + 16, block), F32)],
+        ),
+        out_shape=[sds((k * p, d), BF) for k, p, _ in CHUNKS],
+        compiler_params=params(),
+        name="cut",
+    )(meta, array)
+
+
+def join_kernel(meta_ref, *refs):
+    count = len(CHUNKS)
+    mine, theirs, out_ref, flat = refs[:count], refs[count : 2 * count], refs[-2], refs[-1]
+    rows = flat.shape[0]
+    for lane in range(2):
+        here = meta_ref[0] == lane
+        for place in range(SMALL_MB + 1):
+
+            @pl.when(meta_ref[2 + lane] == place)
+            def _():
+                for start, c, r0, plen, vlen in layout(place):
+                    own = mine[c][r0 : r0 + plen].astype(F32)
+                    value = jnp.where(here, own, theirs[c][r0 : r0 + plen].astype(F32))
+                    flat[start : start + vlen] = value[:vlen]
+
+        out_ref[lane * rows : (lane + 1) * rows] = flat[...].astype(BF)
+
+
+def join(mine, theirs, meta):
+    rows = LEN_LARGE + SMALL_MB * LEN_SMALL
+    d = mine[0].shape[1]
+    block = d // 3
+    return pl.pallas_call(
+        join_kernel,
+        grid_spec=pltpu.PrefetchScalarGridSpec(
+            num_scalar_prefetch=1,
+            grid=(3,),
+            in_specs=[pl.BlockSpec((k * p, block), lambda j, m: (0, j)) for k, p, _ in CHUNKS] * 2,
+            out_specs=pl.BlockSpec((2 * rows, block), lambda j, m: (0, j)),
+            scratch_shapes=[pltpu.VMEM((rows, block), F32)],
+        ),
+        out_shape=sds((2 * rows, d), BF),
+        compiler_params=params(),
+        name="join",
+    )(meta, *mine, *theirs)
 
 
 def blank_kernel(*refs):
@@ -465,10 +693,11 @@
 
 
 KEPT = ("x", "normed", "qkv", "att", "lse", "mid", "n2", "act_o", "act_p", "dg_o", "dg_p", "out")
-
-
-def swap(array, axis, pairs):
-    return lax.ppermute(array, axis, pairs)
+BACK = ("g", "pre_o", "pre_p", "gb", "dqkv", "sums2", "so", "sp", "sums_qkv", "sums1", "gx")
+
+
+def after(value, *earlier):
+    return lax.optimization_barrier((value, earlier))[0]
 
 
 def body(
@@ -476,7 +705,6 @@
     proj_bias, norm2_gain, norm2_bias, up_weight, up_bias, down_weight, down_bias,
 ):
     d = patches.shape[1]
-    rows = LEN_LARGE + SMALL_MB * LEN_SMALL
     half = qkv_weight.shape[-1]
     section = lax.axis_index("section")
     lane = lax.axis_index("tensor")
@@ -507,113 +735,77 @@
         "ub_o": small[None, 2 * half :], "ub_p": small_p[None, 2 * half :],
     }
 
-    place = lax.dynamic_index_in_dim(large_place, lane, 0, keepdims=False)
-    base = lane * rows
-    starts = [place * LEN_SMALL]
-    for j in range(SMALL_MB):
-        slot = j + (j >= place).astype(jnp.int32)
-        starts.append(slot * LEN_SMALL + (LEN_LARGE - LEN_SMALL) * (slot > place).astype(jnp.int32))
-    lens = [LEN_LARGE] + [LEN_SMALL] * SMALL_MB
-
-    def pieces(array):
-        out, at = [], 0
-        for nimg, plen, vlen in CHUNKS:
-            parts = []
-            for _ in range(nimg):
-                part = lax.dynamic_slice(array, (base + starts[at], 0), (vlen, d))
-                parts.append(jnp.pad(part, ((0, plen - vlen), (0, 0))))
-                at += 1
-            out.append(parts[0] if nimg == 1 else jnp.concatenate(parts, axis=0))
-        return out
-
-    def restore(parts):
-        mine = jnp.zeros((rows, d), BF)
-        at = 0
-        for (nimg, plen, vlen), part in zip(CHUNKS, parts):
-            for i in range(nimg):
-                mine = lax.dynamic_update_slice(
-                    mine, part[i * plen : i * plen + vlen], (starts[at], 0)
-                )
-                at += 1
-        theirs = other(mine)
-        first = lane == 0
-        return jnp.concatenate([jnp.where(first, mine, theirs), jnp.where(first, theirs, mine)])
-
-    xs = pieces(patches)
-    gs = pieces(out_grad)
-
-    fwd_like = [
-        jax.eval_shape(functools.partial(forward, chunk=chunk), x, w)
-        for x, chunk in zip(xs, CHUNKS)
-    ]
-    kept = []
-    for x, chunk, like in zip(xs, CHUNKS, fwd_like):
-        kept.append(
-            lax.cond(
-                section == 0,
-                lambda x=x, chunk=chunk: tuple(forward(x, w, chunk)),
-                lambda like=like: blank(like),
-            )
+
+    place = jnp.where(lane == 0, large_place[0], large_place[1])
+    meta = jnp.stack([lane, place, large_place[0], large_place[1]]).astype(jnp.int32)
+    large, smalls = 0, 1
+    xs = cut(patches, meta)
+    gs = cut(out_grad, meta)
+
+    def fwd(c, on, x, otherwise=None):
+        like = jax.eval_shape(functools.partial(forward, chunk=CHUNKS[c]), x, w)
+        return lax.cond(
+            section == on,
+            lambda: tuple(forward(x, w, CHUNKS[c])),
+            lambda: blank(like) if otherwise is None else tuple(otherwise),
         )
-    received = [lax.ppermute(k[-1], "section", [(0, 1)]) for k in kept]
-    kept = [
-        lax.cond(
-            section == 1,
-            lambda r=r, chunk=chunk: tuple(forward(r, w, chunk)),
-            lambda k=k: tuple(k),
+
+    def bwd(c, on, g, kept, otherwise=None):
+        kept = dict(zip(KEPT, kept))
+        like = jax.eval_shape(functools.partial(backward, chunk=CHUNKS[c]), g, kept, w)
+        return lax.cond(
+            section == on,
+            lambda: tuple(backward(g, kept, w, CHUNKS[c])),
+            lambda: blank(like) if otherwise is None else tuple(otherwise),
         )
-        for r, k, chunk in zip(received, kept, CHUNKS)
-    ]
-    outputs = restore([k[-1] for k in kept])
-    kept = [dict(zip(KEPT, k)) for k in kept]
-
-    order = list(reversed(range(len(CHUNKS))))
-    back = [None] * len(CHUNKS)
-    for c in order:
-        like = jax.eval_shape(
-            functools.partial(backward, chunk=CHUNKS[c]), gs[c], kept[c], w
-        )
-        back[c] = lax.cond(
-            section == 1,
-            lambda c=c: tuple(backward(gs[c], kept[c], w, CHUNKS[c])),
-            lambda like=like: blank(like),
-        )
-    received = [lax.ppermute(b[-1], "section", [(1, 0)]) for b in back]
-    for c in order:
-        back[c] = lax.cond(
-            section == 0,
-            lambda c=c: tuple(backward(received[c], kept[c], w, CHUNKS[c])),
-            lambda c=c: tuple(back[c]),
-        )
-    input_grads = restore([b[-1] for b in back])
-
-    g_all = [b[0] for b in back]
-    pre_o = [b[1] for b in back]
-    pre_p = [b[2] for b in back]
-    gb = [b[3] for b in back]
-    dqkv = [b[4] for b in back]
-    field = lambda name: [k[name] for k in kept]
-
-    def reduce(own, partner):
-        return lax.psum(own + other(partner), "dp").astype(F32)
-
-    g_dn = reduce(
-        wgrad(field("act_o"), g_all, True, 768), wgrad(field("act_p"), g_all, True, 768)
-    )
-    g_up = reduce(
-        wgrad(field("n2"), pre_o, False, 768), wgrad(field("n2"), pre_p, False, 768)
-    )
-    pw_all = wgrad(field("att"), gb, True, d)
-    g_pw = reduce(pw_all[:half], pw_all[half:])
-    g_qkv = reduce(*wgrad_qkv(field("normed"), dqkv))
-
-    total = lambda i: sum(b[i] for b in back)
+
+    down = lambda array: lax.ppermute(array, "section", [(0, 1)])
+    up_ = lambda array: lax.ppermute(array, "section", [(1, 0)])
+
+    kept_s = fwd(smalls, 0, xs[smalls])
+    sent_s = down(kept_s[-1])
+    kept_l = fwd(large, 0, after(xs[large], kept_s[-1]))
+    sent_l = down(kept_l[-1])
+    kept_s = fwd(smalls, 1, after(sent_s, kept_l[-1]), kept_s)
+    back_s = bwd(smalls, 1, gs[smalls], kept_s)
+    sent_s = up_(back_s[-1])
+    kept_l = fwd(large, 1, after(sent_l, back_s[-1]), kept_l)
+    back_l = bwd(large, 1, gs[large], kept_l)
+    sent_l = up_(back_l[-1])
+    back_s = bwd(smalls, 0, after(sent_s, back_l[-1]), kept_s, back_s)
+    named = lambda names, values: dict(zip(names, values))
+    part_mlp = wgrad_mlp(named(KEPT, kept_s), named(BACK, back_s))
+    part_attn = wgrad_attn(named(KEPT, kept_s), named(BACK, back_s))
+    outs = [kept_l[-1], kept_s[-1]]
+    outputs = join(outs, [other(a) for a in outs], meta)
+    sent_l = after(sent_l, part_mlp, part_attn, outputs)
+    back_l = bwd(large, 0, sent_l, kept_l, back_l)
+    dn_o, dn_p, up_o, up_p = wgrad_mlp(named(KEPT, kept_l), named(BACK, back_l), part_mlp)
+    qkv_o, qkv_p, pw_all = wgrad_attn(named(KEPT, kept_l), named(BACK, back_l), part_attn)
+    grads = [back_l[-1], back_s[-1]]
+    input_grads = join(grads, [other(a) for a in grads], meta)
+
+    total = lambda i: back_s[i] + back_l[i]
     sums2, so, sp, sums_qkv, sums1 = (total(i) for i in range(5, 10))
     full = jnp.concatenate([sums1[:2].reshape(-1), sums2[:4].reshape(-1)])
     qv = jnp.stack([sums_qkv[0], sums_qkv[2]])
     mine = jnp.concatenate([full, qv[:, :half].reshape(-1), so[0]])
     theirs = jnp.concatenate([full, qv[:, half:].reshape(-1), sp[0]])
-    vec = lax.psum((mine + other(theirs)).reshape(-1, 128), "dp").reshape(-1)
+    vec = (mine + other(theirs)).reshape(-1, 128)
+
+    def flat(qkv):
+        return qkv[:2].reshape(2 * d, half), qkv[2]
+
+    qk_o, v_o = flat(qkv_o)
+    qk_p, v_p = flat(other(qkv_p))
+    summed, vec = dp_sum(
+        [dn_o, qk_o, up_o, v_o, pw_all[:half]],
+        [other(dn_p), qk_p, other(up_p), v_p, other(pw_all[half:])],
+        vec,
+    )
+    g_dn, g_qk, g_up, g_v, g_pw = (a.astype(F32) for a in summed)
+    g_qkv = jnp.concatenate([g_qk.reshape(2, d, half), g_v[None]])
+    vec = vec.reshape(-1)
     one = lambda i: vec[None, i * d : (i + 1) * d]
     return (
         outputs[None],

time: 672 us -> 536 us (0.80)
  waiting for transfers between devices: 291 us -> 78.7 us
  Pallas kernels: 202 us -> 375 us
  blocking collectives: 42 us -> 0 us
  local copies, waits for them, and re-layouts: 50.9 us -> 27.7 us
  between operations: 19.7 us -> 2.98 us
  other arithmetic: 32 us -> 17.2 us
    pallas_call x6 -> x9, Pallas kernels: 41.1 us -> 216 us  [the longest x1 155 us: ring(): pl.pallas_call(functools.partial(ring_kernel, n=n), in_specs=[vmem] * (2...]
    psum x1 -> x0, waiting for transfers between devices: 149 us -> none  [reduce(): return lax.psum(own + other(partner), 'dp').astype(F32)]
    ppermute x4, waiting for transfers between devices: 142 us -> 77.4 us  [the longest x2 71.4 us: body(): up_ = lambda array: lax.ppermute(array, 'section', [(1, 0)])]
    psum x1 -> x0, blocking collectives: 42 us -> none  [body(): vec = lax.psum((mine + other(theirs)).reshape(-1, 128), 'dp').reshape(-1)]
    dynamic_update_slice x8 -> x0, local copies, waits for them, and re-layouts: 23.2 us -> none  [restore(): lax.dynamic_update_slice(mine, part[i * plen:i * plen + vlen], (starts[at...]
    dynamic_slice x4 -> x0, local copies, waits for them, and re-layouts: 6.88 us -> none  [the longest x3 5.64 us: pieces(): part = lax.dynamic_slice(array, (base + starts[at], 0), (vlen, d))]
  transfers between devices with their start and end apart: 17 -> 18, of which waited for: 3 -> 4; matrix products, arithmetic and copies ran while one was open for 10% -> 5% of each run, Pallas kernels for 18% -> 24%
where the time goes in v2:
time: 536 us; the launch traced here: 528 us
  Pallas kernels  375 us (70%)
  waiting for transfers between devices  78.7 us (15%)
  local copies, waits for them, and re-layouts  27.7 us (5%)
  other arithmetic  17.2 us (3%)
  loops' own time  15.9 us (3%)
  starting transfers between devices  10.9 us (2%)
    pallas_call x1, Pallas kernels, ring(): pl.pallas_call(functools.partial(ring_kernel, n=n), in_specs=[vmem] * (2...  155 us
    ppermute x2, waiting for transfers between devices, body(): up_ = lambda array: lax.ppermute(array, 'section', [(1, 0)])  71.4 us
    pallas_call x2, Pallas kernels, attn_bwd(): pl.pallas_call(functools.partial(attn_bwd_kernel, nimg=nimg, plen=plen, v...  36.9 us
    pallas_call x2, Pallas kernels, attn_fwd(): pl.pallas_call(functools.partial(attn_fwd_kernel, nimg=nimg, plen=plen, v...  32.3 us
    pallas_call x2, Pallas kernels, post_bwd(): pl.pallas_call(post_bwd_kernel, grid=(2,), in_specs=[whole((n, d)), whole...  30.8 us
    pallas_call x2, Pallas kernels, post_fwd(): pl.pallas_call(post_fwd_kernel, grid=(2,), in_specs=[whole((n, d)), whole...  29.4 us
    pallas_call x2, Pallas kernels, wgrad_mlp(): pl.pallas_call(functools.partial(wgrad_mlp_kernel, more=len(init)), grid=...  25.6 us
    pallas_call x2, Pallas kernels, pre_bwd(): pl.pallas_call(pre_bwd_kernel, grid=(3,), in_specs=[pl.BlockSpec((1, n, d...  16.8 us
  transfers between devices with their start and end apart: 18, of which 4 were waited for; matrix products, arithmetic and copies ran while one was open for 5% of the time, Pallas kernels for 24%

profile of v2, /device:TPU:0, one launch (start us, length us, event | category | flops | bytes accessed | tf_op | source)
XLA Modules:
  0.0 528.1 jit_solution(3418768325790948616)
XLA Ops:
  8.5 4.4 cut.2
  13.3 32.5 %conditional.8 = ((bf16[624,768]{1,0:T(8,128)(2,1)}, bf16[624,768]{1,0:T(8,128)(2,1)}, bf16[3,624,768]{2,1,0:T(8,128)(2,1)}, bf16[624,768]{1,0:T(8,128)(2,1)}, f...) conditional(s32[]{:T(128)} %convert_element_type.5, () %tuple.66, ...), branch_computations={%region_0.1_spmd, %region_1.2_spmd} | conditional | bytes 15335584 | solution.py:747
  13.3 6.2 %pre_fwd.4 = (bf16[624,768]{1,0:T(8,128)(2,1)}, bf16[3,624,768]{2,1,0:T(8,128)(2,1)S(1)}) custom-call(bf16[624,768]{1,0:T(8,128)(2,1)} %get-tuple-element.809.x_ref, f32[1,768]{1,0:T(1,128)S(1)} %get-tuple-element.373.g_ref, f32[1,768]{1,0:T(1,128)S(1)} %get-tuple-element.374.b_ref, bf16[3,768,384]{2,1,0:T(8,128)(2,1)} %get-tuple-element.375.wo_ref, ...), custom_call_target="tpu_custom_call" | custom-call | tf_op jit(solution)/shard_map/cond/branch_1_fun/pre_fwd/pallas_call | solution.py:79
  19.5 11.2 %attn_fwd.4 = (bf16[624,768]{1,0:T(8,128)(2,1)}, f32[6,2,624]{2,1,0:T(2,128)S(1)}) custom-call(bf16[3,624,768]{2,1,0:T(8,128)(2,1)S(1)} %get-tuple-element.811.q_ref.k_ref.v_ref, bf16[3,624,768]{2,1,0:T(8,128)(2,1)S(1)} %get-tuple-element.811.q_ref.k_ref.v_ref, bf16[3,624,768]{2,1,0:T(8,128)(2,1)S(1)} %get-tuple-element.811.q_ref.k_ref.v_ref), custom_call_target="tpu_custom_call" | custom-call | tf_op jit(solution)/shard_map/cond/branch_1_fun/attn_fwd/pallas_call | solution.py:134
  30.7 15.2 %post_fwd.4 = (f32[624,768]{1,0:T(8,128)}, bf16[624,768]{1,0:T(8,128)(2,1)}, bf16[624,1536]{1,0:T(8,128)(2,1)}, bf16[624,1536]{1,0:T(8,128)(2,1)}, bf16[624,1536...) custom-call(bf16[624,768]{1,0:T(8,128)(2,1)S(1)} %copy-done.18, ...), custom_call_target="tpu_custom_call" | custom-call | tf_op jit(solution)/shard_map/cond/branch_1_fun/post_fwd/pallas_call | solution.py:195
  48.1 42.4 %conditional.9 = ((bf16[592,768]{1,0:T(8,128)(2,1)}, bf16[592,768]{1,0:T(8,128)(2,1)}, bf16[3,592,768]{2,1,0:T(8,128)(2,1)}, bf16[592,768]{1,0:T(8,128)(2,1)}, f...) conditional(s32[]{:T(128)} %convert_element_type.5, () %tuple.65, ...), branch_computations={%region_2.3_spmd, %region_3.4_spmd} | conditional | bytes 16711868 | solution.py:747
  48.4 6.7 %pre_fwd.5 = (bf16[592,768]{1,0:T(8,128)(2,1)}, bf16[3,592,768]{2,1,0:T(8,128)(2,1)}) custom-call(bf16[592,768]{1,0:T(8,128)(2,1)} %get-tuple-element.833.x_ref, f32[1,768]{1,0:T(1,128)S(1)} %get-tuple-element.402.g_ref, f32[1,768]{1,0:T(1,128)S(1)} %get-tuple-element.403.b_ref, bf16[3,768,384]{2,1,0:T(8,128)(2,1)} %get-tuple-element.404.wo_ref, ...), custom_call_target="tpu_custom_call" | custom-call | tf_op jit(solution)/shard_map/cond/branch_1_fun/pre_fwd/pallas_call | solution.py:79
  55.0 21.1 %attn_fwd.5 = (bf16[592,768]{1,0:T(8,128)(2,1)S(1)}, f32[6,2,592]{2,1,0:T(2,128)S(1)}) custom-call(bf16[3,592,768]{2,1,0:T(8,128)(2,1)} %get-tuple-element.835.q_ref.k_ref.v_ref, bf16[3,592,768]{2,1,0:T(8,128)(2,1)} %get-tuple-element.835.q_ref.k_ref.v_ref, bf16[3,592,768]{2,1,0:T(8,128)(2,1)} %get-tuple-element.835.q_ref.k_ref.v_ref), custom_call_target="tpu_custom_call" | custom-call | tf_op jit(solution)/shard_map/cond/branch_1_fun/attn_fwd/pallas_call | solution.py:134
  76.2 14.2 %post_fwd.5 = (f32[592,768]{1,0:T(8,128)}, bf16[592,768]{1,0:T(8,128)(2,1)}, bf16[592,1536]{1,0:T(8,128)(2,1)}, bf16[592,1536]{1,0:T(8,128)(2,1)}, bf16[592,1536...) custom-call(bf16[592,768]{1,0:T(8,128)(2,1)S(1)} %copy-done.19, ...), custom_call_target="tpu_custom_call" | custom-call | tf_op jit(solution)/shard_map/cond/branch_1_fun/post_fwd/pallas_call | solution.py:195
  92.7 4.5 cut.3
  97.7 6.9 %conditional.11 = ((bf16[624,768]{1,0:T(8,128)(2,1)}, bf16[624,1536]{1,0:T(8,128)(2,1)}, bf16[624,1536]{1,0:T(8,128)(2,1)}, bf16[624,768]{1,0:T(8,128)(2,1)}, bf...) conditional(s32[]{:T(128)} %convert_element_type.4, () %tuple.70, ...), branch_computations={%region_6.7_spmd, %region_7.8_spmd} | conditional | bytes 18579608 | solution.py:756
  106.3 6.0 %collective-permute-done.5 = bf16[592,768]{1,0:T(8,128)(2,1)} collective-permute-done((bf16[592,768]{1,0:T(8,128)(2,1)}, bf16[592,768]{1,0:T(8,128)(2,1)}, u32[]{:S(2)}, u32[]{:S(2)}) %collective-permute-start.5) | collective-permute-done | bytes 909344 | tf_op jit(solution)/shard_map/ppermute | solution.py:762
  112.6 7.4 %conditional.13 = ((bf16[592,768]{1,0:T(8,128)(2,1)}, bf16[592,1536]{1,0:T(8,128)(2,1)}, bf16[592,1536]{1,0:T(8,128)(2,1)}, bf16[592,768]{1,0:T(8,128)(2,1)}, bf...) conditional(s32[]{:T(128)} %convert_element_type.4, () %tuple.76, ...), branch_computations={%region_10.11_spmd, %region_11.12_spmd} | conditional | bytes 17989784 | solution.py:756
  121.2 46.1 %collective-permute-done.10 = bf16[624,768]{1,0:T(8,128)(2,1)} collective-permute-done((bf16[624,768]{1,0:T(8,128)(2,1)}, bf16[624,768]{1,0:T(8,128)(2,1)}, u32[]{:S(2)}, u32[]{:S(2)}) %collective-permute-start.10) | collective-permute-done | bytes 958496 | tf_op jit(solution)/shard_map/ppermute | solution.py:763
  167.3 42.3 %conditional.14 = ((bf16[624,768]{1,0:T(8,128)(2,1)}, bf16[624,1536]{1,0:T(8,128)(2,1)}, bf16[624,1536]{1,0:T(8,128)(2,1)}, bf16[624,768]{1,0:T(8,128)(2,1)}, bf...) conditional(s32[]{:T(128)} %convert_element_type.5, ...), branch_computations={%region_12.13_spmd, %region_13.14_spmd} | conditional | bytes 20496536 | solution.py:756
  167.4 16.3 %post_bwd.6 = (bf16[624,1536]{1,0:T(8,128)(2,1)}, bf16[624,1536]{1,0:T(8,128)(2,1)}, f32[624,768]{1,0:T(8,128)}, bf16[624,768]{1,0:T(8,128)(2,1)}, bf16[624,768]...) custom-call(bf16[624,768]{1,0:T(8,128)(2,1)} %get-tuple-element.948.g_ref, ...), custom_call_target="tpu_custom_call" | custom-call | tf_op jit(solution)/shard_map/cond/branch_1_fun/post_bwd/pallas_call | solution.py:269
  183.8 14.8 %attn_bwd.6 = (bf16[3,624,768]{2,1,0:T(8,128)(2,1)S(1)}, f32[8,768]{1,0:T(8,128)}) custom-call(bf16[3,624,768]{2,1,0:T(8,128)(2,1)S(1)} %get-tuple-element.560.q_ref.k_ref.v_ref, bf16[3,624,768]{2,1,0:T(8,128)(2,1)S(1)} %get-tuple-element.560.q_ref.k_ref.v_ref, bf16[3,624,768]{2,1,0:T(8,128)(2,1)S(1)} %get-tuple-element.560.q_ref.k_ref.v_ref, ...), custom_call_target="tpu_custom_call" | custom-call | tf_op jit(solution)/shard_map/cond/branch_1_fun/attn_bwd/pallas_call | solution.py:334
  198.7 8.7 %pre_bwd.6 = (bf16[624,768]{1,0:T(8,128)(2,1)}, f32[8,768]{1,0:T(8,128)}) custom-call(bf16[3,624,768]{2,1,0:T(8,128)(2,1)S(1)} %get-tuple-element.952.d_ref, bf16[3,768,384]{2,1,0:T(8,128)(2,1)S(1)} %copy-done.12, bf16[3,768,384]{2,1,0:T(8,128)(2,1)} %get-tuple-element.569.wp_ref, bf16[624,768]{1,0:T(8,128)(2,1)} %get-tuple-element.570.x_ref, ...), custom_call_target="tpu_custom_call" | custom-call | tf_op jit(solution)/shard_map/cond/branch_1_fun/pre_bwd/pallas_call | solution.py:375
  209.6 7.4 %wgrad_attn.2 = (bf16[3,768,384]{2,1,0:T(8,128)(2,1)}, bf16[3,768,384]{2,1,0:T(8,128)(2,1)}, bf16[768,768]{1,0:T(8,128)(2,1)}) custom-call(bf16[624,768]{1,0:T(8,128)(2,1)} %get-tuple-element.733.refs_0_, bf16[3,624,768]{2,1,0:T(8,128)(2,1)} %get-tuple-element.734.refs_1_, bf16[624,768]{1,0:T(8,128)(2,1)} %get-tuple-element.735.refs_2_, ...), custom_call_target="tpu_custom_call" | custom-call | tf_op jit(solution)/shard_map/wgrad_attn/pallas_call | solution.py:454
  217.1 11.8 %wgrad_mlp.2 = (bf16[1536,768]{1,0:T(8,128)(2,1)}, bf16[1536,768]{1,0:T(8,128)(2,1)}, bf16[768,1536]{1,0:T(8,128)(2,1)}, bf16[768,1536]{1,0:T(8,128)(2,1)}) custom-call(bf16[624,1536]{1,0:T(8,128)(2,1)S(1)} %copy-done.28, bf16[624,1536]{1,0:T(8,128)(2,1)S(1)} %copy-done.29, bf16[624,768]{1,0:T(8,128)(2,1)S(1)} %copy-done.32, ...), custom_call_target="tpu_custom_call" | custom-call | tf_op jit(solution)/shard_map/wgrad_mlp/pallas_call | solution.py:420
  228.9 6.7 %join.2 = bf16[2336,768]{1,0:T(8,128)(2,1)} custom-call(s32[4]{0:T(128)} %pad_add_fusion.meta_ref, bf16[592,768]{1,0:T(8,128)(2,1)} %get-tuple-element.712.refs_0_, bf16[624,768]{1,0:T(8,128)(2,1)} %get-tuple-element.713.refs_1_, bf16[592,768]{1,0:T(8,128)(2,1)} %collective-permute-done.7.refs_2_, bf16[624,768]{1,0:T(8,128)(2,1)} %collective-permute-done.8.refs_3_), custom_call_target="tpu_custom_call" | custom-call | tf_op jit(solution)/shard_map/join/pallas_call | solution.py:664
  235.5 25.3 %collective-permute-done.9 = bf16[592,768]{1,0:T(8,128)(2,1)} collective-permute-done((bf16[592,768]{1,0:T(8,128)(2,1)}, bf16[592,768]{1,0:T(8,128)(2,1)}, u32[]{:S(2)}, u32[]{:S(2)}) %collective-permute-start.9) | collective-permute-done | bytes 909344 | tf_op jit(solution)/shard_map/ppermute | solution.py:763
  260.9 47.3 %conditional.15 = ((bf16[592,768]{1,0:T(8,128)(2,1)}, bf16[592,1536]{1,0:T(8,128)(2,1)}, bf16[592,1536]{1,0:T(8,128)(2,1)}, bf16[592,768]{1,0:T(8,128)(2,1)}, bf...) conditional(s32[]{:T(128)} %convert_element_type.5, ...), branch_computations={%region_14.15_spmd, %region_15.16_spmd} | conditional | bytes 12730492 | solution.py:756
  261.1 14.5 %post_bwd.7 = (bf16[592,1536]{1,0:T(8,128)(2,1)}, bf16[592,1536]{1,0:T(8,128)(2,1)}, f32[592,768]{1,0:T(8,128)}, bf16[592,768]{1,0:T(8,128)(2,1)}, bf16[592,768]...) custom-call(bf16[592,768]{1,0:T(8,128)(2,1)} %get-tuple-element.970.g_ref, ...), custom_call_target="tpu_custom_call" | custom-call | tf_op jit(solution)/shard_map/cond/branch_1_fun/post_bwd/pallas_call | solution.py:269
  275.6 22.1 %attn_bwd.7 = (bf16[3,592,768]{2,1,0:T(8,128)(2,1)S(1)}, f32[8,768]{1,0:T(8,128)}) custom-call(bf16[3,592,768]{2,1,0:T(8,128)(2,1)} %get-tuple-element.589.q_ref.k_ref.v_ref, bf16[3,592,768]{2,1,0:T(8,128)(2,1)} %get-tuple-element.589.q_ref.k_ref.v_ref, bf16[3,592,768]{2,1,0:T(8,128)(2,1)} %get-tuple-element.589.q_ref.k_ref.v_ref, ...), custom_call_target="tpu_custom_call" | custom-call | tf_op jit(solution)/shard_map/cond/branch_1_fun/attn_bwd/pallas_call | solution.py:334
  297.7 8.1 %pre_bwd.7 = (bf16[592,768]{1,0:T(8,128)(2,1)}, f32[8,768]{1,0:T(8,128)}) custom-call(bf16[3,592,768]{2,1,0:T(8,128)(2,1)S(1)} %get-tuple-element.974.d_ref, bf16[3,768,384]{2,1,0:T(8,128)(2,1)S(1)} %get-tuple-element.597.wo_ref, bf16[3,768,384]{2,1,0:T(8,128)(2,1)} %get-tuple-element.598.wp_ref, bf16[592,768]{1,0:T(8,128)(2,1)S(1)} %get-tuple-element.599.x_ref, ...), custom_call_target="tpu_custom_call" | custom-call | tf_op jit(solution)/shard_map/cond/branch_1_fun/pre_bwd/pallas_call | solution.py:375
  308.2 13.8 %wgrad_mlp.3 = (bf16[1536,768]{1,0:T(8,128)(2,1)}, bf16[1536,768]{1,0:T(8,128)(2,1)}, bf16[768,1536]{1,0:T(8,128)(2,1)}, bf16[768,1536]{1,0:T(8,128)(2,1)}) custom-call(bf16[592,1536]{1,0:T(8,128)(2,1)} %get-tuple-element.743.refs_0_, bf16[592,1536]{1,0:T(8,128)(2,1)} %get-tuple-element.744.refs_1_, bf16[592,768]{1,0:T(8,128)(2,1)} %get-tuple-element.745.refs_2_, ...), custom_call_target="tpu_custom_call" | custom-call | tf_op jit(solution)/shard_map/wgrad_mlp/pallas_call | solution.py:420
  322.7 6.9 %wgrad_attn.3 = (bf16[3,768,384]{2,1,0:T(8,128)(2,1)}, bf16[3,768,384]{2,1,0:T(8,128)(2,1)}, bf16[768,768]{1,0:T(8,128)(2,1)}) custom-call(bf16[592,768]{1,0:T(8,128)(2,1)S(1)} %copy-done.34, bf16[3,592,768]{2,1,0:T(8,128)(2,1)S(1)} %copy-done.17, bf16[592,768]{1,0:T(8,128)(2,1)S(1)} %copy-done.24, bf16[592,768]{1,0:T(8,128)(2,1)S(1)} %copy-done.35, ...), custom_call_target="tpu_custom_call" | custom-call | tf_op jit(solution)/shard_map/wgrad_attn/pallas_call | solution.py:454
  345.0 5.4 %join.3 = bf16[2336,768]{1,0:T(8,128)(2,1)} custom-call(s32[4]{0:T(128)} %pad_add_fusion.meta_ref, bf16[592,768]{1,0:T(8,128)(2,1)S(1)} %copy-done.36, bf16[624,768]{1,0:T(8,128)(2,1)S(1)} %copy-done.33, bf16[592,768]{1,0:T(8,128)(2,1)} %collective-permute-done.11.refs_2_, bf16[624,768]{1,0:T(8,128)(2,1)} %collective-permute-done.12.refs_3_), custom_call_target="tpu_custom_call" | custom-call | tf_op jit(solution)/shard_map/join/pallas_call | solution.py:664
  356.4 154.7 %ring.1 = (bf16[1536,768]{1,0:T(8,128)(2,1)}, bf16[1536,384]{1,0:T(8,128)(2,1)}, bf16[768,1536]{1,0:T(8,128)(2,1)}, bf16[768,384]{1,0:T(8,128)(2,1)}, bf16[384,768]{1,0:T(8,128)(2,1)}, /*index=5*/f32[54,128]{1,0:T(8,128)}) custom-call(bf16[1536,768]{1,0:T(8,128)(2,1)} %get-tuple-element.749.refs_0_, bf16[1536,384]{1,0:T(8,128)(2,1)} %bitcast.113, ...), custom_call_target="tpu_custom_call" | custom-call | tf_op jit(solution)/shard_map/ring/pallas_call | solution.py:567
  512.6 4.4 bitcast_convert_fusion
  517.0 2.8 bitcast_convert_fusion.1
  (176 shorter events, 50.6 us)
Async XLA Ops:
  0.6 12.5 %copy-start.4 = (bf16[1,768,1536]{2,1,0:T(8,128)(2,1)S(1)}, bf16[1,768,1536]{2,1,0:T(8,128)(2,1)}, u32[]{:S(2)}) copy-start(bf16[1,768,1536]{2,1,0:T(8,128)(2,1)} %param.42) | copy-start | bytes 7077892
  0.7 12.4 %collective-permute-start.3 = (bf16[768,1536]{1,0:T(8,128)(2,1)}, bf16[768,1536]{1,0:T(8,128)(2,1)}, u32[]{:S(2)}, u32[]{:S(2)}) collective-permute-start(bf16[768,1536]{1,0:T(8,128)(2,1)} %bitcast.77), channel_id=1, source_target_pairs={{0,8},{8,0},{1,9},{9,1},{2,10},{10,2},{3,11},{11,3},{4,12},{12,4},... | collective-permute-start | bytes 7077896 | tf_op jit(solution)/shard_map/ppermute | solution.py:712
  1.3 11.9 %collective-permute-start.4 = (bf16[1536,768]{1,0:T(8,128)(2,1)}, bf16[1536,768]{1,0:T(8,128)(2,1)}, u32[]{:S(2)}, u32[]{:S(2)}) collective-permute-start(bf16[1536,768]{1,0:T(8,128)(2,1)} %bitcast.86), channel_id=1, source_target_pairs={{0,8},{8,0},{1,9},{9,1},{2,10},{10,2},{3,11},{11,3},{4,12},{12,4},... | collective-permute-start | bytes 7077896 | tf_op jit(solution)/shard_map/ppermute | solution.py:712
  1.4 11.8 %collective-permute-start = (bf16[3,768,384]{2,1,0:T(8,128)(2,1)}, bf16[3,768,384]{2,1,0:T(8,128)(2,1)}, u32[]{:S(2)}, u32[]{:S(2)}) collective-permute-start(bf16[3,768,384]{2,1,0:T(8,128)(2,1)} %bitcast.95), channel_id=1, source_target_pairs={{0,8},{8,0},{1,9},{9,1},{2,10},{10,2},{3,11},{11,3},{4,12},{12,4},... | collective-permute-start | bytes 5308424 | tf_op jit(solution)/shard_map/ppermute | solution.py:712
  3.2 9.7 %collective-permute-start.1 = (f32[2304]{0:T(1024)S(1)}, f32[2304]{0:T(1024)S(1)}, u32[]{:S(2)}, u32[]{:S(2)}) collective-permute-start(f32[2304]{0:T(1024)S(1)} %pad_maximum_fusion.2), channel_id=1, source_target_pairs={{0,8},{8,0},{1,9},{9,1},{2,10},{10,2},{3,11},{11,3},{4,12},{12,4},... | collective-permute-start | bytes 27656 | tf_op jit(solution)/shard_map/ppermute | solution.py:712
  3.6 9.5 %collective-permute-start.2 = (bf16[384,768]{1,0:T(8,128)(2,1)}, bf16[384,768]{1,0:T(8,128)(2,1)}, u32[]{:S(2)}, u32[]{:S(2)}) collective-permute-start(bf16[384,768]{1,0:T(8,128)(2,1)} %bitcast.104), channel_id=1, source_target_pairs={{0,8},{8,0},{1,9},{9,1},{2,10},{10,2},{3,11},{11,3},{4,12},{12,4},... | collective-permute-start | bytes 1769480 | tf_op jit(solution)/shard_map/ppermute | solution.py:712
  45.8 51.4 %collective-permute-start.6 = (bf16[624,768]{1,0:T(8,128)(2,1)}, bf16[624,768]{1,0:T(8,128)(2,1)}, u32[]{:S(2)}, u32[]{:S(2)}) collective-permute-start(bf16[624,768]{1,0:T(8,128)(2,1)} %get-tuple-element.699), channel_id=1, source_target_pairs={{0,16},{1,17},{2,18},{3,19},{4,20},{5,21},{6,22},{7,23},{8,24},{9,... | collective-permute-start | bytes 2875400 | tf_op jit(solution)/shard_map/ppermute | solution.py:762
  55.0 21.2 %copy-start.7 = (bf16[1536,768]{1,0:T(8,128)(2,1)S(1)}, bf16[1536,768]{1,0:T(8,128)(2,1)}, u32[]{:S(2)}) copy-start(bf16[1536,768]{1,0:T(8,128)(2,1)} %get-tuple-element.420.do_ref) | copy-start | bytes 7077892 | tf_op jit(solution)/shard_map/cond
  55.0 21.2 %copy-start.19 = (bf16[592,768]{1,0:T(8,128)(2,1)S(1)}, bf16[592,768]{1,0:T(8,128)(2,1)}, u32[]{:S(2)}) copy-start(bf16[592,768]{1,0:T(8,128)(2,1)} %get-tuple-element.833.x_ref) | copy-start | bytes 2727940 | tf_op jit(solution)/shard_map/cond
  76.2 14.3 %copy-start.22 = (bf16[592,768]{1,0:T(8,128)(2,1)}, bf16[592,768]{1,0:T(8,128)(2,1)S(1)}, u32[]{:S(2)}) copy-start(bf16[592,768]{1,0:T(8,128)(2,1)S(1)} %get-tuple-element.836.att_ref) | copy-start | bytes 2727940 | tf_op jit(solution)/shard_map/cond
  90.4 21.8 %collective-permute-start.5 = (bf16[592,768]{1,0:T(8,128)(2,1)}, bf16[592,768]{1,0:T(8,128)(2,1)}, u32[]{:S(2)}, u32[]{:S(2)}) collective-permute-start(bf16[592,768]{1,0:T(8,128)(2,1)} %get-tuple-element.701), channel_id=1, source_target_pairs={{0,16},{1,17},{2,18},{3,19},{4,20},{5,21},{6,22},{7,23},{8,24},{9,... | collective-permute-start | bytes 2727944 | tf_op jit(solution)/shard_map/ppermute | solution.py:762
  104.6 62.7 %collective-permute-start.10 = (bf16[624,768]{1,0:T(8,128)(2,1)}, bf16[624,768]{1,0:T(8,128)(2,1)}, u32[]{:S(2)}, u32[]{:S(2)}) collective-permute-start(bf16[624,768]{1,0:T(8,128)(2,1)} %get-tuple-element.710), channel_id=1, source_target_pairs={{16,0},{17,1},{18,2},{19,3},{20,4},{21,5},{22,6},{23,7},{24,8},{25... | collective-permute-start | bytes 2875400 | tf_op jit(solution)/shard_map/ppermute | solution.py:763
  105.9 123.0 %collective-permute-start.8 = (bf16[624,768]{1,0:T(8,128)(2,1)}, bf16[624,768]{1,0:T(8,128)(2,1)}, u32[]{:S(2)}, u32[]{:S(2)}) collective-permute-start(bf16[624,768]{1,0:T(8,128)(2,1)} %get-tuple-element.713.refs_1_), channel_id=1, source_target_pairs={{0,8},{8,0},{1,9},{9,1},{2,10},{10,2},{3,11},{11,3},{4,12},{12,4},... | collective-permute-start | bytes 2875400 | tf_op jit(solution)/shard_map/ppermute | solution.py:712
  112.5 116.4 %collective-permute-start.7 = (bf16[592,768]{1,0:T(8,128)(2,1)}, bf16[592,768]{1,0:T(8,128)(2,1)}, u32[]{:S(2)}, u32[]{:S(2)}) collective-permute-start(bf16[592,768]{1,0:T(8,128)(2,1)} %get-tuple-element.712.refs_0_), channel_id=1, source_target_pairs={{0,8},{8,0},{1,9},{9,1},{2,10},{10,2},{3,11},{11,3},{4,12},{12,4},... | collective-permute-start | bytes 2727944 | tf_op jit(solution)/shard_map/ppermute | solution.py:712
  112.5 54.7 %copy-start.2 = (bf16[3,624,768]{2,1,0:T(8,128)(2,1)S(1)}, bf16[3,624,768]{2,1,0:T(8,128)(2,1)}, u32[]{:S(2)}) copy-start(bf16[3,624,768]{2,1,0:T(8,128)(2,1)} %get-tuple-element.707) | copy-start | bytes 8626180
  119.9 140.9 %collective-permute-start.9 = (bf16[592,768]{1,0:T(8,128)(2,1)}, bf16[592,768]{1,0:T(8,128)(2,1)}, u32[]{:S(2)}, u32[]{:S(2)}) collective-permute-start(bf16[592,768]{1,0:T(8,128)(2,1)} %get-tuple-element.721), channel_id=1, source_target_pairs={{16,0},{17,1},{18,2},{19,3},{20,4},{21,5},{22,6},{23,7},{24,8},{25... | collective-permute-start | bytes 2727944 | tf_op jit(solution)/shard_map/ppermute | solution.py:763
  183.8 14.9 %copy-start.12 = (bf16[3,768,384]{2,1,0:T(8,128)(2,1)S(1)}, bf16[3,768,384]{2,1,0:T(8,128)(2,1)}, u32[]{:S(2)}) copy-start(bf16[3,768,384]{2,1,0:T(8,128)(2,1)} %get-tuple-element.568.wo_ref) | copy-start | bytes 5308420 | tf_op jit(solution)/shard_map/cond
  217.1 43.8 %copy-start.20 = (bf16[592,768]{1,0:T(8,128)(2,1)S(1)}, bf16[592,768]{1,0:T(8,128)(2,1)}, u32[]{:S(2)}) copy-start(bf16[592,768]{1,0:T(8,128)(2,1)} %get-tuple-element.720) | copy-start | bytes 2727940
  228.8 32.0 %copy-start.5 = (bf16[1,768,1536]{2,1,0:T(8,128)(2,1)S(1)}, bf16[1,768,1536]{2,1,0:T(8,128)(2,1)}, u32[]{:S(2)}) copy-start(bf16[1,768,1536]{2,1,0:T(8,128)(2,1)} %param.42) | copy-start | bytes 7077892
  228.8 32.0 %copy-start.6 = (bf16[1,1536,768]{2,1,0:T(8,128)(2,1)S(1)}, bf16[1,1536,768]{2,1,0:T(8,128)(2,1)}, u32[]{:S(2)}) copy-start(bf16[1,1536,768]{2,1,0:T(8,128)(2,1)} %param.44) | copy-start | bytes 7077892
  228.8 32.0 %copy-start.9 = (bf16[1,3,768,384]{3,2,1,0:T(8,128)(2,1)S(1)}, bf16[1,3,768,384]{3,2,1,0:T(8,128)(2,1)}, u32[]{:S(2)}) copy-start(bf16[1,3,768,384]{3,2,1,0:T(8,128)(2,1)} %param.36) | copy-start | bytes 5308420
  308.2 14.4 %copy-start.17 = (bf16[3,592,768]{2,1,0:T(8,128)(2,1)S(1)}, bf16[3,592,768]{2,1,0:T(8,128)(2,1)}, u32[]{:S(2)}) copy-start(bf16[3,592,768]{2,1,0:T(8,128)(2,1)} %get-tuple-element.751.refs_1_) | copy-start | bytes 8183812
  308.2 14.4 %copy-start.24 = (bf16[592,768]{1,0:T(8,128)(2,1)S(1)}, bf16[592,768]{1,0:T(8,128)(2,1)}, u32[]{:S(2)}) copy-start(bf16[592,768]{1,0:T(8,128)(2,1)} %get-tuple-element.752.refs_2_) | copy-start | bytes 2727940
  308.2 14.4 %copy-start.34 = (bf16[592,768]{1,0:T(8,128)(2,1)S(1)}, bf16[592,768]{1,0:T(8,128)(2,1)}, u32[]{:S(2)}) copy-start(bf16[592,768]{1,0:T(8,128)(2,1)} %get-tuple-element.750.refs_0_) | copy-start | bytes 2727940
  308.2 14.4 %copy-start.35 = (bf16[592,768]{1,0:T(8,128)(2,1)S(1)}, bf16[592,768]{1,0:T(8,128)(2,1)}, u32[]{:S(2)}) copy-start(bf16[592,768]{1,0:T(8,128)(2,1)} %get-tuple-element.753.refs_3_) | copy-start | bytes 2727940
  322.0 32.8 %collective-permute-start.13 = (bf16[1536,768]{1,0:T(8,128)(2,1)}, bf16[1536,768]{1,0:T(8,128)(2,1)S(1)}, u32[]{:S(2)}, u32[]{:S(2)}) collective-permute-start(bf16[1536,768]{1,0:T(8,128)(2,1)} %get-tuple-element.757), channel_id=1, source_target_pairs={{0,8},{8,0},{1,9},{9,1},{2,10},{10,2},{3,11},{11,3},{4,12},{12,4},... | collective-permute-start | bytes 7077896 | tf_op jit(solution)/shard_map/ppermute | solution.py:712
  322.1 32.7 %collective-permute-start.15 = (bf16[768,1536]{1,0:T(8,128)(2,1)}, bf16[768,1536]{1,0:T(8,128)(2,1)}, u32[]{:S(2)}, u32[]{:S(2)}) collective-permute-start(bf16[768,1536]{1,0:T(8,128)(2,1)} %get-tuple-element.759), channel_id=1, source_target_pairs={{0,8},{8,0},{1,9},{9,1},{2,10},{10,2},{3,11},{11,3},{4,12},{12,4},... | collective-permute-start | bytes 7077896 | tf_op jit(solution)/shard_map/ppermute | solution.py:712
  329.6 20.8 %collective-permute-start.14 = (bf16[3,768,384]{2,1,0:T(8,128)(2,1)}, bf16[3,768,384]{2,1,0:T(8,128)(2,1)}, u32[]{:S(2)}, u32[]{:S(2)}) collective-permute-start(bf16[3,768,384]{2,1,0:T(8,128)(2,1)} %get-tuple-element.758), channel_id=1, source_target_pairs={{0,8},{8,0},{1,9},{9,1},{2,10},{10,2},{3,11},{11,3},{4,12},{12,4},... | collective-permute-start | bytes 5308424 | tf_op jit(solution)/shard_map/ppermute | solution.py:712
  329.6 13.6 %collective-permute-start.11 = (bf16[592,768]{1,0:T(8,128)(2,1)}, bf16[592,768]{1,0:T(8,128)(2,1)}, u32[]{:S(2)}, u32[]{:S(2)}) collective-permute-start(bf16[592,768]{1,0:T(8,128)(2,1)} %get-tuple-element.741.refs_0_), channel_id=1, source_target_pairs={{0,8},{8,0},{1,9},{9,1},{2,10},{10,2},{3,11},{11,3},{4,12},{12,4},... | collective-permute-start | bytes 2727944 | tf_op jit(solution)/shard_map/ppermute | solution.py:712
  335.6 1.3 collective-permute-start.17
  336.9 8.0 %collective-permute-start.12 = (bf16[624,768]{1,0:T(8,128)(2,1)}, bf16[624,768]{1,0:T(8,128)(2,1)}, u32[]{:S(2)}, u32[]{:S(2)}) collective-permute-start(bf16[624,768]{1,0:T(8,128)(2,1)} %get-tuple-element.742.refs_1_), channel_id=1, source_target_pairs={{0,8},{8,0},{1,9},{9,1},{2,10},{10,2},{3,11},{11,3},{4,12},{12,4},... | collective-permute-start | bytes 2875400 | tf_op jit(solution)/shard_map/ppermute | solution.py:712
  343.2 11.6 %collective-permute-start.16 = (bf16[384,768]{1,0:T(8,128)(2,1)S(1)}, bf16[384,768]{1,0:T(8,128)(2,1)S(1)}, u32[]{:S(2)}, u32[]{:S(2)}) collective-permute-start(bf16[384,768]{1,0:T(8,128)(2,1)S(1)} %get-tuple-element.778), channel_id=1, source_target_pairs={{0,8},{8,0},{1,9},{9,1},{2,10},{10,2},{3,11},{11,3},{4,12},{12,4},... | collective-permute-start | bytes 1769480 | tf_op jit(solution)/shard_map/ppermute | solution.py:712
  (32 other events, 253.8 us)

commit v3 on v2

--- a/solution.py
+++ b/solution.py
@@ -14,6 +14,7 @@
 EPSILON = 1e-06
 MASKED = -1e30
 SCALE = HD ** (-0.5)
+SCALE2 = SCALE * 1.4426950408889634
 BF = jnp.bfloat16
 F32 = jnp.float32
 VMEM_LIMIT = 56 * 1024 * 1024
@@ -63,14 +64,18 @@
     return jnp.sum(values.astype(F32), axis=0, keepdims=True)
 
 
-def pre_fwd_kernel(x_ref, g_ref, b_ref, wo_ref, wp_ref, bias_ref, normed_ref, qkv_ref):
-    @pl.when(pl.program_id(0) == 0)
+def pre_fwd_kernel(x_ref, g_ref, b_ref, wo_ref, wp_ref, bo_ref, bp_ref, normed_ref, qkv_ref):
+    s = pl.program_id(0)
+
+    @pl.when(s == 0)
     def _():
         xhat, _ = norm_parts(x_ref[...].astype(F32))
         normed_ref[...] = (xhat * g_ref[...] + b_ref[...]).astype(BF)
 
     weight = jnp.concatenate([wo_ref[0], wp_ref[0]], axis=1)
-    qkv_ref[0] = (nn(normed_ref[...], weight) + bias_ref[0]).astype(BF)
+    biases = jnp.concatenate([bo_ref[...], bp_ref[...]], axis=1)
+    bias = jnp.where(s == 0, biases[:1], jnp.where(s == 1, 0.0, biases[1:]))
+    qkv_ref[0] = (nn(normed_ref[...], weight) + bias).astype(BF)
 
 
 def pre_fwd(x, w):
@@ -85,13 +90,14 @@
             whole((1, d)),
             pl.BlockSpec((1, d, half), lambda s: (s, 0, 0)),
             pl.BlockSpec((1, d, half), lambda s: (s, 0, 0)),
-            pl.BlockSpec((1, 1, 2 * half), lambda s: (s, 0, 0)),
+            whole((2, half)),
+            whole((2, half)),
         ],
         out_specs=[whole((n, d)), pl.BlockSpec((1, n, 2 * half), lambda s: (s, 0, 0))],
         out_shape=[sds((n, d), BF), sds((3, n, 2 * half), BF)],
         compiler_params=params(),
         name="pre_fwd",
-    )(x, w["g1"], w["b1"], w["wqkv_o"], w["wqkv_p"], w["bqkv"])
+    )(x, w["g1"], w["b1"], w["wqkv_o"], w["wqkv_p"], w["bq_o"], w["bq_p"])
 
 
 def mask_keys(scores, vlen):
@@ -103,34 +109,49 @@
 
 
 def qblocks(plen):
-    return [(q, min(256, plen - q)) for q in range(0, plen, 256)]
-
-
-def attn_fwd_kernel(q_ref, k_ref, v_ref, o_ref, l_ref, *, nimg, plen, vlen):
+    step = min(256, plen)
+    return [(q, min(step, 2 * plen - q)) for q in range(0, 2 * plen, step)]
+
+
+def lse_width(chunk):
+    nimg, plen, _ = chunk
+    return nimg * len(qblocks(plen)) * 256
+
+
+def both_heads(rows):
+    head = lax.broadcasted_iota(jnp.int32, rows.shape, 1) // HD
+    none = jnp.zeros_like(rows)
+    return jnp.concatenate([jnp.where(head == h, rows, none) for h in range(2)], axis=0)
+
+
+def one_each(stacked, plen):
+    head = lax.broadcasted_iota(jnp.int32, (plen, stacked.shape[1]), 1) // HD
+    return jnp.where(head == 0, stacked[:plen], stacked[plen:])
+
+
+def attn_fwd_kernel(q_ref, k_ref, v_ref, o_ref, l_ref, o_tmp, *, nimg, plen, vlen):
+    at = 0
     for im in range(nimg):
-        r0 = im * plen
-        k = k_ref[0, r0 : r0 + plen]
-        vt = v_ref[0, r0 : r0 + plen].T
+        rows = slice(im * plen, (im + 1) * plen)
+        k = k_ref[0, rows]
+        vt = v_ref[0, rows].T
+        queries = both_heads(q_ref[0, rows])
         for q0, qw in qblocks(plen):
-            q = q_ref[0, r0 + q0 : r0 + q0 + qw]
-            head = lax.broadcasted_iota(jnp.int32, q.shape, 1) // HD
-            outs = []
-            for h in range(2):
-                qm = jnp.where(head == h, q, jnp.zeros_like(q))
-                st = mask_keys(nt(k, qm), vlen)
-                top = jnp.max(st, axis=0, keepdims=True)
-                e = jnp.exp((st - top) * SCALE)
-                total = jnp.sum(e, axis=0, keepdims=True)
-                p = (e * (1.0 / total)).astype(BF)
-                outs.append(nn(vt[h * HD : (h + 1) * HD], p))
-                l_ref[0, h : h + 1, r0 + q0 : r0 + q0 + qw] = top * SCALE + jnp.log(total)
-            o_ref[r0 + q0 : r0 + q0 + qw] = jnp.concatenate(outs, axis=0).T.astype(BF)
+            st = mask_keys(nt(k, queries[q0 : q0 + qw]), vlen)
+            top = jnp.max(st, axis=0, keepdims=True)
+            e = jnp.exp2((st - top) * SCALE2)
+            total = jnp.sum(e, axis=0, keepdims=True)
+            o_tmp[q0 : q0 + qw] = (nn(vt, e.astype(BF)) * (1.0 / total)).T
+            l_ref[0, :, at : at + qw] = top * SCALE2 + jnp.log2(total)
+            at += 256
+        o_ref[rows] = one_each(o_tmp, plen).astype(BF)
 
 
 def attn_fwd(qkv, chunk):
     nimg, plen, vlen = chunk
     _, n, d = qkv.shape
     pairs = d // 128
+    width = lse_width(chunk)
     return pl.pallas_call(
         functools.partial(attn_fwd_kernel, nimg=nimg, plen=plen, vlen=vlen),
         grid=(pairs,),
@@ -139,9 +160,10 @@
         ],
         out_specs=[
             pl.BlockSpec((n, 128), lambda p: (0, p)),
-            pl.BlockSpec((1, 2, n), lambda p: (p, 0, 0)),
-        ],
-        out_shape=[sds((n, d), BF), sds((pairs, 2, n), F32)],
+            pl.BlockSpec((1, 1, width), lambda p: (p, 0, 0)),
+        ],
+        out_shape=[sds((n, d), BF), sds((pairs, 1, width), F32)],
+        scratch_shapes=[pltpu.VMEM((2 * plen, 128), F32)],
         compiler_params=params(),
         name="attn_fwd",
     )(qkv, qkv, qkv)
@@ -220,12 +242,12 @@
     normed, qkv = pre_fwd(x, w)
     att, lse = attn_fwd(qkv, chunk)
     mid, n2, act_o, act_p, dg_o, dg_p, out = post_fwd(x, att, w)
-    return (x, normed, qkv, att, lse, mid, n2, act_o, act_p, dg_o, dg_p, out)
+    return (normed, qkv, att, lse, mid, n2, act_o, act_p, dg_o, dg_p, out)
 
 
 def post_bwd_kernel(
     g_ref, mid_ref, gain_ref, go_ref, gp_ref, uo_ref, up_ref, do_ref, dp_ref, pwo_ref, pwp_ref,
-    qo_ref, qp_ref, gm_ref, gb_ref, ga_ref, sums_ref, so_ref, sp_ref, acc_ref,
+    qo_ref, qp_ref, gm_ref, gb_ref, ga_ref, sums_ref, so_ref, sp_ref, copy_ref, acc_ref,
 ):
     j = pl.program_id(0)
     g = g_ref[...]
@@ -233,6 +255,7 @@
     @pl.when(j == 0)
     def _():
         acc_ref[...] = jnp.zeros_like(acc_ref)
+        copy_ref[...] = g
 
     for dg_ref, u_ref, d_ref, q_ref, s_ref in (
         (go_ref, uo_ref, do_ref, qo_ref, so_ref),
@@ -275,11 +298,12 @@
         ],
         out_specs=[
             cols(n), cols(n), whole((n, d)), whole((n, d)), whole((n, d)), whole((8, d)),
-            cols(1), cols(1),
+            cols(1), cols(1), whole((n, d)),
         ],
         out_shape=[
             sds((n, fh), BF), sds((n, fh), BF), sds((n, d), F32), sds((n, d), BF),
             sds((n, d), BF), sds((8, d), F32), sds((1, fh), F32), sds((1, fh), F32),
+            sds((n, d), BF),
         ],
         scratch_shapes=[pltpu.VMEM((n, d), F32)],
         compiler_params=params(),
@@ -290,39 +314,37 @@
     )
 
 
-def attn_bwd_kernel(q_ref, k_ref, v_ref, ga_ref, l_ref, d_ref, s_ref, *, nimg, plen, vlen):
+def attn_bwd_kernel(q_ref, k_ref, v_ref, ga_ref, l_ref, d_ref, s_ref, dq_tmp, *, nimg, plen, vlen):
     sums = [jnp.zeros((1, 128), F32) for _ in range(3)]
+    at = 0
     for im in range(nimg):
-        r0 = im * plen
-        k = k_ref[0, r0 : r0 + plen]
-        v = v_ref[0, r0 : r0 + plen]
+        rows = slice(im * plen, (im + 1) * plen)
+        k = k_ref[0, rows]
+        v = v_ref[0, rows]
         kt = k.T
+        queries = both_heads(q_ref[0, rows])
+        grads = both_heads(ga_ref[rows])
         dk = jnp.zeros((plen, 128), F32)
         dv = jnp.zeros((plen, 128), F32)
         for q0, qw in qblocks(plen):
-            q = q_ref[0, r0 + q0 : r0 + q0 + qw]
-            ga = ga_ref[r0 + q0 : r0 + q0 + qw]
-            head = lax.broadcasted_iota(jnp.int32, q.shape, 1) // HD
-            outs = []
-            for h in range(2):
-                qm = jnp.where(head == h, q, jnp.zeros_like(q))
-                gam = jnp.where(head == h, ga, jnp.zeros_like(ga))
-                lse = l_ref[0, h : h + 1, r0 + q0 : r0 + q0 + qw]
-                st = mask_keys(nt(k, qm), vlen)
-                p = jnp.exp(st * SCALE - lse)
-                gp = nt(v, gam)
-                dv += nn(p.astype(BF), gam)
-                pg = p * gp
-                ds = (pg - p * jnp.sum(pg, axis=0, keepdims=True)).astype(BF)
-                dk += nn(ds, qm)
-                outs.append(nn(kt[h * HD : (h + 1) * HD], ds))
-            dq = (jnp.concatenate(outs, axis=0).T * SCALE).astype(BF)
-            d_ref[0, r0 + q0 : r0 + q0 + qw] = dq
-            sums[0] += rowsum(dq)
+            q = queries[q0 : q0 + qw]
+            ga = grads[q0 : q0 + qw]
+            st = mask_keys(nt(k, q), vlen)
+            p = jnp.exp2(st * SCALE2 - l_ref[0, :, at : at + qw])
+            gp = nt(v, ga)
+            dv += nn(p.astype(BF), ga)
+            pg = p * gp
+            ds = (pg - p * jnp.sum(pg, axis=0, keepdims=True)).astype(BF)
+            dk += nn(ds, q)
+            dq_tmp[q0 : q0 + qw] = nn(kt, ds).T
+            at += 256
+        dq = (one_each(dq_tmp, plen) * SCALE).astype(BF)
         dkb = (dk * SCALE).astype(BF)
         dvb = dv.astype(BF)
-        d_ref[1, r0 : r0 + plen] = dkb
-        d_ref[2, r0 : r0 + plen] = dvb
+        d_ref[0, rows] = dq
+        d_ref[1, rows] = dkb
+        d_ref[2, rows] = dvb
+        sums[0] += rowsum(dq)
         sums[2] += rowsum(dvb)
     s_ref[...] = jnp.concatenate(sums + [jnp.zeros((5, 128), F32)], axis=0)
 
@@ -335,12 +357,16 @@
         functools.partial(attn_bwd_kernel, nimg=nimg, plen=plen, vlen=vlen),
         grid=(pairs,),
         in_specs=[pl.BlockSpec((1, n, 128), lambda p, s=s: (s, 0, p)) for s in range(3)]
-        + [pl.BlockSpec((n, 128), lambda p: (0, p)), pl.BlockSpec((1, 2, n), lambda p: (p, 0, 0))],
+        + [
+            pl.BlockSpec((n, 128), lambda p: (0, p)),
+            pl.BlockSpec((1, 1, lse_width(chunk)), lambda p: (p, 0, 0)),
+        ],
         out_specs=[
             pl.BlockSpec((3, n, 128), lambda p: (0, 0, p)),
             pl.BlockSpec((8, 128), lambda p: (0, p)),
         ],
         out_shape=[sds((3, n, d), BF), sds((8, d), F32)],
+        scratch_shapes=[pltpu.VMEM((2 * plen, 128), F32)],
         compiler_params=params(),
         name="attn_bwd",
     )(qkv, qkv, qkv, ga, lse)
@@ -389,11 +415,11 @@
     )(dqkv, w["wqkv_o"], w["wqkv_p"], x, w["g1"], gm)
 
 
-def backward(g, kept, w, chunk):
-    pre_o, pre_p, gm, gb, ga, sums2, so, sp = post_bwd(g, kept, w)
+def backward(g, x, kept, w, chunk):
+    pre_o, pre_p, gm, gb, ga, sums2, so, sp, copy = post_bwd(g, kept, w)
     dqkv, sums_qkv = attn_bwd(kept["qkv"], ga, kept["lse"], chunk)
-    gx, sums1 = pre_bwd(dqkv, kept["x"], gm, w)
-    return (g, pre_o, pre_p, gb, dqkv, sums2, so, sp, sums_qkv, sums1, gx)
+    gx, sums1 = pre_bwd(dqkv, x, gm, w)
+    return (copy, pre_o, pre_p, gb, dqkv, sums2, so, sp, sums_qkv, sums1, gx)
 
 
 def wgrad_mlp_kernel(*refs, more):
@@ -432,50 +458,87 @@
 def wgrad_attn_kernel(*refs, more):
     normed, dqkv, att, gb = refs[:4]
     init = refs[4 : 4 + more]
-    o_ref, p_ref, w_ref = refs[4 + more :]
+    outs = refs[4 + more :]
+    s = pl.program_id(0)
     total = tn(normed[...], dqkv[0])
-    branch = tn(att[...], gb[...])
-    half = o_ref.shape[-1]
-    own, partner = total[:, :half], total[:, half:]
-    if more:
-        own += init[0][0].astype(F32)
-        partner += init[1][0].astype(F32)
-        branch += init[2][...].astype(F32)
-    o_ref[0] = own.astype(BF)
-    p_ref[0] = partner.astype(BF)
-    w_ref[...] = branch.astype(BF)
+    half = outs[0].shape[-1]
+    for i, value in enumerate((total[:, :half], total[:, half:])):
+        if more:
+            value += init[i][0].astype(F32)
+        outs[i][0] = value.astype(BF)
+    for i in range(2):
+
+        @pl.when(s == i)
+        def _():
+            value = tn(att[...], gb[...])
+            if more:
+                value += init[2 + i][...].astype(F32)
+            outs[2 + i][...] = value.astype(BF)
 
 
 def wgrad_attn(kept, back, init=()):
     n, d = kept["normed"].shape
-    half, block = d // 2, d // 3
+    half = d // 2
     part = pl.BlockSpec((1, d, half), lambda s: (s, 0, 0))
-    outs = [part, part, pl.BlockSpec((block, d), lambda s: (s, 0))]
+    outs = [part, part, whole((half, d)), whole((half, d))]
     return pl.pallas_call(
         functools.partial(wgrad_attn_kernel, more=len(init)),
         grid=(3,),
         in_specs=[
             whole((n, d)), pl.BlockSpec((1, n, d), lambda s: (s, 0, 0)),
-            pl.BlockSpec((n, block), lambda s: (0, s)), whole((n, d)),
+            pl.BlockSpec((n, half), lambda s: (0, jnp.minimum(s, 1))), whole((n, d)),
         ]
         + outs[: len(init)],
         out_specs=outs,
-        out_shape=[sds((3, d, half), BF)] * 2 + [sds((d, d), BF)],
+        out_shape=[sds((3, d, half), BF)] * 2 + [sds((half, d), BF)] * 2,
         compiler_params=params(),
         name="wgrad_attn",
     )(kept["normed"], back["dqkv"], kept["att"], back["gb"], *init)
 
 
 RING = 8
-WAYS = (1, 1, -1, -1, -1)
-
-
-def ring_kernel(*refs, n):
-    owns, others, vec_ref = refs[:n], refs[n : 2 * n], refs[2 * n]
-    outs, vsum_ref = refs[2 * n + 1 : 3 * n + 1], refs[3 * n + 1]
-    slots, vslot = refs[3 * n + 2 : 4 * n + 2], refs[4 * n + 2]
-    send, recv, vsend, vrecv = refs[4 * n + 3 :]
+VEC_ROWS = 16
+
+
+def items_of(d):
+    return ((0, 0, 2 * d, 1), (2, 0, 2 * d, 1), (1, 0, d, -1), (2, 2 * d, d, -1), (3, 0, d // 2, -1))
+
+
+def vector_block(sums):
+    s1, s2, sq, so, sp = sums
+    d = s1.shape[1]
+    wide = lambda v: [v[:, i : i + d] for i in range(0, v.shape[1], d)]
+    rows = [s1[:2], s2[:4], sq[0:1], sq[2:3]] + wide(so) + wide(sp)
+    used = 8 + 2 * (so.shape[1] // d)
+    return jnp.concatenate(rows + [jnp.zeros((VEC_ROWS - used, d), F32)], axis=0)
+
+
+def as_own(block, fold):
+    half = block.shape[1] // 2
+    qv = block[6:8]
+    return jnp.concatenate(
+        [
+            block[:6], jnp.concatenate([qv[:, half:], qv[:, :half]], axis=1),
+            block[8 + fold : 8 + 2 * fold], block[8 : 8 + fold], block[8 + 2 * fold :],
+        ],
+        axis=0,
+    )
+
+
+def ring_kernel(*refs, n, items, fold):
+    owns, gifts = refs[:n], refs[n : 2 * n]
+    sums = refs[2 * n : 2 * n + 10]
+    at = 2 * n + 10
+    outs, vsum_ref = refs[at : at + n], refs[at + n]
+    at += n + 1
+    theirs = refs[at : at + n]
+    at += n
+    m = len(items)
+    slots = refs[at : at + m]
+    vbuf, vother, vmine, vslot, send, recv, xsend, xrecv, vsend, vrecv, vxs, vxr = refs[at + m :]
+    mesh_id = pl.DeviceIdType.MESH
     me = lax.axis_index("dp")
+    partner = {"tensor": 1 - lax.axis_index("tensor")}
     z, x = me // 2, me % 2
     pos = z + x * (RING - 1 - 2 * z)
 
@@ -485,17 +548,32 @@
 
     barrier = pltpu.get_barrier_semaphore()
     for k in range(1, RING):
-        pl.semaphore_signal(
-            barrier, inc=1, device_id=member(pos + k), device_id_type=pl.DeviceIdType.MESH
+        pl.semaphore_signal(barrier, inc=1, device_id=member(pos + k), device_id_type=mesh_id)
+    pl.semaphore_signal(barrier, inc=1, device_id=partner, device_id_type=mesh_id)
+    pl.semaphore_wait(barrier, RING)
+
+    def part(arrays, a, chunk):
+        i, first, rows, _ = items[a]
+        rows = rows // RING
+        return arrays[i].at[pl.ds(pl.multiple_of(first + (chunk % RING) * rows, rows), rows)]
+
+    def chunk_at(a, step):
+        return pos + 2 * RING - items[a][3] * step
+
+    def exchange(a, step):
+        return pltpu.make_async_remote_copy(
+            src_ref=part(gifts, a, chunk_at(a, step)),
+            dst_ref=part(theirs, a, chunk_at(a, step)),
+            send_sem=xsend.at[a, step],
+            recv_sem=xrecv.at[a, step],
+            device_id=partner,
+            device_id_type=mesh_id,
         )
-    pl.semaphore_wait(barrier, RING - 1)
-
-    def part(ref, chunk):
-        rows = ref.shape[0] // RING
-        return ref.at[pl.ds(pl.multiple_of((chunk % RING) * rows, rows), rows)]
-
-    def mine(a, chunk):
-        return part(owns[a], chunk)[...].astype(F32) + part(others[a], chunk)[...].astype(F32)
+
+    def mine(a, step):
+        exchange(a, step).wait_recv()
+        chunk = chunk_at(a, step)
+        return part(owns, a, chunk)[...].astype(F32) + part(theirs, a, chunk)[...].astype(F32)
 
     def remote(src, dst, a, step):
         return pltpu.make_async_remote_copy(
@@ -503,90 +581,149 @@
             dst_ref=dst,
             send_sem=send.at[a, step],
             recv_sem=recv.at[a, step],
-            device_id=member(pos + WAYS[a] + RING),
-            device_id_type=pl.DeviceIdType.MESH,
+            device_id=member(pos + items[a][3] + RING),
+            device_id_type=mesh_id,
         )
 
     def vcopy(k):
         return pltpu.make_async_remote_copy(
-            src_ref=vec_ref,
+            src_ref=vmine,
             dst_ref=vslot.at[k - 1],
             send_sem=vsend.at[k - 1],
             recv_sem=vrecv.at[k - 1],
             device_id=member(pos + k),
-            device_id_type=pl.DeviceIdType.MESH,
+            device_id_type=mesh_id,
         )
 
-    for a in range(n):
-        slots[a][0] = mine(a, pos).astype(BF)
+    vexchange = pltpu.make_async_remote_copy(
+        src_ref=vbuf, dst_ref=vother, send_sem=vxs, recv_sem=vxr,
+        device_id=partner, device_id_type=mesh_id,
+    )
+
+    for step in range(2):
+        for a in range(m):
+            exchange(a, step).start()
+    vbuf[...] = vector_block([sums[i][...] + sums[5 + i][...] for i in range(5)])
+    vexchange.start()
+    for a in range(m):
+        slots[a][0] = mine(a, 0).astype(BF)
         remote(slots[a].at[0], slots[a].at[1], a, 0).start()
+
+    def scatter(s, carry):
+        for a in range(m):
+            exchange(a, s + 1).start()
+        for a in range(m):
+            here = slots[a].at[s]
+            own = mine(a, s)
+            remote(here, here, a, s - 1).wait_recv()
+            here[...] = (here[...].astype(F32) + own).astype(BF)
+            remote(here, slots[a].at[s + 1], a, s).start()
+        return carry
+
+    lax.fori_loop(1, RING - 1, scatter, 0)
+    vexchange.wait()
+    vmine[...] = vbuf[...] + as_own(vother[...], fold)
     for k in range(1, RING):
         vcopy(k).start()
-
-    def scatter(s, carry):
-        for a in range(n):
-            here = slots[a].at[s]
-            remote(here, here, a, s - 1).wait_recv()
-            here[...] = (here[...].astype(F32) + mine(a, pos + 2 * RING - WAYS[a] * s)).astype(BF)
-            remote(here, slots[a].at[s + 1], a, s).start()
-        return carry
-
-    lax.fori_loop(1, RING - 1, scatter, 0)
-    for a in range(n):
+    for a in range(m):
         last = slots[a].at[RING - 1]
+        own = mine(a, RING - 1)
         remote(last, last, a, RING - 2).wait_recv()
-        own = part(outs[a], pos + RING + WAYS[a])
-        own[...] = (last[...].astype(F32) + mine(a, pos + RING + WAYS[a])).astype(BF)
-        remote(own, own, a, RING - 1).start()
+        done = part(outs, a, chunk_at(a, RING - 1))
+        done[...] = (last[...].astype(F32) + own).astype(BF)
+        remote(done, done, a, RING - 1).start()
 
     def gather(t, carry):
-        for a in range(n):
-            here = part(outs[a], pos + 2 * RING + WAYS[a] * (1 - t))
+        for a in range(m):
+            here = part(outs, a, chunk_at(a, t - 1))
             remote(here, here, a, RING - 2 + t).wait_recv()
             remote(here, here, a, RING - 1 + t).start()
         return carry
 
     lax.fori_loop(1, RING - 1, gather, 0)
-    total = vec_ref[...]
+    total = vmine[...]
     for k in range(1, RING):
         vcopy(k).wait()
         total += vslot[k - 1]
     vsum_ref[...] = total
-    for a in range(n):
-        here = part(outs[a], pos + 2 * RING + WAYS[a] * (2 - RING))
+    for a in range(m):
+        here = part(outs, a, chunk_at(a, RING - 2))
         remote(here, here, a, 2 * RING - 3).wait_recv()
-    for a in range(n):
+    for a in range(m):
         for s in range(RING - 1):
             remote(slots[a].at[0], slots[a].at[0], a, s).wait_send()
-            remote(part(outs[a], pos), part(outs[a], pos), a, RING - 1 + s).wait_send()
-
-
-def ring(owns, others, vec):
+            here = part(outs, a, pos)
+            remote(here, here, a, RING - 1 + s).wait_send()
+        for s in range(RING):
+            exchange(a, s).wait_send()
+
+
+def ring(owns, gifts, sums_s, sums_l):
     n = len(owns)
+    d = owns[0].shape[1]
+    items = items_of(d)
+    m = len(items)
     vmem = pl.BlockSpec(memory_space=pltpu.VMEM)
+    dma = pltpu.SemaphoreType.DMA
+    vec = pltpu.VMEM((VEC_ROWS, d), F32)
     out = pl.pallas_call(
-        functools.partial(ring_kernel, n=n),
-        in_specs=[vmem] * (2 * n + 1),
+        functools.partial(ring_kernel, n=n, items=items, fold=sums_s[3].shape[1] // d),
+        in_specs=[vmem] * (2 * n + 10),
         out_specs=[vmem] * (n + 1),
-        out_shape=[sds(a.shape, BF) for a in owns] + [sds(vec.shape, F32)],
-        scratch_shapes=[pltpu.VMEM((RING, a.shape[0] // RING, a.shape[1]), BF) for a in owns]
+        out_shape=[sds(a.shape, BF) for a in owns] + [sds((VEC_ROWS, d), F32)],
+        scratch_shapes=[pltpu.VMEM(a.shape, BF) for a in owns]
+        + [pltpu.VMEM((RING, rows // RING, owns[i].shape[1]), BF) for i, _, rows, _ in items]
         + [
-            pltpu.VMEM((RING - 1,) + vec.shape, F32),
-            pltpu.SemaphoreType.DMA((n, 2 * RING - 2)),
-            pltpu.SemaphoreType.DMA((n, 2 * RING - 2)),
-            pltpu.SemaphoreType.DMA((RING - 1,)),
-            pltpu.SemaphoreType.DMA((RING - 1,)),
+            vec, vec, vec, pltpu.VMEM((RING - 1, VEC_ROWS, d), F32),
+            dma((m, 2 * RING - 2)), dma((m, 2 * RING - 2)), dma((m, RING)), dma((m, RING)),
+            dma((RING - 1,)), dma((RING - 1,)), dma, dma,
         ],
         compiler_params=params(collective_id=1, has_side_effects=True),
         name="ring",
-    )(*owns, *others, vec)
+    )(*owns, *gifts, *sums_s, *sums_l)
     return out[:n], out[n]
 
 
-def dp_sum(owns, others, vec):
+def dp_sum(owns, gifts, sums_s, sums_l):
     if lax.axis_size("dp") == RING:
-        return ring(owns, others, vec)
-    return [lax.psum(a + b, "dp") for a, b in zip(owns, others)], lax.psum(vec, "dp")
+        return ring(owns, gifts, sums_s, sums_l)
+    other = lambda array: lax.ppermute(array, "tensor", [(0, 1), (1, 0)])
+    fold = sums_s[3].shape[1] // owns[0].shape[1]
+    block = vector_block([a + b for a, b in zip(sums_s, sums_l)])
+    summed = [lax.psum(a + other(b), "dp") for a, b in zip(owns, gifts)]
+    return summed, lax.psum(block + as_own(other(block), fold), "dp")
+
+
+def finish_kernel(*refs, fold):
+    grads, vec, outs = refs[:4], refs[4], refs[5:]
+    for g, out in zip(grads, outs):
+        out[0] = g[...].astype(F32)
+
+    @pl.when(pl.program_id(0) == 0)
+    def _():
+        half = vec.shape[1] // 2
+        for i in range(6):
+            outs[4 + i][...] = vec[i : i + 1]
+        outs[10][0] = vec[6:8, :half]
+        outs[11][...] = jnp.concatenate([vec[8 + i : 9 + i] for i in range(fold)], axis=1)
+
+
+def finish(grads, vec):
+    d = vec.shape[1]
+    fold = grads[1].shape[1] // d
+    steps = 8
+    rows_in = lambda a: pl.BlockSpec((a.shape[0] // steps, a.shape[1]), lambda j: (j, 0))
+    rows_out = lambda a: pl.BlockSpec((1, a.shape[0] // steps, a.shape[1]), lambda j: (0, j, 0))
+    small = [(1, d)] * 6 + [(1, 2, d // 2), (1, fold * d)]
+    return pl.pallas_call(
+        functools.partial(finish_kernel, fold=fold),
+        grid=(steps,),
+        in_specs=[rows_in(a) for a in grads] + [whole(vec.shape)],
+        out_specs=[rows_out(a) for a in grads] + [whole(a) for a in small],
+        out_shape=[sds((1,) + a.shape, F32) for a in grads] + [sds(a, F32) for a in small],
+        compiler_params=params(),
+        name="finish",
+    )(*grads, vec)
 
 
 def starts_of(place):
@@ -612,7 +749,7 @@
     flat[rows:] = jnp.zeros((flat.shape[0] - rows, flat.shape[1]), F32)
     for place in range(SMALL_MB + 1):
 
-        @pl.when(meta_ref[1] == place)
+        @pl.when(meta_ref[1 + meta_ref[0]] == place)
         def _():
             for start, c, r0, plen, vlen in layout(place):
                 value = flat[start : start + plen]
@@ -647,7 +784,7 @@
         here = meta_ref[0] == lane
         for place in range(SMALL_MB + 1):
 
-            @pl.when(meta_ref[2 + lane] == place)
+            @pl.when(meta_ref[1 + lane] == place)
             def _():
                 for start, c, r0, plen, vlen in layout(place):
                     own = mine[c][r0 : r0 + plen].astype(F32)
@@ -692,7 +829,7 @@
     )
 
 
-KEPT = ("x", "normed", "qkv", "att", "lse", "mid", "n2", "act_o", "act_p", "dg_o", "dg_p", "out")
+KEPT = ("normed", "qkv", "att", "lse", "mid", "n2", "act_o", "act_p", "dg_o", "dg_p", "out")
 BACK = ("g", "pre_o", "pre_p", "gb", "dqkv", "sums2", "so", "sp", "sums_qkv", "sums1", "gx")
 
 
@@ -712,32 +849,16 @@
     other = lambda array: lax.ppermute(array, "tensor", both)
 
     wqkv, pw, up, dn = qkv_weight[0], proj_weight[0], up_weight[0], down_weight[0]
-    small = jnp.concatenate([qv_bias[0].reshape(-1), up_bias[0]])
-    small_p = other(small)
-    zero_bias = jnp.zeros((half,), F32)
-
-    def qkv_bias(own, partner):
-        own, partner = own[: 2 * half].reshape(2, half), partner[: 2 * half].reshape(2, half)
-        return jnp.stack(
-            [
-                jnp.concatenate([own[0], partner[0]]),
-                jnp.concatenate([zero_bias, zero_bias]),
-                jnp.concatenate([own[1], partner[1]]),
-            ]
-        )[:, None, :]
-
     w = {
         "g1": norm1_gain, "b1": norm1_bias, "g2": norm2_gain, "b2": norm2_bias,
         "pb": proj_bias, "db": down_bias,
         "wqkv_o": wqkv, "wqkv_p": other(wqkv), "pw_o": pw, "pw_p": other(pw),
         "up_o": up, "up_p": other(up), "dn_o": dn, "dn_p": other(dn),
-        "bqkv": qkv_bias(small, small_p),
-        "ub_o": small[None, 2 * half :], "ub_p": small_p[None, 2 * half :],
+        "bq_o": qv_bias[0], "bq_p": other(qv_bias[0]), "ub_o": up_bias, "ub_p": other(up_bias),
     }
 
 
-    place = jnp.where(lane == 0, large_place[0], large_place[1])
-    meta = jnp.stack([lane, place, large_place[0], large_place[1]]).astype(jnp.int32)
+    meta = jnp.concatenate([lane[None], large_place])
     large, smalls = 0, 1
     xs = cut(patches, meta)
     gs = cut(out_grad, meta)
@@ -750,12 +871,12 @@
             lambda: blank(like) if otherwise is None else tuple(otherwise),
         )
 
-    def bwd(c, on, g, kept, otherwise=None):
+    def bwd(c, on, g, x, kept, otherwise=None):
         kept = dict(zip(KEPT, kept))
-        like = jax.eval_shape(functools.partial(backward, chunk=CHUNKS[c]), g, kept, w)
+        like = jax.eval_shape(functools.partial(backward, chunk=CHUNKS[c]), g, x, kept, w)
         return lax.cond(
             section == on,
-            lambda: tuple(backward(g, kept, w, CHUNKS[c])),
+            lambda: tuple(backward(g, x, kept, w, CHUNKS[c])),
             lambda: blank(like) if otherwise is None else tuple(otherwise),
         )
 
@@ -763,65 +884,39 @@
     up_ = lambda array: lax.ppermute(array, "section", [(1, 0)])
 
     kept_s = fwd(smalls, 0, xs[smalls])
-    sent_s = down(kept_s[-1])
+    in_s = down(kept_s[-1])
     kept_l = fwd(large, 0, after(xs[large], kept_s[-1]))
-    sent_l = down(kept_l[-1])
-    kept_s = fwd(smalls, 1, after(sent_s, kept_l[-1]), kept_s)
-    back_s = bwd(smalls, 1, gs[smalls], kept_s)
+    in_l = down(kept_l[-1])
+    in_s = after(in_s, kept_l[-1])
+    kept_s = fwd(smalls, 1, in_s, kept_s)
+    back_s = bwd(smalls, 1, gs[smalls], in_s, kept_s)
     sent_s = up_(back_s[-1])
-    kept_l = fwd(large, 1, after(sent_l, back_s[-1]), kept_l)
-    back_l = bwd(large, 1, gs[large], kept_l)
+    in_l = after(in_l, back_s[-1])
+    kept_l = fwd(large, 1, in_l, kept_l)
+    back_l = bwd(large, 1, gs[large], in_l, kept_l)
     sent_l = up_(back_l[-1])
-    back_s = bwd(smalls, 0, after(sent_s, back_l[-1]), kept_s, back_s)
+    back_s = bwd(smalls, 0, after(sent_s, back_l[-1]), xs[smalls], kept_s, back_s)
     named = lambda names, values: dict(zip(names, values))
     part_mlp = wgrad_mlp(named(KEPT, kept_s), named(BACK, back_s))
     part_attn = wgrad_attn(named(KEPT, kept_s), named(BACK, back_s))
     outs = [kept_l[-1], kept_s[-1]]
     outputs = join(outs, [other(a) for a in outs], meta)
     sent_l = after(sent_l, part_mlp, part_attn, outputs)
-    back_l = bwd(large, 0, sent_l, kept_l, back_l)
+    back_l = bwd(large, 0, sent_l, xs[large], kept_l, back_l)
     dn_o, dn_p, up_o, up_p = wgrad_mlp(named(KEPT, kept_l), named(BACK, back_l), part_mlp)
-    qkv_o, qkv_p, pw_all = wgrad_attn(named(KEPT, kept_l), named(BACK, back_l), part_attn)
+    qkv_o, qkv_p, pw_o, pw_p = wgrad_attn(named(KEPT, kept_l), named(BACK, back_l), part_attn)
     grads = [back_l[-1], back_s[-1]]
     input_grads = join(grads, [other(a) for a in grads], meta)
 
-    total = lambda i: back_s[i] + back_l[i]
-    sums2, so, sp, sums_qkv, sums1 = (total(i) for i in range(5, 10))
-    full = jnp.concatenate([sums1[:2].reshape(-1), sums2[:4].reshape(-1)])
-    qv = jnp.stack([sums_qkv[0], sums_qkv[2]])
-    mine = jnp.concatenate([full, qv[:, :half].reshape(-1), so[0]])
-    theirs = jnp.concatenate([full, qv[:, half:].reshape(-1), sp[0]])
-    vec = (mine + other(theirs)).reshape(-1, 128)
-
-    def flat(qkv):
-        return qkv[:2].reshape(2 * d, half), qkv[2]
-
-    qk_o, v_o = flat(qkv_o)
-    qk_p, v_p = flat(other(qkv_p))
+    rows = lambda qkv: qkv.reshape(3 * d, half)
+    sums = lambda back: [named(BACK, back)[k] for k in ("sums1", "sums2", "sums_qkv", "so", "sp")]
     summed, vec = dp_sum(
-        [dn_o, qk_o, up_o, v_o, pw_all[:half]],
-        [other(dn_p), qk_p, other(up_p), v_p, other(pw_all[half:])],
-        vec,
+        [dn_o, up_o, rows(qkv_o), pw_o], [dn_p, up_p, rows(qkv_p), pw_p], sums(back_s), sums(back_l)
     )
-    g_dn, g_qk, g_up, g_v, g_pw = (a.astype(F32) for a in summed)
-    g_qkv = jnp.concatenate([g_qk.reshape(2, d, half), g_v[None]])
-    vec = vec.reshape(-1)
-    one = lambda i: vec[None, i * d : (i + 1) * d]
+    g_dn, g_up, g_qkv, g_pw, g1, b1, g2, b2, pb, db, qv, ub = finish(summed, vec)
     return (
-        outputs[None],
-        input_grads[None],
-        one(0),
-        one(1),
-        g_qkv[None],
-        vec[6 * d : 6 * d + 2 * half].reshape(1, 2, half),
-        g_pw[None],
-        one(4),
-        one(2),
-        one(3),
-        g_up[None],
-        vec[None, 6 * d + 2 * half :],
-        g_dn[None],
-        one(5),
+        outputs[None], input_grads[None], g1, b1, g_qkv.reshape(1, 3, d, half), qv, g_pw, pb,
+        g2, b2, g_up, ub, g_dn, db,
     )
 
 

time: 536 us -> 496 us (0.925)
  local copies, waits for them, and re-layouts: 27.7 us -> 0.19 us
  other arithmetic: 17.2 us -> 1.21 us
  Pallas kernels: 375 us -> 381 us
    pallas_call x1 -> x2, Pallas kernels: 155 us -> 170 us  [the longest x1 161 us: ring(): pl.pallas_call(functools.partial(ring_kernel, n=n, items=items, fold=sums...]
    broadcast_in_dim x4 -> x0, other arithmetic: 10.3 us -> none  [the longest x1 4.36 us: body(): g_dn[None]]
    ppermute x14 -> x10, waiting for transfers between devices: 1.29 us -> 10.3 us  [body(): other = lambda array: lax.ppermute(array, 'tensor', both)]
    ppermute x2, waiting for transfers between devices: 71.4 us -> 63.5 us  [body(): up_ = lambda array: lax.ppermute(array, 'section', [(1, 0)])]
    pallas_call x2, Pallas kernels: 32.3 us -> 24.4 us  [attn_fwd(): pl.pallas_call(functools.partial(attn_fwd_kernel, nimg=nimg, plen=plen, v...]
    slice x8 -> x0, local copies, waits for them, and re-layouts: 7.8 us -> none  [the longest x2 4.8 us: flat(): return (qkv[:2].reshape(2 * d, half), qkv[2])]
    unnamed x85 -> x68, local copies, waits for them, and re-layouts: 7.3 us -> 0.15 us
  transfers between devices with their start and end apart: 18 -> 14, of which waited for: 4 -> 4; matrix products, arithmetic and copies ran while one was open for 5% -> 0% of each run, Pallas kernels for 24% -> 71%
where the time goes in v3:
time: 496 us; the launch traced here: 489 us
  Pallas kernels  381 us (77%)
  waiting for transfers between devices  79.6 us (16%)
  loops' own time  15.8 us (3%)
  starting transfers between devices  9.31 us (2%)
    pallas_call x1, Pallas kernels, ring(): pl.pallas_call(functools.partial(ring_kernel, n=n, items=items, fold=sums...  161 us
    ppermute x2, waiting for transfers between devices, body(): up_ = lambda array: lax.ppermute(array, 'section', [(1, 0)])  63.5 us
    pallas_call x2, Pallas kernels, attn_bwd(): pl.pallas_call(functools.partial(attn_bwd_kernel, nimg=nimg, plen=plen, v...  34.5 us
    pallas_call x2, Pallas kernels, post_bwd(): pl.pallas_call(post_bwd_kernel, grid=(2,), in_specs=[whole((n, d)), whole...  31.5 us
    pallas_call x2, Pallas kernels, post_fwd(): pl.pallas_call(post_fwd_kernel, grid=(2,), in_specs=[whole((n, d)), whole...  29.3 us
    pallas_call x2, Pallas kernels, wgrad_mlp(): pl.pallas_call(functools.partial(wgrad_mlp_kernel, more=len(init)), grid=...  24.8 us
    pallas_call x2, Pallas kernels, attn_fwd(): pl.pallas_call(functools.partial(attn_fwd_kernel, nimg=nimg, plen=plen, v...  24.4 us
    pallas_call x2, Pallas kernels, wgrad_attn(): pl.pallas_call(functools.partial(wgrad_attn_kernel, more=len(init)), grid...  17.3 us
  transfers between devices with their start and end apart: 14, of which 4 were waited for; matrix products, arithmetic and copies ran while one was open for 0% of the time, Pallas kernels for 71%

profile of v3, /device:TPU:0, one launch (start us, length us, event | category | flops | bytes accessed | tf_op | source)
XLA Modules:
  0.0 488.9 jit_solution(11213068174107943718)
XLA Ops:
  2.3 10.2 %collective-permute-done.1 = f32[2,384]{1,0:T(2,128)S(1)} collective-permute-done((f32[2,384]{1,0:T(2,128)}, f32[2,384]{1,0:T(2,128)S(1)}, u32[]{:S(2)}, u32[]{:S(2)}) %collective-permute-start.1) | collective-permute-done | bytes 3104 | tf_op jit(solution)/shard_map/ppermute | solution.py:849
  14.1 4.5 cut.2
  18.8 29.6 %conditional.8 = ((bf16[624,768]{1,0:T(8,128)(2,1)}, bf16[3,624,768]{2,1,0:T(8,128)(2,1)}, bf16[624,768]{1,0:T(8,128)(2,1)}, f32[6,1,1536]{2,1,0:T(1,128)S(1)}, ...) conditional(s32[]{:T(128)} %convert_element_type.5, () %tuple.66, ...), branch_computations={%region_0.0_spmd, %region_1.0_spmd} | conditional | bytes 15335576 | solution.py:868
  18.8 5.4 %pre_fwd.4 = (bf16[624,768]{1,0:T(8,128)(2,1)}, bf16[3,624,768]{2,1,0:T(8,128)(2,1)S(1)}) custom-call(bf16[624,768]{1,0:T(8,128)(2,1)} %get-tuple-element.376.x_ref, f32[1,768]{1,0:T(1,128)S(1)} %get-tuple-element.377.g_ref, f32[1,768]{1,0:T(1,128)S(1)} %get-tuple-element.378.b_ref, bf16[3,768,384]{2,1,0:T(8,128)(2,1)} %get-tuple-element.379.wo_ref, ...), custom_call_target="tpu_custom_call" | custom-call | tf_op jit(solution)/shard_map/cond/branch_1_fun/pre_fwd/pallas_call | solution.py:84
  24.2 9.0 %attn_fwd.4 = (bf16[624,768]{1,0:T(8,128)(2,1)}, f32[6,1,1536]{2,1,0:T(1,128)S(1)}) custom-call(bf16[3,624,768]{2,1,0:T(8,128)(2,1)S(1)} %get-tuple-element.822.q_ref.k_ref.v_ref, bf16[3,624,768]{2,1,0:T(8,128)(2,1)S(1)} %get-tuple-element.822.q_ref.k_ref.v_ref, bf16[3,624,768]{2,1,0:T(8,128)(2,1)S(1)} %get-tuple-element.822.q_ref.k_ref.v_ref), custom_call_target="tpu_custom_call" | custom-call | tf_op jit(solution)/shard_map/cond/branch_1_fun/attn_fwd/pallas_call | solution.py:155
  33.2 15.1 %post_fwd.4 = (f32[624,768]{1,0:T(8,128)}, bf16[624,768]{1,0:T(8,128)(2,1)}, bf16[624,1536]{1,0:T(8,128)(2,1)}, bf16[624,1536]{1,0:T(8,128)(2,1)}, bf16[624,1536...) custom-call(bf16[624,768]{1,0:T(8,128)(2,1)S(1)} %copy-done.17, ...), custom_call_target="tpu_custom_call" | custom-call | tf_op jit(solution)/shard_map/cond/branch_1_fun/post_fwd/pallas_call | solution.py:217
  50.6 36.3 %conditional.9 = ((bf16[592,768]{1,0:T(8,128)(2,1)}, bf16[3,592,768]{2,1,0:T(8,128)(2,1)}, bf16[592,768]{1,0:T(8,128)(2,1)}, f32[6,1,1280]{2,1,0:T(1,128)S(1)}, ...) conditional(s32[]{:T(128)} %convert_element_type.5, () %tuple.65, ...), branch_computations={%region_2.0_spmd, %region_3.0_spmd} | conditional | bytes 16711860 | solution.py:868
  50.8 6.5 %pre_fwd.5 = (bf16[592,768]{1,0:T(8,128)(2,1)}, bf16[3,592,768]{2,1,0:T(8,128)(2,1)}) custom-call(bf16[592,768]{1,0:T(8,128)(2,1)} %get-tuple-element.406.x_ref, f32[1,768]{1,0:T(1,128)S(1)} %get-tuple-element.407.g_ref, f32[1,768]{1,0:T(1,128)S(1)} %get-tuple-element.408.b_ref, bf16[3,768,384]{2,1,0:T(8,128)(2,1)} %get-tuple-element.409.wo_ref, ...), custom_call_target="tpu_custom_call" | custom-call | tf_op jit(solution)/shard_map/cond/branch_1_fun/pre_fwd/pallas_call | solution.py:84
  57.2 15.4 %attn_fwd.5 = (bf16[592,768]{1,0:T(8,128)(2,1)S(1)}, f32[6,1,1280]{2,1,0:T(1,128)S(1)}) custom-call(bf16[3,592,768]{2,1,0:T(8,128)(2,1)} %get-tuple-element.844.q_ref.k_ref.v_ref, bf16[3,592,768]{2,1,0:T(8,128)(2,1)} %get-tuple-element.844.q_ref.k_ref.v_ref, bf16[3,592,768]{2,1,0:T(8,128)(2,1)} %get-tuple-element.844.q_ref.k_ref.v_ref), custom_call_target="tpu_custom_call" | custom-call | tf_op jit(solution)/shard_map/cond/branch_1_fun/attn_fwd/pallas_call | solution.py:155
  72.7 14.2 %post_fwd.5 = (f32[592,768]{1,0:T(8,128)}, bf16[592,768]{1,0:T(8,128)(2,1)}, bf16[592,1536]{1,0:T(8,128)(2,1)}, bf16[592,1536]{1,0:T(8,128)(2,1)}, bf16[592,1536...) custom-call(bf16[592,768]{1,0:T(8,128)(2,1)S(1)} %copy-done.22, ...), custom_call_target="tpu_custom_call" | custom-call | tf_op jit(solution)/shard_map/cond/branch_1_fun/post_fwd/pallas_call | solution.py:217
  89.1 4.5 cut.3
  93.9 7.2 %conditional.11 = ((bf16[624,768]{1,0:T(8,128)(2,1)}, bf16[624,1536]{1,0:T(8,128)(2,1)}, bf16[624,1536]{1,0:T(8,128)(2,1)}, bf16[624,768]{1,0:T(8,128)(2,1)}, bf...) conditional(s32[]{:T(128)} %convert_element_type.4, () %tuple.70, ...), branch_computations={%region_6.0_spmd, %region_7.0_spmd} | conditional | bytes 18579608 | solution.py:877
  102.6 5.9 %collective-permute-done.6 = bf16[592,768]{1,0:T(8,128)(2,1)} collective-permute-done((bf16[592,768]{1,0:T(8,128)(2,1)}, bf16[592,768]{1,0:T(8,128)(2,1)}, u32[]{:S(2)}, u32[]{:S(2)}) %collective-permute-start.6) | collective-permute-done | bytes 909344 | tf_op jit(solution)/shard_map/ppermute | solution.py:883
  108.7 7.1 %conditional.13 = ((bf16[592,768]{1,0:T(8,128)(2,1)}, bf16[592,1536]{1,0:T(8,128)(2,1)}, bf16[592,1536]{1,0:T(8,128)(2,1)}, bf16[592,768]{1,0:T(8,128)(2,1)}, bf...) conditional(s32[]{:T(128)} %convert_element_type.4, () %tuple.76, ...), branch_computations={%region_10.0_spmd, %region_11.0_spmd} | conditional | bytes 17989784 | solution.py:877
  117.1 47.1 %collective-permute-done.11 = bf16[624,768]{1,0:T(8,128)(2,1)} collective-permute-done((bf16[624,768]{1,0:T(8,128)(2,1)}, bf16[624,768]{1,0:T(8,128)(2,1)}, u32[]{:S(2)}, u32[]{:S(2)}) %collective-permute-start.11) | collective-permute-done | bytes 958496 | tf_op jit(solution)/shard_map/ppermute | solution.py:884
  164.3 40.3 %conditional.14 = ((bf16[624,768]{1,0:T(8,128)(2,1)}, bf16[624,1536]{1,0:T(8,128)(2,1)}, bf16[624,1536]{1,0:T(8,128)(2,1)}, bf16[624,768]{1,0:T(8,128)(2,1)}, bf...) conditional(s32[]{:T(128)} %convert_element_type.5, ...), branch_computations={%region_12.0_spmd, %region_13.0_spmd} | conditional | bytes 18579608 | solution.py:877
  164.7 16.7 %post_bwd.6 = (bf16[624,1536]{1,0:T(8,128)(2,1)}, bf16[624,1536]{1,0:T(8,128)(2,1)}, f32[624,768]{1,0:T(8,128)}, bf16[624,768]{1,0:T(8,128)(2,1)}, bf16[624,768]...) custom-call(bf16[624,768]{1,0:T(8,128)(2,1)} %get-tuple-element.556., ...), custom_call_target="tpu_custom_call" | custom-call | tf_op jit(solution)/shard_map/cond/branch_1_fun/post_bwd/pallas_call | solution.py:292
  181.4 14.5 %attn_bwd.6 = (bf16[3,624,768]{2,1,0:T(8,128)(2,1)S(1)}, f32[8,768]{1,0:T(8,128)}) custom-call(bf16[3,624,768]{2,1,0:T(8,128)(2,1)S(1)} %get-tuple-element.571.q_ref.k_ref.v_ref, bf16[3,624,768]{2,1,0:T(8,128)(2,1)S(1)} %get-tuple-element.571.q_ref.k_ref.v_ref, bf16[3,624,768]{2,1,0:T(8,128)(2,1)S(1)} %get-tuple-element.571.q_ref.k_ref.v_ref, ...), custom_call_target="tpu_custom_call" | custom-call | tf_op jit(solution)/shard_map/cond/branch_1_fun/attn_bwd/pallas_call | solution.py:356
  195.9 8.7 %pre_bwd.6 = (bf16[624,768]{1,0:T(8,128)(2,1)}, f32[8,768]{1,0:T(8,128)}) custom-call(bf16[3,624,768]{2,1,0:T(8,128)(2,1)S(1)} %get-tuple-element.957.d_ref, bf16[3,768,384]{2,1,0:T(8,128)(2,1)S(1)} %copy-done.12, bf16[3,768,384]{2,1,0:T(8,128)(2,1)} %get-tuple-element.580.wp_ref, bf16[624,768]{1,0:T(8,128)(2,1)} %get-tuple-element.581.x_ref, ...), custom_call_target="tpu_custom_call" | custom-call | tf_op jit(solution)/shard_map/cond/branch_1_fun/pre_bwd/pallas_call | solution.py:401
  204.6 8.4 %wgrad_attn.2 = (bf16[3,768,384]{2,1,0:T(8,128)(2,1)}, bf16[3,768,384]{2,1,0:T(8,128)(2,1)}, bf16[384,768]{1,0:T(8,128)(2,1)}, bf16[384,768]{1,0:T(8,128)(2,1)}) custom-call(bf16[624,768]{1,0:T(8,128)(2,1)} %get-tuple-element.754.refs_0_, bf16[3,624,768]{2,1,0:T(8,128)(2,1)} %get-tuple-element.755.refs_1_, bf16[624,768]{1,0:T(8,128)(2,1)} %get-tuple-element.756.refs_2_, ...), custom_call_target="tpu_custom_call" | custom-call | tf_op jit(solution)/shard_map/wgrad_attn/pallas_call | solution.py:484
  213.1 12.1 %wgrad_mlp.2 = (bf16[1536,768]{1,0:T(8,128)(2,1)}, bf16[1536,768]{1,0:T(8,128)(2,1)}, bf16[768,1536]{1,0:T(8,128)(2,1)}, bf16[768,1536]{1,0:T(8,128)(2,1)}) custom-call(bf16[624,1536]{1,0:T(8,128)(2,1)S(1)} %copy-done.24, bf16[624,1536]{1,0:T(8,128)(2,1)S(1)} %copy-done.25, bf16[624,768]{1,0:T(8,128)(2,1)} %get-tuple-element.745.refs_2_, ...), custom_call_target="tpu_custom_call" | custom-call | tf_op jit(solution)/shard_map/wgrad_mlp/pallas_call | solution.py:446
  225.2 6.3 %join.2 = bf16[2336,768]{1,0:T(8,128)(2,1)} custom-call(s32[3]{0:T(128)} %pad_add_fusion.meta_ref, bf16[592,768]{1,0:T(8,128)(2,1)} %get-tuple-element.734.refs_0_, bf16[624,768]{1,0:T(8,128)(2,1)S(1)} %copy-done.30, bf16[592,768]{1,0:T(8,128)(2,1)} %collective-permute-done.8.refs_2_, bf16[624,768]{1,0:T(8,128)(2,1)} %collective-permute-done.9.refs_3_), custom_call_target="tpu_custom_call" | custom-call | tf_op jit(solution)/shard_map/join/pallas_call | solution.py:801
  231.5 16.4 %collective-permute-done.10 = bf16[592,768]{1,0:T(8,128)(2,1)} collective-permute-done((bf16[592,768]{1,0:T(8,128)(2,1)}, bf16[592,768]{1,0:T(8,128)(2,1)}, u32[]{:S(2)}, u32[]{:S(2)}) %collective-permute-start.10) | collective-permute-done | bytes 909344 | tf_op jit(solution)/shard_map/ppermute | solution.py:884
  247.9 43.3 %conditional.15 = ((bf16[592,768]{1,0:T(8,128)(2,1)}, bf16[592,1536]{1,0:T(8,128)(2,1)}, bf16[592,1536]{1,0:T(8,128)(2,1)}, bf16[592,768]{1,0:T(8,128)(2,1)}, bf...) conditional(s32[]{:T(128)} %convert_element_type.5, ...), branch_computations={%region_14.0_spmd, %region_15.0_spmd} | conditional | bytes 14549144 | solution.py:877
  248.1 14.8 %post_bwd.7 = (bf16[592,1536]{1,0:T(8,128)(2,1)}, bf16[592,1536]{1,0:T(8,128)(2,1)}, f32[592,768]{1,0:T(8,128)}, bf16[592,768]{1,0:T(8,128)(2,1)}, bf16[592,768]...) custom-call(bf16[592,768]{1,0:T(8,128)(2,1)} %get-tuple-element.586.g_r, ...), custom_call_target="tpu_custom_call" | custom-call | tf_op jit(solution)/shard_map/cond/branch_1_fun/post_bwd/pallas_call | solution.py:292
  262.9 20.0 %attn_bwd.7 = (bf16[3,592,768]{2,1,0:T(8,128)(2,1)S(1)}, f32[8,768]{1,0:T(8,128)}) custom-call(bf16[3,592,768]{2,1,0:T(8,128)(2,1)} %get-tuple-element.601.q_ref.k_ref.v_ref, bf16[3,592,768]{2,1,0:T(8,128)(2,1)} %get-tuple-element.601.q_ref.k_ref.v_ref, bf16[3,592,768]{2,1,0:T(8,128)(2,1)} %get-tuple-element.601.q_ref.k_ref.v_ref, ...), custom_call_target="tpu_custom_call" | custom-call | tf_op jit(solution)/shard_map/cond/branch_1_fun/attn_bwd/pallas_call | solution.py:356
  282.9 8.1 %pre_bwd.7 = (bf16[592,768]{1,0:T(8,128)(2,1)}, f32[8,768]{1,0:T(8,128)}) custom-call(bf16[3,592,768]{2,1,0:T(8,128)(2,1)S(1)} %get-tuple-element.979.d_ref, bf16[3,768,384]{2,1,0:T(8,128)(2,1)S(1)} %get-tuple-element.609.wo_ref, bf16[3,768,384]{2,1,0:T(8,128)(2,1)} %get-tuple-element.610.wp_ref, bf16[592,768]{1,0:T(8,128)(2,1)S(1)} %copy-done.23, ...), custom_call_target="tpu_custom_call" | custom-call | tf_op jit(solution)/shard_map/cond/branch_1_fun/pre_bwd/pallas_call | solution.py:401
  291.3 8.9 %wgrad_attn.3 = (bf16[3,768,384]{2,1,0:T(8,128)(2,1)}, bf16[3,768,384]{2,1,0:T(8,128)(2,1)}, bf16[384,768]{1,0:T(8,128)(2,1)}, bf16[384,768]{1,0:T(8,128)(2,1)}) custom-call(bf16[592,768]{1,0:T(8,128)(2,1)} %get-tuple-element.773.refs_0_, bf16[3,592,768]{2,1,0:T(8,128)(2,1)} %get-tuple-element.774.refs_1_, bf16[592,768]{1,0:T(8,128)(2,1)S(1)} %copy-done.21, ...), custom_call_target="tpu_custom_call" | custom-call | tf_op jit(solution)/shard_map/wgrad_attn/pallas_call | solution.py:484
  300.4 12.7 %wgrad_mlp.3 = (bf16[1536,768]{1,0:T(8,128)(2,1)}, bf16[1536,768]{1,0:T(8,128)(2,1)}, bf16[768,1536]{1,0:T(8,128)(2,1)}, bf16[768,1536]{1,0:T(8,128)(2,1)}) custom-call(bf16[592,1536]{1,0:T(8,128)(2,1)S(1)} %copy-done.27, bf16[592,1536]{1,0:T(8,128)(2,1)S(1)} %copy-done.28, bf16[592,768]{1,0:T(8,128)(2,1)S(1)} %copy-done.32, ...), custom_call_target="tpu_custom_call" | custom-call | tf_op jit(solution)/shard_map/wgrad_mlp/pallas_call | solution.py:446
  313.2 160.6 %ring.1 = (bf16[1536,768]{1,0:T(8,128)(2,1)}, bf16[768,1536]{1,0:T(8,128)(2,1)}, bf16[2304,384]{1,0:T(8,128)(2,1)}, bf16[384,768]{1,0:T(8,128)(2,1)}, f32[16,768]{1,0:T(8,128)}) custom-call(bf16[1536,768]{1,0:T(8,128)(2,1)} %get-tuple-element.771.refs_0_, bf16[768,1536]{1,0:T(8,128)(2,1)} %get-tuple-element.772.refs_1_, bf16[2304,384]{1,0:T(8,128)(2,1)} %bitcast.49, ...), custom_call_target="tpu_custom_call" | custom-call | tf_op jit(solution)/shard_map/ring/pallas_call | solution.py:669
  473.8 9.4 %finish.1 = (f32[1,1536,768]{2,1,0:T(8,128)}, f32[1,768,1536]{2,1,0:T(8,128)}, f32[1,2304,384]{2,1,0:T(8,128)}, f32[1,384,768]{2,1,0:T(8,128)}, f32[1,768]{1,0:T...) custom-call(bf16[1536,768]{1,0:T(8,128)(2,1)} %get-tuple-element.793, ...), custom_call_target="tpu_custom_call" | custom-call | tf_op jit(solution)/shard_map/finish/pallas_call | solution.py:718
  483.3 5.4 %join.3 = bf16[2336,768]{1,0:T(8,128)(2,1)} custom-call(s32[3]{0:T(128)} %pad_add_fusion.meta_ref, bf16[592,768]{1,0:T(8,128)(2,1)S(1)} %copy-done.33, bf16[624,768]{1,0:T(8,128)(2,1)S(1)} %copy-done.31, bf16[592,768]{1,0:T(8,128)(2,1)} %collective-permute-done.12.refs_2_, bf16[624,768]{1,0:T(8,128)(2,1)} %collective-permute-done.13.refs_3_), custom_call_target="tpu_custom_call" | custom-call | tf_op jit(solution)/shard_map/join/pallas_call | solution.py:801
  (115 shorter events, 11.1 us)
Async XLA Ops:
  0.6 18.0 %copy-start.4 = (bf16[1,768,1536]{2,1,0:T(8,128)(2,1)S(1)}, bf16[1,768,1536]{2,1,0:T(8,128)(2,1)}, u32[]{:S(2)}) copy-start(bf16[1,768,1536]{2,1,0:T(8,128)(2,1)} %param.42) | copy-start | bytes 7077892
  0.7 18.0 %copy-start.13 = (bf16[1,384,768]{2,1,0:T(8,128)(2,1)S(1)}, bf16[1,384,768]{2,1,0:T(8,128)(2,1)}, u32[]{:S(2)}) copy-start(bf16[1,384,768]{2,1,0:T(8,128)(2,1)} %param.38) | copy-start | bytes 1769476
  0.7 18.0 %copy-start.38 = (f32[1,2,384]{2,1,0:T(2,128)S(1)}, f32[1,2,384]{2,1,0:T(2,128)}, u32[]{:S(2)}) copy-start(f32[1,2,384]{2,1,0:T(2,128)} %param.37) | copy-start | bytes 9220
  0.7 18.0 %copy-start.36 = (f32[1,1536]{1,0:T(1,128)S(1)}, f32[1,1536]{1,0:T(1,128)}, u32[]{:S(2)}) copy-start(f32[1,1536]{1,0:T(1,128)} %param.43) | copy-start | bytes 18436
  0.7 18.0 %copy-start.34 = (f32[1,768]{1,0:T(1,128)S(1)}, f32[1,768]{1,0:T(1,128)}, u32[]{:S(2)}) copy-start(f32[1,768]{1,0:T(1,128)} %param.34) | copy-start | bytes 9220
  0.7 18.0 %copy-start.37 = (f32[1,768]{1,0:T(1,128)S(1)}, f32[1,768]{1,0:T(1,128)}, u32[]{:S(2)}) copy-start(f32[1,768]{1,0:T(1,128)} %param.35) | copy-start | bytes 9220
  0.7 18.0 %copy-start.39 = (f32[1,768]{1,0:T(1,128)S(1)}, f32[1,768]{1,0:T(1,128)}, u32[]{:S(2)}) copy-start(f32[1,768]{1,0:T(1,128)} %param.39) | copy-start | bytes 9220
  0.7 18.0 %copy-start.35 = (f32[1,768]{1,0:T(1,128)S(1)}, f32[1,768]{1,0:T(1,128)}, u32[]{:S(2)}) copy-start(f32[1,768]{1,0:T(1,128)} %param.40) | copy-start | bytes 9220
  0.7 18.0 %copy-start.40 = (f32[1,768]{1,0:T(1,128)S(1)}, f32[1,768]{1,0:T(1,128)}, u32[]{:S(2)}) copy-start(f32[1,768]{1,0:T(1,128)} %param.41) | copy-start | bytes 9220
  0.7 18.0 %copy-start.41 = (f32[1,768]{1,0:T(1,128)S(1)}, f32[1,768]{1,0:T(1,128)}, u32[]{:S(2)}) copy-start(f32[1,768]{1,0:T(1,128)} %param.45) | copy-start | bytes 9220
  0.8 17.9 %collective-permute-start.3 = (bf16[768,1536]{1,0:T(8,128)(2,1)}, bf16[768,1536]{1,0:T(8,128)(2,1)}, u32[]{:S(2)}, u32[]{:S(2)}) collective-permute-start(bf16[768,1536]{1,0:T(8,128)(2,1)} %bitcast.11), channel_id=1, source_target_pairs={{0,8},{8,0},{1,9},{9,1},{2,10},{10,2},{3,11},{11,3},{4,12},{12,4},... | collective-permute-start | bytes 7077896 | tf_op jit(solution)/shard_map/ppermute | solution.py:849
  1.3 17.4 %collective-permute-start.5 = (bf16[1536,768]{1,0:T(8,128)(2,1)}, bf16[1536,768]{1,0:T(8,128)(2,1)}, u32[]{:S(2)}, u32[]{:S(2)}) collective-permute-start(bf16[1536,768]{1,0:T(8,128)(2,1)} %bitcast.20), channel_id=1, source_target_pairs={{0,8},{8,0},{1,9},{9,1},{2,10},{10,2},{3,11},{11,3},{4,12},{12,4},... | collective-permute-start | bytes 7077896 | tf_op jit(solution)/shard_map/ppermute | solution.py:849
  1.4 17.3 %collective-permute-start = (bf16[3,768,384]{2,1,0:T(8,128)(2,1)}, bf16[3,768,384]{2,1,0:T(8,128)(2,1)}, u32[]{:S(2)}, u32[]{:S(2)}) collective-permute-start(bf16[3,768,384]{2,1,0:T(8,128)(2,1)} %bitcast.29), channel_id=1, source_target_pairs={{0,8},{8,0},{1,9},{9,1},{2,10},{10,2},{3,11},{11,3},{4,12},{12,4},... | collective-permute-start | bytes 5308424 | tf_op jit(solution)/shard_map/ppermute | solution.py:849
  1.8 16.8 %collective-permute-start.2 = (bf16[384,768]{1,0:T(8,128)(2,1)}, bf16[384,768]{1,0:T(8,128)(2,1)}, u32[]{:S(2)}, u32[]{:S(2)}) collective-permute-start(bf16[384,768]{1,0:T(8,128)(2,1)} %bitcast.38), channel_id=1, source_target_pairs={{0,8},{8,0},{1,9},{9,1},{2,10},{10,2},{3,11},{11,3},{4,12},{12,4},... | collective-permute-start | bytes 1769480 | tf_op jit(solution)/shard_map/ppermute | solution.py:849
  1.9 10.7 %collective-permute-start.1 = (f32[2,384]{1,0:T(2,128)}, f32[2,384]{1,0:T(2,128)S(1)}, u32[]{:S(2)}, u32[]{:S(2)}) collective-permute-start(f32[2,384]{1,0:T(2,128)} %bitcast.51), channel_id=1, source_target_pairs={{0,8},{8,0},{1,9},{9,1},{2,10},{10,2},{3,11},{11,3},{4,12},{12,4},... | collective-permute-start | bytes 9224 | tf_op jit(solution)/shard_map/ppermute | solution.py:849
  12.6 6.1 %collective-permute-start.4 = (f32[1,1536]{1,0:T(1,128)}, f32[1,1536]{1,0:T(1,128)S(1)}, u32[]{:S(2)}, u32[]{:S(2)}) collective-permute-start(f32[1,1536]{1,0:T(1,128)} %param.43), channel_id=1, source_target_pairs={{0,8},{8,0},{1,9},{9,1},{2,10},{10,2},{3,11},{11,3},{4,12},{12,4},... | collective-permute-start | bytes 18440 | tf_op jit(solution)/shard_map/ppermute | solution.py:849
  48.3 45.3 %collective-permute-start.7 = (bf16[624,768]{1,0:T(8,128)(2,1)}, bf16[624,768]{1,0:T(8,128)(2,1)}, u32[]{:S(2)}, u32[]{:S(2)}) collective-permute-start(bf16[624,768]{1,0:T(8,128)(2,1)} %get-tuple-element.722), channel_id=1, source_target_pairs={{0,16},{1,17},{2,18},{3,19},{4,20},{5,21},{6,22},{7,23},{8,24},{9,... | collective-permute-start | bytes 2875400 | tf_op jit(solution)/shard_map/ppermute | solution.py:883
  57.2 15.5 %copy-start.7 = (bf16[1536,768]{1,0:T(8,128)(2,1)S(1)}, bf16[1536,768]{1,0:T(8,128)(2,1)}, u32[]{:S(2)}) copy-start(bf16[1536,768]{1,0:T(8,128)(2,1)} %get-tuple-element.426.do_ref) | copy-start | bytes 7077892 | tf_op jit(solution)/shard_map/cond
  57.2 15.5 %copy-start.22 = (bf16[592,768]{1,0:T(8,128)(2,1)S(1)}, bf16[592,768]{1,0:T(8,128)(2,1)}, u32[]{:S(2)}) copy-start(bf16[592,768]{1,0:T(8,128)(2,1)} %get-tuple-element.406.x_ref) | copy-start | bytes 2727940 | tf_op jit(solution)/shard_map/cond
  86.9 21.6 %collective-permute-start.6 = (bf16[592,768]{1,0:T(8,128)(2,1)}, bf16[592,768]{1,0:T(8,128)(2,1)}, u32[]{:S(2)}, u32[]{:S(2)}) collective-permute-start(bf16[592,768]{1,0:T(8,128)(2,1)} %get-tuple-element.724), channel_id=1, source_target_pairs={{0,16},{1,17},{2,18},{3,19},{4,20},{5,21},{6,22},{7,23},{8,24},{9,... | collective-permute-start | bytes 2727944 | tf_op jit(solution)/shard_map/ppermute | solution.py:883
  101.1 63.1 %collective-permute-start.11 = (bf16[624,768]{1,0:T(8,128)(2,1)}, bf16[624,768]{1,0:T(8,128)(2,1)}, u32[]{:S(2)}, u32[]{:S(2)}) collective-permute-start(bf16[624,768]{1,0:T(8,128)(2,1)} %get-tuple-element.732), channel_id=1, source_target_pairs={{16,0},{17,1},{18,2},{19,3},{20,4},{21,5},{22,6},{23,7},{24,8},{25... | collective-permute-start | bytes 2875400 | tf_op jit(solution)/shard_map/ppermute | solution.py:884
  102.4 122.8 %collective-permute-start.9 = (bf16[624,768]{1,0:T(8,128)(2,1)}, bf16[624,768]{1,0:T(8,128)(2,1)}, u32[]{:S(2)}, u32[]{:S(2)}) collective-permute-start(bf16[624,768]{1,0:T(8,128)(2,1)} %get-tuple-element.735.refs_1_), channel_id=1, source_target_pairs={{0,8},{8,0},{1,9},{9,1},{2,10},{10,2},{3,11},{11,3},{4,12},{12,4},... | collective-permute-start | bytes 2875400 | tf_op jit(solution)/shard_map/ppermute | solution.py:849
  108.6 116.5 %collective-permute-start.8 = (bf16[592,768]{1,0:T(8,128)(2,1)}, bf16[592,768]{1,0:T(8,128)(2,1)}, u32[]{:S(2)}, u32[]{:S(2)}) collective-permute-start(bf16[592,768]{1,0:T(8,128)(2,1)} %get-tuple-element.734.refs_0_), channel_id=1, source_target_pairs={{0,8},{8,0},{1,9},{9,1},{2,10},{10,2},{3,11},{11,3},{4,12},{12,4},... | collective-permute-start | bytes 2727944 | tf_op jit(solution)/shard_map/ppermute | solution.py:849
  108.7 55.5 %copy-start.2 = (bf16[3,624,768]{2,1,0:T(8,128)(2,1)S(1)}, bf16[3,624,768]{2,1,0:T(8,128)(2,1)}, u32[]{:S(2)}) copy-start(bf16[3,624,768]{2,1,0:T(8,128)(2,1)} %get-tuple-element.730) | copy-start | bytes 8626180
  115.8 132.0 %collective-permute-start.10 = (bf16[592,768]{1,0:T(8,128)(2,1)}, bf16[592,768]{1,0:T(8,128)(2,1)}, u32[]{:S(2)}, u32[]{:S(2)}) collective-permute-start(bf16[592,768]{1,0:T(8,128)(2,1)} %get-tuple-element.742), channel_id=1, source_target_pairs={{16,0},{17,1},{18,2},{19,3},{20,4},{21,5},{22,6},{23,7},{24,8},{25... | collective-permute-start | bytes 2727944 | tf_op jit(solution)/shard_map/ppermute | solution.py:884
  204.6 278.7 %collective-permute-start.13 = (bf16[624,768]{1,0:T(8,128)(2,1)}, bf16[624,768]{1,0:T(8,128)(2,1)}, u32[]{:S(2)}, u32[]{:S(2)}) collective-permute-start(bf16[624,768]{1,0:T(8,128)(2,1)} %get-tuple-element.764.refs_1_), channel_id=1, source_target_pairs={{0,8},{8,0},{1,9},{9,1},{2,10},{10,2},{3,11},{11,3},{4,12},{12,4},... | collective-permute-start | bytes 2875400 | tf_op jit(solution)/shard_map/ppermute | solution.py:849
  225.2 22.7 %copy-start.5 = (bf16[1,768,1536]{2,1,0:T(8,128)(2,1)S(1)}, bf16[1,768,1536]{2,1,0:T(8,128)(2,1)}, u32[]{:S(2)}) copy-start(bf16[1,768,1536]{2,1,0:T(8,128)(2,1)} %param.42) | copy-start | bytes 7077892
  225.2 22.7 %copy-start.6 = (bf16[1,1536,768]{2,1,0:T(8,128)(2,1)S(1)}, bf16[1,1536,768]{2,1,0:T(8,128)(2,1)}, u32[]{:S(2)}) copy-start(bf16[1,1536,768]{2,1,0:T(8,128)(2,1)} %param.44) | copy-start | bytes 7077892
  225.2 22.7 %copy-start.9 = (bf16[1,3,768,384]{3,2,1,0:T(8,128)(2,1)S(1)}, bf16[1,3,768,384]{3,2,1,0:T(8,128)(2,1)}, u32[]{:S(2)}) copy-start(bf16[1,3,768,384]{3,2,1,0:T(8,128)(2,1)} %param.36) | copy-start | bytes 5308420
  247.9 43.4 %copy-start.21 = (bf16[592,768]{1,0:T(8,128)(2,1)S(1)}, bf16[592,768]{1,0:T(8,128)(2,1)}, u32[]{:S(2)}) copy-start(bf16[592,768]{1,0:T(8,128)(2,1)} %get-tuple-element.775.refs_2_) | copy-start | bytes 2727940
  262.9 20.0 %copy-start.23 = (bf16[592,768]{1,0:T(8,128)(2,1)S(1)}, bf16[592,768]{1,0:T(8,128)(2,1)}, u32[]{:S(2)}) copy-start(bf16[592,768]{1,0:T(8,128)(2,1)} %get-tuple-element.611.x_ref) | copy-start | bytes 2727940 | tf_op jit(solution)/shard_map/cond
  291.2 192.0 %collective-permute-start.12 = (bf16[592,768]{1,0:T(8,128)(2,1)}, bf16[592,768]{1,0:T(8,128)(2,1)}, u32[]{:S(2)}, u32[]{:S(2)}) collective-permute-start(bf16[592,768]{1,0:T(8,128)(2,1)} %get-tuple-element.763.refs_0_), channel_id=1, source_target_pairs={{0,8},{8,0},{1,9},{9,1},{2,10},{10,2},{3,11},{11,3},{4,12},{12,4},... | collective-permute-start | bytes 2727944 | tf_op jit(solution)/shard_map/ppermute | solution.py:849
  (25 other events, 271.2 us)

commit v4 on v3

--- a/solution.py
+++ b/solution.py
@@ -21,8 +21,8 @@
 CHUNKS = ((1, 592, LEN_LARGE), (SMALL_MB, 208, LEN_SMALL))
 
 
-def params(**more):
-    return pltpu.CompilerParams(vmem_limit_bytes=VMEM_LIMIT, **more)
+def params(limit=VMEM_LIMIT, **more):
+    return pltpu.CompilerParams(vmem_limit_bytes=limit, **more)
 
 
 def nn(a, b):
@@ -64,40 +64,34 @@
     return jnp.sum(values.astype(F32), axis=0, keepdims=True)
 
 
-def pre_fwd_kernel(x_ref, g_ref, b_ref, wo_ref, wp_ref, bo_ref, bp_ref, normed_ref, qkv_ref):
-    s = pl.program_id(0)
-
-    @pl.when(s == 0)
-    def _():
-        xhat, _ = norm_parts(x_ref[...].astype(F32))
-        normed_ref[...] = (xhat * g_ref[...] + b_ref[...]).astype(BF)
-
-    weight = jnp.concatenate([wo_ref[0], wp_ref[0]], axis=1)
-    biases = jnp.concatenate([bo_ref[...], bp_ref[...]], axis=1)
-    bias = jnp.where(s == 0, biases[:1], jnp.where(s == 1, 0.0, biases[1:]))
-    qkv_ref[0] = (nn(normed_ref[...], weight) + bias).astype(BF)
-
-
-def pre_fwd(x, w):
-    n, d = x.shape
-    half = w["wqkv_o"].shape[-1]
-    return pl.pallas_call(
-        pre_fwd_kernel,
-        grid=(3,),
-        in_specs=[
-            whole((n, d)),
-            whole((1, d)),
-            whole((1, d)),
-            pl.BlockSpec((1, d, half), lambda s: (s, 0, 0)),
-            pl.BlockSpec((1, d, half), lambda s: (s, 0, 0)),
-            whole((2, half)),
-            whole((2, half)),
-        ],
-        out_specs=[whole((n, d)), pl.BlockSpec((1, n, 2 * half), lambda s: (s, 0, 0))],
-        out_shape=[sds((n, d), BF), sds((3, n, 2 * half), BF)],
-        compiler_params=params(),
-        name="pre_fwd",
-    )(x, w["g1"], w["b1"], w["wqkv_o"], w["wqkv_p"], w["bq_o"], w["bq_p"])
+def fetch(pairs, sems):
+    return [pltpu.make_async_copy(src, dst, sems.at[i]) for i, (src, dst) in enumerate(pairs)]
+
+
+def weight_loads(w, wq, pw, up, dn):
+    wqo, wqp, pwo, pwp, upo, upp, dno, dnp = w
+    half, fh = wqo.shape[-1], dno.shape[0]
+    return {
+        "qkv": [(wqo, wq.at[:, :, :half]), (wqp, wq.at[:, :, half:])],
+        "proj": [(pwo, pw.at[:half]), (pwp, pw.at[half:])],
+        "up": [(upo, up.at[:, :fh]), (upp, up.at[:, fh:])],
+        "down": [(dno, dn.at[:fh]), (dnp, dn.at[fh:])],
+    }
+
+
+def weights_of(w):
+    return [w[k] for k in ("wqkv_o", "wqkv_p", "pw_o", "pw_p", "up_o", "up_p", "dn_o", "dn_p")]
+
+
+def weight_scratch(d, ff):
+    return [
+        pltpu.VMEM((3, d, d), BF), pltpu.VMEM((d, d), BF), pltpu.VMEM((d, ff), BF),
+        pltpu.VMEM((ff, d), BF),
+    ]
+
+
+def lanes(at, width):
+    return pl.ds(pl.multiple_of(at * width, width), width)
 
 
 def mask_keys(scores, vlen):
@@ -129,44 +123,24 @@
     return jnp.where(head == 0, stacked[:plen], stacked[plen:])
 
 
-def attn_fwd_kernel(q_ref, k_ref, v_ref, o_ref, l_ref, o_tmp, *, nimg, plen, vlen):
+def attn_fwd_pair(p, qkv, att, lse, o_tmp, chunk):
+    nimg, plen, vlen = chunk
+    cols = lanes(p, 128)
     at = 0
     for im in range(nimg):
         rows = slice(im * plen, (im + 1) * plen)
-        k = k_ref[0, rows]
-        vt = v_ref[0, rows].T
-        queries = both_heads(q_ref[0, rows])
+        k = qkv[1, rows, cols]
+        vt = qkv[2, rows, cols].T
+        queries = both_heads(qkv[0, rows, cols])
         for q0, qw in qblocks(plen):
             st = mask_keys(nt(k, queries[q0 : q0 + qw]), vlen)
             top = jnp.max(st, axis=0, keepdims=True)
             e = jnp.exp2((st - top) * SCALE2)
             total = jnp.sum(e, axis=0, keepdims=True)
             o_tmp[q0 : q0 + qw] = (nn(vt, e.astype(BF)) * (1.0 / total)).T
-            l_ref[0, :, at : at + qw] = top * SCALE2 + jnp.log2(total)
+            lse[p, :, at : at + qw] = top * SCALE2 + jnp.log2(total)
             at += 256
-        o_ref[rows] = one_each(o_tmp, plen).astype(BF)
-
-
-def attn_fwd(qkv, chunk):
-    nimg, plen, vlen = chunk
-    _, n, d = qkv.shape
-    pairs = d // 128
-    width = lse_width(chunk)
-    return pl.pallas_call(
-        functools.partial(attn_fwd_kernel, nimg=nimg, plen=plen, vlen=vlen),
-        grid=(pairs,),
-        in_specs=[
-            pl.BlockSpec((1, n, 128), lambda p, s=s: (s, 0, p)) for s in range(3)
-        ],
-        out_specs=[
-            pl.BlockSpec((n, 128), lambda p: (0, p)),
-            pl.BlockSpec((1, 1, width), lambda p: (p, 0, 0)),
-        ],
-        out_shape=[sds((n, d), BF), sds((pairs, 1, width), F32)],
-        scratch_shapes=[pltpu.VMEM((2 * plen, 128), F32)],
-        compiler_params=params(),
-        name="attn_fwd",
-    )(qkv, qkv, qkv)
+        att[rows, cols] = one_each(o_tmp, plen).astype(BF)
 
 
 def gelu_parts(x):
@@ -175,284 +149,315 @@
     return x * cdf, cdf + x * pdf
 
 
-def post_fwd_kernel(
-    x_ref, att_ref, pwo_ref, pwp_ref, pb_ref, g_ref, b_ref, uo_ref, up_ref, ubo_ref, ubp_ref,
-    do_ref, dp_ref, db_ref,
-    mid_ref, n2_ref, ao_ref, ap_ref, go_ref, gp_ref, out_ref, acc_ref,
-):
-    j = pl.program_id(0)
-
-    @pl.when(j == 0)
-    def _():
-        weight = jnp.concatenate([pwo_ref[...], pwp_ref[...]], axis=0)
-        mid = x_ref[...].astype(F32) + (nn(att_ref[...], weight) + pb_ref[...])
-        mid_ref[...] = mid
-        xhat, _ = norm_parts(mid)
-        n2_ref[...] = (xhat * g_ref[...] + b_ref[...]).astype(BF)
-        acc_ref[...] = mid + db_ref[...]
-
-    n2 = n2_ref[...]
-    for u_ref, ub_ref, d_ref, a_ref, dg_ref in (
-        (uo_ref, ubo_ref, do_ref, ao_ref, go_ref),
-        (up_ref, ubp_ref, dp_ref, ap_ref, gp_ref),
-    ):
-        act, slope = gelu_parts(nn(n2, u_ref[...]) + ub_ref[...])
-        act = act.astype(BF)
-        a_ref[...] = act
-        dg_ref[...] = slope.astype(BF)
-        acc_ref[...] += nn(act, d_ref[...])
-
-    @pl.when(j == pl.num_programs(0) - 1)
-    def _():
-        out_ref[...] = acc_ref[...].astype(BF)
-
-
-def post_fwd(x, att, w):
+FF_STEPS = 2
+WGRAD_STEPS = 4
+
+
+def fwd_kernel(*refs, chunk):
+    x_ref, g1, b1, bqo, bqp, pb, g2, b2, ubo, ubp, db = refs[:11]
+    weights, outs = refs[11:19], refs[19:28]
+    wq, pw, up, dn = refs[28:32]
+    held = refs[32:41]
+    acc, o_tmp, ub, in_sem, out_sem, ff_sem = refs[41:]
+    normed, qkv, att, lse, mid, n2, act, dg, out = held
+    ff = dn.shape[0]
+    fb = ff // FF_STEPS
+    loads = weight_loads(weights, wq, pw, up, dn)
+    names = ("qkv", "proj", "up", "down")
+    loads = {k: fetch(loads[k], in_sem.at[i]) for i, k in enumerate(names)}
+    saves = fetch(list(zip(held[:6] + held[8:], outs[:6] + outs[8:])), out_sem)
+    for c in loads["qkv"]:
+        c.start()
+    xhat, _ = norm_parts(x_ref[...].astype(F32))
+    normed[...] = (xhat * g1[...] + b1[...]).astype(BF)
+    saves[0].start()
+    ub[...] = jnp.concatenate([ubo[...], ubp[...]], axis=1)
+    biases = jnp.concatenate([bqo[...], bqp[...]], axis=1)
+    for c in loads["qkv"]:
+        c.wait()
+    for k in names[1:]:
+        for c in loads[k]:
+            c.start()
+
+    def project(s, carry):
+        bias = jnp.where(s == 0, biases[:1], jnp.where(s == 1, 0.0, biases[1:]))
+        qkv[s] = (nn(normed[...], wq[s]) + bias).astype(BF)
+        return carry
+
+    lax.fori_loop(0, 3, project, 0)
+    saves[1].start()
+
+    def attend(p, carry):
+        attn_fwd_pair(p, qkv, att, lse, o_tmp, chunk)
+        return carry
+
+    lax.fori_loop(0, lse.shape[0], attend, 0)
+    saves[2].start()
+    saves[3].start()
+    for c in loads["proj"]:
+        c.wait()
+    middle = x_ref[...].astype(F32) + (nn(att[...], pw[...]) + pb[...])
+    mid[...] = middle
+    saves[4].start()
+    xhat, _ = norm_parts(middle)
+    n2[...] = (xhat * g2[...] + b2[...]).astype(BF)
+    saves[5].start()
+    acc[...] = middle + db[...]
+    for k in ("up", "down"):
+        for c in loads[k]:
+            c.wait()
+
+    def block_saves(j):
+        cols = lanes(j, fb)
+        pairs = [(act.at[:, cols], outs[6].at[:, cols]), (dg.at[:, cols], outs[7].at[:, cols])]
+        return fetch(pairs, ff_sem.at[j])
+
+    def mlp(j, carry):
+        cols = lanes(j, fb)
+        value, slope = gelu_parts(nn(n2[...], up[:, cols]) + ub[:, cols])
+        value = value.astype(BF)
+        act[:, cols] = value
+        dg[:, cols] = slope.astype(BF)
+        for c in block_saves(j):
+            c.start()
+        acc[...] += nn(value, dn[cols])
+        return carry
+
+    lax.fori_loop(0, FF_STEPS, mlp, 0)
+    out[...] = acc[...].astype(BF)
+    saves[6].start()
+    for c in saves:
+        c.wait()
+    for j in range(FF_STEPS):
+        for c in block_saves(j):
+            c.wait()
+
+
+def forward(x, w, chunk):
     n, d = x.shape
-    half = w["pw_o"].shape[0]
-    fh = w["up_o"].shape[1]
-    fb = fh // 2
-    cols = lambda rows: pl.BlockSpec((rows, fb), lambda j: (0, j))
-    rows_ = pl.BlockSpec((fb, d), lambda j: (j, 0))
+    ff = 2 * w["dn_o"].shape[0]
+    pairs = d // 128
+    kept = [
+        ((n, d), BF), ((3, n, d), BF), ((n, d), BF), ((pairs, 1, lse_width(chunk)), F32),
+        ((n, d), F32), ((n, d), BF), ((n, ff), BF), ((n, ff), BF), ((n, d), BF),
+    ]
+    vmem = pl.BlockSpec(memory_space=pltpu.VMEM)
+    hbm = pl.BlockSpec(memory_space=pl.ANY)
     return pl.pallas_call(
-        post_fwd_kernel,
-        grid=(2,),
-        in_specs=[
-            whole((n, d)), whole((n, d)), whole((half, d)), whole((half, d)), whole((1, d)),
-            whole((1, d)), whole((1, d)), cols(d), cols(d), cols(1), cols(1), rows_, rows_,
-            whole((1, d)),
+        functools.partial(fwd_kernel, chunk=chunk),
+        in_specs=[vmem] * 11 + [hbm] * 8,
+        out_specs=[hbm] * len(kept),
+        out_shape=[sds(*k) for k in kept],
+        scratch_shapes=weight_scratch(d, ff)
+        + [pltpu.VMEM(*k) for k in kept]
+        + [
+            pltpu.VMEM((n, d), F32), pltpu.VMEM((2 * chunk[1], 128), F32),
+            pltpu.VMEM((1, ff), F32), pltpu.SemaphoreType.DMA((4, 2)),
+            pltpu.SemaphoreType.DMA((7,)), pltpu.SemaphoreType.DMA((FF_STEPS, 2)),
         ],
-        out_specs=[
-            whole((n, d)), whole((n, d)), cols(n), cols(n), cols(n), cols(n), whole((n, d)),
-        ],
-        out_shape=[
-            sds((n, d), F32), sds((n, d), BF), sds((n, fh), BF), sds((n, fh), BF),
-            sds((n, fh), BF), sds((n, fh), BF), sds((n, d), BF),
-        ],
-        scratch_shapes=[pltpu.VMEM((n, d), F32)],
         compiler_params=params(),
-        name="post_fwd",
+        name="fwd",
     )(
-        x, att, w["pw_o"], w["pw_p"], w["pb"], w["g2"], w["b2"], w["up_o"], w["up_p"],
-        w["ub_o"], w["ub_p"], w["dn_o"], w["dn_p"], w["db"],
-    )
-
-
-def forward(x, w, chunk):
-    normed, qkv = pre_fwd(x, w)
-    att, lse = attn_fwd(qkv, chunk)
-    mid, n2, act_o, act_p, dg_o, dg_p, out = post_fwd(x, att, w)
-    return (normed, qkv, att, lse, mid, n2, act_o, act_p, dg_o, dg_p, out)
-
-
-def post_bwd_kernel(
-    g_ref, mid_ref, gain_ref, go_ref, gp_ref, uo_ref, up_ref, do_ref, dp_ref, pwo_ref, pwp_ref,
-    qo_ref, qp_ref, gm_ref, gb_ref, ga_ref, sums_ref, so_ref, sp_ref, copy_ref, acc_ref,
-):
-    j = pl.program_id(0)
-    g = g_ref[...]
-
-    @pl.when(j == 0)
-    def _():
-        acc_ref[...] = jnp.zeros_like(acc_ref)
-        copy_ref[...] = g
-
-    for dg_ref, u_ref, d_ref, q_ref, s_ref in (
-        (go_ref, uo_ref, do_ref, qo_ref, so_ref),
-        (gp_ref, up_ref, dp_ref, qp_ref, sp_ref),
-    ):
-        pre = (nt(g, d_ref[...]) * dg_ref[...].astype(F32)).astype(BF)
-        q_ref[...] = pre
-        s_ref[...] = rowsum(pre)
-        acc_ref[...] += nt(pre, u_ref[...])
-
-    @pl.when(j == pl.num_programs(0) - 1)
-    def _():
-        gn = acc_ref[...]
-        xhat, rstd = norm_parts(mid_ref[...])
-        gm = norm_back(xhat, rstd, gn, gain_ref[...]) + g.astype(F32)
-        gm_ref[...] = gm
-        gb = gm.astype(BF)
-        gb_ref[...] = gb
-        weight = jnp.concatenate([pwo_ref[...], pwp_ref[...]], axis=0)
-        ga_ref[...] = nt(gb, weight).astype(BF)
-        sums_ref[...] = jnp.concatenate(
-            [rowsum(gn * xhat), rowsum(gn), rowsum(gb), rowsum(g)]
-            + [jnp.zeros((4, gn.shape[1]), F32)], axis=0
-        )
-
-
-def post_bwd(g, kept, w):
-    n, d = g.shape
-    half = w["pw_o"].shape[0]
-    fh = w["up_o"].shape[1]
-    fb = fh // 2
-    cols = lambda rows: pl.BlockSpec((rows, fb), lambda j: (0, j))
-    rows_ = pl.BlockSpec((fb, d), lambda j: (j, 0))
-    return pl.pallas_call(
-        post_bwd_kernel,
-        grid=(2,),
-        in_specs=[
-            whole((n, d)), whole((n, d)), whole((1, d)), cols(n), cols(n), cols(d), cols(d),
-            rows_, rows_, whole((half, d)), whole((half, d)),
-        ],
-        out_specs=[
-            cols(n), cols(n), whole((n, d)), whole((n, d)), whole((n, d)), whole((8, d)),
-            cols(1), cols(1), whole((n, d)),
-        ],
-        out_shape=[
-            sds((n, fh), BF), sds((n, fh), BF), sds((n, d), F32), sds((n, d), BF),
-            sds((n, d), BF), sds((8, d), F32), sds((1, fh), F32), sds((1, fh), F32),
-            sds((n, d), BF),
-        ],
-        scratch_shapes=[pltpu.VMEM((n, d), F32)],
-        compiler_params=params(),
-        name="post_bwd",
-    )(
-        g, kept["mid"], w["g2"], kept["dg_o"], kept["dg_p"], w["up_o"], w["up_p"], w["dn_o"],
-        w["dn_p"], w["pw_o"], w["pw_p"],
-    )
-
-
-def attn_bwd_kernel(q_ref, k_ref, v_ref, ga_ref, l_ref, d_ref, s_ref, dq_tmp, *, nimg, plen, vlen):
-    sums = [jnp.zeros((1, 128), F32) for _ in range(3)]
+        x, w["g1"], w["b1"], w["bq_o"], w["bq_p"], w["pb"], w["g2"], w["b2"], w["ub_o"],
+        w["ub_p"], w["db"], *weights_of(w),
+    )
+
+
+def attn_bwd_pair(p, qkv, gatt, lse, dqkv, sums, dq_tmp, chunk):
+    nimg, plen, vlen = chunk
+    cols = lanes(p, 128)
+    total_q, total_v = jnp.zeros((1, 128), F32), jnp.zeros((1, 128), F32)
     at = 0
     for im in range(nimg):
         rows = slice(im * plen, (im + 1) * plen)
-        k = k_ref[0, rows]
-        v = v_ref[0, rows]
+        k = qkv[1, rows, cols]
+        v = qkv[2, rows, cols]
         kt = k.T
-        queries = both_heads(q_ref[0, rows])
-        grads = both_heads(ga_ref[rows])
+        queries = both_heads(qkv[0, rows, cols])
+        grads = both_heads(gatt[rows, cols])
         dk = jnp.zeros((plen, 128), F32)
         dv = jnp.zeros((plen, 128), F32)
         for q0, qw in qblocks(plen):
             q = queries[q0 : q0 + qw]
             ga = grads[q0 : q0 + qw]
             st = mask_keys(nt(k, q), vlen)
-            p = jnp.exp2(st * SCALE2 - l_ref[0, :, at : at + qw])
+            pr = jnp.exp2(st * SCALE2 - lse[p, :, at : at + qw])
             gp = nt(v, ga)
-            dv += nn(p.astype(BF), ga)
-            pg = p * gp
-            ds = (pg - p * jnp.sum(pg, axis=0, keepdims=True)).astype(BF)
+            dv += nn(pr.astype(BF), ga)
+            pg = pr * gp
+            ds = (pg - pr * jnp.sum(pg, axis=0, keepdims=True)).astype(BF)
             dk += nn(ds, q)
             dq_tmp[q0 : q0 + qw] = nn(kt, ds).T
             at += 256
         dq = (one_each(dq_tmp, plen) * SCALE).astype(BF)
-        dkb = (dk * SCALE).astype(BF)
         dvb = dv.astype(BF)
-        d_ref[0, rows] = dq
-        d_ref[1, rows] = dkb
-        d_ref[2, rows] = dvb
-        sums[0] += rowsum(dq)
-        sums[2] += rowsum(dvb)
-    s_ref[...] = jnp.concatenate(sums + [jnp.zeros((5, 128), F32)], axis=0)
-
-
-def attn_bwd(qkv, ga, lse, chunk):
-    nimg, plen, vlen = chunk
-    _, n, d = qkv.shape
-    pairs = d // 128
-    return pl.pallas_call(
-        functools.partial(attn_bwd_kernel, nimg=nimg, plen=plen, vlen=vlen),
-        grid=(pairs,),
-        in_specs=[pl.BlockSpec((1, n, 128), lambda p, s=s: (s, 0, p)) for s in range(3)]
+        dqkv[0, rows, cols] = dq
+        dqkv[1, rows, cols] = (dk * SCALE).astype(BF)
+        dqkv[2, rows, cols] = dvb
+        total_q += rowsum(dq)
+        total_v += rowsum(dvb)
+    sums[:, cols] = jnp.concatenate(
+        [total_q, jnp.zeros_like(total_q), total_v, jnp.zeros((5, 128), F32)], axis=0
+    )
+
+
+def bwd_kernel(*refs, chunk):
+    g_ref, g2, g1 = refs[:3]
+    mid_h, dg_h, qkv_h, lse_h, x_h = refs[3:8]
+    weights, outs = refs[8:16], refs[16:21]
+    sums2, sff, sums_qkv, sums1 = refs[21:25]
+    wq, pw, up, dn = refs[25:29]
+    mid, dg, qkv, lse, x, pre, gb, dqkv, gx, gm, ga, acc, dq_tmp, in_sem, late_sem, out_sem, ff_sem = refs[29:]
+    ff = dn.shape[0]
+    fb = ff // FF_STEPS
+    loads = weight_loads(weights, wq, pw, up, dn)
+    names = ("proj", "qkv")
+    loads = {k: fetch(loads[k], in_sem.at[i]) for i, k in enumerate(names)}
+    late = fetch([(mid_h, mid), (qkv_h, qkv), (lse_h, lse), (x_h, x)], late_sem)
+    saves = fetch(list(zip((pre, gb, dqkv, gx, g_ref), outs)), out_sem)
+
+    def block_loads(j):
+        if isinstance(j, int):
+            owner, first = divmod(j * fb, ff // 2)
+            rows = slice(first, first + fb)
+            cols = slice(j * fb, (j + 1) * fb)
+        else:
+            owner, rows, cols = 0, slice(0, fb), lanes(j, fb)
+        pairs = [
+            (weights[6 + owner].at[rows], dn.at[cols]),
+            (dg_h.at[:, cols], dg.at[:, cols]),
+            (weights[4 + owner].at[:, rows], up.at[:, cols]),
+        ]
+        return fetch(pairs, ff_sem.at[j])
+
+    for j in range(FF_STEPS):
+        for c in block_loads(j):
+            c.start()
+    saves[4].start()
+    for c in late:
+        c.start()
+    for k in ("proj", "qkv"):
+        for c in loads[k]:
+            c.start()
+    acc[...] = jnp.zeros_like(acc)
+
+    def mlp(j, carry):
+        cols = lanes(j, fb)
+        for c in block_loads(j):
+            c.wait()
+        value = (nt(g_ref[...], dn[cols]) * dg[:, cols].astype(F32)).astype(BF)
+        pre[:, cols] = value
+        sff[:, cols] = rowsum(value)
+        acc[...] += nt(value, up[:, cols])
+        return carry
+
+    lax.fori_loop(0, FF_STEPS, mlp, 0)
+    saves[0].start()
+    late[0].wait()
+    gn = acc[...]
+    xhat, rstd = norm_parts(mid[...])
+    grad = norm_back(xhat, rstd, gn, g2[...]) + g_ref[...].astype(F32)
+    gm[...] = grad
+    branch = grad.astype(BF)
+    gb[...] = branch
+    saves[1].start()
+    sums2[...] = jnp.concatenate(
+        [rowsum(gn * xhat), rowsum(gn), rowsum(branch), rowsum(g_ref[...])]
+        + [jnp.zeros((4, gn.shape[1]), F32)], axis=0
+    )
+    for c in loads["proj"]:
+        c.wait()
+    ga[...] = nt(gb[...], pw[...]).astype(BF)
+    late[1].wait()
+    late[2].wait()
+
+    def attend(p, carry):
+        attn_bwd_pair(p, qkv, ga, lse, dqkv, sums_qkv, dq_tmp, chunk)
+        return carry
+
+    lax.fori_loop(0, lse.shape[0], attend, 0)
+    saves[2].start()
+    for c in loads["qkv"]:
+        c.wait()
+    late[3].wait()
+    acc[...] = nt(dqkv[0], wq[0])
+
+    def project(s, carry):
+        acc[...] += nt(dqkv[s], wq[s])
+        return carry
+
+    lax.fori_loop(1, 3, project, 0)
+    gn = acc[...]
+    xhat, rstd = norm_parts(x[...].astype(F32))
+    gx[...] = (norm_back(xhat, rstd, gn, g1[...]) + gm[...]).astype(BF)
+    saves[3].start()
+    sums1[...] = jnp.concatenate(
+        [rowsum(gn * xhat), rowsum(gn), jnp.zeros((6, gn.shape[1]), F32)], axis=0
+    )
+    for c in saves:
+        c.wait()
+
+
+def backward(g, x, kept, w, chunk):
+    n, d = g.shape
+    ff = kept["act"].shape[1]
+    vmem = pl.BlockSpec(memory_space=pltpu.VMEM)
+    hbm = pl.BlockSpec(memory_space=pl.ANY)
+    wide, tall = ((n, d), BF), ((n, ff), BF)
+    three, flat = ((3, n, d), BF), ((n, d), F32)
+    lse = (kept["lse"].shape, F32)
+    dma = pltpu.SemaphoreType.DMA
+    pre, gb, dqkv, gx, copy, sums2, sff, sums_qkv, sums1 = pl.pallas_call(
+        functools.partial(bwd_kernel, chunk=chunk),
+        in_specs=[vmem] * 3 + [hbm] * 13,
+        out_specs=[hbm] * 5 + [vmem] * 4,
+        out_shape=[sds(*k) for k in (tall, wide, three, wide, wide)]
+        + [sds((8, d), F32), sds((1, ff), F32), sds((8, d), F32), sds((8, d), F32)],
+        scratch_shapes=weight_scratch(d, ff)
         + [
-            pl.BlockSpec((n, 128), lambda p: (0, p)),
-            pl.BlockSpec((1, 1, lse_width(chunk)), lambda p: (p, 0, 0)),
-        ],
-        out_specs=[
-            pl.BlockSpec((3, n, 128), lambda p: (0, 0, p)),
-            pl.BlockSpec((8, 128), lambda p: (0, p)),
-        ],
-        out_shape=[sds((3, n, d), BF), sds((8, d), F32)],
-        scratch_shapes=[pltpu.VMEM((2 * plen, 128), F32)],
+            pltpu.VMEM(*k)
+            for k in (flat, tall, three, lse, wide, tall, wide, three, wide, flat, wide, flat)
+        ]
+        + [pltpu.VMEM((2 * chunk[1], 128), F32), dma((2, 2)), dma((4,)), dma((5,)), dma((FF_STEPS, 3))],
         compiler_params=params(),
-        name="attn_bwd",
-    )(qkv, qkv, qkv, ga, lse)
-
-
-def pre_bwd_kernel(d_ref, wo_ref, wp_ref, x_ref, gain_ref, gm_ref, out_ref, sums_ref, acc_ref):
+        name="bwd",
+    )(
+        g, w["g2"], w["g1"], kept["mid"], kept["dg"], kept["qkv"], kept["lse"], x, *weights_of(w)
+    )
+    return (copy, pre, gb, dqkv, sums2, sff, sums_qkv, sums1, gx)
+
+
+def wgrad_mlp_kernel(act, n2, pre, g, *refs, more):
+    init, outs = refs[:more], refs[more:]
     j = pl.program_id(0)
-    weight = jnp.concatenate([wo_ref[0], wp_ref[0]], axis=1)
-    part = nt(d_ref[0], weight)
-
-    @pl.when(j == 0)
-    def _():
-        acc_ref[...] = part
-
-    @pl.when(j > 0)
-    def _():
-        acc_ref[...] += part
-
-    @pl.when(j == pl.num_programs(0) - 1)
-    def _():
-        gn = acc_ref[...]
-        xhat, rstd = norm_parts(x_ref[...].astype(F32))
-        out_ref[...] = (norm_back(xhat, rstd, gn, gain_ref[...]) + gm_ref[...]).astype(BF)
-        sums_ref[...] = jnp.concatenate(
-            [rowsum(gn * xhat), rowsum(gn), jnp.zeros((6, gn.shape[1]), F32)], axis=0
-        )
-
-
-def pre_bwd(dqkv, x, gm, w):
-    _, n, d = dqkv.shape
-    half = w["wqkv_o"].shape[-1]
-    return pl.pallas_call(
-        pre_bwd_kernel,
-        grid=(3,),
-        in_specs=[
-            pl.BlockSpec((1, n, d), lambda s: (s, 0, 0)),
-            pl.BlockSpec((1, d, half), lambda s: (s, 0, 0)),
-            pl.BlockSpec((1, d, half), lambda s: (s, 0, 0)),
-            whole((n, d)), whole((1, d)), whole((n, d)),
-        ],
-        out_specs=[whole((n, d)), whole((8, d))],
-        out_shape=[sds((n, d), BF), sds((8, d), F32)],
-        scratch_shapes=[pltpu.VMEM((n, d), F32)],
-        compiler_params=params(),
-        name="pre_bwd",
-    )(dqkv, w["wqkv_o"], w["wqkv_p"], x, w["g1"], gm)
-
-
-def backward(g, x, kept, w, chunk):
-    pre_o, pre_p, gm, gb, ga, sums2, so, sp, copy = post_bwd(g, kept, w)
-    dqkv, sums_qkv = attn_bwd(kept["qkv"], ga, kept["lse"], chunk)
-    gx, sums1 = pre_bwd(dqkv, x, gm, w)
-    return (copy, pre_o, pre_p, gb, dqkv, sums2, so, sp, sums_qkv, sums1, gx)
-
-
-def wgrad_mlp_kernel(*refs, more):
-    ao, ap, n2, po, pp, g = refs[:6]
-    init = refs[6 : 6 + more]
-    outs = refs[6 + more :]
-    g, n2 = g[...], n2[...]
-    results = (
-        tn(ao[...], g), tn(ap[...], g), tn(n2, po[...]), tn(n2, pp[...]),
-    )
-    for i, (out, value) in enumerate(zip(outs, results)):
-        if more:
-            value += init[i][...].astype(F32)
-        out[...] = value.astype(BF)
+    down, up = tn(act[...], g[...]), tn(n2[...], pre[...])
+    for i in range(2):
+
+        @pl.when(j // (WGRAD_STEPS // 2) == i)
+        def _():
+            for at, value in ((i, down), (2 + i, up)):
+                if more:
+                    value = value + init[at][...].astype(F32)
+                outs[at][...] = value.astype(BF)
 
 
 def wgrad_mlp(kept, back, init=()):
     n, d = back["g"].shape
-    fh = kept["act_o"].shape[1]
-    fb = fh // 4
-    cols = lambda rows: pl.BlockSpec((rows, fb), lambda j: (0, j))
-    rows_ = pl.BlockSpec((fb, d), lambda j: (j, 0))
-    outs = [rows_, rows_, cols(d), cols(d)]
+    ff = kept["act"].shape[1]
+    fb, last = ff // WGRAD_STEPS, WGRAD_STEPS // 2 - 1
+    cols = pl.BlockSpec((n, fb), lambda j: (0, j))
+    at = [lambda j: jnp.minimum(j, last), lambda j: jnp.maximum(j - last - 1, 0)]
+    outs = [pl.BlockSpec((fb, d), lambda j, i=i: (at[i](j), 0)) for i in range(2)]
+    outs += [pl.BlockSpec((d, fb), lambda j, i=i: (0, at[i](j))) for i in range(2)]
     return pl.pallas_call(
         functools.partial(wgrad_mlp_kernel, more=len(init)),
-        grid=(4,),
-        in_specs=[cols(n), cols(n), whole((n, d)), cols(n), cols(n), whole((n, d))]
-        + outs[: len(init)],
+        grid=(WGRAD_STEPS,),
+        in_specs=[cols, whole((n, d)), cols, whole((n, d))] + outs[: len(init)],
         out_specs=outs,
-        out_shape=[sds((fh, d), BF)] * 2 + [sds((d, fh), BF)] * 2,
+        out_shape=[sds((ff // 2, d), BF)] * 2 + [sds((d, ff // 2), BF)] * 2,
         compiler_params=params(),
         name="wgrad_mlp",
-    )(kept["act_o"], kept["act_p"], kept["n2"], back["pre_o"], back["pre_p"], back["g"], *init)
+    )(kept["act"], kept["n2"], back["pre"], back["g"], *init)
 
 
 def wgrad_attn_kernel(*refs, more):
@@ -501,15 +506,15 @@
 
 
 def items_of(d):
-    return ((0, 0, 2 * d, 1), (2, 0, 2 * d, 1), (1, 0, d, -1), (2, 2 * d, d, -1), (3, 0, d // 2, -1))
+    return ((0, 0, 2 * d, 1), (1, 0, d, -1), (2, 2 * d, d, -1), (2, 0, 2 * d, 1), (3, 0, d // 2, -1))
 
 
 def vector_block(sums):
-    s1, s2, sq, so, sp = sums
+    s1, s2, sq, ff = sums
     d = s1.shape[1]
     wide = lambda v: [v[:, i : i + d] for i in range(0, v.shape[1], d)]
-    rows = [s1[:2], s2[:4], sq[0:1], sq[2:3]] + wide(so) + wide(sp)
-    used = 8 + 2 * (so.shape[1] // d)
+    rows = [s1[:2], s2[:4], sq[0:1], sq[2:3]] + wide(ff)
+    used = 8 + ff.shape[1] // d
     return jnp.concatenate(rows + [jnp.zeros((VEC_ROWS - used, d), F32)], axis=0)
 
 
@@ -527,8 +532,8 @@
 
 def ring_kernel(*refs, n, items, fold):
     owns, gifts = refs[:n], refs[n : 2 * n]
-    sums = refs[2 * n : 2 * n + 10]
-    at = 2 * n + 10
+    sums = refs[2 * n : 2 * n + 8]
+    at = 2 * n + 8
     outs, vsum_ref = refs[at : at + n], refs[at + n]
     at += n + 1
     theirs = refs[at : at + n]
@@ -603,7 +608,7 @@
     for step in range(2):
         for a in range(m):
             exchange(a, step).start()
-    vbuf[...] = vector_block([sums[i][...] + sums[5 + i][...] for i in range(5)])
+    vbuf[...] = vector_block([sums[i][...] + sums[4 + i][...] for i in range(4)])
     vexchange.start()
     for a in range(m):
         slots[a][0] = mine(a, 0).astype(BF)
@@ -667,8 +672,8 @@
     dma = pltpu.SemaphoreType.DMA
     vec = pltpu.VMEM((VEC_ROWS, d), F32)
     out = pl.pallas_call(
-        functools.partial(ring_kernel, n=n, items=items, fold=sums_s[3].shape[1] // d),
-        in_specs=[vmem] * (2 * n + 10),
+        functools.partial(ring_kernel, n=n, items=items, fold=sums_s[3].shape[1] // (2 * d)),
+        in_specs=[vmem] * (2 * n + 8),
         out_specs=[vmem] * (n + 1),
         out_shape=[sds(a.shape, BF) for a in owns] + [sds((VEC_ROWS, d), F32)],
         scratch_shapes=[pltpu.VMEM(a.shape, BF) for a in owns]
@@ -688,7 +693,7 @@
     if lax.axis_size("dp") == RING:
         return ring(owns, gifts, sums_s, sums_l)
     other = lambda array: lax.ppermute(array, "tensor", [(0, 1), (1, 0)])
-    fold = sums_s[3].shape[1] // owns[0].shape[1]
+    fold = sums_s[3].shape[1] // (2 * owns[0].shape[1])
     block = vector_block([a + b for a, b in zip(sums_s, sums_l)])
     summed = [lax.psum(a + other(b), "dp") for a, b in zip(owns, gifts)]
     return summed, lax.psum(block + as_own(other(block), fold), "dp")
@@ -829,8 +834,8 @@
     )
 
 
-KEPT = ("normed", "qkv", "att", "lse", "mid", "n2", "act_o", "act_p", "dg_o", "dg_p", "out")
-BACK = ("g", "pre_o", "pre_p", "gb", "dqkv", "sums2", "so", "sp", "sums_qkv", "sums1", "gx")
+KEPT = ("normed", "qkv", "att", "lse", "mid", "n2", "act", "dg", "out")
+BACK = ("g", "pre", "gb", "dqkv", "sums2", "sff", "sums_qkv", "sums1", "gx")
 
 
 def after(value, *earlier):
@@ -849,6 +854,8 @@
     other = lambda array: lax.ppermute(array, "tensor", both)
 
     wqkv, pw, up, dn = qkv_weight[0], proj_weight[0], up_weight[0], down_weight[0]
+    meta = jnp.concatenate([lane[None], large_place])
+    xs = cut(patches, meta)
     w = {
         "g1": norm1_gain, "b1": norm1_bias, "g2": norm2_gain, "b2": norm2_bias,
         "pb": proj_bias, "db": down_bias,
@@ -858,34 +865,31 @@
     }
 
 
-    meta = jnp.concatenate([lane[None], large_place])
     large, smalls = 0, 1
-    xs = cut(patches, meta)
     gs = cut(out_grad, meta)
 
-    def fwd(c, on, x, otherwise=None):
-        like = jax.eval_shape(functools.partial(forward, chunk=CHUNKS[c]), x, w)
+    def pick(on, make, otherwise=None):
+        like = jax.eval_shape(make)
         return lax.cond(
             section == on,
-            lambda: tuple(forward(x, w, CHUNKS[c])),
+            lambda: tuple(make()),
             lambda: blank(like) if otherwise is None else tuple(otherwise),
         )
 
+    def fwd(c, on, x, otherwise=None):
+        return pick(on, lambda: forward(x, w, CHUNKS[c]), otherwise)
+
     def bwd(c, on, g, x, kept, otherwise=None):
         kept = dict(zip(KEPT, kept))
-        like = jax.eval_shape(functools.partial(backward, chunk=CHUNKS[c]), g, x, kept, w)
-        return lax.cond(
-            section == on,
-            lambda: tuple(backward(g, x, kept, w, CHUNKS[c])),
-            lambda: blank(like) if otherwise is None else tuple(otherwise),
-        )
+        return pick(on, lambda: backward(g, x, kept, w, CHUNKS[c]), otherwise)
 
     down = lambda array: lax.ppermute(array, "section", [(0, 1)])
     up_ = lambda array: lax.ppermute(array, "section", [(1, 0)])
 
     kept_s = fwd(smalls, 0, xs[smalls])
     in_s = down(kept_s[-1])
-    kept_l = fwd(large, 0, after(xs[large], kept_s[-1]))
+    x_l = after(xs[large], kept_s[-1])
+    kept_l = fwd(large, 0, x_l)
     in_l = down(kept_l[-1])
     in_s = after(in_s, kept_l[-1])
     kept_s = fwd(smalls, 1, in_s, kept_s)
@@ -909,7 +913,7 @@
     input_grads = join(grads, [other(a) for a in grads], meta)
 
     rows = lambda qkv: qkv.reshape(3 * d, half)
-    sums = lambda back: [named(BACK, back)[k] for k in ("sums1", "sums2", "sums_qkv", "so", "sp")]
+    sums = lambda back: [named(BACK, back)[k] for k in ("sums1", "sums2", "sums_qkv", "sff")]
     summed, vec = dp_sum(
         [dn_o, up_o, rows(qkv_o), pw_o], [dn_p, up_p, rows(qkv_p), pw_p], sums(back_s), sums(back_l)
     )

time: 496 us -> 461 us (0.929)
  Pallas kernels: 381 us -> 358 us
  waiting for transfers between devices: 79.6 us -> 67.1 us
    pallas_call x12 -> x4, Pallas kernels: 148 us -> 123 us  [the longest x2 67.5 us: backward(): pl.pallas_call(functools.partial(bwd_kernel, chunk=chunk), in_specs=[vmem...]
    ppermute x2, waiting for transfers between devices: 63.5 us -> 51.1 us  [body(): up_ = lambda array: lax.ppermute(array, 'section', [(1, 0)])]
  transfers between devices with their start and end apart: 14 -> 14, of which waited for: 4 -> 4; matrix products, arithmetic and copies ran while one was open for 0% -> 0% of each run, Pallas kernels for 71% -> 72%
where the time goes in v4:
time: 461 us; the launch traced here: 454 us
  Pallas kernels  358 us (78%)
  waiting for transfers between devices  67.1 us (15%)
  loops' own time  16 us (3%)
  starting transfers between devices  9.46 us (2%)
    pallas_call x1, Pallas kernels, ring(): pl.pallas_call(functools.partial(ring_kernel, n=n, items=items, fold=sums...  159 us
    pallas_call x2, Pallas kernels, backward(): pl.pallas_call(functools.partial(bwd_kernel, chunk=chunk), in_specs=[vmem...  67.5 us
    pallas_call x2, Pallas kernels, forward(): pl.pallas_call(functools.partial(fwd_kernel, chunk=chunk), in_specs=[vmem...  55.6 us
    ppermute x2, waiting for transfers between devices, body(): up_ = lambda array: lax.ppermute(array, 'section', [(1, 0)])  51.1 us
    pallas_call x2, Pallas kernels, wgrad_mlp(): pl.pallas_call(functools.partial(wgrad_mlp_kernel, more=len(init)), grid=...  28.3 us
    pallas_call x2, Pallas kernels, wgrad_attn(): pl.pallas_call(functools.partial(wgrad_attn_kernel, more=len(init)), grid...  17.6 us
    another operation x8, loops' own time, pick(): lax.cond(section == on, lambda: tuple(make()), lambda: blank(like) if oth...  16 us
    pallas_call x2, Pallas kernels, join(): pl.pallas_call(join_kernel, grid_spec=pltpu.PrefetchScalarGridSpec(num_sc...  11.3 us
  transfers between devices with their start and end apart: 14, of which 4 were waited for; matrix products, arithmetic and copies ran while one was open for 0% of the time, Pallas kernels for 72%

profile of v4, /device:TPU:0, one launch (start us, length us, event | category | flops | bytes accessed | tf_op | source)
XLA Modules:
  0.0 453.9 jit_solution(10728302268550814469)
XLA Ops:
  0.7 0.6 collective-permute-start.4
  1.3 0.4 collective-permute-start.2
  2.3 10.2 %collective-permute-done = f32[2,384]{1,0:T(2,128)} collective-permute-done((f32[2,384]{1,0:T(2,128)}, f32[2,384]{1,0:T(2,128)}, u32[]{:S(2)}, u32[]{:S(2)}) %collective-permute-start) | collective-permute-done | bytes 3104 | tf_op jit(solution)/shard_map/ppermute | solution.py:854
  12.9 1.2 pad_add_fusion.meta_ref
  14.1 4.5 cut.2
  18.7 24.8 %conditional.8 = ((bf16[624,768]{1,0:T(8,128)(2,1)}, bf16[3,624,768]{2,1,0:T(8,128)(2,1)}, bf16[624,768]{1,0:T(8,128)(2,1)}, f32[6,1,1536]{2,1,0:T(1,128)}, f32[...) conditional(s32[]{:T(128)} %convert_element_type.5, () %tuple.62, ...), branch_computations={%region_0.0_spmd, %region_1.0_spmd} | conditional | bytes 8 | solution.py:873
  18.7 24.8 %fwd.4 = (bf16[624,768]{1,0:T(8,128)(2,1)}, bf16[3,624,768]{2,1,0:T(8,128)(2,1)}, bf16[624,768]{1,0:T(8,128)(2,1)}, f32[6,1,1536]{2,1,0:T(1,128)}, f32[624,768]{...) custom-call(bf16[624,768]{1,0:T(8,128)(2,1)} %get-tuple-element.352., ...), custom_call_target="tpu_custom_call" | custom-call | tf_op jit(solution)/shard_map/cond/branch_1_fun/fwd/pallas_call | solution.py:246
  43.6 2.2 collective-permute-start.7
  45.8 30.9 %conditional.9 = ((bf16[592,768]{1,0:T(8,128)(2,1)}, bf16[3,592,768]{2,1,0:T(8,128)(2,1)}, bf16[592,768]{1,0:T(8,128)(2,1)}, f32[6,1,1280]{2,1,0:T(1,128)}, f32[...) conditional(s32[]{:T(128)} %convert_element_type.5, () %tuple.61, ...), branch_computations={%region_2.0_spmd, %region_3.0_spmd} | conditional | bytes 8 | solution.py:873
  46.0 30.7 %fwd.5 = (bf16[592,768]{1,0:T(8,128)(2,1)}, bf16[3,592,768]{2,1,0:T(8,128)(2,1)}, bf16[592,768]{1,0:T(8,128)(2,1)}, f32[6,1,1280]{2,1,0:T(1,128)}, f32[592,768]{...) custom-call(bf16[592,768]{1,0:T(8,128)(2,1)} %get-tuple-element.371., ...), custom_call_target="tpu_custom_call" | custom-call | tf_op jit(solution)/shard_map/cond/branch_1_fun/fwd/pallas_call | solution.py:246
  76.8 2.3 collective-permute-start.6
  79.0 4.5 cut.3
  83.8 7.3 %conditional.11 = ((bf16[624,768]{1,0:T(8,128)(2,1)}, bf16[624,3072]{1,0:T(8,128)(2,1)}, bf16[624,768]{1,0:T(8,128)(2,1)}, bf16[3,624,768]{2,1,0:T(8,128)(2,1)},...) conditional(s32[]{:T(128)} %convert_element_type.4, () %tuple.66, ...), branch_computations={%region_6.0_spmd, %region_7.0_spmd} | conditional | bytes 80 | solution.py:873
  91.1 1.3 collective-permute-start.11
  92.6 5.8 %collective-permute-done.6 = bf16[592,768]{1,0:T(8,128)(2,1)} collective-permute-done((bf16[592,768]{1,0:T(8,128)(2,1)}, bf16[592,768]{1,0:T(8,128)(2,1)}, u32[]{:S(2)}, u32[]{:S(2)}) %collective-permute-start.6) | collective-permute-done | bytes 909344 | tf_op jit(solution)/shard_map/ppermute | solution.py:886
  98.6 7.3 %conditional.13 = ((bf16[592,768]{1,0:T(8,128)(2,1)}, bf16[592,3072]{1,0:T(8,128)(2,1)}, bf16[592,768]{1,0:T(8,128)(2,1)}, bf16[3,592,768]{2,1,0:T(8,128)(2,1)},...) conditional(s32[]{:T(128)} %convert_element_type.4, () %tuple.72, ...), branch_computations={%region_10.0_spmd, %region_11.0_spmd} | conditional | bytes 80 | solution.py:873
  105.9 1.3 collective-permute-start.10
  107.2 40.8 %collective-permute-done.11 = bf16[624,768]{1,0:T(8,128)(2,1)} collective-permute-done((bf16[624,768]{1,0:T(8,128)(2,1)}, bf16[624,768]{1,0:T(8,128)(2,1)}, u32[]{:S(2)}, u32[]{:S(2)}) %collective-permute-start.11) | collective-permute-done | bytes 958496 | tf_op jit(solution)/shard_map/ppermute | solution.py:887
  148.1 31.6 %conditional.14 = ((bf16[624,768]{1,0:T(8,128)(2,1)}, bf16[624,3072]{1,0:T(8,128)(2,1)}, bf16[624,768]{1,0:T(8,128)(2,1)}, bf16[3,624,768]{2,1,0:T(8,128)(2,1)},...) conditional(s32[]{:T(128)} %convert_element_type.5, ...), branch_computations={%region_12.0_spmd, %region_13.0_spmd} | conditional | bytes 80 | solution.py:873
  148.4 31.2 %bwd.6 = (bf16[624,3072]{1,0:T(8,128)(2,1)}, bf16[624,768]{1,0:T(8,128)(2,1)}, bf16[3,624,768]{2,1,0:T(8,128)(2,1)}, bf16[624,768]{1,0:T(8,128)(2,1)}, bf16[624,...) custom-call(bf16[624,768]{1,0:T(8,128)(2,1)} %get-tuple-element.478.refs_0_,, ...), custom_call_target="tpu_custom_call" | custom-call | tf_op jit(solution)/shard_map/cond/branch_1_fun/bwd/pallas_call | solution.py:410
  179.8 8.4 %wgrad_attn.2 = (bf16[3,768,384]{2,1,0:T(8,128)(2,1)}, bf16[3,768,384]{2,1,0:T(8,128)(2,1)}, bf16[384,768]{1,0:T(8,128)(2,1)}, bf16[384,768]{1,0:T(8,128)(2,1)}) custom-call(bf16[624,768]{1,0:T(8,128)(2,1)} %get-tuple-element.654.refs_0_, bf16[3,624,768]{2,1,0:T(8,128)(2,1)} %get-tuple-element.655.refs_1_, bf16[624,768]{1,0:T(8,128)(2,1)} %get-tuple-element.656.refs_2_, ...), custom_call_target="tpu_custom_call" | custom-call | tf_op jit(solution)/shard_map/wgrad_attn/pallas_call | solution.py:489
  188.2 13.4 %wgrad_mlp.2 = (bf16[1536,768]{1,0:T(8,128)(2,1)}, bf16[1536,768]{1,0:T(8,128)(2,1)}, bf16[768,1536]{1,0:T(8,128)(2,1)}, bf16[768,1536]{1,0:T(8,128)(2,1)}) custom-call(bf16[624,3072]{1,0:T(8,128)(2,1)S(1)} %copy-done.2, bf16[624,768]{1,0:T(8,128)(2,1)} %get-tuple-element.646.n2, bf16[624,3072]{1,0:T(8,128)(2,1)} %get-tuple-element.648.pre, ...), custom_call_target="tpu_custom_call" | custom-call | tf_op jit(solution)/shard_map/wgrad_mlp/pallas_call | solution.py:452
  201.6 5.9 %join.2 = bf16[2336,768]{1,0:T(8,128)(2,1)} custom-call(s32[3]{0:T(128)} %pad_add_fusion.meta_ref, bf16[592,768]{1,0:T(8,128)(2,1)S(1)} %copy-done.8, bf16[624,768]{1,0:T(8,128)(2,1)} %get-tuple-element.638.refs_1_, bf16[592,768]{1,0:T(8,128)(2,1)} %collective-permute-done.8.refs_2_, bf16[624,768]{1,0:T(8,128)(2,1)} %collective-permute-done.9.refs_3_), custom_call_target="tpu_custom_call" | custom-call | tf_op jit(solution)/shard_map/join/pallas_call | solution.py:806
  207.5 10.3 %collective-permute-done.10 = bf16[592,768]{1,0:T(8,128)(2,1)} collective-permute-done((bf16[592,768]{1,0:T(8,128)(2,1)}, bf16[592,768]{1,0:T(8,128)(2,1)}, u32[]{:S(2)}, u32[]{:S(2)}) %collective-permute-start.10) | collective-permute-done | bytes 909344 | tf_op jit(solution)/shard_map/ppermute | solution.py:887
  217.8 36.6 %conditional.15 = ((bf16[592,768]{1,0:T(8,128)(2,1)}, bf16[592,3072]{1,0:T(8,128)(2,1)}, bf16[592,768]{1,0:T(8,128)(2,1)}, bf16[3,592,768]{2,1,0:T(8,128)(2,1)},...) conditional(s32[]{:T(128)} %convert_element_type.5, ...), branch_computations={%region_14.0_spmd, %region_15.0_spmd} | conditional | bytes 80 | solution.py:873
  217.9 36.3 %bwd.7 = (bf16[592,3072]{1,0:T(8,128)(2,1)}, bf16[592,768]{1,0:T(8,128)(2,1)}, bf16[3,592,768]{2,1,0:T(8,128)(2,1)}, bf16[592,768]{1,0:T(8,128)(2,1)}, bf16[592,...) custom-call(bf16[592,768]{1,0:T(8,128)(2,1)} %get-tuple-element.503.refs_0_,, ...), custom_call_target="tpu_custom_call" | custom-call | tf_op jit(solution)/shard_map/cond/branch_1_fun/bwd/pallas_call | solution.py:410
  254.5 9.2 %wgrad_attn.3 = (bf16[3,768,384]{2,1,0:T(8,128)(2,1)}, bf16[3,768,384]{2,1,0:T(8,128)(2,1)}, bf16[384,768]{1,0:T(8,128)(2,1)}, bf16[384,768]{1,0:T(8,128)(2,1)}) custom-call(bf16[592,768]{1,0:T(8,128)(2,1)} %get-tuple-element.671.refs_0_, bf16[3,592,768]{2,1,0:T(8,128)(2,1)} %get-tuple-element.672.refs_1_, bf16[592,768]{1,0:T(8,128)(2,1)} %get-tuple-element.673.refs_2_, ...), custom_call_target="tpu_custom_call" | custom-call | tf_op jit(solution)/shard_map/wgrad_attn/pallas_call | solution.py:489
  263.9 14.9 %wgrad_mlp.3 = (bf16[1536,768]{1,0:T(8,128)(2,1)}, bf16[1536,768]{1,0:T(8,128)(2,1)}, bf16[768,1536]{1,0:T(8,128)(2,1)}, bf16[768,1536]{1,0:T(8,128)(2,1)}) custom-call(bf16[592,3072]{1,0:T(8,128)(2,1)S(1)} %copy-done.3, bf16[592,768]{1,0:T(8,128)(2,1)S(1)} %copy-done.5, bf16[592,3072]{1,0:T(8,128)(2,1)} %get-tuple-element.667.pre, ...), custom_call_target="tpu_custom_call" | custom-call | tf_op jit(solution)/shard_map/wgrad_mlp/pallas_call | solution.py:452
  278.9 159.0 %ring.1 = (bf16[1536,768]{1,0:T(8,128)(2,1)}, bf16[768,1536]{1,0:T(8,128)(2,1)}, bf16[2304,384]{1,0:T(8,128)(2,1)}, bf16[384,768]{1,0:T(8,128)(2,1)}, f32[16,768]{1,0:T(8,128)}) custom-call(bf16[1536,768]{1,0:T(8,128)(2,1)} %get-tuple-element.669.refs_0_, bf16[768,1536]{1,0:T(8,128)(2,1)} %get-tuple-element.670.refs_1_, bf16[2304,384]{1,0:T(8,128)(2,1)} %bitcast.49, ...), custom_call_target="tpu_custom_call" | custom-call | tf_op jit(solution)/shard_map/ring/pallas_call | solution.py:674
  437.9 9.4 %finish.1 = (f32[1,1536,768]{2,1,0:T(8,128)}, f32[1,768,1536]{2,1,0:T(8,128)}, f32[1,2304,384]{2,1,0:T(8,128)}, f32[1,384,768]{2,1,0:T(8,128)}, f32[1,768]{1,0:T...) custom-call(bf16[1536,768]{1,0:T(8,128)(2,1)} %get-tuple-element.689, ...), custom_call_target="tpu_custom_call" | custom-call | tf_op jit(solution)/shard_map/finish/pallas_call | solution.py:723
  447.4 0.9 copy-done.7
  448.3 5.4 %join.3 = bf16[2336,768]{1,0:T(8,128)(2,1)} custom-call(s32[3]{0:T(128)} %pad_add_fusion.meta_ref, bf16[592,768]{1,0:T(8,128)(2,1)S(1)} %copy-done.9, bf16[624,768]{1,0:T(8,128)(2,1)S(1)} %copy-done.4, bf16[592,768]{1,0:T(8,128)(2,1)} %copy-done.7, bf16[624,768]{1,0:T(8,128)(2,1)} %collective-permute-done.13.refs_3_), custom_call_target="tpu_custom_call" | custom-call | tf_op jit(solution)/shard_map/join/pallas_call | solution.py:806
  (63 shorter events, 1.9 us)
Async XLA Ops:
  0.6 18.0 %copy-start = (bf16[1,768,1536]{2,1,0:T(8,128)(2,1)S(1)}, bf16[1,768,1536]{2,1,0:T(8,128)(2,1)}, u32[]{:S(2)}) copy-start(bf16[1,768,1536]{2,1,0:T(8,128)(2,1)} %param.42) | copy-start | bytes 7077892
  0.7 18.0 %copy-start.1 = (bf16[1,384,768]{2,1,0:T(8,128)(2,1)S(1)}, bf16[1,384,768]{2,1,0:T(8,128)(2,1)}, u32[]{:S(2)}) copy-start(bf16[1,384,768]{2,1,0:T(8,128)(2,1)} %param.38) | copy-start | bytes 1769476
  0.7 18.0 %copy-start.12 = (f32[1,1536]{1,0:T(1,128)S(1)}, f32[1,1536]{1,0:T(1,128)}, u32[]{:S(2)}) copy-start(f32[1,1536]{1,0:T(1,128)} %param.43) | copy-start | bytes 18436
  0.7 18.0 %copy-start.10 = (f32[1,768]{1,0:T(1,128)S(1)}, f32[1,768]{1,0:T(1,128)}, u32[]{:S(2)}) copy-start(f32[1,768]{1,0:T(1,128)} %param.34) | copy-start | bytes 9220
  0.7 18.0 %copy-start.11 = (f32[1,768]{1,0:T(1,128)S(1)}, f32[1,768]{1,0:T(1,128)}, u32[]{:S(2)}) copy-start(f32[1,768]{1,0:T(1,128)} %param.40) | copy-start | bytes 9220
  0.7 18.0 %collective-permute-start.4 = (bf16[768,1536]{1,0:T(8,128)(2,1)}, bf16[768,1536]{1,0:T(8,128)(2,1)}, u32[]{:S(2)}, u32[]{:S(2)}) collective-permute-start(bf16[768,1536]{1,0:T(8,128)(2,1)} %bitcast.11), channel_id=1, source_target_pairs={{0,8},{8,0},{1,9},{9,1},{2,10},{10,2},{3,11},{11,3},{4,12},{12,4},... | collective-permute-start | bytes 7077896 | tf_op jit(solution)/shard_map/ppermute | solution.py:854
  1.3 17.4 %collective-permute-start.5 = (bf16[1536,768]{1,0:T(8,128)(2,1)}, bf16[1536,768]{1,0:T(8,128)(2,1)}, u32[]{:S(2)}, u32[]{:S(2)}) collective-permute-start(bf16[1536,768]{1,0:T(8,128)(2,1)} %bitcast.20), channel_id=1, source_target_pairs={{0,8},{8,0},{1,9},{9,1},{2,10},{10,2},{3,11},{11,3},{4,12},{12,4},... | collective-permute-start | bytes 7077896 | tf_op jit(solution)/shard_map/ppermute | solution.py:854
  1.3 17.3 %collective-permute-start.2 = (bf16[3,768,384]{2,1,0:T(8,128)(2,1)}, bf16[3,768,384]{2,1,0:T(8,128)(2,1)}, u32[]{:S(2)}, u32[]{:S(2)}) collective-permute-start(bf16[3,768,384]{2,1,0:T(8,128)(2,1)} %bitcast.29), channel_id=1, source_target_pairs={{0,8},{8,0},{1,9},{9,1},{2,10},{10,2},{3,11},{11,3},{4,12},{12,4},... | collective-permute-start | bytes 5308424 | tf_op jit(solution)/shard_map/ppermute | solution.py:854
  1.8 16.9 %collective-permute-start.3 = (bf16[384,768]{1,0:T(8,128)(2,1)}, bf16[384,768]{1,0:T(8,128)(2,1)S(1)}, u32[]{:S(2)}, u32[]{:S(2)}) collective-permute-start(bf16[384,768]{1,0:T(8,128)(2,1)} %bitcast.38), channel_id=1, source_target_pairs={{0,8},{8,0},{1,9},{9,1},{2,10},{10,2},{3,11},{11,3},{4,12},{12,4},... | collective-permute-start | bytes 1769480 | tf_op jit(solution)/shard_map/ppermute | solution.py:854
  1.8 10.7 %collective-permute-start = (f32[2,384]{1,0:T(2,128)}, f32[2,384]{1,0:T(2,128)}, u32[]{:S(2)}, u32[]{:S(2)}) collective-permute-start(f32[2,384]{1,0:T(2,128)} %bitcast.51), channel_id=1, source_target_pairs={{0,8},{8,0},{1,9},{9,1},{2,10},{10,2},{3,11},{11,3},{4,12},{12,4},... | collective-permute-start | bytes 9224 | tf_op jit(solution)/shard_map/ppermute | solution.py:854
  12.5 6.1 %collective-permute-start.1 = (f32[1,1536]{1,0:T(1,128)}, f32[1,1536]{1,0:T(1,128)}, u32[]{:S(2)}, u32[]{:S(2)}) collective-permute-start(f32[1,1536]{1,0:T(1,128)} %param.43), channel_id=1, source_target_pairs={{0,8},{8,0},{1,9},{9,1},{2,10},{10,2},{3,11},{11,3},{4,12},{12,4},... | collective-permute-start | bytes 18440 | tf_op jit(solution)/shard_map/ppermute | solution.py:854
  43.6 40.0 %collective-permute-start.7 = (bf16[624,768]{1,0:T(8,128)(2,1)}, bf16[624,768]{1,0:T(8,128)(2,1)}, u32[]{:S(2)}, u32[]{:S(2)}) collective-permute-start(bf16[624,768]{1,0:T(8,128)(2,1)} %get-tuple-element.626), channel_id=1, source_target_pairs={{0,16},{1,17},{2,18},{3,19},{4,20},{5,21},{6,22},{7,23},{8,24},{9,... | collective-permute-start | bytes 2875400 | tf_op jit(solution)/shard_map/ppermute | solution.py:886
  76.8 21.6 %collective-permute-start.6 = (bf16[592,768]{1,0:T(8,128)(2,1)}, bf16[592,768]{1,0:T(8,128)(2,1)}, u32[]{:S(2)}, u32[]{:S(2)}) collective-permute-start(bf16[592,768]{1,0:T(8,128)(2,1)} %get-tuple-element.628), channel_id=1, source_target_pairs={{0,16},{1,17},{2,18},{3,19},{4,20},{5,21},{6,22},{7,23},{8,24},{9,... | collective-permute-start | bytes 2727944 | tf_op jit(solution)/shard_map/ppermute | solution.py:886
  91.1 56.9 %collective-permute-start.11 = (bf16[624,768]{1,0:T(8,128)(2,1)}, bf16[624,768]{1,0:T(8,128)(2,1)}, u32[]{:S(2)}, u32[]{:S(2)}) collective-permute-start(bf16[624,768]{1,0:T(8,128)(2,1)} %get-tuple-element.635), channel_id=1, source_target_pairs={{16,0},{17,1},{18,2},{19,3},{20,4},{21,5},{22,6},{23,7},{24,8},{25... | collective-permute-start | bytes 2875400 | tf_op jit(solution)/shard_map/ppermute | solution.py:887
  92.4 109.2 %collective-permute-start.9 = (bf16[624,768]{1,0:T(8,128)(2,1)}, bf16[624,768]{1,0:T(8,128)(2,1)}, u32[]{:S(2)}, u32[]{:S(2)}) collective-permute-start(bf16[624,768]{1,0:T(8,128)(2,1)} %get-tuple-element.638.refs_1_), channel_id=1, source_target_pairs={{0,8},{8,0},{1,9},{9,1},{2,10},{10,2},{3,11},{11,3},{4,12},{12,4},... | collective-permute-start | bytes 2875400 | tf_op jit(solution)/shard_map/ppermute | solution.py:854
  98.6 103.0 %collective-permute-start.8 = (bf16[592,768]{1,0:T(8,128)(2,1)}, bf16[592,768]{1,0:T(8,128)(2,1)}, u32[]{:S(2)}, u32[]{:S(2)}) collective-permute-start(bf16[592,768]{1,0:T(8,128)(2,1)} %get-tuple-element.637.refs_0_), channel_id=1, source_target_pairs={{0,8},{8,0},{1,9},{9,1},{2,10},{10,2},{3,11},{11,3},{4,12},{12,4},... | collective-permute-start | bytes 2727944 | tf_op jit(solution)/shard_map/ppermute | solution.py:854
  105.9 111.8 %collective-permute-start.10 = (bf16[592,768]{1,0:T(8,128)(2,1)}, bf16[592,768]{1,0:T(8,128)(2,1)}, u32[]{:S(2)}, u32[]{:S(2)}) collective-permute-start(bf16[592,768]{1,0:T(8,128)(2,1)} %get-tuple-element.644), channel_id=1, source_target_pairs={{16,0},{17,1},{18,2},{19,3},{20,4},{21,5},{22,6},{23,7},{24,8},{25... | collective-permute-start | bytes 2727944 | tf_op jit(solution)/shard_map/ppermute | solution.py:887
  179.7 267.7 %collective-permute-start.13 = (bf16[624,768]{1,0:T(8,128)(2,1)}, bf16[624,768]{1,0:T(8,128)(2,1)}, u32[]{:S(2)}, u32[]{:S(2)}) collective-permute-start(bf16[624,768]{1,0:T(8,128)(2,1)} %get-tuple-element.664.refs_1_), channel_id=1, source_target_pairs={{0,8},{8,0},{1,9},{9,1},{2,10},{10,2},{3,11},{11,3},{4,12},{12,4},... | collective-permute-start | bytes 2875400 | tf_op jit(solution)/shard_map/ppermute | solution.py:854
  188.2 13.5 %copy-start.8 = (bf16[592,768]{1,0:T(8,128)(2,1)S(1)}, bf16[592,768]{1,0:T(8,128)(2,1)}, u32[]{:S(2)}) copy-start(bf16[592,768]{1,0:T(8,128)(2,1)} %get-tuple-element.637.refs_0_) | copy-start | bytes 2727940
  254.4 192.9 %collective-permute-start.12 = (bf16[592,768]{1,0:T(8,128)(2,1)}, bf16[592,768]{1,0:T(8,128)(2,1)S(1)}, u32[]{:S(2)}, u32[]{:S(2)}) collective-permute-start(bf16[592,768]{1,0:T(8,128)(2,1)} %get-tuple-element.663.refs_0_), channel_id=1, source_target_pairs={{0,8},{8,0},{1,9},{9,1},{2,10},{10,2},{3,11},{11,3},{4,12},{12,4},... | collective-permute-start | bytes 2727944 | tf_op jit(solution)/shard_map/ppermute | solution.py:854
  254.5 9.3 %copy-start.3 = (bf16[592,3072]{1,0:T(8,128)(2,1)S(1)}, bf16[592,3072]{1,0:T(8,128)(2,1)}, u32[]{:S(2)}) copy-start(bf16[592,3072]{1,0:T(8,128)(2,1)} %get-tuple-element.665.act) | copy-start | bytes 10911748
  254.5 9.3 %copy-start.5 = (bf16[592,768]{1,0:T(8,128)(2,1)S(1)}, bf16[592,768]{1,0:T(8,128)(2,1)}, u32[]{:S(2)}) copy-start(bf16[592,768]{1,0:T(8,128)(2,1)} %get-tuple-element.666.n2) | copy-start | bytes 2727940
  263.8 15.0 %copy-start.13 = (f32[8,768]{1,0:T(8,128)S(1)}, f32[8,768]{1,0:T(8,128)}, u32[]{:S(2)}) copy-start(f32[8,768]{1,0:T(8,128)} %get-tuple-element.682.refs_9_) | copy-start | bytes 73732
  263.8 15.0 %copy-start.14 = (f32[8,768]{1,0:T(8,128)S(1)}, f32[8,768]{1,0:T(8,128)}, u32[]{:S(2)}) copy-start(f32[8,768]{1,0:T(8,128)} %get-tuple-element.683.refs_10_) | copy-start | bytes 73732
  263.8 15.0 %copy-start.15 = (f32[8,768]{1,0:T(8,128)S(1)}, f32[8,768]{1,0:T(8,128)}, u32[]{:S(2)}) copy-start(f32[8,768]{1,0:T(8,128)} %get-tuple-element.681.refs_8_) | copy-start | bytes 73732
  263.8 15.0 %copy-start.16 = (f32[8,768]{1,0:T(8,128)S(1)}, f32[8,768]{1,0:T(8,128)}, u32[]{:S(2)}) copy-start(f32[8,768]{1,0:T(8,128)} %get-tuple-element.686.refs_13_) | copy-start | bytes 73732
  263.8 15.0 %copy-start.17 = (f32[8,768]{1,0:T(8,128)S(1)}, f32[8,768]{1,0:T(8,128)}, u32[]{:S(2)}) copy-start(f32[8,768]{1,0:T(8,128)} %get-tuple-element.687.refs_14_) | copy-start | bytes 73732
  263.8 15.0 %copy-start.18 = (f32[8,768]{1,0:T(8,128)S(1)}, f32[8,768]{1,0:T(8,128)}, u32[]{:S(2)}) copy-start(f32[8,768]{1,0:T(8,128)} %get-tuple-element.685.refs_12_) | copy-start | bytes 73732
  263.8 15.0 %copy-start.19 = (f32[1,3072]{1,0:T(1,128)S(1)}, f32[1,3072]{1,0:T(1,128)}, u32[]{:S(2)}) copy-start(f32[1,3072]{1,0:T(1,128)} %get-tuple-element.684.refs_11_) | copy-start | bytes 36868
  263.9 15.0 %copy-start.20 = (f32[1,3072]{1,0:T(1,128)S(1)}, f32[1,3072]{1,0:T(1,128)}, u32[]{:S(2)}) copy-start(f32[1,3072]{1,0:T(1,128)} %get-tuple-element.688.refs_15_) | copy-start | bytes 36868
  437.9 10.4 %copy-start.4 = (bf16[624,768]{1,0:T(8,128)(2,1)S(1)}, bf16[624,768]{1,0:T(8,128)(2,1)}, u32[]{:S(2)}) copy-start(bf16[624,768]{1,0:T(8,128)(2,1)} %get-tuple-element.664.refs_1_) | copy-start | bytes 2875396
  437.9 10.4 %copy-start.9 = (bf16[592,768]{1,0:T(8,128)(2,1)S(1)}, bf16[592,768]{1,0:T(8,128)(2,1)}, u32[]{:S(2)}) copy-start(bf16[592,768]{1,0:T(8,128)(2,1)} %get-tuple-element.663.refs_0_) | copy-start | bytes 2727940
  (3 other events, 18.6 us)

commit v5 on v4

--- a/solution.py
+++ b/solution.py
@@ -123,24 +123,32 @@
     return jnp.where(head == 0, stacked[:plen], stacked[plen:])
 
 
+def blocks_of(chunk):
+    nimg, plen, _ = chunk
+    return [(im, q0, qw) for im in range(nimg) for q0, qw in qblocks(plen)]
+
+
 def attn_fwd_pair(p, qkv, att, lse, o_tmp, chunk):
     nimg, plen, vlen = chunk
     cols = lanes(p, 128)
-    at = 0
-    for im in range(nimg):
-        rows = slice(im * plen, (im + 1) * plen)
-        k = qkv[1, rows, cols]
-        vt = qkv[2, rows, cols].T
-        queries = both_heads(qkv[0, rows, cols])
-        for q0, qw in qblocks(plen):
-            st = mask_keys(nt(k, queries[q0 : q0 + qw]), vlen)
-            top = jnp.max(st, axis=0, keepdims=True)
-            e = jnp.exp2((st - top) * SCALE2)
-            total = jnp.sum(e, axis=0, keepdims=True)
-            o_tmp[q0 : q0 + qw] = (nn(vt, e.astype(BF)) * (1.0 / total)).T
-            lse[p, :, at : at + qw] = top * SCALE2 + jnp.log2(total)
-            at += 256
-        att[rows, cols] = one_each(o_tmp, plen).astype(BF)
+    images = [slice(im * plen, (im + 1) * plen) for im in range(nimg)]
+    k = [qkv[1, rows, cols] for rows in images]
+    vt = [qkv[2, rows, cols].T for rows in images]
+    queries = [both_heads(qkv[0, rows, cols]) for rows in images]
+    blocks = blocks_of(chunk)
+    scores = lambda im, q0, qw: nt(k[im], queries[im][q0 : q0 + qw])
+    coming = scores(*blocks[0])
+    for i, (im, q0, qw) in enumerate(blocks):
+        st = mask_keys(coming, vlen)
+        if i + 1 < len(blocks):
+            coming = scores(*blocks[i + 1])
+        top = jnp.max(st, axis=0, keepdims=True)
+        e = jnp.exp2((st - top) * SCALE2)
+        total = jnp.sum(e, axis=0, keepdims=True)
+        o_tmp[q0 : q0 + qw] = (nn(vt[im], e.astype(BF)) * (1.0 / total)).T
+        lse[p, :, i * 256 : i * 256 + qw] = top * SCALE2 + jnp.log2(total)
+        if q0 + qw == 2 * plen:
+            att[images[im], cols] = one_each(o_tmp, plen).astype(BF)
 
 
 def gelu_parts(x):
@@ -154,11 +162,11 @@
 
 
 def fwd_kernel(*refs, chunk):
-    x_ref, g1, b1, bqo, bqp, pb, g2, b2, ubo, ubp, db = refs[:11]
-    weights, outs = refs[11:19], refs[19:28]
-    wq, pw, up, dn = refs[28:32]
-    held = refs[32:41]
-    acc, o_tmp, ub, in_sem, out_sem, ff_sem = refs[41:]
+    x_ref, g1, b1, own_bias, other_bias, pb, g2, b2, db = refs[:9]
+    weights, outs = refs[9:17], refs[17:26]
+    wq, pw, up, dn = refs[26:30]
+    held = refs[30:39]
+    acc, o_tmp, ub, in_sem, out_sem, ff_sem = refs[39:]
     normed, qkv, att, lse, mid, n2, act, dg, out = held
     ff = dn.shape[0]
     fb = ff // FF_STEPS
@@ -171,8 +179,13 @@
     xhat, _ = norm_parts(x_ref[...].astype(F32))
     normed[...] = (xhat * g1[...] + b1[...]).astype(BF)
     saves[0].start()
-    ub[...] = jnp.concatenate([ubo[...], ubp[...]], axis=1)
-    biases = jnp.concatenate([bqo[...], bqp[...]], axis=1)
+    half = wq.shape[1] // 2
+
+    def bias_of(first, last):
+        return jnp.concatenate([own_bias[:, first:last], other_bias[:, first:last]], axis=1)
+
+    q_bias, v_bias = bias_of(0, half), bias_of(half, 2 * half)
+    ub[...] = bias_of(2 * half, own_bias.shape[1])
     for c in loads["qkv"]:
         c.wait()
     for k in names[1:]:
@@ -180,7 +193,7 @@
             c.start()
 
     def project(s, carry):
-        bias = jnp.where(s == 0, biases[:1], jnp.where(s == 1, 0.0, biases[1:]))
+        bias = jnp.where(s == 0, q_bias, jnp.where(s == 1, 0.0, v_bias))
         qkv[s] = (nn(normed[...], wq[s]) + bias).astype(BF)
         return carry
 
@@ -245,7 +258,7 @@
     hbm = pl.BlockSpec(memory_space=pl.ANY)
     return pl.pallas_call(
         functools.partial(fwd_kernel, chunk=chunk),
-        in_specs=[vmem] * 11 + [hbm] * 8,
+        in_specs=[vmem] * 9 + [hbm] * 8,
         out_specs=[hbm] * len(kept),
         out_shape=[sds(*k) for k in kept],
         scratch_shapes=weight_scratch(d, ff)
@@ -258,44 +271,52 @@
         compiler_params=params(),
         name="fwd",
     )(
-        x, w["g1"], w["b1"], w["bq_o"], w["bq_p"], w["pb"], w["g2"], w["b2"], w["ub_o"],
-        w["ub_p"], w["db"], *weights_of(w),
-    )
-
-
-def attn_bwd_pair(p, qkv, gatt, lse, dqkv, sums, dq_tmp, chunk):
+        x, w["g1"], w["b1"], w["bias_o"], w["bias_p"], w["pb"], w["g2"], w["b2"], w["db"],
+        *weights_of(w),
+    )
+
+
+def attn_bwd_pair(p, qkv, att, gatt, lse, dqkv, sums, dq_tmp, chunk):
     nimg, plen, vlen = chunk
     cols = lanes(p, 128)
+    images = [slice(im * plen, (im + 1) * plen) for im in range(nimg)]
+    k = [qkv[1, rows, cols] for rows in images]
+    v = [qkv[2, rows, cols] for rows in images]
+    queries = [both_heads(qkv[0, rows, cols]) for rows in images]
+    grads = [both_heads(gatt[rows, cols]) for rows in images]
+    blocks = blocks_of(chunk)
+
+    def scores(im, q0, qw):
+        return nt(k[im], queries[im][q0 : q0 + qw]), nt(v[im], grads[im][q0 : q0 + qw])
+
     total_q, total_v = jnp.zeros((1, 128), F32), jnp.zeros((1, 128), F32)
-    at = 0
-    for im in range(nimg):
-        rows = slice(im * plen, (im + 1) * plen)
-        k = qkv[1, rows, cols]
-        v = qkv[2, rows, cols]
-        kt = k.T
-        queries = both_heads(qkv[0, rows, cols])
-        grads = both_heads(gatt[rows, cols])
-        dk = jnp.zeros((plen, 128), F32)
-        dv = jnp.zeros((plen, 128), F32)
-        for q0, qw in qblocks(plen):
-            q = queries[q0 : q0 + qw]
-            ga = grads[q0 : q0 + qw]
-            st = mask_keys(nt(k, q), vlen)
-            pr = jnp.exp2(st * SCALE2 - lse[p, :, at : at + qw])
-            gp = nt(v, ga)
-            dv += nn(pr.astype(BF), ga)
-            pg = pr * gp
-            ds = (pg - pr * jnp.sum(pg, axis=0, keepdims=True)).astype(BF)
-            dk += nn(ds, q)
-            dq_tmp[q0 : q0 + qw] = nn(kt, ds).T
-            at += 256
-        dq = (one_each(dq_tmp, plen) * SCALE).astype(BF)
-        dvb = dv.astype(BF)
-        dqkv[0, rows, cols] = dq
-        dqkv[1, rows, cols] = (dk * SCALE).astype(BF)
-        dqkv[2, rows, cols] = dvb
-        total_q += rowsum(dq)
-        total_v += rowsum(dvb)
+    coming = scores(*blocks[0])
+    for i, (im, q0, qw) in enumerate(blocks):
+        rows = images[im]
+        if q0 == 0:
+            kt = k[im].T
+            products = both_heads(gatt[rows, cols].astype(F32) * att[rows, cols].astype(F32))
+            dk = jnp.zeros((plen, 128), F32)
+            dv = jnp.zeros((plen, 128), F32)
+        q = queries[im][q0 : q0 + qw]
+        ga = grads[im][q0 : q0 + qw]
+        st, gp = mask_keys(coming[0], vlen), coming[1]
+        if i + 1 < len(blocks):
+            coming = scores(*blocks[i + 1])
+        pr = jnp.exp2(st * SCALE2 - lse[p, :, i * 256 : i * 256 + qw])
+        dv += nn(pr.astype(BF), ga)
+        delta = jnp.sum(products[q0 : q0 + qw].T, axis=0, keepdims=True)
+        ds = (pr * (gp - delta)).astype(BF)
+        dk += nn(ds, q)
+        dq_tmp[q0 : q0 + qw] = nn(kt, ds).T
+        if q0 + qw == 2 * plen:
+            dq = (one_each(dq_tmp, plen) * SCALE).astype(BF)
+            dvb = dv.astype(BF)
+            dqkv[0, rows, cols] = dq
+            dqkv[1, rows, cols] = (dk * SCALE).astype(BF)
+            dqkv[2, rows, cols] = dvb
+            total_q += rowsum(dq)
+            total_v += rowsum(dvb)
     sums[:, cols] = jnp.concatenate(
         [total_q, jnp.zeros_like(total_q), total_v, jnp.zeros((5, 128), F32)], axis=0
     )
@@ -303,17 +324,17 @@
 
 def bwd_kernel(*refs, chunk):
     g_ref, g2, g1 = refs[:3]
-    mid_h, dg_h, qkv_h, lse_h, x_h = refs[3:8]
-    weights, outs = refs[8:16], refs[16:21]
-    sums2, sff, sums_qkv, sums1 = refs[21:25]
-    wq, pw, up, dn = refs[25:29]
-    mid, dg, qkv, lse, x, pre, gb, dqkv, gx, gm, ga, acc, dq_tmp, in_sem, late_sem, out_sem, ff_sem = refs[29:]
+    mid_h, dg_h, qkv_h, lse_h, x_h, att_h = refs[3:9]
+    weights, outs = refs[9:17], refs[17:22]
+    sums2, sff, sums_qkv, sums1 = refs[22:26]
+    wq, pw, up, dn = refs[26:30]
+    mid, dg, qkv, lse, x, att, pre, gb, dqkv, gx, gm, ga, acc, dq_tmp, in_sem, late_sem, out_sem, ff_sem = refs[30:]
     ff = dn.shape[0]
     fb = ff // FF_STEPS
     loads = weight_loads(weights, wq, pw, up, dn)
     names = ("proj", "qkv")
     loads = {k: fetch(loads[k], in_sem.at[i]) for i, k in enumerate(names)}
-    late = fetch([(mid_h, mid), (qkv_h, qkv), (lse_h, lse), (x_h, x)], late_sem)
+    late = fetch([(mid_h, mid), (qkv_h, qkv), (lse_h, lse), (att_h, att), (x_h, x)], late_sem)
     saves = fetch(list(zip((pre, gb, dqkv, gx, g_ref), outs)), out_sem)
 
     def block_loads(j):
@@ -368,18 +389,18 @@
     for c in loads["proj"]:
         c.wait()
     ga[...] = nt(gb[...], pw[...]).astype(BF)
-    late[1].wait()
-    late[2].wait()
+    for c in late[1:4]:
+        c.wait()
 
     def attend(p, carry):
-        attn_bwd_pair(p, qkv, ga, lse, dqkv, sums_qkv, dq_tmp, chunk)
+        attn_bwd_pair(p, qkv, att, ga, lse, dqkv, sums_qkv, dq_tmp, chunk)
         return carry
 
     lax.fori_loop(0, lse.shape[0], attend, 0)
     saves[2].start()
     for c in loads["qkv"]:
         c.wait()
-    late[3].wait()
+    late[4].wait()
     acc[...] = nt(dqkv[0], wq[0])
 
     def project(s, carry):
@@ -409,20 +430,20 @@
     dma = pltpu.SemaphoreType.DMA
     pre, gb, dqkv, gx, copy, sums2, sff, sums_qkv, sums1 = pl.pallas_call(
         functools.partial(bwd_kernel, chunk=chunk),
-        in_specs=[vmem] * 3 + [hbm] * 13,
+        in_specs=[vmem] * 3 + [hbm] * 14,
         out_specs=[hbm] * 5 + [vmem] * 4,
         out_shape=[sds(*k) for k in (tall, wide, three, wide, wide)]
         + [sds((8, d), F32), sds((1, ff), F32), sds((8, d), F32), sds((8, d), F32)],
         scratch_shapes=weight_scratch(d, ff)
         + [
             pltpu.VMEM(*k)
-            for k in (flat, tall, three, lse, wide, tall, wide, three, wide, flat, wide, flat)
+            for k in (flat, tall, three, lse, wide, wide, tall, wide, three, wide, flat, wide, flat)
         ]
-        + [pltpu.VMEM((2 * chunk[1], 128), F32), dma((2, 2)), dma((4,)), dma((5,)), dma((FF_STEPS, 3))],
+        + [pltpu.VMEM((2 * chunk[1], 128), F32), dma((2, 2)), dma((5,)), dma((5,)), dma((FF_STEPS, 3))],
         compiler_params=params(),
         name="bwd",
     )(
-        g, w["g2"], w["g1"], kept["mid"], kept["dg"], kept["qkv"], kept["lse"], x, *weights_of(w)
+        g, w["g2"], w["g1"], kept["mid"], kept["dg"], kept["qkv"], kept["lse"], x, kept["att"], *weights_of(w)
     )
     return (copy, pre, gb, dqkv, sums2, sff, sums_qkv, sums1, gx)
 
@@ -856,12 +877,14 @@
     wqkv, pw, up, dn = qkv_weight[0], proj_weight[0], up_weight[0], down_weight[0]
     meta = jnp.concatenate([lane[None], large_place])
     xs = cut(patches, meta)
+    bias = jnp.concatenate([qv_bias.reshape(1, 2 * half), up_bias], axis=1)
+    bias_parts = after((bias, other(bias)), xs)
     w = {
         "g1": norm1_gain, "b1": norm1_bias, "g2": norm2_gain, "b2": norm2_bias,
         "pb": proj_bias, "db": down_bias,
         "wqkv_o": wqkv, "wqkv_p": other(wqkv), "pw_o": pw, "pw_p": other(pw),
         "up_o": up, "up_p": other(up), "dn_o": dn, "dn_p": other(dn),
-        "bq_o": qv_bias[0], "bq_p": other(qv_bias[0]), "ub_o": up_bias, "ub_p": other(up_bias),
+        **dict(zip(("bias_o", "bias_p"), bias_parts)),
     }
 
 

time: 461 us -> 434 us (0.941)
  Pallas kernels: 358 us -> 343 us
  waiting for transfers between devices: 67.1 us -> 52.9 us
    pallas_call x2, Pallas kernels: 67.5 us -> 58.6 us  [backward(): pl.pallas_call(functools.partial(bwd_kernel, chunk=chunk), in_specs=[vmem...]
    ppermute x10 -> x9, waiting for transfers between devices: 10.3 us -> 1.95 us  [body(): other = lambda array: lax.ppermute(array, 'tensor', both)]
    ppermute x2, waiting for transfers between devices: 51.1 us -> 44.9 us  [body(): up_ = lambda array: lax.ppermute(array, 'section', [(1, 0)])]
    pallas_call x2, Pallas kernels: 55.6 us -> 50.2 us  [forward(): pl.pallas_call(functools.partial(fwd_kernel, chunk=chunk), in_specs=[vmem...]
  transfers between devices with their start and end apart: 14 -> 13, of which waited for: 4 -> 4; matrix products, arithmetic and copies ran while one was open for 0% -> 1% of each run, Pallas kernels for 72% -> 74%
where the time goes in v5:
time: 434 us; the launch traced here: 427 us
  Pallas kernels  343 us (79%)
  waiting for transfers between devices  52.9 us (12%)
  loops' own time  15.4 us (4%)
  starting transfers between devices  9.3 us (2%)
    pallas_call x1, Pallas kernels, ring(): pl.pallas_call(functools.partial(ring_kernel, n=n, items=items, fold=sums...  159 us
    pallas_call x2, Pallas kernels, backward(): pl.pallas_call(functools.partial(bwd_kernel, chunk=chunk), in_specs=[vmem...  58.6 us
    pallas_call x2, Pallas kernels, forward(): pl.pallas_call(functools.partial(fwd_kernel, chunk=chunk), in_specs=[vmem...  50.2 us
    ppermute x2, waiting for transfers between devices, body(): up_ = lambda array: lax.ppermute(array, 'section', [(1, 0)])  44.9 us
    pallas_call x2, Pallas kernels, wgrad_mlp(): pl.pallas_call(functools.partial(wgrad_mlp_kernel, more=len(init)), grid=...  28.3 us
    pallas_call x2, Pallas kernels, wgrad_attn(): pl.pallas_call(functools.partial(wgrad_attn_kernel, more=len(init)), grid...  17.6 us
    another operation x8, loops' own time, pick(): lax.cond(section == on, lambda: tuple(make()), lambda: blank(like) if oth...  15.4 us
    pallas_call x2, Pallas kernels, join(): pl.pallas_call(join_kernel, grid_spec=pltpu.PrefetchScalarGridSpec(num_sc...  11.2 us
  transfers between devices with their start and end apart: 13, of which 4 were waited for; matrix products, arithmetic and copies ran while one was open for 1% of the time, Pallas kernels for 74%

profile of v5, /device:TPU:0, one launch (start us, length us, event | category | flops | bytes accessed | tf_op | source)
XLA Modules:
  0.0 427.0 jit_solution(1129004556970206639)
XLA Ops:
  1.9 0.7 copy.29
  3.1 1.3 constant_dynamic-update-slice_fusion
  4.9 1.2 pad_add_fusion.meta_ref
  6.1 4.5 %cut.2 = (bf16[592,768]{1,0:T(8,128)(2,1)}, bf16[624,768]{1,0:T(8,128)(2,1)}) custom-call(s32[3]{0:T(128)} %pad_add_fusion.meta_ref, bf16[2336,768]{1,0:T(8,128)(2,1)} %x_ref.2), custom_call_target="tpu_custom_call" | custom-call | tf_op jit(solution)/shard_map/cut/pallas_call | solution.py:790
  10.6 1.9 collective-permute-done
  12.6 23.2 %conditional.8 = ((bf16[624,768]{1,0:T(8,128)(2,1)}, bf16[3,624,768]{2,1,0:T(8,128)(2,1)}, bf16[624,768]{1,0:T(8,128)(2,1)}, f32[6,1,1536]{2,1,0:T(1,128)}, f32[...) conditional(s32[]{:T(128)} %convert_element_type.5, () %tuple.63, ...), branch_computations={%region_0.0_spmd, %region_1.0_spmd} | conditional | bytes 8 | solution.py:896
  12.6 23.2 %fwd.4 = (bf16[624,768]{1,0:T(8,128)(2,1)}, bf16[3,624,768]{2,1,0:T(8,128)(2,1)}, bf16[624,768]{1,0:T(8,128)(2,1)}, f32[6,1,1536]{2,1,0:T(1,128)}, f32[624,768]{...) custom-call(bf16[624,768]{1,0:T(8,128)(2,1)} %get-tuple-element.344., ...), custom_call_target="tpu_custom_call" | custom-call | tf_op jit(solution)/shard_map/cond/branch_1_fun/fwd/pallas_call | solution.py:259
  35.8 2.2 collective-permute-start.6
  38.1 27.2 %conditional.9 = ((bf16[592,768]{1,0:T(8,128)(2,1)}, bf16[3,592,768]{2,1,0:T(8,128)(2,1)}, bf16[592,768]{1,0:T(8,128)(2,1)}, f32[6,1,1280]{2,1,0:T(1,128)}, f32[...) conditional(s32[]{:T(128)} %convert_element_type.5, () %tuple.62, ...), branch_computations={%region_2.0_spmd, %region_3.0_spmd} | conditional | bytes 8 | solution.py:896
  38.3 27.0 %fwd.5 = (bf16[592,768]{1,0:T(8,128)(2,1)}, bf16[3,592,768]{2,1,0:T(8,128)(2,1)}, bf16[592,768]{1,0:T(8,128)(2,1)}, f32[6,1,1280]{2,1,0:T(1,128)}, f32[592,768]{...) custom-call(bf16[592,768]{1,0:T(8,128)(2,1)} %get-tuple-element.361., ...), custom_call_target="tpu_custom_call" | custom-call | tf_op jit(solution)/shard_map/cond/branch_1_fun/fwd/pallas_call | solution.py:259
  65.3 2.3 collective-permute-start.5
  67.6 4.5 %cut.3 = (bf16[592,768]{1,0:T(8,128)(2,1)}, bf16[624,768]{1,0:T(8,128)(2,1)}) custom-call(s32[3]{0:T(128)} %pad_add_fusion.meta_ref, bf16[2336,768]{1,0:T(8,128)(2,1)} %x_ref.3), custom_call_target="tpu_custom_call" | custom-call | tf_op jit(solution)/shard_map/cut/pallas_call | solution.py:790
  72.3 7.1 %conditional.11 = ((bf16[624,768]{1,0:T(8,128)(2,1)}, bf16[624,3072]{1,0:T(8,128)(2,1)}, bf16[624,768]{1,0:T(8,128)(2,1)}, bf16[3,624,768]{2,1,0:T(8,128)(2,1)},...) conditional(s32[]{:T(128)} %convert_element_type.4, () %tuple.68, ...), branch_computations={%region_6.0_spmd, %region_7.0_spmd} | conditional | bytes 80 | solution.py:896
  79.4 1.3 collective-permute-start.10
  81.1 6.0 %collective-permute-done.5 = bf16[592,768]{1,0:T(8,128)(2,1)} collective-permute-done((bf16[592,768]{1,0:T(8,128)(2,1)}, bf16[592,768]{1,0:T(8,128)(2,1)}, u32[]{:S(2)}, u32[]{:S(2)}) %collective-permute-start.5) | collective-permute-done | bytes 909344 | tf_op jit(solution)/shard_map/ppermute | solution.py:909
  87.4 7.0 %conditional.13 = ((bf16[592,768]{1,0:T(8,128)(2,1)}, bf16[592,3072]{1,0:T(8,128)(2,1)}, bf16[592,768]{1,0:T(8,128)(2,1)}, bf16[3,592,768]{2,1,0:T(8,128)(2,1)},...) conditional(s32[]{:T(128)} %convert_element_type.4, () %tuple.74, ...), branch_computations={%region_10.0_spmd, %region_11.0_spmd} | conditional | bytes 80 | solution.py:896
  94.4 1.3 collective-permute-start.9
  95.7 39.5 %collective-permute-done.10 = bf16[624,768]{1,0:T(8,128)(2,1)} collective-permute-done((bf16[624,768]{1,0:T(8,128)(2,1)}, bf16[624,768]{1,0:T(8,128)(2,1)}, u32[]{:S(2)}, u32[]{:S(2)}) %collective-permute-start.10) | collective-permute-done | bytes 958496 | tf_op jit(solution)/shard_map/ppermute | solution.py:910
  135.2 27.7 %conditional.14 = ((bf16[624,768]{1,0:T(8,128)(2,1)}, bf16[624,3072]{1,0:T(8,128)(2,1)}, bf16[624,768]{1,0:T(8,128)(2,1)}, bf16[3,624,768]{2,1,0:T(8,128)(2,1)},...) conditional(s32[]{:T(128)} %convert_element_type.5, ...), branch_computations={%region_12.0_spmd, %region_13.0_spmd} | conditional | bytes 80 | solution.py:896
  135.6 27.3 %bwd.6 = (bf16[624,3072]{1,0:T(8,128)(2,1)}, bf16[624,768]{1,0:T(8,128)(2,1)}, bf16[3,624,768]{2,1,0:T(8,128)(2,1)}, bf16[624,768]{1,0:T(8,128)(2,1)}, bf16[624,...) custom-call(bf16[624,768]{1,0:T(8,128)(2,1)} %get-tuple-element.464.refs_0_,, ...), custom_call_target="tpu_custom_call" | custom-call | tf_op jit(solution)/shard_map/cond/branch_1_fun/bwd/pallas_call | solution.py:431
  163.0 8.4 %wgrad_attn.2 = (bf16[3,768,384]{2,1,0:T(8,128)(2,1)}, bf16[3,768,384]{2,1,0:T(8,128)(2,1)}, bf16[384,768]{1,0:T(8,128)(2,1)}, bf16[384,768]{1,0:T(8,128)(2,1)}) custom-call(bf16[624,768]{1,0:T(8,128)(2,1)} %get-tuple-element.648.refs_0_, bf16[3,624,768]{2,1,0:T(8,128)(2,1)} %get-tuple-element.649.refs_1_, bf16[624,768]{1,0:T(8,128)(2,1)} %get-tuple-element.627.refs_2_, ...), custom_call_target="tpu_custom_call" | custom-call | tf_op jit(solution)/shard_map/wgrad_attn/pallas_call | solution.py:510
  171.4 13.4 %wgrad_mlp.2 = (bf16[1536,768]{1,0:T(8,128)(2,1)}, bf16[1536,768]{1,0:T(8,128)(2,1)}, bf16[768,1536]{1,0:T(8,128)(2,1)}, bf16[768,1536]{1,0:T(8,128)(2,1)}) custom-call(bf16[624,3072]{1,0:T(8,128)(2,1)S(1)} %copy-done.2, bf16[624,768]{1,0:T(8,128)(2,1)} %get-tuple-element.640.n2, bf16[624,3072]{1,0:T(8,128)(2,1)} %get-tuple-element.642.pre, ...), custom_call_target="tpu_custom_call" | custom-call | tf_op jit(solution)/shard_map/wgrad_mlp/pallas_call | solution.py:473
  184.9 5.8 %join.2 = bf16[2336,768]{1,0:T(8,128)(2,1)} custom-call(s32[3]{0:T(128)} %pad_add_fusion.meta_ref, bf16[592,768]{1,0:T(8,128)(2,1)S(1)} %copy-done.8, bf16[624,768]{1,0:T(8,128)(2,1)} %get-tuple-element.631.refs_1_, bf16[592,768]{1,0:T(8,128)(2,1)} %collective-permute-done.7.refs_2_, bf16[624,768]{1,0:T(8,128)(2,1)} %collective-permute-done.8.refs_3_), custom_call_target="tpu_custom_call" | custom-call | tf_op jit(solution)/shard_map/join/pallas_call | solution.py:827
  190.7 5.4 %collective-permute-done.9 = bf16[592,768]{1,0:T(8,128)(2,1)} collective-permute-done((bf16[592,768]{1,0:T(8,128)(2,1)}, bf16[592,768]{1,0:T(8,128)(2,1)}, u32[]{:S(2)}, u32[]{:S(2)}) %collective-permute-start.9) | collective-permute-done | bytes 909344 | tf_op jit(solution)/shard_map/ppermute | solution.py:910
  196.0 31.7 %conditional.15 = ((bf16[592,768]{1,0:T(8,128)(2,1)}, bf16[592,3072]{1,0:T(8,128)(2,1)}, bf16[592,768]{1,0:T(8,128)(2,1)}, bf16[3,592,768]{2,1,0:T(8,128)(2,1)},...) conditional(s32[]{:T(128)} %convert_element_type.5, ...), branch_computations={%region_14.0_spmd, %region_15.0_spmd} | conditional | bytes 80 | solution.py:896
  196.2 31.4 %bwd.7 = (bf16[592,3072]{1,0:T(8,128)(2,1)}, bf16[592,768]{1,0:T(8,128)(2,1)}, bf16[3,592,768]{2,1,0:T(8,128)(2,1)}, bf16[592,768]{1,0:T(8,128)(2,1)}, bf16[592,...) custom-call(bf16[592,768]{1,0:T(8,128)(2,1)} %get-tuple-element.490.refs_0_,, ...), custom_call_target="tpu_custom_call" | custom-call | tf_op jit(solution)/shard_map/cond/branch_1_fun/bwd/pallas_call | solution.py:431
  227.9 9.2 %wgrad_attn.3 = (bf16[3,768,384]{2,1,0:T(8,128)(2,1)}, bf16[3,768,384]{2,1,0:T(8,128)(2,1)}, bf16[384,768]{1,0:T(8,128)(2,1)}, bf16[384,768]{1,0:T(8,128)(2,1)}) custom-call(bf16[592,768]{1,0:T(8,128)(2,1)} %get-tuple-element.664.refs_0_, bf16[3,592,768]{2,1,0:T(8,128)(2,1)} %get-tuple-element.665.refs_1_, bf16[592,768]{1,0:T(8,128)(2,1)} %get-tuple-element.637.refs_2_, ...), custom_call_target="tpu_custom_call" | custom-call | tf_op jit(solution)/shard_map/wgrad_attn/pallas_call | solution.py:510
  237.2 14.9 %wgrad_mlp.3 = (bf16[1536,768]{1,0:T(8,128)(2,1)}, bf16[1536,768]{1,0:T(8,128)(2,1)}, bf16[768,1536]{1,0:T(8,128)(2,1)}, bf16[768,1536]{1,0:T(8,128)(2,1)}) custom-call(bf16[592,3072]{1,0:T(8,128)(2,1)S(1)} %copy-done.3, bf16[592,768]{1,0:T(8,128)(2,1)S(1)} %copy-done.5, bf16[592,3072]{1,0:T(8,128)(2,1)} %get-tuple-element.660.pre, ...), custom_call_target="tpu_custom_call" | custom-call | tf_op jit(solution)/shard_map/wgrad_mlp/pallas_call | solution.py:473
  252.2 158.8 %ring.1 = (bf16[1536,768]{1,0:T(8,128)(2,1)}, bf16[768,1536]{1,0:T(8,128)(2,1)}, bf16[2304,384]{1,0:T(8,128)(2,1)}, bf16[384,768]{1,0:T(8,128)(2,1)}, f32[16,768]{1,0:T(8,128)}) custom-call(bf16[1536,768]{1,0:T(8,128)(2,1)} %get-tuple-element.662.refs_0_, bf16[768,1536]{1,0:T(8,128)(2,1)} %get-tuple-element.663.refs_1_, bf16[2304,384]{1,0:T(8,128)(2,1)} %bitcast.50, ...), custom_call_target="tpu_custom_call" | custom-call | tf_op jit(solution)/shard_map/ring/pallas_call | solution.py:695
  411.0 9.4 %finish.1 = (f32[1,1536,768]{2,1,0:T(8,128)}, f32[1,768,1536]{2,1,0:T(8,128)}, f32[1,2304,384]{2,1,0:T(8,128)}, f32[1,384,768]{2,1,0:T(8,128)}, f32[1,768]{1,0:T...) custom-call(bf16[1536,768]{1,0:T(8,128)(2,1)} %get-tuple-element.681, ...), custom_call_target="tpu_custom_call" | custom-call | tf_op jit(solution)/shard_map/finish/pallas_call | solution.py:744
  420.5 0.9 copy-done.7
  421.4 5.4 %join.3 = bf16[2336,768]{1,0:T(8,128)(2,1)} custom-call(s32[3]{0:T(128)} %pad_add_fusion.meta_ref, bf16[592,768]{1,0:T(8,128)(2,1)S(1)} %copy-done.9, bf16[624,768]{1,0:T(8,128)(2,1)S(1)} %copy-done.4, bf16[592,768]{1,0:T(8,128)(2,1)} %copy-done.7, bf16[624,768]{1,0:T(8,128)(2,1)} %collective-permute-done.12.refs_3_), custom_call_target="tpu_custom_call" | custom-call | tf_op jit(solution)/shard_map/join/pallas_call | solution.py:827
  (66 shorter events, 3.3 us)
Async XLA Ops:
  0.6 11.9 %copy-start = (bf16[1,768,1536]{2,1,0:T(8,128)(2,1)S(1)}, bf16[1,768,1536]{2,1,0:T(8,128)(2,1)}, u32[]{:S(2)}) copy-start(bf16[1,768,1536]{2,1,0:T(8,128)(2,1)} %param.42) | copy-start | bytes 7077892
  0.7 11.9 %copy-start.1 = (bf16[1,384,768]{2,1,0:T(8,128)(2,1)S(1)}, bf16[1,384,768]{2,1,0:T(8,128)(2,1)}, u32[]{:S(2)}) copy-start(bf16[1,384,768]{2,1,0:T(8,128)(2,1)} %param.38) | copy-start | bytes 1769476
  0.7 11.9 %copy-start.10 = (f32[1,768]{1,0:T(1,128)S(1)}, f32[1,768]{1,0:T(1,128)}, u32[]{:S(2)}) copy-start(f32[1,768]{1,0:T(1,128)} %param.34) | copy-start | bytes 9220
  0.7 11.9 %copy-start.12 = (f32[1,768]{1,0:T(1,128)S(1)}, f32[1,768]{1,0:T(1,128)}, u32[]{:S(2)}) copy-start(f32[1,768]{1,0:T(1,128)} %param.35) | copy-start | bytes 9220
  0.7 11.9 %copy-start.13 = (f32[1,768]{1,0:T(1,128)S(1)}, f32[1,768]{1,0:T(1,128)}, u32[]{:S(2)}) copy-start(f32[1,768]{1,0:T(1,128)} %param.39) | copy-start | bytes 9220
  0.7 11.9 %copy-start.11 = (f32[1,768]{1,0:T(1,128)S(1)}, f32[1,768]{1,0:T(1,128)}, u32[]{:S(2)}) copy-start(f32[1,768]{1,0:T(1,128)} %param.40) | copy-start | bytes 9220
  0.7 11.8 %collective-permute-start.3 = (bf16[768,1536]{1,0:T(8,128)(2,1)}, bf16[768,1536]{1,0:T(8,128)(2,1)}, u32[]{:S(2)}, u32[]{:S(2)}) collective-permute-start(bf16[768,1536]{1,0:T(8,128)(2,1)} %bitcast.12), channel_id=1, source_target_pairs={{0,8},{8,0},{1,9},{9,1},{2,10},{10,2},{3,11},{11,3},{4,12},{12,4},... | collective-permute-start | bytes 7077896 | tf_op jit(solution)/shard_map/ppermute | solution.py:875
  1.3 11.3 %collective-permute-start.4 = (bf16[1536,768]{1,0:T(8,128)(2,1)}, bf16[1536,768]{1,0:T(8,128)(2,1)}, u32[]{:S(2)}, u32[]{:S(2)}) collective-permute-start(bf16[1536,768]{1,0:T(8,128)(2,1)} %bitcast.21), channel_id=1, source_target_pairs={{0,8},{8,0},{1,9},{9,1},{2,10},{10,2},{3,11},{11,3},{4,12},{12,4},... | collective-permute-start | bytes 7077896 | tf_op jit(solution)/shard_map/ppermute | solution.py:875
  1.3 11.2 %collective-permute-start.1 = (bf16[3,768,384]{2,1,0:T(8,128)(2,1)}, bf16[3,768,384]{2,1,0:T(8,128)(2,1)}, u32[]{:S(2)}, u32[]{:S(2)}) collective-permute-start(bf16[3,768,384]{2,1,0:T(8,128)(2,1)} %bitcast.30), channel_id=1, source_target_pairs={{0,8},{8,0},{1,9},{9,1},{2,10},{10,2},{3,11},{11,3},{4,12},{12,4},... | collective-permute-start | bytes 5308424 | tf_op jit(solution)/shard_map/ppermute | solution.py:875
  1.8 10.8 %collective-permute-start.2 = (bf16[384,768]{1,0:T(8,128)(2,1)}, bf16[384,768]{1,0:T(8,128)(2,1)S(1)}, u32[]{:S(2)}, u32[]{:S(2)}) collective-permute-start(bf16[384,768]{1,0:T(8,128)(2,1)} %bitcast.39), channel_id=1, source_target_pairs={{0,8},{8,0},{1,9},{9,1},{2,10},{10,2},{3,11},{11,3},{4,12},{12,4},... | collective-permute-start | bytes 1769480 | tf_op jit(solution)/shard_map/ppermute | solution.py:875
  4.4 8.1 %collective-permute-start = (f32[1,2304]{1,0:T(1,128)}, f32[1,2304]{1,0:T(1,128)}, u32[]{:S(2)}, u32[]{:S(2)}) collective-permute-start(f32[1,2304]{1,0:T(1,128)} %constant_dynamic-update-slice_fusion), channel_id=1, source_target_pairs={{0,8},{8,0},{1,9},{9,1},{2,10},{10,2},{3,11},{11,3},{4,12},{12,4},... | collective-permute-start | bytes 27656 | tf_op jit(solution)/shard_map/ppermute | solution.py:875
  35.8 36.3 %collective-permute-start.6 = (bf16[624,768]{1,0:T(8,128)(2,1)}, bf16[624,768]{1,0:T(8,128)(2,1)}, u32[]{:S(2)}, u32[]{:S(2)}) collective-permute-start(bf16[624,768]{1,0:T(8,128)(2,1)} %get-tuple-element.618), channel_id=1, source_target_pairs={{0,16},{1,17},{2,18},{3,19},{4,20},{5,21},{6,22},{7,23},{8,24},{9,... | collective-permute-start | bytes 2875400 | tf_op jit(solution)/shard_map/ppermute | solution.py:909
  65.3 21.9 %collective-permute-start.5 = (bf16[592,768]{1,0:T(8,128)(2,1)}, bf16[592,768]{1,0:T(8,128)(2,1)}, u32[]{:S(2)}, u32[]{:S(2)}) collective-permute-start(bf16[592,768]{1,0:T(8,128)(2,1)} %get-tuple-element.620), channel_id=1, source_target_pairs={{0,16},{1,17},{2,18},{3,19},{4,20},{5,21},{6,22},{7,23},{8,24},{9,... | collective-permute-start | bytes 2727944 | tf_op jit(solution)/shard_map/ppermute | solution.py:909
  79.4 55.8 %collective-permute-start.10 = (bf16[624,768]{1,0:T(8,128)(2,1)}, bf16[624,768]{1,0:T(8,128)(2,1)}, u32[]{:S(2)}, u32[]{:S(2)}) collective-permute-start(bf16[624,768]{1,0:T(8,128)(2,1)} %get-tuple-element.628), channel_id=1, source_target_pairs={{16,0},{17,1},{18,2},{19,3},{20,4},{21,5},{22,6},{23,7},{24,8},{25... | collective-permute-start | bytes 2875400 | tf_op jit(solution)/shard_map/ppermute | solution.py:910
  80.7 104.1 %collective-permute-start.8 = (bf16[624,768]{1,0:T(8,128)(2,1)}, bf16[624,768]{1,0:T(8,128)(2,1)}, u32[]{:S(2)}, u32[]{:S(2)}) collective-permute-start(bf16[624,768]{1,0:T(8,128)(2,1)} %get-tuple-element.631.refs_1_), channel_id=1, source_target_pairs={{0,8},{8,0},{1,9},{9,1},{2,10},{10,2},{3,11},{11,3},{4,12},{12,4},... | collective-permute-start | bytes 2875400 | tf_op jit(solution)/shard_map/ppermute | solution.py:875
  87.3 97.5 %collective-permute-start.7 = (bf16[592,768]{1,0:T(8,128)(2,1)}, bf16[592,768]{1,0:T(8,128)(2,1)}, u32[]{:S(2)}, u32[]{:S(2)}) collective-permute-start(bf16[592,768]{1,0:T(8,128)(2,1)} %get-tuple-element.630.refs_0_), channel_id=1, source_target_pairs={{0,8},{8,0},{1,9},{9,1},{2,10},{10,2},{3,11},{11,3},{4,12},{12,4},... | collective-permute-start | bytes 2727944 | tf_op jit(solution)/shard_map/ppermute | solution.py:875
  94.4 101.6 %collective-permute-start.9 = (bf16[592,768]{1,0:T(8,128)(2,1)}, bf16[592,768]{1,0:T(8,128)(2,1)}, u32[]{:S(2)}, u32[]{:S(2)}) collective-permute-start(bf16[592,768]{1,0:T(8,128)(2,1)} %get-tuple-element.638), channel_id=1, source_target_pairs={{16,0},{17,1},{18,2},{19,3},{20,4},{21,5},{22,6},{23,7},{24,8},{25... | collective-permute-start | bytes 2727944 | tf_op jit(solution)/shard_map/ppermute | solution.py:910
  162.9 257.5 %collective-permute-start.12 = (bf16[624,768]{1,0:T(8,128)(2,1)}, bf16[624,768]{1,0:T(8,128)(2,1)}, u32[]{:S(2)}, u32[]{:S(2)}) collective-permute-start(bf16[624,768]{1,0:T(8,128)(2,1)} %get-tuple-element.657.refs_1_), channel_id=1, source_target_pairs={{0,8},{8,0},{1,9},{9,1},{2,10},{10,2},{3,11},{11,3},{4,12},{12,4},... | collective-permute-start | bytes 2875400 | tf_op jit(solution)/shard_map/ppermute | solution.py:875
  171.4 13.5 %copy-start.8 = (bf16[592,768]{1,0:T(8,128)(2,1)S(1)}, bf16[592,768]{1,0:T(8,128)(2,1)}, u32[]{:S(2)}) copy-start(bf16[592,768]{1,0:T(8,128)(2,1)} %get-tuple-element.630.refs_0_) | copy-start | bytes 2727940
  227.8 192.7 %collective-permute-start.11 = (bf16[592,768]{1,0:T(8,128)(2,1)}, bf16[592,768]{1,0:T(8,128)(2,1)S(1)}, u32[]{:S(2)}, u32[]{:S(2)}) collective-permute-start(bf16[592,768]{1,0:T(8,128)(2,1)} %get-tuple-element.656.refs_0_), channel_id=1, source_target_pairs={{0,8},{8,0},{1,9},{9,1},{2,10},{10,2},{3,11},{11,3},{4,12},{12,4},... | collective-permute-start | bytes 2727944 | tf_op jit(solution)/shard_map/ppermute | solution.py:875
  227.8 9.3 %copy-start.3 = (bf16[592,3072]{1,0:T(8,128)(2,1)S(1)}, bf16[592,3072]{1,0:T(8,128)(2,1)}, u32[]{:S(2)}) copy-start(bf16[592,3072]{1,0:T(8,128)(2,1)} %get-tuple-element.658.act) | copy-start | bytes 10911748
  227.9 9.3 %copy-start.5 = (bf16[592,768]{1,0:T(8,128)(2,1)S(1)}, bf16[592,768]{1,0:T(8,128)(2,1)}, u32[]{:S(2)}) copy-start(bf16[592,768]{1,0:T(8,128)(2,1)} %get-tuple-element.659.n2) | copy-start | bytes 2727940
  237.1 15.0 %copy-start.14 = (f32[8,768]{1,0:T(8,128)S(1)}, f32[8,768]{1,0:T(8,128)}, u32[]{:S(2)}) copy-start(f32[8,768]{1,0:T(8,128)} %get-tuple-element.674.refs_9_) | copy-start | bytes 73732
  237.1 15.0 %copy-start.15 = (f32[8,768]{1,0:T(8,128)S(1)}, f32[8,768]{1,0:T(8,128)}, u32[]{:S(2)}) copy-start(f32[8,768]{1,0:T(8,128)} %get-tuple-element.675.refs_10_) | copy-start | bytes 73732
  237.2 15.0 %copy-start.16 = (f32[8,768]{1,0:T(8,128)S(1)}, f32[8,768]{1,0:T(8,128)}, u32[]{:S(2)}) copy-start(f32[8,768]{1,0:T(8,128)} %get-tuple-element.673.refs_8_) | copy-start | bytes 73732
  237.2 15.0 %copy-start.17 = (f32[8,768]{1,0:T(8,128)S(1)}, f32[8,768]{1,0:T(8,128)}, u32[]{:S(2)}) copy-start(f32[8,768]{1,0:T(8,128)} %get-tuple-element.678.refs_13_) | copy-start | bytes 73732
  237.2 15.0 %copy-start.18 = (f32[8,768]{1,0:T(8,128)S(1)}, f32[8,768]{1,0:T(8,128)}, u32[]{:S(2)}) copy-start(f32[8,768]{1,0:T(8,128)} %get-tuple-element.679.refs_14_) | copy-start | bytes 73732
  237.2 15.0 %copy-start.19 = (f32[8,768]{1,0:T(8,128)S(1)}, f32[8,768]{1,0:T(8,128)}, u32[]{:S(2)}) copy-start(f32[8,768]{1,0:T(8,128)} %get-tuple-element.677.refs_12_) | copy-start | bytes 73732
  237.2 15.0 %copy-start.20 = (f32[1,3072]{1,0:T(1,128)S(1)}, f32[1,3072]{1,0:T(1,128)}, u32[]{:S(2)}) copy-start(f32[1,3072]{1,0:T(1,128)} %get-tuple-element.676.refs_11_) | copy-start | bytes 36868
  237.2 15.0 %copy-start.21 = (f32[1,3072]{1,0:T(1,128)S(1)}, f32[1,3072]{1,0:T(1,128)}, u32[]{:S(2)}) copy-start(f32[1,3072]{1,0:T(1,128)} %get-tuple-element.680.refs_15_) | copy-start | bytes 36868
  411.0 10.4 %copy-start.4 = (bf16[624,768]{1,0:T(8,128)(2,1)S(1)}, bf16[624,768]{1,0:T(8,128)(2,1)}, u32[]{:S(2)}) copy-start(bf16[624,768]{1,0:T(8,128)(2,1)} %get-tuple-element.657.refs_1_) | copy-start | bytes 2875396
  411.0 10.4 %copy-start.9 = (bf16[592,768]{1,0:T(8,128)(2,1)S(1)}, bf16[592,768]{1,0:T(8,128)(2,1)}, u32[]{:S(2)}) copy-start(bf16[592,768]{1,0:T(8,128)(2,1)} %get-tuple-element.656.refs_0_) | copy-start | bytes 2727940
  (3 other events, 18.6 us)

commit v6 on v5

--- a/solution.py
+++ b/solution.py
@@ -552,13 +552,17 @@
 
 
 def ring_kernel(*refs, n, items, fold):
-    owns, gifts = refs[:n], refs[n : 2 * n]
-    sums = refs[2 * n : 2 * n + 8]
-    at = 2 * n + 8
+    normed, dqkv, att, gb = refs[:4]
+    parts, sums = refs[4:8], refs[12:20]
+    at = 20
     outs, vsum_ref = refs[at : at + n], refs[at + n]
     at += n + 1
     theirs = refs[at : at + n]
     at += n
+    own_qkv, own_pw, gift_qkv, gift_pw = refs[at : at + 4]
+    owns = refs[8:10] + (own_qkv, own_pw)
+    gifts = refs[10:12] + (gift_qkv, gift_pw)
+    at += 4
     m = len(items)
     slots = refs[at : at + m]
     vbuf, vother, vmine, vslot, send, recv, xsend, xrecv, vsend, vrecv, vxs, vxr = refs[at + m :]
@@ -626,14 +630,27 @@
         device_id=partner, device_id_type=mesh_id,
     )
 
-    for step in range(2):
-        for a in range(m):
-            exchange(a, step).start()
+    def begin(arrays):
+        for step in range(2):
+            for a in arrays:
+                exchange(a, step).start()
+        for a in arrays:
+            slots[a][0] = mine(a, 0).astype(BF)
+            remote(slots[a].at[0], slots[a].at[1], a, 0).start()
+
+    begin(range(2))
     vbuf[...] = vector_block([sums[i][...] + sums[4 + i][...] for i in range(4)])
     vexchange.start()
-    for a in range(m):
-        slots[a][0] = mine(a, 0).astype(BF)
-        remote(slots[a].at[0], slots[a].at[1], a, 0).start()
+    d = normed.shape[1]
+    half = d // 2
+    for s in range(3):
+        total = tn(normed[...], dqkv[s])
+        rows = slice(s * d, (s + 1) * d)
+        own_qkv[rows] = (total[:, :half] + parts[0][s].astype(F32)).astype(BF)
+        gift_qkv[rows] = (total[:, half:] + parts[1][s].astype(F32)).astype(BF)
+    own_pw[...] = (tn(att[:, :half], gb[...]) + parts[2][...].astype(F32)).astype(BF)
+    gift_pw[...] = (tn(att[:, half:], gb[...]) + parts[3][...].astype(F32)).astype(BF)
+    begin(range(2, m))
 
     def scatter(s, carry):
         for a in range(m):
@@ -684,21 +701,23 @@
             exchange(a, s).wait_send()
 
 
-def ring(owns, gifts, sums_s, sums_l):
-    n = len(owns)
-    d = owns[0].shape[1]
+def ring(mlp, kept, back, parts, sums):
+    d = kept["normed"].shape[1]
+    shapes = [mlp[0].shape, mlp[2].shape, (3 * d, d // 2), (d // 2, d)]
+    n = len(shapes)
     items = items_of(d)
     m = len(items)
     vmem = pl.BlockSpec(memory_space=pltpu.VMEM)
+    hbm = pl.BlockSpec(memory_space=pl.ANY)
     dma = pltpu.SemaphoreType.DMA
     vec = pltpu.VMEM((VEC_ROWS, d), F32)
     out = pl.pallas_call(
-        functools.partial(ring_kernel, n=n, items=items, fold=sums_s[3].shape[1] // (2 * d)),
-        in_specs=[vmem] * (2 * n + 8),
+        functools.partial(ring_kernel, n=n, items=items, fold=sums[3].shape[1] // (2 * d)),
+        in_specs=[vmem] * 10 + [hbm] * 2 + [vmem] * 8,
         out_specs=[vmem] * (n + 1),
-        out_shape=[sds(a.shape, BF) for a in owns] + [sds((VEC_ROWS, d), F32)],
-        scratch_shapes=[pltpu.VMEM(a.shape, BF) for a in owns]
-        + [pltpu.VMEM((RING, rows // RING, owns[i].shape[1]), BF) for i, _, rows, _ in items]
+        out_shape=[sds(a, BF) for a in shapes] + [sds((VEC_ROWS, d), F32)],
+        scratch_shapes=[pltpu.VMEM(a, BF) for a in shapes + 2 * shapes[2:]]
+        + [pltpu.VMEM((RING, rows // RING, shapes[i][1]), BF) for i, _, rows, _ in items]
         + [
             vec, vec, vec, pltpu.VMEM((RING - 1, VEC_ROWS, d), F32),
             dma((m, 2 * RING - 2)), dma((m, 2 * RING - 2)), dma((m, RING)), dma((m, RING)),
@@ -706,16 +725,23 @@
         ],
         compiler_params=params(collective_id=1, has_side_effects=True),
         name="ring",
-    )(*owns, *gifts, *sums_s, *sums_l)
+    )(
+        kept["normed"], back["dqkv"], kept["att"], back["gb"], *parts, mlp[0], mlp[2], mlp[1],
+        mlp[3], *sums,
+    )
     return out[:n], out[n]
 
 
-def dp_sum(owns, gifts, sums_s, sums_l):
+def dp_sum(mlp, kept, back, parts, sums):
     if lax.axis_size("dp") == RING:
-        return ring(owns, gifts, sums_s, sums_l)
+        return ring(mlp, kept, back, parts, sums)
     other = lambda array: lax.ppermute(array, "tensor", [(0, 1), (1, 0)])
-    fold = sums_s[3].shape[1] // (2 * owns[0].shape[1])
-    block = vector_block([a + b for a, b in zip(sums_s, sums_l)])
+    qkv_o, qkv_p, pw_o, pw_p = wgrad_attn(kept, back, parts)
+    rows = lambda qkv: qkv.reshape(-1, qkv.shape[2])
+    owns = [mlp[0], mlp[2], rows(qkv_o), pw_o]
+    gifts = [mlp[1], mlp[3], rows(qkv_p), pw_p]
+    fold = sums[3].shape[1] // (2 * pw_o.shape[1])
+    block = vector_block([a + b for a, b in zip(sums[:4], sums[4:])])
     summed = [lax.psum(a + other(b), "dp") for a, b in zip(owns, gifts)]
     return summed, lax.psum(block + as_own(other(block), fold), "dp")
 
@@ -930,15 +956,13 @@
     outputs = join(outs, [other(a) for a in outs], meta)
     sent_l = after(sent_l, part_mlp, part_attn, outputs)
     back_l = bwd(large, 0, sent_l, xs[large], kept_l, back_l)
-    dn_o, dn_p, up_o, up_p = wgrad_mlp(named(KEPT, kept_l), named(BACK, back_l), part_mlp)
-    qkv_o, qkv_p, pw_o, pw_p = wgrad_attn(named(KEPT, kept_l), named(BACK, back_l), part_attn)
+    mlp = wgrad_mlp(named(KEPT, kept_l), named(BACK, back_l), part_mlp)
     grads = [back_l[-1], back_s[-1]]
     input_grads = join(grads, [other(a) for a in grads], meta)
 
-    rows = lambda qkv: qkv.reshape(3 * d, half)
     sums = lambda back: [named(BACK, back)[k] for k in ("sums1", "sums2", "sums_qkv", "sff")]
     summed, vec = dp_sum(
-        [dn_o, up_o, rows(qkv_o), pw_o], [dn_p, up_p, rows(qkv_p), pw_p], sums(back_s), sums(back_l)
+        mlp, named(KEPT, kept_l), named(BACK, back_l), part_attn, sums(back_s) + sums(back_l)
     )
     g_dn, g_up, g_qkv, g_pw, g1, b1, g2, b2, pb, db, qv, ub = finish(summed, vec)
     return (

time: 434 us -> 425 us (0.979)
  Pallas kernels: 343 us -> 334 us
    pallas_call x2 -> x1, Pallas kernels: 17.6 us -> 8.37 us  [wgrad_attn(): pl.pallas_call(functools.partial(wgrad_attn_kernel, more=len(init)), grid...]
  transfers between devices with their start and end apart: 13 -> 13, of which waited for: 4 -> 4; matrix products, arithmetic and copies ran while one was open for 1% -> 1% of each run, Pallas kernels for 74% -> 73%
where the time goes in v6:
time: 425 us; the launch traced here: 418 us
  Pallas kernels  334 us (79%)
  waiting for transfers between devices  52.8 us (12%)
  loops' own time  15.4 us (4%)
  starting transfers between devices  9.32 us (2%)
    pallas_call x1, Pallas kernels, ring(): pl.pallas_call(functools.partial(ring_kernel, n=n, items=items, fold=sums...  158 us
    pallas_call x2, Pallas kernels, backward(): pl.pallas_call(functools.partial(bwd_kernel, chunk=chunk), in_specs=[vmem...  58.6 us
    pallas_call x2, Pallas kernels, forward(): pl.pallas_call(functools.partial(fwd_kernel, chunk=chunk), in_specs=[vmem...  50.2 us
    ppermute x2, waiting for transfers between devices, body(): up_ = lambda array: lax.ppermute(array, 'section', [(1, 0)])  44.8 us
    pallas_call x2, Pallas kernels, wgrad_mlp(): pl.pallas_call(functools.partial(wgrad_mlp_kernel, more=len(init)), grid=...  29.5 us
    another operation x8, loops' own time, pick(): lax.cond(section == on, lambda: tuple(make()), lambda: blank(like) if oth...  15.4 us
    pallas_call x2, Pallas kernels, join(): pl.pallas_call(join_kernel, grid_spec=pltpu.PrefetchScalarGridSpec(num_sc...  11.2 us
    pallas_call x1, Pallas kernels, finish(): pl.pallas_call(functools.partial(finish_kernel, fold=fold), grid=(steps,)...  9.44 us
  transfers between devices with their start and end apart: 13, of which 4 were waited for; matrix products, arithmetic and copies ran while one was open for 1% of the time, Pallas kernels for 73%

profile of v6, /device:TPU:0, one launch (start us, length us, event | category | flops | bytes accessed | tf_op | source)
XLA Modules:
  0.0 417.8 jit_solution(2633336744501574538)
XLA Ops:
  1.9 0.7 copy.29
  2.5 0.6 constant_dynamic-update-slice_fusion.1
  3.1 1.3 constant_dynamic-update-slice_fusion
  4.9 1.2 pad_add_fusion.meta_ref
  6.1 4.5 %cut.2 = (bf16[592,768]{1,0:T(8,128)(2,1)}, bf16[624,768]{1,0:T(8,128)(2,1)}) custom-call(s32[3]{0:T(128)} %pad_add_fusion.meta_ref, bf16[2336,768]{1,0:T(8,128)(2,1)} %x_ref.2), custom_call_target="tpu_custom_call" | custom-call | tf_op jit(solution)/shard_map/cut/pallas_call | solution.py:816
  10.6 1.9 collective-permute-done
  12.6 23.2 %conditional.8 = ((bf16[624,768]{1,0:T(8,128)(2,1)}, bf16[3,624,768]{2,1,0:T(8,128)(2,1)}, bf16[624,768]{1,0:T(8,128)(2,1)}, f32[6,1,1536]{2,1,0:T(1,128)}, f32[...) conditional(s32[]{:T(128)} %convert_element_type.5, () %tuple.63, ...), branch_computations={%region_0.0_spmd, %region_1.0_spmd} | conditional | bytes 8 | solution.py:922
  12.6 23.2 %fwd.4 = (bf16[624,768]{1,0:T(8,128)(2,1)}, bf16[3,624,768]{2,1,0:T(8,128)(2,1)}, bf16[624,768]{1,0:T(8,128)(2,1)}, f32[6,1,1536]{2,1,0:T(1,128)}, f32[624,768]{...) custom-call(bf16[624,768]{1,0:T(8,128)(2,1)} %get-tuple-element.344., ...), custom_call_target="tpu_custom_call" | custom-call | tf_op jit(solution)/shard_map/cond/branch_1_fun/fwd/pallas_call | solution.py:259
  35.8 2.2 collective-permute-start.6
  38.1 27.2 %conditional.9 = ((bf16[592,768]{1,0:T(8,128)(2,1)}, bf16[3,592,768]{2,1,0:T(8,128)(2,1)}, bf16[592,768]{1,0:T(8,128)(2,1)}, f32[6,1,1280]{2,1,0:T(1,128)}, f32[...) conditional(s32[]{:T(128)} %convert_element_type.5, () %tuple.62, ...), branch_computations={%region_2.0_spmd, %region_3.0_spmd} | conditional | bytes 8 | solution.py:922
  38.3 27.0 %fwd.5 = (bf16[592,768]{1,0:T(8,128)(2,1)}, bf16[3,592,768]{2,1,0:T(8,128)(2,1)}, bf16[592,768]{1,0:T(8,128)(2,1)}, f32[6,1,1280]{2,1,0:T(1,128)}, f32[592,768]{...) custom-call(bf16[592,768]{1,0:T(8,128)(2,1)} %get-tuple-element.361., ...), custom_call_target="tpu_custom_call" | custom-call | tf_op jit(solution)/shard_map/cond/branch_1_fun/fwd/pallas_call | solution.py:259
  65.3 2.3 collective-permute-start.5
  67.6 4.5 %cut.3 = (bf16[592,768]{1,0:T(8,128)(2,1)}, bf16[624,768]{1,0:T(8,128)(2,1)}) custom-call(s32[3]{0:T(128)} %pad_add_fusion.meta_ref, bf16[2336,768]{1,0:T(8,128)(2,1)} %x_ref.3), custom_call_target="tpu_custom_call" | custom-call | tf_op jit(solution)/shard_map/cut/pallas_call | solution.py:816
  72.3 7.1 %conditional.11 = ((bf16[624,768]{1,0:T(8,128)(2,1)}, bf16[624,3072]{1,0:T(8,128)(2,1)}, bf16[624,768]{1,0:T(8,128)(2,1)}, bf16[3,624,768]{2,1,0:T(8,128)(2,1)},...) conditional(s32[]{:T(128)} %convert_element_type.4, () %tuple.68, ...), branch_computations={%region_6.0_spmd, %region_7.0_spmd} | conditional | bytes 80 | solution.py:922
  79.4 1.3 collective-permute-start.10
  81.2 6.0 %collective-permute-done.5 = bf16[592,768]{1,0:T(8,128)(2,1)} collective-permute-done((bf16[592,768]{1,0:T(8,128)(2,1)}, bf16[592,768]{1,0:T(8,128)(2,1)}, u32[]{:S(2)}, u32[]{:S(2)}) %collective-permute-start.5) | collective-permute-done | bytes 909344 | tf_op jit(solution)/shard_map/ppermute | solution.py:935
  87.4 7.0 %conditional.13 = ((bf16[592,768]{1,0:T(8,128)(2,1)}, bf16[592,3072]{1,0:T(8,128)(2,1)}, bf16[592,768]{1,0:T(8,128)(2,1)}, bf16[3,592,768]{2,1,0:T(8,128)(2,1)},...) conditional(s32[]{:T(128)} %convert_element_type.4, () %tuple.74, ...), branch_computations={%region_10.0_spmd, %region_11.0_spmd} | conditional | bytes 80 | solution.py:922
  94.4 1.3 collective-permute-start.9
  95.7 39.5 %collective-permute-done.10 = bf16[624,768]{1,0:T(8,128)(2,1)} collective-permute-done((bf16[624,768]{1,0:T(8,128)(2,1)}, bf16[624,768]{1,0:T(8,128)(2,1)}, u32[]{:S(2)}, u32[]{:S(2)}) %collective-permute-start.10) | collective-permute-done | bytes 958496 | tf_op jit(solution)/shard_map/ppermute | solution.py:936
  135.2 27.7 %conditional.14 = ((bf16[624,768]{1,0:T(8,128)(2,1)}, bf16[624,3072]{1,0:T(8,128)(2,1)}, bf16[624,768]{1,0:T(8,128)(2,1)}, bf16[3,624,768]{2,1,0:T(8,128)(2,1)},...) conditional(s32[]{:T(128)} %convert_element_type.5, ...), branch_computations={%region_12.0_spmd, %region_13.0_spmd} | conditional | bytes 80 | solution.py:922
  135.6 27.3 %bwd.6 = (bf16[624,3072]{1,0:T(8,128)(2,1)}, bf16[624,768]{1,0:T(8,128)(2,1)}, bf16[3,624,768]{2,1,0:T(8,128)(2,1)}, bf16[624,768]{1,0:T(8,128)(2,1)}, bf16[624,...) custom-call(bf16[624,768]{1,0:T(8,128)(2,1)} %get-tuple-element.464.refs_0_,, ...), custom_call_target="tpu_custom_call" | custom-call | tf_op jit(solution)/shard_map/cond/branch_1_fun/bwd/pallas_call | solution.py:431
  163.0 8.4 %wgrad_attn.1 = (bf16[3,768,384]{2,1,0:T(8,128)(2,1)}, bf16[3,768,384]{2,1,0:T(8,128)(2,1)}, bf16[384,768]{1,0:T(8,128)(2,1)}, bf16[384,768]{1,0:T(8,128)(2,1)}) custom-call(bf16[624,768]{1,0:T(8,128)(2,1)} %get-tuple-element.644.refs_0_, bf16[3,624,768]{2,1,0:T(8,128)(2,1)} %get-tuple-element.645.refs_1_, bf16[624,768]{1,0:T(8,128)(2,1)} %get-tuple-element.623.refs_2_, ...), custom_call_target="tpu_custom_call" | custom-call | tf_op jit(solution)/shard_map/wgrad_attn/pallas_call | solution.py:510
  171.4 13.4 %wgrad_mlp.2 = (bf16[1536,768]{1,0:T(8,128)(2,1)}, bf16[1536,768]{1,0:T(8,128)(2,1)}, bf16[768,1536]{1,0:T(8,128)(2,1)}, bf16[768,1536]{1,0:T(8,128)(2,1)}) custom-call(bf16[624,3072]{1,0:T(8,128)(2,1)S(1)} %copy-done.3, bf16[624,768]{1,0:T(8,128)(2,1)} %get-tuple-element.636.n2, bf16[624,3072]{1,0:T(8,128)(2,1)} %get-tuple-element.638.pre, ...), custom_call_target="tpu_custom_call" | custom-call | tf_op jit(solution)/shard_map/wgrad_mlp/pallas_call | solution.py:473
  184.9 5.9 %join.2 = bf16[2336,768]{1,0:T(8,128)(2,1)} custom-call(s32[3]{0:T(128)} %pad_add_fusion.meta_ref, bf16[592,768]{1,0:T(8,128)(2,1)S(1)} %copy-done.9, bf16[624,768]{1,0:T(8,128)(2,1)} %get-tuple-element.627.refs_1_, bf16[592,768]{1,0:T(8,128)(2,1)} %collective-permute-done.7.refs_2_, bf16[624,768]{1,0:T(8,128)(2,1)} %collective-permute-done.8.refs_3_), custom_call_target="tpu_custom_call" | custom-call | tf_op jit(solution)/shard_map/join/pallas_call | solution.py:853
  190.7 5.3 %collective-permute-done.9 = bf16[592,768]{1,0:T(8,128)(2,1)} collective-permute-done((bf16[592,768]{1,0:T(8,128)(2,1)}, bf16[592,768]{1,0:T(8,128)(2,1)}, u32[]{:S(2)}, u32[]{:S(2)}) %collective-permute-start.9) | collective-permute-done | bytes 909344 | tf_op jit(solution)/shard_map/ppermute | solution.py:936
  196.0 31.7 %conditional.15 = ((bf16[592,768]{1,0:T(8,128)(2,1)}, bf16[592,3072]{1,0:T(8,128)(2,1)}, bf16[592,768]{1,0:T(8,128)(2,1)}, bf16[3,592,768]{2,1,0:T(8,128)(2,1)},...) conditional(s32[]{:T(128)} %convert_element_type.5, ...), branch_computations={%region_14.0_spmd, %region_15.0_spmd} | conditional | bytes 80 | solution.py:922
  196.2 31.4 %bwd.7 = (bf16[592,3072]{1,0:T(8,128)(2,1)}, bf16[592,768]{1,0:T(8,128)(2,1)}, bf16[3,592,768]{2,1,0:T(8,128)(2,1)}, bf16[592,768]{1,0:T(8,128)(2,1)}, bf16[592,...) custom-call(bf16[592,768]{1,0:T(8,128)(2,1)} %get-tuple-element.490.refs_0_,, ...), custom_call_target="tpu_custom_call" | custom-call | tf_op jit(solution)/shard_map/cond/branch_1_fun/bwd/pallas_call | solution.py:431
  228.0 16.1 %wgrad_mlp.3 = (bf16[1536,768]{1,0:T(8,128)(2,1)}, bf16[1536,768]{1,0:T(8,128)(2,1)}, bf16[768,1536]{1,0:T(8,128)(2,1)}, bf16[768,1536]{1,0:T(8,128)(2,1)}) custom-call(bf16[592,3072]{1,0:T(8,128)(2,1)} %get-tuple-element.657.act, bf16[592,768]{1,0:T(8,128)(2,1)} %get-tuple-element.658.n2, bf16[592,3072]{1,0:T(8,128)(2,1)} %get-tuple-element.659.pre, ...), custom_call_target="tpu_custom_call" | custom-call | tf_op jit(solution)/shard_map/wgrad_mlp/pallas_call | solution.py:473
  244.2 157.5 %ring.1 = (bf16[1536,768]{1,0:T(8,128)(2,1)}, bf16[768,1536]{1,0:T(8,128)(2,1)}, bf16[2304,384]{1,0:T(8,128)(2,1)}, bf16[384,768]{1,0:T(8,128)(2,1)}, f32[16,768]{1,0:T(8,128)}) custom-call(bf16[592,768]{1,0:T(8,128)(2,1)S(1)} %copy-done.6, bf16[3,592,768]{2,1,0:T(8,128)(2,1)S(1)} %copy-done.4, bf16[592,768]{1,0:T(8,128)(2,1)S(1)} %copy-done.2, ...), custom_call_target="tpu_custom_call" | custom-call | tf_op jit(solution)/shard_map/ring/pallas_call | solution.py:714
  401.7 9.4 %finish.1 = (f32[1,1536,768]{2,1,0:T(8,128)}, f32[1,768,1536]{2,1,0:T(8,128)}, f32[1,2304,384]{2,1,0:T(8,128)}, f32[1,384,768]{2,1,0:T(8,128)}, f32[1,768]{1,0:T...) custom-call(bf16[1536,768]{1,0:T(8,128)(2,1)} %get-tuple-element.673, ...), custom_call_target="tpu_custom_call" | custom-call | tf_op jit(solution)/shard_map/finish/pallas_call | solution.py:770
  411.2 0.9 copy-done.8
  412.1 5.4 %join.3 = bf16[2336,768]{1,0:T(8,128)(2,1)} custom-call(s32[3]{0:T(128)} %pad_add_fusion.meta_ref, bf16[592,768]{1,0:T(8,128)(2,1)S(1)} %copy-done.10, bf16[624,768]{1,0:T(8,128)(2,1)S(1)} %copy-done.5, bf16[592,768]{1,0:T(8,128)(2,1)} %copy-done.8, bf16[624,768]{1,0:T(8,128)(2,1)} %collective-permute-done.12.refs_3_), custom_call_target="tpu_custom_call" | custom-call | tf_op jit(solution)/shard_map/join/pallas_call | solution.py:853
  (67 shorter events, 2.7 us)
Async XLA Ops:
  0.6 11.9 %copy-start = (bf16[1,768,1536]{2,1,0:T(8,128)(2,1)S(1)}, bf16[1,768,1536]{2,1,0:T(8,128)(2,1)}, u32[]{:S(2)}) copy-start(bf16[1,768,1536]{2,1,0:T(8,128)(2,1)} %param.42) | copy-start | bytes 7077892
  0.7 11.9 %copy-start.1 = (bf16[1,384,768]{2,1,0:T(8,128)(2,1)S(1)}, bf16[1,384,768]{2,1,0:T(8,128)(2,1)}, u32[]{:S(2)}) copy-start(bf16[1,384,768]{2,1,0:T(8,128)(2,1)} %param.38) | copy-start | bytes 1769476
  0.7 11.9 %copy-start.11 = (f32[1,768]{1,0:T(1,128)S(1)}, f32[1,768]{1,0:T(1,128)}, u32[]{:S(2)}) copy-start(f32[1,768]{1,0:T(1,128)} %param.34) | copy-start | bytes 9220
  0.7 11.9 %copy-start.13 = (f32[1,768]{1,0:T(1,128)S(1)}, f32[1,768]{1,0:T(1,128)}, u32[]{:S(2)}) copy-start(f32[1,768]{1,0:T(1,128)} %param.35) | copy-start | bytes 9220
  0.7 11.9 %copy-start.14 = (f32[1,768]{1,0:T(1,128)S(1)}, f32[1,768]{1,0:T(1,128)}, u32[]{:S(2)}) copy-start(f32[1,768]{1,0:T(1,128)} %param.39) | copy-start | bytes 9220
  0.7 11.9 %copy-start.12 = (f32[1,768]{1,0:T(1,128)S(1)}, f32[1,768]{1,0:T(1,128)}, u32[]{:S(2)}) copy-start(f32[1,768]{1,0:T(1,128)} %param.40) | copy-start | bytes 9220
  0.7 11.8 %collective-permute-start.3 = (bf16[768,1536]{1,0:T(8,128)(2,1)}, bf16[768,1536]{1,0:T(8,128)(2,1)}, u32[]{:S(2)}, u32[]{:S(2)}) collective-permute-start(bf16[768,1536]{1,0:T(8,128)(2,1)} %bitcast.10), channel_id=1, source_target_pairs={{0,8},{8,0},{1,9},{9,1},{2,10},{10,2},{3,11},{11,3},{4,12},{12,4},... | collective-permute-start | bytes 7077896 | tf_op jit(solution)/shard_map/ppermute | solution.py:901
  1.3 11.3 %collective-permute-start.4 = (bf16[1536,768]{1,0:T(8,128)(2,1)}, bf16[1536,768]{1,0:T(8,128)(2,1)}, u32[]{:S(2)}, u32[]{:S(2)}) collective-permute-start(bf16[1536,768]{1,0:T(8,128)(2,1)} %bitcast.19), channel_id=1, source_target_pairs={{0,8},{8,0},{1,9},{9,1},{2,10},{10,2},{3,11},{11,3},{4,12},{12,4},... | collective-permute-start | bytes 7077896 | tf_op jit(solution)/shard_map/ppermute | solution.py:901
  1.3 11.2 %collective-permute-start.1 = (bf16[3,768,384]{2,1,0:T(8,128)(2,1)}, bf16[3,768,384]{2,1,0:T(8,128)(2,1)}, u32[]{:S(2)}, u32[]{:S(2)}) collective-permute-start(bf16[3,768,384]{2,1,0:T(8,128)(2,1)} %bitcast.28), channel_id=1, source_target_pairs={{0,8},{8,0},{1,9},{9,1},{2,10},{10,2},{3,11},{11,3},{4,12},{12,4},... | collective-permute-start | bytes 5308424 | tf_op jit(solution)/shard_map/ppermute | solution.py:901
  1.8 10.8 %collective-permute-start.2 = (bf16[384,768]{1,0:T(8,128)(2,1)}, bf16[384,768]{1,0:T(8,128)(2,1)S(1)}, u32[]{:S(2)}, u32[]{:S(2)}) collective-permute-start(bf16[384,768]{1,0:T(8,128)(2,1)} %bitcast.37), channel_id=1, source_target_pairs={{0,8},{8,0},{1,9},{9,1},{2,10},{10,2},{3,11},{11,3},{4,12},{12,4},... | collective-permute-start | bytes 1769480 | tf_op jit(solution)/shard_map/ppermute | solution.py:901
  4.4 8.1 %collective-permute-start = (f32[1,2304]{1,0:T(1,128)}, f32[1,2304]{1,0:T(1,128)}, u32[]{:S(2)}, u32[]{:S(2)}) collective-permute-start(f32[1,2304]{1,0:T(1,128)} %constant_dynamic-update-slice_fusion), channel_id=1, source_target_pairs={{0,8},{8,0},{1,9},{9,1},{2,10},{10,2},{3,11},{11,3},{4,12},{12,4},... | collective-permute-start | bytes 27656 | tf_op jit(solution)/shard_map/ppermute | solution.py:901
  35.8 36.3 %collective-permute-start.6 = (bf16[624,768]{1,0:T(8,128)(2,1)}, bf16[624,768]{1,0:T(8,128)(2,1)}, u32[]{:S(2)}, u32[]{:S(2)}) collective-permute-start(bf16[624,768]{1,0:T(8,128)(2,1)} %get-tuple-element.614), channel_id=1, source_target_pairs={{0,16},{1,17},{2,18},{3,19},{4,20},{5,21},{6,22},{7,23},{8,24},{9,... | collective-permute-start | bytes 2875400 | tf_op jit(solution)/shard_map/ppermute | solution.py:935
  65.3 21.9 %collective-permute-start.5 = (bf16[592,768]{1,0:T(8,128)(2,1)}, bf16[592,768]{1,0:T(8,128)(2,1)}, u32[]{:S(2)}, u32[]{:S(2)}) collective-permute-start(bf16[592,768]{1,0:T(8,128)(2,1)} %get-tuple-element.616), channel_id=1, source_target_pairs={{0,16},{1,17},{2,18},{3,19},{4,20},{5,21},{6,22},{7,23},{8,24},{9,... | collective-permute-start | bytes 2727944 | tf_op jit(solution)/shard_map/ppermute | solution.py:935
  79.4 55.8 %collective-permute-start.10 = (bf16[624,768]{1,0:T(8,128)(2,1)}, bf16[624,768]{1,0:T(8,128)(2,1)}, u32[]{:S(2)}, u32[]{:S(2)}) collective-permute-start(bf16[624,768]{1,0:T(8,128)(2,1)} %get-tuple-element.624), channel_id=1, source_target_pairs={{16,0},{17,1},{18,2},{19,3},{20,4},{21,5},{22,6},{23,7},{24,8},{25... | collective-permute-start | bytes 2875400 | tf_op jit(solution)/shard_map/ppermute | solution.py:936
  80.7 104.1 %collective-permute-start.8 = (bf16[624,768]{1,0:T(8,128)(2,1)}, bf16[624,768]{1,0:T(8,128)(2,1)}, u32[]{:S(2)}, u32[]{:S(2)}) collective-permute-start(bf16[624,768]{1,0:T(8,128)(2,1)} %get-tuple-element.627.refs_1_), channel_id=1, source_target_pairs={{0,8},{8,0},{1,9},{9,1},{2,10},{10,2},{3,11},{11,3},{4,12},{12,4},... | collective-permute-start | bytes 2875400 | tf_op jit(solution)/shard_map/ppermute | solution.py:901
  87.3 97.5 %collective-permute-start.7 = (bf16[592,768]{1,0:T(8,128)(2,1)}, bf16[592,768]{1,0:T(8,128)(2,1)}, u32[]{:S(2)}, u32[]{:S(2)}) collective-permute-start(bf16[592,768]{1,0:T(8,128)(2,1)} %get-tuple-element.626.refs_0_), channel_id=1, source_target_pairs={{0,8},{8,0},{1,9},{9,1},{2,10},{10,2},{3,11},{11,3},{4,12},{12,4},... | collective-permute-start | bytes 2727944 | tf_op jit(solution)/shard_map/ppermute | solution.py:901
  94.4 101.6 %collective-permute-start.9 = (bf16[592,768]{1,0:T(8,128)(2,1)}, bf16[592,768]{1,0:T(8,128)(2,1)}, u32[]{:S(2)}, u32[]{:S(2)}) collective-permute-start(bf16[592,768]{1,0:T(8,128)(2,1)} %get-tuple-element.634), channel_id=1, source_target_pairs={{16,0},{17,1},{18,2},{19,3},{20,4},{21,5},{22,6},{23,7},{24,8},{25... | collective-permute-start | bytes 2727944 | tf_op jit(solution)/shard_map/ppermute | solution.py:936
  162.9 248.3 %collective-permute-start.12 = (bf16[624,768]{1,0:T(8,128)(2,1)}, bf16[624,768]{1,0:T(8,128)(2,1)}, u32[]{:S(2)}, u32[]{:S(2)}) collective-permute-start(bf16[624,768]{1,0:T(8,128)(2,1)} %get-tuple-element.653.refs_1_), channel_id=1, source_target_pairs={{0,8},{8,0},{1,9},{9,1},{2,10},{10,2},{3,11},{11,3},{4,12},{12,4},... | collective-permute-start | bytes 2875400 | tf_op jit(solution)/shard_map/ppermute | solution.py:901
  171.4 13.5 %copy-start.9 = (bf16[592,768]{1,0:T(8,128)(2,1)S(1)}, bf16[592,768]{1,0:T(8,128)(2,1)}, u32[]{:S(2)}) copy-start(bf16[592,768]{1,0:T(8,128)(2,1)} %get-tuple-element.626.refs_0_) | copy-start | bytes 2727940
  227.8 183.4 %collective-permute-start.11 = (bf16[592,768]{1,0:T(8,128)(2,1)}, bf16[592,768]{1,0:T(8,128)(2,1)S(1)}, u32[]{:S(2)}, u32[]{:S(2)}) collective-permute-start(bf16[592,768]{1,0:T(8,128)(2,1)} %get-tuple-element.652.refs_0_), channel_id=1, source_target_pairs={{0,8},{8,0},{1,9},{9,1},{2,10},{10,2},{3,11},{11,3},{4,12},{12,4},... | collective-permute-start | bytes 2727944 | tf_op jit(solution)/shard_map/ppermute | solution.py:901
  227.8 16.2 %copy-start.2 = (bf16[592,768]{1,0:T(8,128)(2,1)S(1)}, bf16[592,768]{1,0:T(8,128)(2,1)}, u32[]{:S(2)}) copy-start(bf16[592,768]{1,0:T(8,128)(2,1)} %get-tuple-element.633.refs_2_) | copy-start | bytes 2727940
  227.9 16.2 %copy-start.4 = (bf16[3,592,768]{2,1,0:T(8,128)(2,1)S(1)}, bf16[3,592,768]{2,1,0:T(8,128)(2,1)}, u32[]{:S(2)}) copy-start(bf16[3,592,768]{2,1,0:T(8,128)(2,1)} %get-tuple-element.655.refs_1_) | copy-start | bytes 8183812
  227.9 16.2 %copy-start.6 = (bf16[592,768]{1,0:T(8,128)(2,1)S(1)}, bf16[592,768]{1,0:T(8,128)(2,1)}, u32[]{:S(2)}) copy-start(bf16[592,768]{1,0:T(8,128)(2,1)} %get-tuple-element.654.refs_0_) | copy-start | bytes 2727940
  227.9 16.2 %copy-start.7 = (bf16[592,768]{1,0:T(8,128)(2,1)S(1)}, bf16[592,768]{1,0:T(8,128)(2,1)}, u32[]{:S(2)}) copy-start(bf16[592,768]{1,0:T(8,128)(2,1)} %get-tuple-element.656.refs_3_) | copy-start | bytes 2727940
  227.9 16.2 %copy-start.15 = (f32[8,768]{1,0:T(8,128)S(1)}, f32[8,768]{1,0:T(8,128)}, u32[]{:S(2)}) copy-start(f32[8,768]{1,0:T(8,128)} %get-tuple-element.666.refs_13_) | copy-start | bytes 73732
  227.9 16.2 %copy-start.16 = (f32[8,768]{1,0:T(8,128)S(1)}, f32[8,768]{1,0:T(8,128)}, u32[]{:S(2)}) copy-start(f32[8,768]{1,0:T(8,128)} %get-tuple-element.667.refs_14_) | copy-start | bytes 73732
  227.9 16.2 %copy-start.17 = (f32[8,768]{1,0:T(8,128)S(1)}, f32[8,768]{1,0:T(8,128)}, u32[]{:S(2)}) copy-start(f32[8,768]{1,0:T(8,128)} %get-tuple-element.665.refs_12_) | copy-start | bytes 73732
  227.9 16.2 %copy-start.18 = (f32[8,768]{1,0:T(8,128)S(1)}, f32[8,768]{1,0:T(8,128)}, u32[]{:S(2)}) copy-start(f32[8,768]{1,0:T(8,128)} %get-tuple-element.670.refs_17_) | copy-start | bytes 73732
  227.9 16.2 %copy-start.19 = (f32[8,768]{1,0:T(8,128)S(1)}, f32[8,768]{1,0:T(8,128)}, u32[]{:S(2)}) copy-start(f32[8,768]{1,0:T(8,128)} %get-tuple-element.671.refs_18_) | copy-start | bytes 73732
  227.9 16.2 %copy-start.20 = (f32[8,768]{1,0:T(8,128)S(1)}, f32[8,768]{1,0:T(8,128)}, u32[]{:S(2)}) copy-start(f32[8,768]{1,0:T(8,128)} %get-tuple-element.669.refs_16_) | copy-start | bytes 73732
  227.9 16.2 %copy-start.21 = (f32[1,3072]{1,0:T(1,128)S(1)}, f32[1,3072]{1,0:T(1,128)}, u32[]{:S(2)}) copy-start(f32[1,3072]{1,0:T(1,128)} %get-tuple-element.668.refs_15_) | copy-start | bytes 36868
  228.0 16.2 %copy-start.22 = (f32[1,3072]{1,0:T(1,128)S(1)}, f32[1,3072]{1,0:T(1,128)}, u32[]{:S(2)}) copy-start(f32[1,3072]{1,0:T(1,128)} %get-tuple-element.672.refs_19_) | copy-start | bytes 36868
  (4 other events, 30.1 us)

commit v7 on v6

--- a/solution.py
+++ b/solution.py
@@ -555,17 +555,19 @@
     normed, dqkv, att, gb = refs[:4]
     parts, sums = refs[4:8], refs[12:20]
     at = 20
-    outs, vsum_ref = refs[at : at + n], refs[at + n]
+    results, vsum_ref = refs[at : at + n], refs[at + n]
     at += n + 1
-    theirs = refs[at : at + n]
-    at += n
+    outs, theirs = refs[at : at + n], refs[at + n : at + 2 * n]
+    at += 2 * n
     own_qkv, own_pw, gift_qkv, gift_pw = refs[at : at + 4]
     owns = refs[8:10] + (own_qkv, own_pw)
     gifts = refs[10:12] + (gift_qkv, gift_pw)
     at += 4
     m = len(items)
     slots = refs[at : at + m]
-    vbuf, vother, vmine, vslot, send, recv, xsend, xrecv, vsend, vrecv, vxs, vxr = refs[at + m :]
+    vbuf, vother, vmine, vslot, send, recv, xsend, xrecv, flushed, vsend, vrecv, vxs, vxr = refs[
+        at + m :
+    ]
     mesh_id = pl.DeviceIdType.MESH
     me = lax.axis_index("dp")
     partner = {"tensor": 1 - lax.axis_index("tensor")}
@@ -613,6 +615,12 @@
             recv_sem=recv.at[a, step],
             device_id=member(pos + items[a][3] + RING),
             device_id_type=mesh_id,
+        )
+
+    def flush(a, k):
+        chunk = chunk_at(a, k - 1)
+        return pltpu.make_async_copy(
+            part(outs, a, chunk), part(results, a, chunk), flushed.at[a, k]
         )
 
     def vcopy(k):
@@ -675,12 +683,14 @@
         done = part(outs, a, chunk_at(a, RING - 1))
         done[...] = (last[...].astype(F32) + own).astype(BF)
         remote(done, done, a, RING - 1).start()
+        flush(a, 0).start()
 
     def gather(t, carry):
         for a in range(m):
             here = part(outs, a, chunk_at(a, t - 1))
             remote(here, here, a, RING - 2 + t).wait_recv()
             remote(here, here, a, RING - 1 + t).start()
+            flush(a, t).start()
         return carry
 
     lax.fori_loop(1, RING - 1, gather, 0)
@@ -692,6 +702,7 @@
     for a in range(m):
         here = part(outs, a, chunk_at(a, RING - 2))
         remote(here, here, a, 2 * RING - 3).wait_recv()
+        flush(a, RING - 1).start()
     for a in range(m):
         for s in range(RING - 1):
             remote(slots[a].at[0], slots[a].at[0], a, s).wait_send()
@@ -699,6 +710,7 @@
             remote(here, here, a, RING - 1 + s).wait_send()
         for s in range(RING):
             exchange(a, s).wait_send()
+            flush(a, s).wait()
 
 
 def ring(mlp, kept, back, parts, sums):
@@ -714,13 +726,14 @@
     out = pl.pallas_call(
         functools.partial(ring_kernel, n=n, items=items, fold=sums[3].shape[1] // (2 * d)),
         in_specs=[vmem] * 10 + [hbm] * 2 + [vmem] * 8,
-        out_specs=[vmem] * (n + 1),
+        out_specs=[hbm] * n + [vmem],
         out_shape=[sds(a, BF) for a in shapes] + [sds((VEC_ROWS, d), F32)],
-        scratch_shapes=[pltpu.VMEM(a, BF) for a in shapes + 2 * shapes[2:]]
+        scratch_shapes=[pltpu.VMEM(a, BF) for a in 2 * shapes + 2 * shapes[2:]]
         + [pltpu.VMEM((RING, rows // RING, shapes[i][1]), BF) for i, _, rows, _ in items]
         + [
             vec, vec, vec, pltpu.VMEM((RING - 1, VEC_ROWS, d), F32),
             dma((m, 2 * RING - 2)), dma((m, 2 * RING - 2)), dma((m, RING)), dma((m, RING)),
+            dma((m, RING)),
             dma((RING - 1,)), dma((RING - 1,)), dma, dma,
         ],
         compiler_params=params(collective_id=1, has_side_effects=True),
@@ -833,15 +846,14 @@
     mine, theirs, out_ref, flat = refs[:count], refs[count : 2 * count], refs[-2], refs[-1]
     rows = flat.shape[0]
     for lane in range(2):
-        here = meta_ref[0] == lane
         for place in range(SMALL_MB + 1):
-
-            @pl.when(meta_ref[1 + lane] == place)
-            def _():
-                for start, c, r0, plen, vlen in layout(place):
-                    own = mine[c][r0 : r0 + plen].astype(F32)
-                    value = jnp.where(here, own, theirs[c][r0 : r0 + plen].astype(F32))
-                    flat[start : start + vlen] = value[:vlen]
+            for own, source in ((True, mine), (False, theirs)):
+
+                @pl.when((meta_ref[1 + lane] == place) & ((meta_ref[0] == lane) == own))
+                def _():
+                    for start, c, r0, plen, vlen in layout(place):
+                        value = source[c][r0 : r0 + plen].astype(F32)
+                        flat[start : start + vlen] = value[:vlen]
 
         out_ref[lane * rows : (lane + 1) * rows] = flat[...].astype(BF)
 

time: 425 us -> 423 us (level)
  no operation moved by 1% of the time
where the time goes in v7:
time: 423 us; the launch traced here: 416 us
  Pallas kernels  332 us (78%)
  waiting for transfers between devices  52.7 us (12%)
  loops' own time  15.7 us (4%)
  starting transfers between devices  9.32 us (2%)
    pallas_call x1, Pallas kernels, ring(): pl.pallas_call(functools.partial(ring_kernel, n=n, items=items, fold=sums...  156 us
    pallas_call x2, Pallas kernels, backward(): pl.pallas_call(functools.partial(bwd_kernel, chunk=chunk), in_specs=[vmem...  58.6 us
    pallas_call x2, Pallas kernels, forward(): pl.pallas_call(functools.partial(fwd_kernel, chunk=chunk), in_specs=[vmem...  50.2 us
    ppermute x2, waiting for transfers between devices, body(): up_ = lambda array: lax.ppermute(array, 'section', [(1, 0)])  44.7 us
    pallas_call x2, Pallas kernels, wgrad_mlp(): pl.pallas_call(functools.partial(wgrad_mlp_kernel, more=len(init)), grid=...  29.5 us
    another operation x8, loops' own time, pick(): lax.cond(section == on, lambda: tuple(make()), lambda: blank(like) if oth...  15.7 us
    pallas_call x2, Pallas kernels, join(): pl.pallas_call(join_kernel, grid_spec=pltpu.PrefetchScalarGridSpec(num_sc...  11 us
    pallas_call x1, Pallas kernels, finish(): pl.pallas_call(functools.partial(finish_kernel, fold=fold), grid=(steps,)...  9.44 us
  transfers between devices with their start and end apart: 13, of which 4 were waited for; matrix products, arithmetic and copies ran while one was open for 1% of the time, Pallas kernels for 73%

profile of v7, /device:TPU:0, one launch (start us, length us, event | category | flops | bytes accessed | tf_op | source)
XLA Modules:
  0.0 416.2 jit_solution(6223394420362291542)
XLA Ops:
  1.9 0.7 copy.29
  2.5 0.6 constant_dynamic-update-slice_fusion.1
  3.1 1.3 constant_dynamic-update-slice_fusion
  4.9 1.2 pad_add_fusion.meta_ref
  6.1 4.5 %cut.2 = (bf16[592,768]{1,0:T(8,128)(2,1)}, bf16[624,768]{1,0:T(8,128)(2,1)}) custom-call(s32[3]{0:T(128)} %pad_add_fusion.meta_ref, bf16[2336,768]{1,0:T(8,128)(2,1)} %x_ref.2), custom_call_target="tpu_custom_call" | custom-call | tf_op jit(solution)/shard_map/cut/pallas_call | solution.py:829
  10.6 1.9 collective-permute-done
  12.6 23.2 %conditional.8 = ((bf16[624,768]{1,0:T(8,128)(2,1)}, bf16[3,624,768]{2,1,0:T(8,128)(2,1)}, bf16[624,768]{1,0:T(8,128)(2,1)}, f32[6,1,1536]{2,1,0:T(1,128)}, f32[...) conditional(s32[]{:T(128)} %convert_element_type.5, () %tuple.63, ...), branch_computations={%region_0.0_spmd, %region_1.0_spmd} | conditional | bytes 8 | solution.py:934
  12.6 23.2 %fwd.4 = (bf16[624,768]{1,0:T(8,128)(2,1)}, bf16[3,624,768]{2,1,0:T(8,128)(2,1)}, bf16[624,768]{1,0:T(8,128)(2,1)}, f32[6,1,1536]{2,1,0:T(1,128)}, f32[624,768]{...) custom-call(bf16[624,768]{1,0:T(8,128)(2,1)} %get-tuple-element.344., ...), custom_call_target="tpu_custom_call" | custom-call | tf_op jit(solution)/shard_map/cond/branch_1_fun/fwd/pallas_call | solution.py:259
  35.8 2.2 collective-permute-start.6
  38.1 27.2 %conditional.9 = ((bf16[592,768]{1,0:T(8,128)(2,1)}, bf16[3,592,768]{2,1,0:T(8,128)(2,1)}, bf16[592,768]{1,0:T(8,128)(2,1)}, f32[6,1,1280]{2,1,0:T(1,128)}, f32[...) conditional(s32[]{:T(128)} %convert_element_type.5, () %tuple.62, ...), branch_computations={%region_2.0_spmd, %region_3.0_spmd} | conditional | bytes 8 | solution.py:934
  38.3 27.0 %fwd.5 = (bf16[592,768]{1,0:T(8,128)(2,1)}, bf16[3,592,768]{2,1,0:T(8,128)(2,1)}, bf16[592,768]{1,0:T(8,128)(2,1)}, f32[6,1,1280]{2,1,0:T(1,128)}, f32[592,768]{...) custom-call(bf16[592,768]{1,0:T(8,128)(2,1)} %get-tuple-element.361., ...), custom_call_target="tpu_custom_call" | custom-call | tf_op jit(solution)/shard_map/cond/branch_1_fun/fwd/pallas_call | solution.py:259
  65.3 2.3 collective-permute-start.5
  67.6 4.5 %cut.3 = (bf16[592,768]{1,0:T(8,128)(2,1)}, bf16[624,768]{1,0:T(8,128)(2,1)}) custom-call(s32[3]{0:T(128)} %pad_add_fusion.meta_ref, bf16[2336,768]{1,0:T(8,128)(2,1)} %x_ref.3), custom_call_target="tpu_custom_call" | custom-call | tf_op jit(solution)/shard_map/cut/pallas_call | solution.py:829
  72.3 7.1 %conditional.11 = ((bf16[624,768]{1,0:T(8,128)(2,1)}, bf16[624,3072]{1,0:T(8,128)(2,1)}, bf16[624,768]{1,0:T(8,128)(2,1)}, bf16[3,624,768]{2,1,0:T(8,128)(2,1)},...) conditional(s32[]{:T(128)} %convert_element_type.4, () %tuple.68, ...), branch_computations={%region_6.0_spmd, %region_7.0_spmd} | conditional | bytes 80 | solution.py:934
  79.4 1.3 collective-permute-start.10
  81.2 6.0 %collective-permute-done.5 = bf16[592,768]{1,0:T(8,128)(2,1)} collective-permute-done((bf16[592,768]{1,0:T(8,128)(2,1)}, bf16[592,768]{1,0:T(8,128)(2,1)}, u32[]{:S(2)}, u32[]{:S(2)}) %collective-permute-start.5) | collective-permute-done | bytes 909344 | tf_op jit(solution)/shard_map/ppermute | solution.py:947
  87.4 7.0 %conditional.13 = ((bf16[592,768]{1,0:T(8,128)(2,1)}, bf16[592,3072]{1,0:T(8,128)(2,1)}, bf16[592,768]{1,0:T(8,128)(2,1)}, bf16[3,592,768]{2,1,0:T(8,128)(2,1)},...) conditional(s32[]{:T(128)} %convert_element_type.4, () %tuple.74, ...), branch_computations={%region_10.0_spmd, %region_11.0_spmd} | conditional | bytes 80 | solution.py:934
  94.4 1.3 collective-permute-start.9
  95.7 39.5 %collective-permute-done.10 = bf16[624,768]{1,0:T(8,128)(2,1)} collective-permute-done((bf16[624,768]{1,0:T(8,128)(2,1)}, bf16[624,768]{1,0:T(8,128)(2,1)}, u32[]{:S(2)}, u32[]{:S(2)}) %collective-permute-start.10) | collective-permute-done | bytes 958496 | tf_op jit(solution)/shard_map/ppermute | solution.py:948
  135.2 27.9 %conditional.14 = ((bf16[624,768]{1,0:T(8,128)(2,1)}, bf16[624,3072]{1,0:T(8,128)(2,1)}, bf16[624,768]{1,0:T(8,128)(2,1)}, bf16[3,624,768]{2,1,0:T(8,128)(2,1)},...) conditional(s32[]{:T(128)} %convert_element_type.5, ...), branch_computations={%region_12.0_spmd, %region_13.0_spmd} | conditional | bytes 80 | solution.py:934
  135.5 27.2 %bwd.6 = (bf16[624,3072]{1,0:T(8,128)(2,1)}, bf16[624,768]{1,0:T(8,128)(2,1)}, bf16[3,624,768]{2,1,0:T(8,128)(2,1)}, bf16[624,768]{1,0:T(8,128)(2,1)}, bf16[624,...) custom-call(bf16[624,768]{1,0:T(8,128)(2,1)} %get-tuple-element.464.refs_0_,, ...), custom_call_target="tpu_custom_call" | custom-call | tf_op jit(solution)/shard_map/cond/branch_1_fun/bwd/pallas_call | solution.py:431
  163.3 8.4 %wgrad_attn.1 = (bf16[3,768,384]{2,1,0:T(8,128)(2,1)}, bf16[3,768,384]{2,1,0:T(8,128)(2,1)}, bf16[384,768]{1,0:T(8,128)(2,1)}, bf16[384,768]{1,0:T(8,128)(2,1)}) custom-call(bf16[624,768]{1,0:T(8,128)(2,1)} %get-tuple-element.644.refs_0_, bf16[3,624,768]{2,1,0:T(8,128)(2,1)} %get-tuple-element.645.refs_1_, bf16[624,768]{1,0:T(8,128)(2,1)} %get-tuple-element.623.refs_2_, ...), custom_call_target="tpu_custom_call" | custom-call | tf_op jit(solution)/shard_map/wgrad_attn/pallas_call | solution.py:510
  171.7 13.4 %wgrad_mlp.2 = (bf16[1536,768]{1,0:T(8,128)(2,1)}, bf16[1536,768]{1,0:T(8,128)(2,1)}, bf16[768,1536]{1,0:T(8,128)(2,1)}, bf16[768,1536]{1,0:T(8,128)(2,1)}) custom-call(bf16[624,3072]{1,0:T(8,128)(2,1)S(1)} %copy-done.3, bf16[624,768]{1,0:T(8,128)(2,1)} %get-tuple-element.636.n2, bf16[624,3072]{1,0:T(8,128)(2,1)} %get-tuple-element.638.pre, ...), custom_call_target="tpu_custom_call" | custom-call | tf_op jit(solution)/shard_map/wgrad_mlp/pallas_call | solution.py:473
  185.1 5.7 %join.2 = bf16[2336,768]{1,0:T(8,128)(2,1)} custom-call(s32[3]{0:T(128)} %pad_add_fusion.meta_ref, bf16[592,768]{1,0:T(8,128)(2,1)S(1)} %copy-done.9, bf16[624,768]{1,0:T(8,128)(2,1)} %get-tuple-element.627.refs_1_, bf16[592,768]{1,0:T(8,128)(2,1)} %collective-permute-done.7.refs_2_, bf16[624,768]{1,0:T(8,128)(2,1)} %collective-permute-done.8.refs_3_), custom_call_target="tpu_custom_call" | custom-call | tf_op jit(solution)/shard_map/join/pallas_call | solution.py:865
  190.8 5.2 %collective-permute-done.9 = bf16[592,768]{1,0:T(8,128)(2,1)} collective-permute-done((bf16[592,768]{1,0:T(8,128)(2,1)}, bf16[592,768]{1,0:T(8,128)(2,1)}, u32[]{:S(2)}, u32[]{:S(2)}) %collective-permute-start.9) | collective-permute-done | bytes 909344 | tf_op jit(solution)/shard_map/ppermute | solution.py:948
  196.0 31.7 %conditional.15 = ((bf16[592,768]{1,0:T(8,128)(2,1)}, bf16[592,3072]{1,0:T(8,128)(2,1)}, bf16[592,768]{1,0:T(8,128)(2,1)}, bf16[3,592,768]{2,1,0:T(8,128)(2,1)},...) conditional(s32[]{:T(128)} %convert_element_type.5, ...), branch_computations={%region_14.0_spmd, %region_15.0_spmd} | conditional | bytes 80 | solution.py:934
  196.2 31.4 %bwd.7 = (bf16[592,3072]{1,0:T(8,128)(2,1)}, bf16[592,768]{1,0:T(8,128)(2,1)}, bf16[3,592,768]{2,1,0:T(8,128)(2,1)}, bf16[592,768]{1,0:T(8,128)(2,1)}, bf16[592,...) custom-call(bf16[592,768]{1,0:T(8,128)(2,1)} %get-tuple-element.490.refs_0_,, ...), custom_call_target="tpu_custom_call" | custom-call | tf_op jit(solution)/shard_map/cond/branch_1_fun/bwd/pallas_call | solution.py:431
  228.0 16.1 %wgrad_mlp.3 = (bf16[1536,768]{1,0:T(8,128)(2,1)}, bf16[1536,768]{1,0:T(8,128)(2,1)}, bf16[768,1536]{1,0:T(8,128)(2,1)}, bf16[768,1536]{1,0:T(8,128)(2,1)}) custom-call(bf16[592,3072]{1,0:T(8,128)(2,1)} %get-tuple-element.657.act, bf16[592,768]{1,0:T(8,128)(2,1)} %get-tuple-element.658.n2, bf16[592,3072]{1,0:T(8,128)(2,1)} %get-tuple-element.659.pre, ...), custom_call_target="tpu_custom_call" | custom-call | tf_op jit(solution)/shard_map/wgrad_mlp/pallas_call | solution.py:473
  244.2 156.1 %ring.1 = (bf16[1536,768]{1,0:T(8,128)(2,1)}, bf16[768,1536]{1,0:T(8,128)(2,1)}, bf16[2304,384]{1,0:T(8,128)(2,1)}, bf16[384,768]{1,0:T(8,128)(2,1)}, f32[16,768]{1,0:T(8,128)}) custom-call(bf16[592,768]{1,0:T(8,128)(2,1)S(1)} %copy-done.6, bf16[3,592,768]{2,1,0:T(8,128)(2,1)S(1)} %copy-done.4, bf16[592,768]{1,0:T(8,128)(2,1)S(1)} %copy-done.2, ...), custom_call_target="tpu_custom_call" | custom-call | tf_op jit(solution)/shard_map/ring/pallas_call | solution.py:726
  400.3 9.4 %finish.1 = (f32[1,1536,768]{2,1,0:T(8,128)}, f32[1,768,1536]{2,1,0:T(8,128)}, f32[1,2304,384]{2,1,0:T(8,128)}, f32[1,384,768]{2,1,0:T(8,128)}, f32[1,768]{1,0:T...) custom-call(bf16[1536,768]{1,0:T(8,128)(2,1)} %get-tuple-element.673, ...), custom_call_target="tpu_custom_call" | custom-call | tf_op jit(solution)/shard_map/finish/pallas_call | solution.py:783
  409.8 0.9 copy-done.8
  410.7 5.3 %join.3 = bf16[2336,768]{1,0:T(8,128)(2,1)} custom-call(s32[3]{0:T(128)} %pad_add_fusion.meta_ref, bf16[592,768]{1,0:T(8,128)(2,1)S(1)} %copy-done.10, bf16[624,768]{1,0:T(8,128)(2,1)S(1)} %copy-done.5, bf16[592,768]{1,0:T(8,128)(2,1)} %copy-done.8, bf16[624,768]{1,0:T(8,128)(2,1)} %collective-permute-done.12.refs_3_), custom_call_target="tpu_custom_call" | custom-call | tf_op jit(solution)/shard_map/join/pallas_call | solution.py:865
  (67 shorter events, 2.7 us)
Async XLA Ops:
  0.6 11.9 %copy-start = (bf16[1,768,1536]{2,1,0:T(8,128)(2,1)S(1)}, bf16[1,768,1536]{2,1,0:T(8,128)(2,1)}, u32[]{:S(2)}) copy-start(bf16[1,768,1536]{2,1,0:T(8,128)(2,1)} %param.42) | copy-start | bytes 7077892
  0.7 11.9 %copy-start.1 = (bf16[1,384,768]{2,1,0:T(8,128)(2,1)S(1)}, bf16[1,384,768]{2,1,0:T(8,128)(2,1)}, u32[]{:S(2)}) copy-start(bf16[1,384,768]{2,1,0:T(8,128)(2,1)} %param.38) | copy-start | bytes 1769476
  0.7 11.9 %copy-start.11 = (f32[1,768]{1,0:T(1,128)S(1)}, f32[1,768]{1,0:T(1,128)}, u32[]{:S(2)}) copy-start(f32[1,768]{1,0:T(1,128)} %param.34) | copy-start | bytes 9220
  0.7 11.9 %copy-start.13 = (f32[1,768]{1,0:T(1,128)S(1)}, f32[1,768]{1,0:T(1,128)}, u32[]{:S(2)}) copy-start(f32[1,768]{1,0:T(1,128)} %param.35) | copy-start | bytes 9220
  0.7 11.9 %copy-start.14 = (f32[1,768]{1,0:T(1,128)S(1)}, f32[1,768]{1,0:T(1,128)}, u32[]{:S(2)}) copy-start(f32[1,768]{1,0:T(1,128)} %param.39) | copy-start | bytes 9220
  0.7 11.9 %copy-start.12 = (f32[1,768]{1,0:T(1,128)S(1)}, f32[1,768]{1,0:T(1,128)}, u32[]{:S(2)}) copy-start(f32[1,768]{1,0:T(1,128)} %param.40) | copy-start | bytes 9220
  0.7 11.8 %collective-permute-start.3 = (bf16[768,1536]{1,0:T(8,128)(2,1)}, bf16[768,1536]{1,0:T(8,128)(2,1)}, u32[]{:S(2)}, u32[]{:S(2)}) collective-permute-start(bf16[768,1536]{1,0:T(8,128)(2,1)} %bitcast.10), channel_id=1, source_target_pairs={{0,8},{8,0},{1,9},{9,1},{2,10},{10,2},{3,11},{11,3},{4,12},{12,4},... | collective-permute-start | bytes 7077896 | tf_op jit(solution)/shard_map/ppermute | solution.py:913
  1.3 11.3 %collective-permute-start.4 = (bf16[1536,768]{1,0:T(8,128)(2,1)}, bf16[1536,768]{1,0:T(8,128)(2,1)}, u32[]{:S(2)}, u32[]{:S(2)}) collective-permute-start(bf16[1536,768]{1,0:T(8,128)(2,1)} %bitcast.19), channel_id=1, source_target_pairs={{0,8},{8,0},{1,9},{9,1},{2,10},{10,2},{3,11},{11,3},{4,12},{12,4},... | collective-permute-start | bytes 7077896 | tf_op jit(solution)/shard_map/ppermute | solution.py:913
  1.3 11.2 %collective-permute-start.1 = (bf16[3,768,384]{2,1,0:T(8,128)(2,1)}, bf16[3,768,384]{2,1,0:T(8,128)(2,1)}, u32[]{:S(2)}, u32[]{:S(2)}) collective-permute-start(bf16[3,768,384]{2,1,0:T(8,128)(2,1)} %bitcast.28), channel_id=1, source_target_pairs={{0,8},{8,0},{1,9},{9,1},{2,10},{10,2},{3,11},{11,3},{4,12},{12,4},... | collective-permute-start | bytes 5308424 | tf_op jit(solution)/shard_map/ppermute | solution.py:913
  1.8 10.8 %collective-permute-start.2 = (bf16[384,768]{1,0:T(8,128)(2,1)}, bf16[384,768]{1,0:T(8,128)(2,1)S(1)}, u32[]{:S(2)}, u32[]{:S(2)}) collective-permute-start(bf16[384,768]{1,0:T(8,128)(2,1)} %bitcast.37), channel_id=1, source_target_pairs={{0,8},{8,0},{1,9},{9,1},{2,10},{10,2},{3,11},{11,3},{4,12},{12,4},... | collective-permute-start | bytes 1769480 | tf_op jit(solution)/shard_map/ppermute | solution.py:913
  4.4 8.1 %collective-permute-start = (f32[1,2304]{1,0:T(1,128)}, f32[1,2304]{1,0:T(1,128)}, u32[]{:S(2)}, u32[]{:S(2)}) collective-permute-start(f32[1,2304]{1,0:T(1,128)} %constant_dynamic-update-slice_fusion), channel_id=1, source_target_pairs={{0,8},{8,0},{1,9},{9,1},{2,10},{10,2},{3,11},{11,3},{4,12},{12,4},... | collective-permute-start | bytes 27656 | tf_op jit(solution)/shard_map/ppermute | solution.py:913
  35.8 36.3 %collective-permute-start.6 = (bf16[624,768]{1,0:T(8,128)(2,1)}, bf16[624,768]{1,0:T(8,128)(2,1)}, u32[]{:S(2)}, u32[]{:S(2)}) collective-permute-start(bf16[624,768]{1,0:T(8,128)(2,1)} %get-tuple-element.614), channel_id=1, source_target_pairs={{0,16},{1,17},{2,18},{3,19},{4,20},{5,21},{6,22},{7,23},{8,24},{9,... | collective-permute-start | bytes 2875400 | tf_op jit(solution)/shard_map/ppermute | solution.py:947
  65.3 21.9 %collective-permute-start.5 = (bf16[592,768]{1,0:T(8,128)(2,1)}, bf16[592,768]{1,0:T(8,128)(2,1)}, u32[]{:S(2)}, u32[]{:S(2)}) collective-permute-start(bf16[592,768]{1,0:T(8,128)(2,1)} %get-tuple-element.616), channel_id=1, source_target_pairs={{0,16},{1,17},{2,18},{3,19},{4,20},{5,21},{6,22},{7,23},{8,24},{9,... | collective-permute-start | bytes 2727944 | tf_op jit(solution)/shard_map/ppermute | solution.py:947
  79.4 55.8 %collective-permute-start.10 = (bf16[624,768]{1,0:T(8,128)(2,1)}, bf16[624,768]{1,0:T(8,128)(2,1)}, u32[]{:S(2)}, u32[]{:S(2)}) collective-permute-start(bf16[624,768]{1,0:T(8,128)(2,1)} %get-tuple-element.624), channel_id=1, source_target_pairs={{16,0},{17,1},{18,2},{19,3},{20,4},{21,5},{22,6},{23,7},{24,8},{25... | collective-permute-start | bytes 2875400 | tf_op jit(solution)/shard_map/ppermute | solution.py:948
  80.7 104.4 %collective-permute-start.8 = (bf16[624,768]{1,0:T(8,128)(2,1)}, bf16[624,768]{1,0:T(8,128)(2,1)}, u32[]{:S(2)}, u32[]{:S(2)}) collective-permute-start(bf16[624,768]{1,0:T(8,128)(2,1)} %get-tuple-element.627.refs_1_), channel_id=1, source_target_pairs={{0,8},{8,0},{1,9},{9,1},{2,10},{10,2},{3,11},{11,3},{4,12},{12,4},... | collective-permute-start | bytes 2875400 | tf_op jit(solution)/shard_map/ppermute | solution.py:913
  87.3 97.8 %collective-permute-start.7 = (bf16[592,768]{1,0:T(8,128)(2,1)}, bf16[592,768]{1,0:T(8,128)(2,1)}, u32[]{:S(2)}, u32[]{:S(2)}) collective-permute-start(bf16[592,768]{1,0:T(8,128)(2,1)} %get-tuple-element.626.refs_0_), channel_id=1, source_target_pairs={{0,8},{8,0},{1,9},{9,1},{2,10},{10,2},{3,11},{11,3},{4,12},{12,4},... | collective-permute-start | bytes 2727944 | tf_op jit(solution)/shard_map/ppermute | solution.py:913
  94.4 101.6 %collective-permute-start.9 = (bf16[592,768]{1,0:T(8,128)(2,1)}, bf16[592,768]{1,0:T(8,128)(2,1)}, u32[]{:S(2)}, u32[]{:S(2)}) collective-permute-start(bf16[592,768]{1,0:T(8,128)(2,1)} %get-tuple-element.634), channel_id=1, source_target_pairs={{16,0},{17,1},{18,2},{19,3},{20,4},{21,5},{22,6},{23,7},{24,8},{25... | collective-permute-start | bytes 2727944 | tf_op jit(solution)/shard_map/ppermute | solution.py:948
  163.2 246.5 %collective-permute-start.12 = (bf16[624,768]{1,0:T(8,128)(2,1)}, bf16[624,768]{1,0:T(8,128)(2,1)}, u32[]{:S(2)}, u32[]{:S(2)}) collective-permute-start(bf16[624,768]{1,0:T(8,128)(2,1)} %get-tuple-element.653.refs_1_), channel_id=1, source_target_pairs={{0,8},{8,0},{1,9},{9,1},{2,10},{10,2},{3,11},{11,3},{4,12},{12,4},... | collective-permute-start | bytes 2875400 | tf_op jit(solution)/shard_map/ppermute | solution.py:913
  171.7 13.5 %copy-start.9 = (bf16[592,768]{1,0:T(8,128)(2,1)S(1)}, bf16[592,768]{1,0:T(8,128)(2,1)}, u32[]{:S(2)}) copy-start(bf16[592,768]{1,0:T(8,128)(2,1)} %get-tuple-element.626.refs_0_) | copy-start | bytes 2727940
  227.8 182.0 %collective-permute-start.11 = (bf16[592,768]{1,0:T(8,128)(2,1)}, bf16[592,768]{1,0:T(8,128)(2,1)S(1)}, u32[]{:S(2)}, u32[]{:S(2)}) collective-permute-start(bf16[592,768]{1,0:T(8,128)(2,1)} %get-tuple-element.652.refs_0_), channel_id=1, source_target_pairs={{0,8},{8,0},{1,9},{9,1},{2,10},{10,2},{3,11},{11,3},{4,12},{12,4},... | collective-permute-start | bytes 2727944 | tf_op jit(solution)/shard_map/ppermute | solution.py:913
  227.8 16.2 %copy-start.2 = (bf16[592,768]{1,0:T(8,128)(2,1)S(1)}, bf16[592,768]{1,0:T(8,128)(2,1)}, u32[]{:S(2)}) copy-start(bf16[592,768]{1,0:T(8,128)(2,1)} %get-tuple-element.633.refs_2_) | copy-start | bytes 2727940
  227.9 16.2 %copy-start.4 = (bf16[3,592,768]{2,1,0:T(8,128)(2,1)S(1)}, bf16[3,592,768]{2,1,0:T(8,128)(2,1)}, u32[]{:S(2)}) copy-start(bf16[3,592,768]{2,1,0:T(8,128)(2,1)} %get-tuple-element.655.refs_1_) | copy-start | bytes 8183812
  227.9 16.2 %copy-start.6 = (bf16[592,768]{1,0:T(8,128)(2,1)S(1)}, bf16[592,768]{1,0:T(8,128)(2,1)}, u32[]{:S(2)}) copy-start(bf16[592,768]{1,0:T(8,128)(2,1)} %get-tuple-element.654.refs_0_) | copy-start | bytes 2727940
  227.9 16.2 %copy-start.7 = (bf16[592,768]{1,0:T(8,128)(2,1)S(1)}, bf16[592,768]{1,0:T(8,128)(2,1)}, u32[]{:S(2)}) copy-start(bf16[592,768]{1,0:T(8,128)(2,1)} %get-tuple-element.656.refs_3_) | copy-start | bytes 2727940
  227.9 16.2 %copy-start.15 = (f32[8,768]{1,0:T(8,128)S(1)}, f32[8,768]{1,0:T(8,128)}, u32[]{:S(2)}) copy-start(f32[8,768]{1,0:T(8,128)} %get-tuple-element.666.refs_13_) | copy-start | bytes 73732
  227.9 16.2 %copy-start.16 = (f32[8,768]{1,0:T(8,128)S(1)}, f32[8,768]{1,0:T(8,128)}, u32[]{:S(2)}) copy-start(f32[8,768]{1,0:T(8,128)} %get-tuple-element.667.refs_14_) | copy-start | bytes 73732
  227.9 16.2 %copy-start.17 = (f32[8,768]{1,0:T(8,128)S(1)}, f32[8,768]{1,0:T(8,128)}, u32[]{:S(2)}) copy-start(f32[8,768]{1,0:T(8,128)} %get-tuple-element.665.refs_12_) | copy-start | bytes 73732
  227.9 16.2 %copy-start.18 = (f32[8,768]{1,0:T(8,128)S(1)}, f32[8,768]{1,0:T(8,128)}, u32[]{:S(2)}) copy-start(f32[8,768]{1,0:T(8,128)} %get-tuple-element.670.refs_17_) | copy-start | bytes 73732
  227.9 16.2 %copy-start.19 = (f32[8,768]{1,0:T(8,128)S(1)}, f32[8,768]{1,0:T(8,128)}, u32[]{:S(2)}) copy-start(f32[8,768]{1,0:T(8,128)} %get-tuple-element.671.refs_18_) | copy-start | bytes 73732
  227.9 16.2 %copy-start.20 = (f32[8,768]{1,0:T(8,128)S(1)}, f32[8,768]{1,0:T(8,128)}, u32[]{:S(2)}) copy-start(f32[8,768]{1,0:T(8,128)} %get-tuple-element.669.refs_16_) | copy-start | bytes 73732
  227.9 16.2 %copy-start.21 = (f32[1,3072]{1,0:T(1,128)S(1)}, f32[1,3072]{1,0:T(1,128)}, u32[]{:S(2)}) copy-start(f32[1,3072]{1,0:T(1,128)} %get-tuple-element.668.refs_15_) | copy-start | bytes 36868
  228.0 16.2 %copy-start.22 = (f32[1,3072]{1,0:T(1,128)S(1)}, f32[1,3072]{1,0:T(1,128)}, u32[]{:S(2)}) copy-start(f32[1,3072]{1,0:T(1,128)} %get-tuple-element.672.refs_19_) | copy-start | bytes 36868
  (4 other events, 30.1 us)

commit v8 on v7

--- a/solution.py
+++ b/solution.py
@@ -552,8 +552,7 @@
 
 
 def ring_kernel(*refs, n, items, fold):
-    normed, dqkv, att, gb = refs[:4]
-    parts, sums = refs[4:8], refs[12:20]
+    sums = refs[12:20]
     at = 20
     results, vsum_ref = refs[at : at + n], refs[at + n]
     at += n + 1
@@ -565,9 +564,15 @@
     at += 4
     m = len(items)
     slots = refs[at : at + m]
-    vbuf, vother, vmine, vslot, send, recv, xsend, xrecv, flushed, vsend, vrecv, vxs, vxr = refs[
-        at + m :
+    vbuf, vother, vmine, vslot, send, recv, xsend, xrecv, flushed, vsend, vrecv, vxs, vxr, early_sem = refs[
+        at + m : at + m + 14
     ]
+    early = refs[at + m + 14 :]
+    normed, dqkv, att, gb = early[:4]
+    parts = early[4:]
+    fetches = fetch(list(zip(refs[:8], early)), early_sem)
+    for c in fetches:
+        c.start()
     mesh_id = pl.DeviceIdType.MESH
     me = lax.axis_index("dp")
     partner = {"tensor": 1 - lax.axis_index("tensor")}
@@ -649,6 +654,8 @@
     begin(range(2))
     vbuf[...] = vector_block([sums[i][...] + sums[4 + i][...] for i in range(4)])
     vexchange.start()
+    for c in fetches:
+        c.wait()
     d = normed.shape[1]
     half = d // 2
     for s in range(3):
@@ -723,9 +730,10 @@
     hbm = pl.BlockSpec(memory_space=pl.ANY)
     dma = pltpu.SemaphoreType.DMA
     vec = pltpu.VMEM((VEC_ROWS, d), F32)
+    early = (kept["normed"], back["dqkv"], kept["att"], back["gb"], *parts)
     out = pl.pallas_call(
         functools.partial(ring_kernel, n=n, items=items, fold=sums[3].shape[1] // (2 * d)),
-        in_specs=[vmem] * 10 + [hbm] * 2 + [vmem] * 8,
+        in_specs=[hbm] * 8 + [vmem] * 2 + [hbm] * 2 + [vmem] * 8,
         out_specs=[hbm] * n + [vmem],
         out_shape=[sds(a, BF) for a in shapes] + [sds((VEC_ROWS, d), F32)],
         scratch_shapes=[pltpu.VMEM(a, BF) for a in 2 * shapes + 2 * shapes[2:]]
@@ -734,13 +742,13 @@
             vec, vec, vec, pltpu.VMEM((RING - 1, VEC_ROWS, d), F32),
             dma((m, 2 * RING - 2)), dma((m, 2 * RING - 2)), dma((m, RING)), dma((m, RING)),
             dma((m, RING)),
-            dma((RING - 1,)), dma((RING - 1,)), dma, dma,
-        ],
+            dma((RING - 1,)), dma((RING - 1,)), dma, dma, dma((8,)),
+        ]
+        + [pltpu.VMEM(a.shape, BF) for a in early],
         compiler_params=params(collective_id=1, has_side_effects=True),
         name="ring",
     )(
-        kept["normed"], back["dqkv"], kept["att"], back["gb"], *parts, mlp[0], mlp[2], mlp[1],
-        mlp[3], *sums,
+        *early, mlp[0], mlp[2], mlp[1], mlp[3], *sums,
     )
     return out[:n], out[n]
 

time: 423 us -> 423 us (level)
  no operation moved by 1% of the time
where the time goes in v8:
time: 423 us; the launch traced here: 416 us
  Pallas kernels  332 us (78%)
  waiting for transfers between devices  52.7 us (12%)
  loops' own time  15.7 us (4%)
  starting transfers between devices  9.32 us (2%)
    pallas_call x1, Pallas kernels, ring(): pl.pallas_call(functools.partial(ring_kernel, n=n, items=items, fold=sums...  156 us
    pallas_call x2, Pallas kernels, backward(): pl.pallas_call(functools.partial(bwd_kernel, chunk=chunk), in_specs=[vmem...  58.6 us
    pallas_call x2, Pallas kernels, forward(): pl.pallas_call(functools.partial(fwd_kernel, chunk=chunk), in_specs=[vmem...  50.2 us
    ppermute x2, waiting for transfers between devices, body(): up_ = lambda array: lax.ppermute(array, 'section', [(1, 0)])  44.8 us
    pallas_call x2, Pallas kernels, wgrad_mlp(): pl.pallas_call(functools.partial(wgrad_mlp_kernel, more=len(init)), grid=...  29.5 us
    another operation x8, loops' own time, pick(): lax.cond(section == on, lambda: tuple(make()), lambda: blank(like) if oth...  15.7 us
    pallas_call x2, Pallas kernels, join(): pl.pallas_call(join_kernel, grid_spec=pltpu.PrefetchScalarGridSpec(num_sc...  10.9 us
    pallas_call x1, Pallas kernels, finish(): pl.pallas_call(functools.partial(finish_kernel, fold=fold), grid=(steps,)...  9.44 us
  transfers between devices with their start and end apart: 13, of which 4 were waited for; matrix products, arithmetic and copies ran while one was open for 1% of the time, Pallas kernels for 73%

profile of v8, /device:TPU:0, one launch (start us, length us, event | category | flops | bytes accessed | tf_op | source)
XLA Modules:
  0.0 416.0 jit_solution(4498273650087039583)
XLA Ops:
  1.9 0.7 copy.29
  2.5 0.6 constant_dynamic-update-slice_fusion.1
  3.1 1.3 constant_dynamic-update-slice_fusion
  4.9 1.2 pad_add_fusion.meta_ref
  6.1 4.5 %cut.2 = (bf16[592,768]{1,0:T(8,128)(2,1)}, bf16[624,768]{1,0:T(8,128)(2,1)}) custom-call(s32[3]{0:T(128)} %pad_add_fusion.meta_ref, bf16[2336,768]{1,0:T(8,128)(2,1)} %x_ref.2), custom_call_target="tpu_custom_call" | custom-call | tf_op jit(solution)/shard_map/cut/pallas_call | solution.py:837
  10.6 1.9 collective-permute-done
  12.6 23.2 %conditional.8 = ((bf16[624,768]{1,0:T(8,128)(2,1)}, bf16[3,624,768]{2,1,0:T(8,128)(2,1)}, bf16[624,768]{1,0:T(8,128)(2,1)}, f32[6,1,1536]{2,1,0:T(1,128)}, f32[...) conditional(s32[]{:T(128)} %convert_element_type.5, () %tuple.63, ...), branch_computations={%region_0.0_spmd, %region_1.0_spmd} | conditional | bytes 8 | solution.py:942
  12.6 23.2 %fwd.4 = (bf16[624,768]{1,0:T(8,128)(2,1)}, bf16[3,624,768]{2,1,0:T(8,128)(2,1)}, bf16[624,768]{1,0:T(8,128)(2,1)}, f32[6,1,1536]{2,1,0:T(1,128)}, f32[624,768]{...) custom-call(bf16[624,768]{1,0:T(8,128)(2,1)} %get-tuple-element.344., ...), custom_call_target="tpu_custom_call" | custom-call | tf_op jit(solution)/shard_map/cond/branch_1_fun/fwd/pallas_call | solution.py:259
  35.8 2.2 collective-permute-start.6
  38.1 27.2 %conditional.9 = ((bf16[592,768]{1,0:T(8,128)(2,1)}, bf16[3,592,768]{2,1,0:T(8,128)(2,1)}, bf16[592,768]{1,0:T(8,128)(2,1)}, f32[6,1,1280]{2,1,0:T(1,128)}, f32[...) conditional(s32[]{:T(128)} %convert_element_type.5, () %tuple.62, ...), branch_computations={%region_2.0_spmd, %region_3.0_spmd} | conditional | bytes 8 | solution.py:942
  38.3 27.0 %fwd.5 = (bf16[592,768]{1,0:T(8,128)(2,1)}, bf16[3,592,768]{2,1,0:T(8,128)(2,1)}, bf16[592,768]{1,0:T(8,128)(2,1)}, f32[6,1,1280]{2,1,0:T(1,128)}, f32[592,768]{...) custom-call(bf16[592,768]{1,0:T(8,128)(2,1)} %get-tuple-element.361., ...), custom_call_target="tpu_custom_call" | custom-call | tf_op jit(solution)/shard_map/cond/branch_1_fun/fwd/pallas_call | solution.py:259
  65.3 2.3 collective-permute-start.5
  67.6 4.5 %cut.3 = (bf16[592,768]{1,0:T(8,128)(2,1)}, bf16[624,768]{1,0:T(8,128)(2,1)}) custom-call(s32[3]{0:T(128)} %pad_add_fusion.meta_ref, bf16[2336,768]{1,0:T(8,128)(2,1)} %x_ref.3), custom_call_target="tpu_custom_call" | custom-call | tf_op jit(solution)/shard_map/cut/pallas_call | solution.py:837
  72.3 7.1 %conditional.11 = ((bf16[624,768]{1,0:T(8,128)(2,1)}, bf16[624,3072]{1,0:T(8,128)(2,1)}, bf16[624,768]{1,0:T(8,128)(2,1)}, bf16[3,624,768]{2,1,0:T(8,128)(2,1)},...) conditional(s32[]{:T(128)} %convert_element_type.4, () %tuple.68, ...), branch_computations={%region_6.0_spmd, %region_7.0_spmd} | conditional | bytes 80 | solution.py:942
  79.4 1.3 collective-permute-start.10
  81.2 6.0 %collective-permute-done.5 = bf16[592,768]{1,0:T(8,128)(2,1)} collective-permute-done((bf16[592,768]{1,0:T(8,128)(2,1)}, bf16[592,768]{1,0:T(8,128)(2,1)}, u32[]{:S(2)}, u32[]{:S(2)}) %collective-permute-start.5) | collective-permute-done | bytes 909344 | tf_op jit(solution)/shard_map/ppermute | solution.py:955
  87.4 7.0 %conditional.13 = ((bf16[592,768]{1,0:T(8,128)(2,1)}, bf16[592,3072]{1,0:T(8,128)(2,1)}, bf16[592,768]{1,0:T(8,128)(2,1)}, bf16[3,592,768]{2,1,0:T(8,128)(2,1)},...) conditional(s32[]{:T(128)} %convert_element_type.4, () %tuple.74, ...), branch_computations={%region_10.0_spmd, %region_11.0_spmd} | conditional | bytes 80 | solution.py:942
  94.4 1.3 collective-permute-start.9
  95.7 39.5 %collective-permute-done.10 = bf16[624,768]{1,0:T(8,128)(2,1)} collective-permute-done((bf16[624,768]{1,0:T(8,128)(2,1)}, bf16[624,768]{1,0:T(8,128)(2,1)}, u32[]{:S(2)}, u32[]{:S(2)}) %collective-permute-start.10) | collective-permute-done | bytes 958496 | tf_op jit(solution)/shard_map/ppermute | solution.py:956
  135.2 27.9 %conditional.14 = ((bf16[624,768]{1,0:T(8,128)(2,1)}, bf16[624,3072]{1,0:T(8,128)(2,1)}, bf16[624,768]{1,0:T(8,128)(2,1)}, bf16[3,624,768]{2,1,0:T(8,128)(2,1)},...) conditional(s32[]{:T(128)} %convert_element_type.5, ...), branch_computations={%region_12.0_spmd, %region_13.0_spmd} | conditional | bytes 80 | solution.py:942
  135.5 27.2 %bwd.6 = (bf16[624,3072]{1,0:T(8,128)(2,1)}, bf16[624,768]{1,0:T(8,128)(2,1)}, bf16[3,624,768]{2,1,0:T(8,128)(2,1)}, bf16[624,768]{1,0:T(8,128)(2,1)}, bf16[624,...) custom-call(bf16[624,768]{1,0:T(8,128)(2,1)} %get-tuple-element.464.refs_0_,, ...), custom_call_target="tpu_custom_call" | custom-call | tf_op jit(solution)/shard_map/cond/branch_1_fun/bwd/pallas_call | solution.py:431
  163.3 8.4 %wgrad_attn.1 = (bf16[3,768,384]{2,1,0:T(8,128)(2,1)}, bf16[3,768,384]{2,1,0:T(8,128)(2,1)}, bf16[384,768]{1,0:T(8,128)(2,1)}, bf16[384,768]{1,0:T(8,128)(2,1)}) custom-call(bf16[624,768]{1,0:T(8,128)(2,1)} %get-tuple-element.644.refs_0_, bf16[3,624,768]{2,1,0:T(8,128)(2,1)} %get-tuple-element.645.refs_1_, bf16[624,768]{1,0:T(8,128)(2,1)} %get-tuple-element.623.refs_2_, ...), custom_call_target="tpu_custom_call" | custom-call | tf_op jit(solution)/shard_map/wgrad_attn/pallas_call | solution.py:510
  171.7 13.4 %wgrad_mlp.2 = (bf16[1536,768]{1,0:T(8,128)(2,1)}, bf16[1536,768]{1,0:T(8,128)(2,1)}, bf16[768,1536]{1,0:T(8,128)(2,1)}, bf16[768,1536]{1,0:T(8,128)(2,1)}) custom-call(bf16[624,3072]{1,0:T(8,128)(2,1)S(1)} %copy-done.3, bf16[624,768]{1,0:T(8,128)(2,1)} %get-tuple-element.636.n2, bf16[624,3072]{1,0:T(8,128)(2,1)} %get-tuple-element.638.pre, ...), custom_call_target="tpu_custom_call" | custom-call | tf_op jit(solution)/shard_map/wgrad_mlp/pallas_call | solution.py:473
  185.1 5.7 %join.2 = bf16[2336,768]{1,0:T(8,128)(2,1)} custom-call(s32[3]{0:T(128)} %pad_add_fusion.meta_ref, bf16[592,768]{1,0:T(8,128)(2,1)S(1)} %copy-done.9, bf16[624,768]{1,0:T(8,128)(2,1)} %get-tuple-element.627.refs_1_, bf16[592,768]{1,0:T(8,128)(2,1)} %collective-permute-done.7.refs_2_, bf16[624,768]{1,0:T(8,128)(2,1)} %collective-permute-done.8.refs_3_), custom_call_target="tpu_custom_call" | custom-call | tf_op jit(solution)/shard_map/join/pallas_call | solution.py:873
  190.8 5.2 %collective-permute-done.9 = bf16[592,768]{1,0:T(8,128)(2,1)} collective-permute-done((bf16[592,768]{1,0:T(8,128)(2,1)}, bf16[592,768]{1,0:T(8,128)(2,1)}, u32[]{:S(2)}, u32[]{:S(2)}) %collective-permute-start.9) | collective-permute-done | bytes 909344 | tf_op jit(solution)/shard_map/ppermute | solution.py:956
  196.0 31.7 %conditional.15 = ((bf16[592,768]{1,0:T(8,128)(2,1)}, bf16[592,3072]{1,0:T(8,128)(2,1)}, bf16[592,768]{1,0:T(8,128)(2,1)}, bf16[3,592,768]{2,1,0:T(8,128)(2,1)},...) conditional(s32[]{:T(128)} %convert_element_type.5, ...), branch_computations={%region_14.0_spmd, %region_15.0_spmd} | conditional | bytes 80 | solution.py:942
  196.2 31.4 %bwd.7 = (bf16[592,3072]{1,0:T(8,128)(2,1)}, bf16[592,768]{1,0:T(8,128)(2,1)}, bf16[3,592,768]{2,1,0:T(8,128)(2,1)}, bf16[592,768]{1,0:T(8,128)(2,1)}, bf16[592,...) custom-call(bf16[592,768]{1,0:T(8,128)(2,1)} %get-tuple-element.490.refs_0_,, ...), custom_call_target="tpu_custom_call" | custom-call | tf_op jit(solution)/shard_map/cond/branch_1_fun/bwd/pallas_call | solution.py:431
  228.0 16.1 %wgrad_mlp.3 = (bf16[1536,768]{1,0:T(8,128)(2,1)}, bf16[1536,768]{1,0:T(8,128)(2,1)}, bf16[768,1536]{1,0:T(8,128)(2,1)}, bf16[768,1536]{1,0:T(8,128)(2,1)}) custom-call(bf16[592,3072]{1,0:T(8,128)(2,1)} %get-tuple-element.657.act, bf16[592,768]{1,0:T(8,128)(2,1)} %get-tuple-element.658.n2, bf16[592,3072]{1,0:T(8,128)(2,1)} %get-tuple-element.659.pre, ...), custom_call_target="tpu_custom_call" | custom-call | tf_op jit(solution)/shard_map/wgrad_mlp/pallas_call | solution.py:473
  244.2 155.9 %ring.1 = (bf16[1536,768]{1,0:T(8,128)(2,1)}, bf16[768,1536]{1,0:T(8,128)(2,1)}, bf16[2304,384]{1,0:T(8,128)(2,1)}, bf16[384,768]{1,0:T(8,128)(2,1)}, f32[16,768]{1,0:T(8,128)}) custom-call(bf16[592,768]{1,0:T(8,128)(2,1)S(1)} %copy-done.6, bf16[3,592,768]{2,1,0:T(8,128)(2,1)S(1)} %copy-done.4, bf16[592,768]{1,0:T(8,128)(2,1)S(1)} %copy-done.2, ...), custom_call_target="tpu_custom_call" | custom-call | tf_op jit(solution)/shard_map/ring/pallas_call | solution.py:734
  400.1 9.4 %finish.1 = (f32[1,1536,768]{2,1,0:T(8,128)}, f32[1,768,1536]{2,1,0:T(8,128)}, f32[1,2304,384]{2,1,0:T(8,128)}, f32[1,384,768]{2,1,0:T(8,128)}, f32[1,768]{1,0:T...) custom-call(bf16[1536,768]{1,0:T(8,128)(2,1)} %get-tuple-element.673, ...), custom_call_target="tpu_custom_call" | custom-call | tf_op jit(solution)/shard_map/finish/pallas_call | solution.py:791
  409.6 0.9 copy-done.8
  410.5 5.2 %join.3 = bf16[2336,768]{1,0:T(8,128)(2,1)} custom-call(s32[3]{0:T(128)} %pad_add_fusion.meta_ref, bf16[592,768]{1,0:T(8,128)(2,1)S(1)} %copy-done.10, bf16[624,768]{1,0:T(8,128)(2,1)S(1)} %copy-done.5, bf16[592,768]{1,0:T(8,128)(2,1)} %copy-done.8, bf16[624,768]{1,0:T(8,128)(2,1)} %collective-permute-done.12.refs_3_), custom_call_target="tpu_custom_call" | custom-call | tf_op jit(solution)/shard_map/join/pallas_call | solution.py:873
  (67 shorter events, 2.7 us)
Async XLA Ops:
  0.6 11.9 %copy-start = (bf16[1,768,1536]{2,1,0:T(8,128)(2,1)S(1)}, bf16[1,768,1536]{2,1,0:T(8,128)(2,1)}, u32[]{:S(2)}) copy-start(bf16[1,768,1536]{2,1,0:T(8,128)(2,1)} %param.42) | copy-start | bytes 7077892
  0.7 11.9 %copy-start.1 = (bf16[1,384,768]{2,1,0:T(8,128)(2,1)S(1)}, bf16[1,384,768]{2,1,0:T(8,128)(2,1)}, u32[]{:S(2)}) copy-start(bf16[1,384,768]{2,1,0:T(8,128)(2,1)} %param.38) | copy-start | bytes 1769476
  0.7 11.9 %copy-start.11 = (f32[1,768]{1,0:T(1,128)S(1)}, f32[1,768]{1,0:T(1,128)}, u32[]{:S(2)}) copy-start(f32[1,768]{1,0:T(1,128)} %param.34) | copy-start | bytes 9220
  0.7 11.9 %copy-start.13 = (f32[1,768]{1,0:T(1,128)S(1)}, f32[1,768]{1,0:T(1,128)}, u32[]{:S(2)}) copy-start(f32[1,768]{1,0:T(1,128)} %param.35) | copy-start | bytes 9220
  0.7 11.9 %copy-start.14 = (f32[1,768]{1,0:T(1,128)S(1)}, f32[1,768]{1,0:T(1,128)}, u32[]{:S(2)}) copy-start(f32[1,768]{1,0:T(1,128)} %param.39) | copy-start | bytes 9220
  0.7 11.9 %copy-start.12 = (f32[1,768]{1,0:T(1,128)S(1)}, f32[1,768]{1,0:T(1,128)}, u32[]{:S(2)}) copy-start(f32[1,768]{1,0:T(1,128)} %param.40) | copy-start | bytes 9220
  0.7 11.8 %collective-permute-start.3 = (bf16[768,1536]{1,0:T(8,128)(2,1)}, bf16[768,1536]{1,0:T(8,128)(2,1)}, u32[]{:S(2)}, u32[]{:S(2)}) collective-permute-start(bf16[768,1536]{1,0:T(8,128)(2,1)} %bitcast.10), channel_id=1, source_target_pairs={{0,8},{8,0},{1,9},{9,1},{2,10},{10,2},{3,11},{11,3},{4,12},{12,4},... | collective-permute-start | bytes 7077896 | tf_op jit(solution)/shard_map/ppermute | solution.py:921
  1.3 11.3 %collective-permute-start.4 = (bf16[1536,768]{1,0:T(8,128)(2,1)}, bf16[1536,768]{1,0:T(8,128)(2,1)}, u32[]{:S(2)}, u32[]{:S(2)}) collective-permute-start(bf16[1536,768]{1,0:T(8,128)(2,1)} %bitcast.19), channel_id=1, source_target_pairs={{0,8},{8,0},{1,9},{9,1},{2,10},{10,2},{3,11},{11,3},{4,12},{12,4},... | collective-permute-start | bytes 7077896 | tf_op jit(solution)/shard_map/ppermute | solution.py:921
  1.3 11.2 %collective-permute-start.1 = (bf16[3,768,384]{2,1,0:T(8,128)(2,1)}, bf16[3,768,384]{2,1,0:T(8,128)(2,1)}, u32[]{:S(2)}, u32[]{:S(2)}) collective-permute-start(bf16[3,768,384]{2,1,0:T(8,128)(2,1)} %bitcast.28), channel_id=1, source_target_pairs={{0,8},{8,0},{1,9},{9,1},{2,10},{10,2},{3,11},{11,3},{4,12},{12,4},... | collective-permute-start | bytes 5308424 | tf_op jit(solution)/shard_map/ppermute | solution.py:921
  1.8 10.8 %collective-permute-start.2 = (bf16[384,768]{1,0:T(8,128)(2,1)}, bf16[384,768]{1,0:T(8,128)(2,1)S(1)}, u32[]{:S(2)}, u32[]{:S(2)}) collective-permute-start(bf16[384,768]{1,0:T(8,128)(2,1)} %bitcast.37), channel_id=1, source_target_pairs={{0,8},{8,0},{1,9},{9,1},{2,10},{10,2},{3,11},{11,3},{4,12},{12,4},... | collective-permute-start | bytes 1769480 | tf_op jit(solution)/shard_map/ppermute | solution.py:921
  4.4 8.1 %collective-permute-start = (f32[1,2304]{1,0:T(1,128)}, f32[1,2304]{1,0:T(1,128)}, u32[]{:S(2)}, u32[]{:S(2)}) collective-permute-start(f32[1,2304]{1,0:T(1,128)} %constant_dynamic-update-slice_fusion), channel_id=1, source_target_pairs={{0,8},{8,0},{1,9},{9,1},{2,10},{10,2},{3,11},{11,3},{4,12},{12,4},... | collective-permute-start | bytes 27656 | tf_op jit(solution)/shard_map/ppermute | solution.py:921
  35.8 36.3 %collective-permute-start.6 = (bf16[624,768]{1,0:T(8,128)(2,1)}, bf16[624,768]{1,0:T(8,128)(2,1)}, u32[]{:S(2)}, u32[]{:S(2)}) collective-permute-start(bf16[624,768]{1,0:T(8,128)(2,1)} %get-tuple-element.614), channel_id=1, source_target_pairs={{0,16},{1,17},{2,18},{3,19},{4,20},{5,21},{6,22},{7,23},{8,24},{9,... | collective-permute-start | bytes 2875400 | tf_op jit(solution)/shard_map/ppermute | solution.py:955
  65.3 21.9 %collective-permute-start.5 = (bf16[592,768]{1,0:T(8,128)(2,1)}, bf16[592,768]{1,0:T(8,128)(2,1)}, u32[]{:S(2)}, u32[]{:S(2)}) collective-permute-start(bf16[592,768]{1,0:T(8,128)(2,1)} %get-tuple-element.616), channel_id=1, source_target_pairs={{0,16},{1,17},{2,18},{3,19},{4,20},{5,21},{6,22},{7,23},{8,24},{9,... | collective-permute-start | bytes 2727944 | tf_op jit(solution)/shard_map/ppermute | solution.py:955
  79.4 55.8 %collective-permute-start.10 = (bf16[624,768]{1,0:T(8,128)(2,1)}, bf16[624,768]{1,0:T(8,128)(2,1)}, u32[]{:S(2)}, u32[]{:S(2)}) collective-permute-start(bf16[624,768]{1,0:T(8,128)(2,1)} %get-tuple-element.624), channel_id=1, source_target_pairs={{16,0},{17,1},{18,2},{19,3},{20,4},{21,5},{22,6},{23,7},{24,8},{25... | collective-permute-start | bytes 2875400 | tf_op jit(solution)/shard_map/ppermute | solution.py:956
  80.7 104.4 %collective-permute-start.8 = (bf16[624,768]{1,0:T(8,128)(2,1)}, bf16[624,768]{1,0:T(8,128)(2,1)}, u32[]{:S(2)}, u32[]{:S(2)}) collective-permute-start(bf16[624,768]{1,0:T(8,128)(2,1)} %get-tuple-element.627.refs_1_), channel_id=1, source_target_pairs={{0,8},{8,0},{1,9},{9,1},{2,10},{10,2},{3,11},{11,3},{4,12},{12,4},... | collective-permute-start | bytes 2875400 | tf_op jit(solution)/shard_map/ppermute | solution.py:921
  87.3 97.8 %collective-permute-start.7 = (bf16[592,768]{1,0:T(8,128)(2,1)}, bf16[592,768]{1,0:T(8,128)(2,1)}, u32[]{:S(2)}, u32[]{:S(2)}) collective-permute-start(bf16[592,768]{1,0:T(8,128)(2,1)} %get-tuple-element.626.refs_0_), channel_id=1, source_target_pairs={{0,8},{8,0},{1,9},{9,1},{2,10},{10,2},{3,11},{11,3},{4,12},{12,4},... | collective-permute-start | bytes 2727944 | tf_op jit(solution)/shard_map/ppermute | solution.py:921
  94.4 101.6 %collective-permute-start.9 = (bf16[592,768]{1,0:T(8,128)(2,1)}, bf16[592,768]{1,0:T(8,128)(2,1)}, u32[]{:S(2)}, u32[]{:S(2)}) collective-permute-start(bf16[592,768]{1,0:T(8,128)(2,1)} %get-tuple-element.634), channel_id=1, source_target_pairs={{16,0},{17,1},{18,2},{19,3},{20,4},{21,5},{22,6},{23,7},{24,8},{25... | collective-permute-start | bytes 2727944 | tf_op jit(solution)/shard_map/ppermute | solution.py:956
  163.2 246.4 %collective-permute-start.12 = (bf16[624,768]{1,0:T(8,128)(2,1)}, bf16[624,768]{1,0:T(8,128)(2,1)}, u32[]{:S(2)}, u32[]{:S(2)}) collective-permute-start(bf16[624,768]{1,0:T(8,128)(2,1)} %get-tuple-element.653.refs_1_), channel_id=1, source_target_pairs={{0,8},{8,0},{1,9},{9,1},{2,10},{10,2},{3,11},{11,3},{4,12},{12,4},... | collective-permute-start | bytes 2875400 | tf_op jit(solution)/shard_map/ppermute | solution.py:921
  171.7 13.5 %copy-start.9 = (bf16[592,768]{1,0:T(8,128)(2,1)S(1)}, bf16[592,768]{1,0:T(8,128)(2,1)}, u32[]{:S(2)}) copy-start(bf16[592,768]{1,0:T(8,128)(2,1)} %get-tuple-element.626.refs_0_) | copy-start | bytes 2727940
  227.8 181.8 %collective-permute-start.11 = (bf16[592,768]{1,0:T(8,128)(2,1)}, bf16[592,768]{1,0:T(8,128)(2,1)S(1)}, u32[]{:S(2)}, u32[]{:S(2)}) collective-permute-start(bf16[592,768]{1,0:T(8,128)(2,1)} %get-tuple-element.652.refs_0_), channel_id=1, source_target_pairs={{0,8},{8,0},{1,9},{9,1},{2,10},{10,2},{3,11},{11,3},{4,12},{12,4},... | collective-permute-start | bytes 2727944 | tf_op jit(solution)/shard_map/ppermute | solution.py:921
  227.8 16.2 %copy-start.2 = (bf16[592,768]{1,0:T(8,128)(2,1)S(1)}, bf16[592,768]{1,0:T(8,128)(2,1)}, u32[]{:S(2)}) copy-start(bf16[592,768]{1,0:T(8,128)(2,1)} %get-tuple-element.633.refs_2_) | copy-start | bytes 2727940
  227.9 16.2 %copy-start.4 = (bf16[3,592,768]{2,1,0:T(8,128)(2,1)S(1)}, bf16[3,592,768]{2,1,0:T(8,128)(2,1)}, u32[]{:S(2)}) copy-start(bf16[3,592,768]{2,1,0:T(8,128)(2,1)} %get-tuple-element.655.refs_1_) | copy-start | bytes 8183812
  227.9 16.2 %copy-start.6 = (bf16[592,768]{1,0:T(8,128)(2,1)S(1)}, bf16[592,768]{1,0:T(8,128)(2,1)}, u32[]{:S(2)}) copy-start(bf16[592,768]{1,0:T(8,128)(2,1)} %get-tuple-element.654.refs_0_) | copy-start | bytes 2727940
  227.9 16.2 %copy-start.7 = (bf16[592,768]{1,0:T(8,128)(2,1)S(1)}, bf16[592,768]{1,0:T(8,128)(2,1)}, u32[]{:S(2)}) copy-start(bf16[592,768]{1,0:T(8,128)(2,1)} %get-tuple-element.656.refs_3_) | copy-start | bytes 2727940
  227.9 16.2 %copy-start.15 = (f32[8,768]{1,0:T(8,128)S(1)}, f32[8,768]{1,0:T(8,128)}, u32[]{:S(2)}) copy-start(f32[8,768]{1,0:T(8,128)} %get-tuple-element.666.refs_13_) | copy-start | bytes 73732
  227.9 16.2 %copy-start.16 = (f32[8,768]{1,0:T(8,128)S(1)}, f32[8,768]{1,0:T(8,128)}, u32[]{:S(2)}) copy-start(f32[8,768]{1,0:T(8,128)} %get-tuple-element.667.refs_14_) | copy-start | bytes 73732
  227.9 16.2 %copy-start.17 = (f32[8,768]{1,0:T(8,128)S(1)}, f32[8,768]{1,0:T(8,128)}, u32[]{:S(2)}) copy-start(f32[8,768]{1,0:T(8,128)} %get-tuple-element.665.refs_12_) | copy-start | bytes 73732
  227.9 16.2 %copy-start.18 = (f32[8,768]{1,0:T(8,128)S(1)}, f32[8,768]{1,0:T(8,128)}, u32[]{:S(2)}) copy-start(f32[8,768]{1,0:T(8,128)} %get-tuple-element.670.refs_17_) | copy-start | bytes 73732
  227.9 16.2 %copy-start.19 = (f32[8,768]{1,0:T(8,128)S(1)}, f32[8,768]{1,0:T(8,128)}, u32[]{:S(2)}) copy-start(f32[8,768]{1,0:T(8,128)} %get-tuple-element.671.refs_18_) | copy-start | bytes 73732
  227.9 16.2 %copy-start.20 = (f32[8,768]{1,0:T(8,128)S(1)}, f32[8,768]{1,0:T(8,128)}, u32[]{:S(2)}) copy-start(f32[8,768]{1,0:T(8,128)} %get-tuple-element.669.refs_16_) | copy-start | bytes 73732
  227.9 16.2 %copy-start.21 = (f32[1,3072]{1,0:T(1,128)S(1)}, f32[1,3072]{1,0:T(1,128)}, u32[]{:S(2)}) copy-start(f32[1,3072]{1,0:T(1,128)} %get-tuple-element.668.refs_15_) | copy-start | bytes 36868
  228.0 16.2 %copy-start.22 = (f32[1,3072]{1,0:T(1,128)S(1)}, f32[1,3072]{1,0:T(1,128)}, u32[]{:S(2)}) copy-start(f32[1,3072]{1,0:T(1,128)} %get-tuple-element.672.refs_19_) | copy-start | bytes 36868
  (4 other events, 30.1 us)
